TPU v7x, 32 devices: a whole 2x2x4 slice. The times are simulated.
32 devices in a mesh: seq: 8 (over z, x), fsdp: 4 (over y, core).
Axes of the slice: x: 2, y: 2, z: 4, core: 2. Of those that a mesh axis runs over, the one named last changes fastest.
Arguments:
- tokens: bfloat16 [8, 1024, 1536], P('fsdp', 'seq'), may hold values from -6 to 6
- segments: int32 [8, 1024], P('fsdp'), may hold values from 0 to 7, never falling along the last dimension, each value on 1 to 512 neighbouring positions
- gain_in: float32 [1536], replicated, may hold values from 0.5 to 1.5
- w_in: bfloat16 [1536, 6448], P(('seq', 'fsdp')), may hold values from -0.15625 to 0.15625
- conv_w: float32 [4, 3328], replicated, may hold values from -3 to 3
- conv_b: float32 [3328], replicated, may hold values from -3 to 3
- dt_bias: float32 [48], replicated, may hold values from -6 to -1
- a_log: float32 [48], replicated, may hold values from 0 to 2.5
- skip: float32 [48], replicated, may hold values from 0.5 to 1.5
- gain_out: float32 [3072], replicated, may hold values from 0.5 to 1.5
- w_out: bfloat16 [3072, 1536], P(('seq', 'fsdp')), may hold values from -0.109375 to 0.109375
- cotangent: bfloat16 [8, 1024, 1536], P('fsdp', 'seq'), may hold values from -6 to 6
Outputs:
- mixed: bfloat16 [8, 1024, 1536], P('fsdp', 'seq')
- tokens_grad: float32 [8, 1024, 1536], P('fsdp', 'seq')
- gain_in_grad: float32 [1536], replicated
- w_in_grad: float32 [1536, 6448], P(('seq', 'fsdp'))
- conv_w_grad: float32 [4, 3328], replicated
- conv_b_grad: float32 [3328], replicated
- dt_bias_grad: float32 [48], replicated
- a_log_grad: float32 [48], replicated
- skip_grad: float32 [48], replicated
- gain_out_grad: float32 [3072], replicated
- w_out_grad: float32 [3072, 1536], P(('seq', 'fsdp'))
Inputs may be any that keep to these rules, and one draw needn't show every extreme that they name: `segments`: document numbers never fall along a sequence and start at 0; each document spans 1 to 512 tokens, one exactly 512.
All inputs are finite; a program needn't handle non-finite values.
Results may differ from a plain program's by a relative error of at most 0.0098.
Values may be sent and summed in bfloat16 or wider, within the bound.
A program may use at most 320 MiB of HBM per device.

v0:
```python
import jax
import jax.numpy as jnp
from jax import lax
from jax.sharding import PartitionSpec as P

D = 1536
HEADS = 48
HEAD_DIM = 64
STATE = 128
KERNEL = 4
STRETCH = 256
INNER = 3072
PROJ = 6448


EPSILON = 1e-05
HIGHEST = lax.Precision.HIGHEST


def norm_rows(values, gain):
    return values * lax.rsqrt(jnp.mean(values * values, axis=-1, keepdims=True) + EPSILON) * gain


def gated_norm(mixed_rows, gate, gain):
    return norm_rows(mixed_rows * jax.nn.silu(gate), gain)


def causal_conv(values, seg, weight, bias):
    total = bias + weight[KERNEL - 1] * values
    for offset in range(1, KERNEL):
        shifted = jnp.concatenate(
            [jnp.zeros((offset, values.shape[1]), values.dtype), values[:-offset]], axis=0
        )
        earlier = jnp.concatenate([jnp.full((offset,), -1, jnp.int32), seg[:-offset]], axis=0)
        keep_mask = (earlier == seg)[:, None]
        total = total + weight[KERNEL - 1 - offset] * jnp.where(keep_mask, shifted, 0.0)
    return total


def state_mix(values, b_in, c_in, dt_raw, seg, dt_bias, a_log, skip):
    length = values.shape[0]
    head_count = dt_raw.shape[1]
    blocks = length // STRETCH
    step_size = jax.nn.softplus(dt_raw + dt_bias)
    rates = step_size * -jnp.exp(a_log)
    values_heads = values.reshape(length, head_count, HEAD_DIM)
    order = jnp.arange(STRETCH)
    causal = order[:, None] >= order[None, :]

    def one_block(carried, pieces):
        memory, prev_seg = carried
        x_blk, b_blk, c_blk, dt_blk, rate_blk, seg_blk = pieces
        cumul = jnp.cumsum(rate_blk, axis=0)
        same = causal & (seg_blk[:, None] == seg_blk[None, :])
        spans = cumul.T[:, :, None] - cumul.T[:, None, :]
        decays = jnp.where(same[None], jnp.exp(jnp.where(same[None], spans, 0.0)), 0.0)
        scores = jnp.dot(c_blk, b_blk.T, precision=HIGHEST)
        mixing = decays * scores[None] * dt_blk.T[:, None, :]
        inside = jnp.einsum("hts,shp->thp", mixing, x_blk, precision=HIGHEST)
        carry_on = jnp.where(seg_blk == prev_seg, 1.0, 0.0).astype(jnp.float32)
        entry = jnp.exp(cumul) * carry_on[:, None]
        outside = jnp.einsum("tn,hpn->thp", c_blk, memory, precision=HIGHEST) * entry[:, :, None]
        last_seg = seg_blk[-1]
        to_end = (
            jnp.where((seg_blk == last_seg)[:, None], jnp.exp(cumul[-1][None, :] - cumul), 0.0)
            * dt_blk
        )
        fresh = jnp.einsum("sh,shp,sn->hpn", to_end, x_blk, b_blk, precision=HIGHEST)
        kept_old = jnp.where(last_seg == prev_seg, 1.0, 0.0).astype(jnp.float32)
        memory = memory * (jnp.exp(cumul[-1]) * kept_old)[:, None, None] + fresh
        return ((memory, last_seg), inside + outside)

    pieces = (
        values_heads.reshape(blocks, STRETCH, head_count, HEAD_DIM),
        b_in.reshape(blocks, STRETCH, b_in.shape[1]),
        c_in.reshape(blocks, STRETCH, c_in.shape[1]),
        step_size.reshape(blocks, STRETCH, head_count),
        rates.reshape(blocks, STRETCH, head_count),
        seg.reshape(blocks, STRETCH),
    )
    start = (
        jnp.zeros((head_count, HEAD_DIM, b_in.shape[1]), jnp.float32),
        jnp.array(-1, jnp.int32),
    )
    final_state, outputs = lax.scan(jax.checkpoint(one_block), start, pieces)
    result = outputs.reshape(length, head_count, HEAD_DIM) + values_heads * skip[None, :, None]
    return result.reshape(length, head_count * HEAD_DIM)


def mix_layer(xbc, dt_raw, seg, conv_w, conv_b, dt_bias, a_log, skip):
    act = jax.nn.silu(causal_conv(xbc, seg, conv_w, conv_b))
    width = xbc.shape[1] - 2 * STATE
    return state_mix(
        act[:, :width],
        act[:, width : width + STATE],
        act[:, width + STATE :],
        dt_raw,
        seg,
        dt_bias,
        a_log,
        skip,
    )


def spread_last(piece, start, whole):
    zeros_full = jnp.zeros(piece.shape[:-1] + (whole,), jnp.float32)
    return lax.dynamic_update_slice_in_dim(zeros_full, piece, start, piece.ndim - 1)


def contract_rows(left, right):
    return lax.dot_general(
        left, right, (((0,), (0,)), ((), ())), preferred_element_type=jnp.float32
    )


def contract_cols(left, right):
    return lax.dot_general(
        left, right, (((1,), (1,)), ((), ())), preferred_element_type=jnp.float32
    )


def local(
    tokens,
    segments,
    gain_in,
    w_in,
    conv_w,
    conv_b,
    dt_bias,
    a_log,
    skip,
    gain_out,
    w_out,
    cotangent,
):
    seq_count = lax.axis_size("seq")
    seq_rank = lax.axis_index("seq")
    local_inner = INNER // seq_count
    local_heads = HEADS // seq_count
    x_start = seq_rank * local_inner
    h_start = seq_rank * local_heads
    conv_w_mine = jnp.concatenate(
        [lax.dynamic_slice_in_dim(conv_w, x_start, local_inner, 1), conv_w[:, INNER:]], axis=1
    )
    conv_b_mine = jnp.concatenate(
        [lax.dynamic_slice_in_dim(conv_b, x_start, local_inner, 0), conv_b[INNER:]], axis=0
    )
    dt_bias_mine = lax.dynamic_slice_in_dim(dt_bias, h_start, local_heads, 0)
    a_log_mine = lax.dynamic_slice_in_dim(a_log, h_start, local_heads, 0)
    skip_mine = lax.dynamic_slice_in_dim(skip, h_start, local_heads, 0)
    held = (
        lax.all_gather(w_in, ("seq", "fsdp"), axis=0, tiled=True),
        lax.all_gather(w_out, ("seq", "fsdp"), axis=0, tiled=True),
    )
    big_start = (jnp.zeros((D, PROJ), jnp.float32), jnp.zeros((INNER, D), jnp.float32))
    small_start = (
        jnp.zeros_like(gain_in),
        jnp.zeros_like(gain_out),
        jnp.zeros_like(conv_w_mine),
        jnp.zeros_like(conv_b_mine),
        jnp.zeros_like(dt_bias_mine),
        jnp.zeros_like(a_log_mine),
        jnp.zeros_like(skip_mine),
    )

    def layer(totals, inputs_now):
        big_sums, small_sums = totals
        rows_in, seg_whole, grad_rows = inputs_now
        full_in, full_out = held
        rows_wide = rows_in.astype(jnp.float32)
        normed, pull_in = jax.vjp(norm_rows, rows_wide, gain_in)
        normed_low = normed.astype(jnp.bfloat16)
        projected = jnp.dot(normed_low, full_in, preferred_element_type=jnp.float32).astype(
            jnp.bfloat16
        )
        gate_low = projected[:, :INNER]
        x_low = projected[:, INNER : 2 * INNER]
        bc_low = projected[:, 2 * INNER : 2 * INNER + 2 * STATE]
        dt_low = projected[:, 2 * INNER + 2 * STATE :]
        x_heads, dt_heads = (
            lax.all_to_all(x_low, "seq", split_axis=1, concat_axis=0, tiled=True),
            lax.all_to_all(dt_low, "seq", split_axis=1, concat_axis=0, tiled=True),
        )
        bc_whole = lax.all_gather(bc_low, "seq", axis=0, tiled=True)
        mixed_in = jnp.concatenate([x_heads, bc_whole], axis=1).astype(jnp.float32)

        def local_mix(xbc, dt_raw, weight, bias, bias_dt, log_rate, skip_coef):
            return mix_layer(xbc, dt_raw, seg_whole, weight, bias, bias_dt, log_rate, skip_coef)

        y_heads, pull_mix = jax.vjp(
            local_mix,
            mixed_in,
            dt_heads.astype(jnp.float32),
            conv_w_mine,
            conv_b_mine,
            dt_bias_mine,
            a_log_mine,
            skip_mine,
        )
        y_rows = lax.all_to_all(
            y_heads.astype(jnp.bfloat16), "seq", split_axis=0, concat_axis=1, tiled=True
        )
        y_normed, pull_gate = jax.vjp(
            gated_norm, y_rows.astype(jnp.float32), gate_low.astype(jnp.float32), gain_out
        )
        y_low = y_normed.astype(jnp.bfloat16)
        result = (rows_wide + jnp.dot(y_low, full_out, preferred_element_type=jnp.float32)).astype(
            jnp.bfloat16
        )
        part_out = contract_rows(y_low, grad_rows)
        grad_yn = contract_cols(grad_rows, full_out)
        grad_y, grad_gate, grad_gain_out = pull_gate(grad_yn)
        grad_y_heads = lax.all_to_all(
            grad_y.astype(jnp.bfloat16), "seq", split_axis=1, concat_axis=0, tiled=True
        )
        grad_xbc, grad_dt, grad_cw, grad_cb, grad_db, grad_al, grad_sk = pull_mix(
            grad_y_heads.astype(jnp.float32)
        )
        width = x_heads.shape[1]
        grad_bc = lax.psum_scatter(
            grad_xbc[:, width:], "seq", scatter_dimension=0, tiled=True
        ).astype(jnp.bfloat16)
        grad_x, grad_dt_rows = (
            lax.all_to_all(
                grad_xbc[:, :width].astype(jnp.bfloat16),
                "seq",
                split_axis=0,
                concat_axis=1,
                tiled=True,
            ),
            lax.all_to_all(
                grad_dt.astype(jnp.bfloat16), "seq", split_axis=0, concat_axis=1, tiled=True
            ),
        )
        grad_proj = jnp.concatenate(
            [grad_gate.astype(jnp.bfloat16), grad_x, grad_bc, grad_dt_rows], axis=1
        )
        part_in = contract_rows(normed_low, grad_proj)
        grad_normed = contract_cols(grad_proj, full_in)
        grad_rows_in, grad_gain_in = pull_in(grad_normed)
        grad_rows_in = grad_rows_in + grad_rows.astype(jnp.float32)
        big_sums = (big_sums[0] + part_in, big_sums[1] + part_out)
        terms = (grad_gain_in, grad_gain_out, grad_cw, grad_cb, grad_db, grad_al, grad_sk)
        small_sums = tuple((left + right for left, right in zip(small_sums, terms)))
        return ((big_sums, small_sums), (result, grad_rows_in))

    (big_sums, small_sums), (outputs, input_grads) = lax.scan(
        layer, (big_start, small_start), (tokens, segments, cotangent)
    )
    w_in_grad, w_out_grad = (
        lax.psum_scatter(big_sums[0], ("seq", "fsdp"), scatter_dimension=0, tiled=True),
        lax.psum_scatter(big_sums[1], ("seq", "fsdp"), scatter_dimension=0, tiled=True),
    )
    sum_gain_in, sum_gain_out, sum_cw, sum_cb, sum_db, sum_al, sum_sk = small_sums
    conv_w_full = jnp.concatenate(
        [spread_last(sum_cw[:, :local_inner], x_start, INNER), sum_cw[:, local_inner:]], axis=1
    )
    conv_b_full = jnp.concatenate(
        [spread_last(sum_cb[:local_inner], x_start, INNER), sum_cb[local_inner:]], axis=0
    )
    reduced = lax.psum(
        (
            sum_gain_in,
            sum_gain_out,
            conv_w_full,
            conv_b_full,
            spread_last(sum_db, h_start, HEADS),
            spread_last(sum_al, h_start, HEADS),
            spread_last(sum_sk, h_start, HEADS),
        ),
        ("seq", "fsdp"),
    )
    return (
        outputs,
        input_grads,
        reduced[0],
        w_in_grad,
        reduced[2],
        reduced[3],
        reduced[4],
        reduced[5],
        reduced[6],
        reduced[1],
        w_out_grad,
    )


def solution(mesh):
    placed = (
        P("fsdp", "seq", None),
        P("fsdp", None),
        P(),
        P(("seq", "fsdp"), None),
        P(),
        P(),
        P(),
        P(),
        P(),
        P(),
        P(("seq", "fsdp"), None),
        P("fsdp", "seq", None),
    )
    return jax.shard_map(
        local,
        mesh=mesh,
        in_specs=placed,
        out_specs=(
            P("fsdp", "seq", None),
            P("fsdp", "seq", None),
            P(),
            P(("seq", "fsdp"), None),
            P(),
            P(),
            P(),
            P(),
            P(),
            P(),
            P(("seq", "fsdp"), None),
        ),
        check_vma=False,
    )
```

profile of v0, /device:TPU:1, one launch (start us, length us, event | category | flops | bytes accessed | tf_op | source)
XLA Modules:
  0.0 2252.1 jit_solution(6600027177787615443)
XLA Ops:
  14.4 81.1 %all-gather.5.cloned.1.call-done = bf16[3072,1536]{1,0:T(8,128)(2,1)} async-done(((bf16[96,1536]{1,0:T(8,128)(2,1)}), bf16[3072,1536]{1,0:T(8,128)(2,1)}) %all-gather.5.cloned.1.call-update) | async-done | bytes 9437200 | tf_op jit(solution)/shard_map/all_gather | solution.py:153
  95.5 131.7 %all-gather.3.cloned.1.call-done = bf16[1536,6448]{1,0:T(8,128)(2,1)} async-done(((bf16[48,6448]{1,0:T(8,128)(2,1)}), bf16[1536,6448]{1,0:T(8,128)(2,1)}) %all-gather.3.cloned.1.call-update) | async-done | bytes 19808272 | tf_op jit(solution)/shard_map/all_gather | solution.py:152
  227.2 1291.8 %while.135 = (s32[]{:T(128)}, f32[1536,6448]{0,1:T(8,128)}, f32[3072,1536]{1,0:T(8,128)}, f32[1536]{0:T(1024)}, f32[3072]{0:T(1024)}, /*index=5*/f32[4,640]{1,0:...) while((s32[]{:T(128)}, f32[1536,6448]{0,1:T(8,128)}, ...), condition=%wide.region_34.35_spmd.clone, body=%wide.region_0.34_spmd.clone.sunk | while | flops 13716637696 | bytes 453811968 | solution.py:247
  229.2 12.2 convolution_convert_fusion.2
  256.1 35.6 %all_gather.19 = bf16[1024,256]{0,1:T(8,128)(2,1)S(1)} all-gather(bf16[128,256]{0,1:T(8,128)(2,1)S(1)} %slice.383), channel_id=1, replica_groups=mesh['seq'=8,'fsdp'=4] {'seq'}, dimensions={0}, use_global_device_ids=true | all-gather | bytes 589824 | tf_op jit(solution)/shard_map/while/body/eval_jaxpr/all_gather | solution.py:184
  310.4 97.6 %while.136 = (s32[]{:T(128)}, f32[6,64,128]{2,1,0:T(8,128)S(1)}, s32[]{:T(128)}, f32[4,256,6,64]{1,0,3,2:T(4,128)}, f32[4,6,64,128]{3,2,1,0:T(8,128)}, /*index=5...) while((s32[]{:T(128)}, f32[6,64,128]{2,1,0:T(8,128)S(1)}, ...), condition=%wide.region_5.5_spmd.clone, body=%wide.region_2.4_spmd.clone.sunk | while | flops 707549952 | bytes 5849031 | solution.py:85
  320.4 9.5 dynamic_update_slice.135
  344.9 9.5 dynamic_update_slice.135
  369.3 9.5 dynamic_update_slice.135
  393.7 9.5 dynamic_update_slice.135
  410.5 20.5 all_to_all.205
  447.8 10.7 select_add_fusion.13
  474.1 275.2 %while.137 = (s32[]{:T(128)}, f32[6,64,128]{2,1,0:T(8,128)}, f32[4,256,6,64]{1,0,3,2:T(4,128)}, f32[4,256,128]{2,1,0:T(8,128)}, f32[4,256,128]{2,1,0:T(8,128)}, ...) while((s32[]{:T(128)}, f32[6,64,128]{2,1,0:T(8,128)}, ...), condition=%wide.region_20.20_spmd.clone, body=%wide.region_8.19_spmd.clone.sunk | while | flops 1670560512 | bytes 19600960 | solution.py:85
  519.1 7.6 reduce-window.70
  531.5 9.5 dynamic_update_slice.141
  588.2 7.6 reduce-window.70
  600.5 9.5 dynamic_update_slice.141
  657.2 7.6 reduce-window.70
  669.5 9.5 dynamic_update_slice.141
  726.2 7.6 reduce-window.70
  738.5 9.5 dynamic_update_slice.141
  791.4 45.0 %reduce-scatter.8.cloned.1.call-done = f32[128,256]{0,1:T(8,128)} async-done(((f32[1024,256]{0,1:T(8,128)}), f32[128,256]{0,1:T(8,128)}) %reduce-scatter.8.cloned.1.call-update) | async-done | bytes 131088 | tf_op jit(solution)/shard_map/while/body/eval_jaxpr/reduce_scatter | solution.py:220
  837.4 10.2 fusion.262
  847.7 16.1 select_add_fusion.12
  867.0 12.2 convolution_convert_fusion.2
  893.9 33.7 %all_gather.19 = bf16[1024,256]{0,1:T(8,128)(2,1)S(1)} all-gather(bf16[128,256]{0,1:T(8,128)(2,1)S(1)} %slice.383), channel_id=1, replica_groups=mesh['seq'=8,'fsdp'=4] {'seq'}, dimensions={0}, use_global_device_ids=true | all-gather | bytes 589824 | tf_op jit(solution)/shard_map/while/body/eval_jaxpr/all_gather | solution.py:184
  946.3 97.6 %while.136 = (s32[]{:T(128)}, f32[6,64,128]{2,1,0:T(8,128)S(1)}, s32[]{:T(128)}, f32[4,256,6,64]{1,0,3,2:T(4,128)}, f32[4,6,64,128]{3,2,1,0:T(8,128)}, /*index=5...) while((s32[]{:T(128)}, f32[6,64,128]{2,1,0:T(8,128)S(1)}, ...), condition=%wide.region_5.5_spmd.clone, body=%wide.region_2.4_spmd.clone.sunk | while | flops 707549952 | bytes 5849031 | solution.py:85
  956.3 9.5 dynamic_update_slice.135
  980.7 9.5 dynamic_update_slice.135
  1005.2 9.5 dynamic_update_slice.135
  1029.6 9.5 dynamic_update_slice.135
  1046.4 15.2 all_to_all.205
  1079.2 16.2 select_add_fusion.13
  1105.8 275.3 %while.137 = (s32[]{:T(128)}, f32[6,64,128]{2,1,0:T(8,128)}, f32[4,256,6,64]{1,0,3,2:T(4,128)}, f32[4,256,128]{2,1,0:T(8,128)}, f32[4,256,128]{2,1,0:T(8,128)}, ...) while((s32[]{:T(128)}, f32[6,64,128]{2,1,0:T(8,128)}, ...), condition=%wide.region_20.20_spmd.clone, body=%wide.region_8.19_spmd.clone.sunk | while | flops 1670560512 | bytes 19600960 | solution.py:85
  1150.9 7.6 reduce-window.70
  1163.2 9.5 dynamic_update_slice.141
  1219.9 7.6 reduce-window.70
  1232.2 9.5 dynamic_update_slice.141
  1288.9 7.6 reduce-window.70
  1301.2 9.5 dynamic_update_slice.141
  1370.2 9.5 dynamic_update_slice.141
  1423.7 51.3 %reduce-scatter.8.cloned.1.call-done = f32[128,256]{0,1:T(8,128)} async-done(((f32[1024,256]{0,1:T(8,128)}), f32[128,256]{0,1:T(8,128)}) %reduce-scatter.8.cloned.1.call-update) | async-done | bytes 131088 | tf_op jit(solution)/shard_map/while/body/eval_jaxpr/reduce_scatter | solution.py:220
  1476.0 10.2 fusion.262
  1486.3 29.3 %select_add_fusion.12 = f32[1536,6448]{0,1:T(8,128)} fusion(f32[1536,6448]{0,1:T(8,128)} %get-tuple-element.2421, pred[]{:T(512)S(6)} %compare.26, bf16[128,48]{0,1:T(8,128)(2,1)S(1)} %all_to_all.197, bf16[128,256]{0,1:T(8,128)(2,1)S(1)} %convert_element_type.323, bf16[128,3072]{0,1:T(8,128)(2,1)} %bitcast.480, ...), kind=kOutput, calls=%fused_computation.138.clone.1 | convolution fusion | flops 2562654208 | bytes 81285640 | tf_op jit(solution)/shard_map/while/body/eval_jaxpr/dot_general | solution.py:111
  1526.9 36.8 %copy.295 = f32[1536,6448]{1,0:T(8,128)} copy(f32[1536,6448]{0,1:T(8,128)} %get-tuple-element.1091) | data formatting | bytes 79233024 | tf_op jit(solution)/shard_map/while | solution.py:247
  1563.7 87.3 %all-reduce.20.cloned.1.call-done = (f32[1536]{0:T(1024)}, f32[4,3328]{1,0:T(4,128)}, f32[3328]{0:T(1024)}, f32[48]{0:T(128)}, f32[48]{0:T(128)}, /*index=5*/f32[48]{0:T(128)}, f32[3072]{0:T(1024)}) async-done(((f32[1536]{0:T(1024)}, f32[4,3328]{1,0:T(4,128)}, f32[3328]{0:T(1024)}, f32[48]{0:T(128)}, f32[48]{0:T(128)}, /*index=5*/f32[48]{0:T(128)}, f32[3072]{0:T(1024)}), (f32[1536]{0:T(1024)}, ...) | async-done | bytes 85584 | tf_op jit(solution)/shard_map/psum | solution.py:261
  1651.0 213.8 %reduce-scatter.6.cloned.1.call-done = f32[96,1536]{1,0:T(8,128)} async-done(((f32[3072,1536]{1,0:T(8,128)}), f32[96,1536]{1,0:T(8,128)}) %reduce-scatter.6.cloned.1.call-update) | async-done | bytes 589840 | tf_op jit(solution)/shard_map/reduce_scatter | solution.py:252
  1864.8 371.6 %reduce-scatter.4.cloned.1.call-done = f32[48,6448]{1,0:T(8,128)} async-done(((f32[1536,6448]{1,0:T(8,128)}), f32[48,6448]{1,0:T(8,128)}) %reduce-scatter.4.cloned.1.call-update) | async-done | bytes 1238032 | tf_op jit(solution)/shard_map/reduce_scatter | solution.py:251
  (1498 shorter events, 763.8 us)
Async XLA Ops:
  7.2 88.3 %all-gather.5.cloned.1.call-start = ((), (), s32[]{:S(2)}) async-start(), calls=%async_computation.10 | async-start | bytes 9732096 | tf_op jit(solution)/shard_map/all_gather | solution.py:153
  7.9 219.3 %all-gather.3.cloned.1.call-start = ((), (), s32[]{:S(2)}) async-start(), calls=%async_computation.9 | async-start | bytes 20680704 | tf_op jit(solution)/shard_map/all_gather | solution.py:152
  227.5 64.2 %copy-start.82 = (f32[1,6]{1,0:T(1,128)}, f32[1,6]{1,0:T(1,128)S(1)}, u32[]{:S(2)}) copy-start(f32[1,6]{1,0:T(1,128)S(1)} %get-tuple-element.2479) | copy-start | bytes 76 | tf_op jit(solution)/shard_map/while
  227.5 64.2 %copy-start.84 = (f32[6]{0:T(128)}, f32[6]{0:T(128)S(1)}, u32[]{:S(2)}) copy-start(f32[6]{0:T(128)S(1)} %get-tuple-element.2478) | copy-start | bytes 76 | tf_op jit(solution)/shard_map/while
  227.5 65.0 %copy-start.78 = (f32[640]{0:T(1024)}, f32[640]{0:T(1024)S(1)}, u32[]{:S(2)}) copy-start(f32[640]{0:T(1024)S(1)} %get-tuple-element.2474) | copy-start | bytes 7684 | tf_op jit(solution)/shard_map/while
  242.1 8.8 all-to-all-start
  250.9 40.9 %all-to-all-start.1 = ((bf16[128,8,384]{0,2,1:T(8,128)(2,1)}), bf16[128,8,384]{0,2,1:T(8,128)(2,1)S(1)}, u32[]{:S(2)}, u32[]{:S(2)}) async-start(bf16[128,8,384]{0,2,1:T(8,128)(2,1)} %bitcast.460), calls=%async_computation.1 | async-start | bytes 1572864 | tf_op jit(solution)/shard_map/while/body/eval_jaxpr/all_to_all | solution.py:181
  255.9 154.0 %copy-start.58 = (f32[384]{0:T(512)}, f32[384]{0:T(512)S(1)}, u32[]{:S(2)}) copy-start(f32[384]{0:T(512)S(1)} %mul.1652) | copy-start | bytes 4612 | tf_op jit(solution)/shard_map/while
  256.1 189.8 %copy-start.68 = (pred[1024]{0:T(1024)(128)(4,1)}, pred[1024]{0:T(1024)(128)(4,1)S(1)}, u32[]{:S(2)}) copy-start(pred[1024]{0:T(1024)(128)(4,1)S(1)} %get-tuple-element.2163) | copy-start | bytes 3076 | tf_op jit(solution)/shard_map/while
  256.1 190.5 %copy-start.66 = (pred[1024]{0:T(1024)(128)(4,1)}, pred[1024]{0:T(1024)(128)(4,1)S(1)}, u32[]{:S(2)}) copy-start(pred[1024]{0:T(1024)(128)(4,1)S(1)} %get-tuple-element.2161) | copy-start | bytes 3076 | tf_op jit(solution)/shard_map/while
  256.1 191.0 %copy-start.64 = (pred[1024]{0:T(1024)(128)(4,1)}, pred[1024]{0:T(1024)(128)(4,1)S(1)}, u32[]{:S(2)}) copy-start(pred[1024]{0:T(1024)(128)(4,1)S(1)} %get-tuple-element.2165) | copy-start | bytes 3076 | tf_op jit(solution)/shard_map/while
  441.1 22.5 %all-to-all-start.3 = ((bf16[128,8,384]{0,2,1:T(8,128)(2,1)}), bf16[128,8,384]{0,2,1:T(8,128)(2,1)S(1)}, u32[]{:S(2)}, u32[]{:S(2)}) async-start(bf16[128,8,384]{0,2,1:T(8,128)(2,1)} %bitcast.472), calls=%async_computation.3 | async-start | bytes 1572864 | tf_op jit(solution)/shard_map/while/body/eval_jaxpr/all_to_all | solution.py:213
  445.2 391.2 %reduce-scatter.8.cloned.1.call-start = ((), (), s32[]{:S(2)}) async-start(), calls=%async_computation.14 | async-start | bytes 1179648 | tf_op jit(solution)/shard_map/while/body/eval_jaxpr/reduce_scatter | solution.py:220
  769.7 10.2 all-to-all-start.4
  779.9 57.4 %all-to-all-start.5 = ((bf16[8,128,384]{1,2,0:T(8,128)(2,1)}), bf16[8,128,384]{1,2,0:T(8,128)(2,1)}, u32[]{:S(2)}, u32[]{:S(2)}) async-start(bf16[8,128,384]{1,2,0:T(8,128)(2,1)} %copy_bitcast_fusion.12), calls=%async_computation.6 | async-start | bytes 1572864 | tf_op jit(solution)/shard_map/while/body/eval_jaxpr/all_to_all | solution.py:224
  784.5 52.9 %copy-start.16 = (bf16[128,3072]{0,1:T(8,128)(2,1)S(1)}, bf16[128,3072]{0,1:T(8,128)(2,1)}, u32[]{:S(2)}) copy-start(bf16[128,3072]{0,1:T(8,128)(2,1)} %get-tuple-element.2189) | copy-start | bytes 2359300 | tf_op jit(solution)/shard_map/while
  784.5 52.9 %copy-start.43 = (f32[1536]{0:T(1024)S(1)}, f32[1536]{0:T(1024)}, u32[]{:S(2)}) copy-start(f32[1536]{0:T(1024)} %get-tuple-element.2473) | copy-start | bytes 18436 | tf_op jit(solution)/shard_map/while
  790.7 56.9 %copy-start.63 = (f32[3072]{0:T(1024)}, f32[3072]{0:T(1024)S(1)}, u32[]{:S(2)}) copy-start(f32[3072]{0:T(1024)S(1)} %select_add_fusion.15) | copy-start | bytes 36868 | tf_op jit(solution)/shard_map/while
  791.2 56.4 %copy-start.95 = (f32[6]{0:T(128)}, f32[6]{0:T(128)S(1)}, u32[]{:S(2)}) copy-start(f32[6]{0:T(128)S(1)} %fusion.264) | copy-start | bytes 76 | tf_op jit(solution)/shard_map/while
  791.3 56.4 %copy-start.97 = (f32[6]{0:T(128)}, f32[6]{0:T(128)S(1)}, u32[]{:S(2)}) copy-start(f32[6]{0:T(128)S(1)} %get-tuple-element.2467) | copy-start | bytes 76 | tf_op jit(solution)/shard_map/while
  791.3 56.4 %copy-start.99 = (f32[6]{0:T(128)}, f32[6]{0:T(128)S(1)}, u32[]{:S(2)}) copy-start(f32[6]{0:T(128)S(1)} %get-tuple-element.2468) | copy-start | bytes 76 | tf_op jit(solution)/shard_map/while
  791.3 56.3 %copy-start.81 = (f32[640]{0:T(1024)}, f32[640]{0:T(1024)S(1)}, u32[]{:S(2)}) copy-start(f32[640]{0:T(1024)S(1)} %select_add_fusion.17) | copy-start | bytes 7684 | tf_op jit(solution)/shard_map/while
  791.3 56.3 %copy-start.73 = (f32[4,640]{1,0:T(4,128)}, f32[4,640]{1,0:T(4,128)S(1)}, u32[]{:S(2)}) copy-start(f32[4,640]{1,0:T(4,128)S(1)} %select_add_fusion.16) | copy-start | bytes 30724 | tf_op jit(solution)/shard_map/while
  865.3 62.3 %copy-start.82 = (f32[1,6]{1,0:T(1,128)}, f32[1,6]{1,0:T(1,128)S(1)}, u32[]{:S(2)}) copy-start(f32[1,6]{1,0:T(1,128)S(1)} %get-tuple-element.2479) | copy-start | bytes 76 | tf_op jit(solution)/shard_map/while
  865.3 62.3 %copy-start.84 = (f32[6]{0:T(128)}, f32[6]{0:T(128)S(1)}, u32[]{:S(2)}) copy-start(f32[6]{0:T(128)S(1)} %get-tuple-element.2478) | copy-start | bytes 76 | tf_op jit(solution)/shard_map/while
  865.3 63.1 %copy-start.78 = (f32[640]{0:T(1024)}, f32[640]{0:T(1024)S(1)}, u32[]{:S(2)}) copy-start(f32[640]{0:T(1024)S(1)} %get-tuple-element.2474) | copy-start | bytes 7684 | tf_op jit(solution)/shard_map/while
  879.9 8.7 all-to-all-start
  888.7 39.1 %all-to-all-start.1 = ((bf16[128,8,384]{0,2,1:T(8,128)(2,1)}), bf16[128,8,384]{0,2,1:T(8,128)(2,1)S(1)}, u32[]{:S(2)}, u32[]{:S(2)}) async-start(bf16[128,8,384]{0,2,1:T(8,128)(2,1)} %bitcast.460), calls=%async_computation.1 | async-start | bytes 1572864 | tf_op jit(solution)/shard_map/while/body/eval_jaxpr/all_to_all | solution.py:181
  893.6 152.2 %copy-start.58 = (f32[384]{0:T(512)}, f32[384]{0:T(512)S(1)}, u32[]{:S(2)}) copy-start(f32[384]{0:T(512)S(1)} %mul.1652) | copy-start | bytes 4612 | tf_op jit(solution)/shard_map/while
  893.8 183.4 %copy-start.68 = (pred[1024]{0:T(1024)(128)(4,1)}, pred[1024]{0:T(1024)(128)(4,1)S(1)}, u32[]{:S(2)}) copy-start(pred[1024]{0:T(1024)(128)(4,1)S(1)} %get-tuple-element.2163) | copy-start | bytes 3076 | tf_op jit(solution)/shard_map/while
  893.8 184.1 %copy-start.66 = (pred[1024]{0:T(1024)(128)(4,1)}, pred[1024]{0:T(1024)(128)(4,1)S(1)}, u32[]{:S(2)}) copy-start(pred[1024]{0:T(1024)(128)(4,1)S(1)} %get-tuple-element.2161) | copy-start | bytes 3076 | tf_op jit(solution)/shard_map/while
  893.8 184.7 %copy-start.64 = (pred[1024]{0:T(1024)(128)(4,1)}, pred[1024]{0:T(1024)(128)(4,1)S(1)}, u32[]{:S(2)}) copy-start(pred[1024]{0:T(1024)(128)(4,1)S(1)} %get-tuple-element.2165) | copy-start | bytes 3076 | tf_op jit(solution)/shard_map/while
  1071.8 23.6 %all-to-all-start.3 = ((bf16[128,8,384]{0,2,1:T(8,128)(2,1)}), bf16[128,8,384]{0,2,1:T(8,128)(2,1)S(1)}, u32[]{:S(2)}, u32[]{:S(2)}) async-start(bf16[128,8,384]{0,2,1:T(8,128)(2,1)} %bitcast.472), calls=%async_computation.3 | async-start | bytes 1572864 | tf_op jit(solution)/shard_map/while/body/eval_jaxpr/all_to_all | solution.py:213
  1077.0 398.0 %reduce-scatter.8.cloned.1.call-start = ((), (), s32[]{:S(2)}) async-start(), calls=%async_computation.14 | async-start | bytes 1179648 | tf_op jit(solution)/shard_map/while/body/eval_jaxpr/reduce_scatter | solution.py:220
  1401.5 10.8 all-to-all-start.4
  1412.3 63.6 %all-to-all-start.5 = ((bf16[8,128,384]{1,2,0:T(8,128)(2,1)}), bf16[8,128,384]{1,2,0:T(8,128)(2,1)}, u32[]{:S(2)}, u32[]{:S(2)}) async-start(bf16[8,128,384]{1,2,0:T(8,128)(2,1)} %copy_bitcast_fusion.12), calls=%async_computation.6 | async-start | bytes 1572864 | tf_op jit(solution)/shard_map/while/body/eval_jaxpr/all_to_all | solution.py:224
  1416.9 59.0 %copy-start.16 = (bf16[128,3072]{0,1:T(8,128)(2,1)S(1)}, bf16[128,3072]{0,1:T(8,128)(2,1)}, u32[]{:S(2)}) copy-start(bf16[128,3072]{0,1:T(8,128)(2,1)} %get-tuple-element.2189) | copy-start | bytes 2359300 | tf_op jit(solution)/shard_map/while
  1416.9 59.0 %copy-start.43 = (f32[1536]{0:T(1024)S(1)}, f32[1536]{0:T(1024)}, u32[]{:S(2)}) copy-start(f32[1536]{0:T(1024)} %get-tuple-element.2473) | copy-start | bytes 18436 | tf_op jit(solution)/shard_map/while
  1416.9 59.0 %copy-start.77 = (f32[128]{0:T(128)S(1)}, f32[128]{0:T(128)}, u32[]{:S(2)}) copy-start(f32[128]{0:T(128)} %copy-done.76) | copy-start | bytes 1540 | tf_op jit(solution)/shard_map/while
  1423.0 63.2 %copy-start.63 = (f32[3072]{0:T(1024)}, f32[3072]{0:T(1024)S(1)}, u32[]{:S(2)}) copy-start(f32[3072]{0:T(1024)S(1)} %select_add_fusion.15) | copy-start | bytes 36868 | tf_op jit(solution)/shard_map/while
  1423.5 62.6 %copy-start.95 = (f32[6]{0:T(128)}, f32[6]{0:T(128)S(1)}, u32[]{:S(2)}) copy-start(f32[6]{0:T(128)S(1)} %fusion.264) | copy-start | bytes 76 | tf_op jit(solution)/shard_map/while
  1423.6 62.6 %copy-start.97 = (f32[6]{0:T(128)}, f32[6]{0:T(128)S(1)}, u32[]{:S(2)}) copy-start(f32[6]{0:T(128)S(1)} %get-tuple-element.2467) | copy-start | bytes 76 | tf_op jit(solution)/shard_map/while
  1423.6 62.6 %copy-start.99 = (f32[6]{0:T(128)}, f32[6]{0:T(128)S(1)}, u32[]{:S(2)}) copy-start(f32[6]{0:T(128)S(1)} %get-tuple-element.2468) | copy-start | bytes 76 | tf_op jit(solution)/shard_map/while
  1423.6 62.6 %copy-start.81 = (f32[640]{0:T(1024)}, f32[640]{0:T(1024)S(1)}, u32[]{:S(2)}) copy-start(f32[640]{0:T(1024)S(1)} %select_add_fusion.17) | copy-start | bytes 7684 | tf_op jit(solution)/shard_map/while
  1423.7 62.5 %copy-start.73 = (f32[4,640]{1,0:T(4,128)}, f32[4,640]{1,0:T(4,128)S(1)}, u32[]{:S(2)}) copy-start(f32[4,640]{1,0:T(4,128)S(1)} %select_add_fusion.16) | copy-start | bytes 30724 | tf_op jit(solution)/shard_map/while
  1519.0 131.9 %all-reduce.20.cloned.1.call-start = ((), (), s32[]{:S(2)}) async-start(), calls=%async_computation.13 | async-start | bytes 183296 | tf_op jit(solution)/shard_map/psum | solution.py:261
  1526.2 338.5 %reduce-scatter.6.cloned.1.call-start = ((), (), s32[]{:S(2)}) async-start(), calls=%async_computation.12 | async-start | bytes 19464192 | tf_op jit(solution)/shard_map/reduce_scatter | solution.py:252
  1526.8 709.5 %reduce-scatter.4.cloned.1.call-start = ((), (), s32[]{:S(2)}) async-start(), calls=%async_computation.11 | async-start | bytes 41361408 | tf_op jit(solution)/shard_map/reduce_scatter | solution.py:251
  (304 other events, 2392.2 us)
Sparse Core Ops, SparseCore 0:
  10.9 84.5 all-gather.4
  98.4 128.7 all-gather.2
  769.0 67.3 reduce-scatter.7
  1400.8 74.1 reduce-scatter.7
  1527.1 123.7 all-reduce.19
  1657.8 206.9 reduce-scatter.5
  1871.8 364.5 reduce-scatter.3
where the time goes:
time: 2270 us; the launch traced here: 2250 us
  waiting for transfers between devices  1000 us (44%)
  local copies, waits for them, and re-layouts  464 us (20%)
  matrix products  337 us (15%)
  other arithmetic  257 us (11%)
  blocking collectives  105 us (5%)
  starting transfers between devices  43.1 us (2%)
  loops' own time  27.7 us (1%)
    reduce_scatter x1, waiting for transfers between devices, local(): lax.psum_scatter(big_sums[0], ('seq', 'fsdp'), scatter_dimension=0, tiled...  372 us
    reduce_scatter x1, waiting for transfers between devices, local(): lax.psum_scatter(big_sums[1], ('seq', 'fsdp'), scatter_dimension=0, tiled...  214 us
    dynamic_update_slice x48, local copies, waits for them, and re-layouts, state_mix(): final_state, outputs = lax.scan(jax.checkpoint(one_block), start, pieces)  180 us
    all_gather x1, waiting for transfers between devices, local(): lax.all_gather(w_in, ('seq', 'fsdp'), axis=0, tiled=True)  132 us
    another operation x60, other arithmetic  122 us
    reduce_scatter x2, waiting for transfers between devices, layer(): lax.psum_scatter(grad_xbc[:, width:], 'seq', scatter_dimension=0, tiled=T...  96.3 us
    psum x1, waiting for transfers between devices, local(): lax.psum((sum_gain_in, sum_gain_out, conv_w_full, conv_b_full, spread_las...  87.3 us
    all_gather x1, waiting for transfers between devices, local(): lax.all_gather(w_out, ('seq', 'fsdp'), axis=0, tiled=True)  81.1 us
  transfers between devices with their start and end apart: 17, of which 12 were waited for; matrix products, arithmetic and copies ran while one was open for 4% of the time, Pallas kernels for 0%

commit v1 on v0

v1 whole, which is shorter than its diff:
```python
import functools

import jax
import jax.numpy as jnp
from jax import lax
from jax.experimental import pallas as pl
from jax.experimental.pallas import tpu as pltpu
from jax.sharding import PartitionSpec as P

D = 1536
HEADS = 48
HEAD_DIM = 64
STATE = 128
KERNEL = 4
INNER = 3072
LANES = 128
HALO = 16
EPSILON = 1e-05
F32 = jnp.float32
BF16 = jnp.bfloat16


def mm(a, b):
    return jnp.dot(a.astype(BF16), b.astype(BF16), preferred_element_type=F32)


def mm_tr(a, b):
    return lax.dot_general(
        a.astype(BF16), b.astype(BF16), (((1,), (1,)), ((), ())), preferred_element_type=F32
    )


def tr_mm(a, b):
    return lax.dot_general(
        a.astype(BF16), b.astype(BF16), (((0,), (0,)), ((), ())), preferred_element_type=F32
    )


def pieces(a, count):
    out = []
    for _ in range(count - 1):
        part = a.astype(BF16)
        out.append(part)
        a = a - part.astype(F32)
    out.append(a.astype(BF16))
    return out


def ones_mm(ones, a, count):
    return sum(jnp.dot(ones, part, preferred_element_type=F32) for part in pieces(a, count))


def mm_ones(a, ones, count):
    return sum(jnp.dot(part, ones, preferred_element_type=F32) for part in pieces(a, count))


def mm_ones_tr(a, ones, count):
    return sum(
        lax.dot_general(part, ones, (((1,), (1,)), ((), ())), preferred_element_type=F32)
        for part in pieces(a, count)
    )


def iota(shape, dim):
    return lax.broadcasted_iota(jnp.int32, shape, dim)


def softplus(v):
    return jnp.maximum(v, 0.0) + jnp.log1p(jnp.exp(-jnp.abs(v)))


def sigmoid(v):
    return 1.0 / (1.0 + jnp.exp(-v))


def causal_conv(ext, current, halo, weight, bias, offset):
    length = current.shape[0]
    ext[0:HALO, :] = halo
    ext[HALO : HALO + length, :] = current
    total = bias + weight[KERNEL - 1 : KERNEL, :] * current
    for back in range(1, KERNEL):
        shifted = jnp.where(offset >= back, ext[pl.ds(HALO - back, length), :], 0.0)
        total = total + weight[KERNEL - 1 - back : KERNEL - back, :] * shifted
    return total


def head_tiles(width):
    out = []
    for start in range(0, width, LANES):
        size = min(LANES, width - start)
        heads = [start // HEAD_DIM + i for i in range(size // HEAD_DIM)]
        out.append((start, size, heads))
    return out


def masked_heads(tile, heads):
    if len(heads) == 1:
        return tile
    lane = iota(tile.shape, 1) // HEAD_DIM
    return jnp.concatenate(
        [jnp.where(lane == i, tile, jnp.zeros_like(tile)) for i in range(len(heads))], axis=0
    )


def expander(width):
    return (iota((LANES, width), 1) // HEAD_DIM == iota((LANES, width), 0)).astype(BF16)


def chunk_common(x, xh, tail, tailh, offset, params, ext_x, ext_t, width):
    wx, bx, wt, bt, heads_p = params
    length = x.shape[0]
    conv_x = causal_conv(ext_x, x.astype(F32), xh.astype(F32), wx, bx, offset)
    conv_t = causal_conv(
        ext_t,
        tail[:, : 2 * STATE].astype(F32),
        tailh[:, : 2 * STATE].astype(F32),
        wt,
        bt,
        offset,
    )
    raw = tail[:, 2 * STATE :].astype(F32) + heads_p[0:1, :]
    step = softplus(raw)
    decay_rate = jnp.exp(heads_p[1:2, :])
    rate = -step * decay_rate
    tril = (iota((length, length), 0) >= iota((length, length), 1)).astype(BF16)
    cumul = ones_mm(tril, rate, 3)
    spread = expander(width)
    row = iota((length, 1), 0)
    entry = jnp.where(offset > row.astype(F32), jnp.exp(cumul), 0.0)
    last_off = offset[length - 1 : length, :]
    same_last = row.astype(F32) >= (length - 1) - last_off
    to_end = jnp.where(same_last, jnp.exp(cumul[length - 1 : length, :] - cumul), 0.0)
    step_x = mm_ones(step, spread, 2)
    entry_x = mm_ones(entry, spread, 2)
    end_x = mm_ones(to_end, spread, 2)
    return conv_x, conv_t, raw, step, rate, decay_rate, cumul, spread, step_x, entry_x, end_x


def forward_kernel(
    x_ref, xh_ref, tail_ref, tailh_ref, off_ref, wx_ref, bx_ref, wt_ref, bt_ref, hp_ref, skip_ref,
    y_ref, state_ref, memory, ext_x, ext_t,
):
    seqs, length, width = x_ref.shape[1:]

    @pl.when(pl.program_id(0) == 0)
    def _():
        memory[...] = jnp.zeros_like(memory)

    params = (wx_ref[...], bx_ref[...], wt_ref[...], bt_ref[...], hp_ref[...])
    for q in range(seqs):
        offset = off_ref[0, q]
        conv_x, conv_t, _, _, _, _, cumul, _, step_x, entry_x, end_x = chunk_common(
            x_ref[0, q], xh_ref[0, q], tail_ref[0, q], tailh_ref[0, q], offset, params,
            ext_x.at[q], ext_t.at[q], width,
        )
        xs = conv_x * sigmoid(conv_x)
        act_t = conv_t * sigmoid(conv_t)
        bs = act_t[:, :STATE].astype(BF16)
        cs = act_t[:, STATE:].astype(BF16)
        scaled = xs * step_x
        scores = mm_tr(cs, bs)
        gap = iota((length, length), 0) - iota((length, length), 1)
        same = (gap >= 0) & (gap.astype(F32) <= offset)
        cumul_t = cumul.T
        old = memory[q]
        old_low = old.astype(BF16)
        state_ref[0, q] = old_low
        outside = mm(cs, old_low) * entry_x + skip_ref[...] * xs
        for start, size, heads in head_tiles(width):
            mixing = []
            for head in heads:
                spans = cumul[:, head : head + 1] - cumul_t[head : head + 1, :]
                decays = jnp.exp(jnp.where(same, spans, -1e30))
                mixing.append((decays * scores).astype(BF16))
            tile = masked_heads(scaled[:, start : start + size].astype(BF16), heads)
            mix = mixing[0] if len(heads) == 1 else jnp.concatenate(mixing, axis=1)
            inside = jnp.dot(mix, tile, preferred_element_type=F32)
            y_ref[0, q, :, start : start + size] = (
                inside + outside[:, start : start + size]
            ).astype(BF16)
        fresh = tr_mm(bs, scaled * end_x)
        memory[q] = old * entry_x[length - 1 : length, :] + fresh


def backward_kernel(
    x_ref, xh_ref, tail_ref, tailh_ref, off_ref, offr_ref, rem_ref, dy_ref, state_ref,
    wx_ref, bx_ref, wt_ref, bt_ref, hp_ref, skip_ref,
    dx_ref, dtail_ref, gx_ref, gt_ref, gh_ref,
    memory, ext_x, ext_t, next_x, next_t,
):
    seqs, length, width = x_ref.shape[1:]

    @pl.when(pl.program_id(0) == 0)
    def _():
        memory[...] = jnp.zeros_like(memory)
        gx_ref[...] = jnp.zeros_like(gx_ref)
        gt_ref[...] = jnp.zeros_like(gt_ref)
        gh_ref[...] = jnp.zeros_like(gh_ref)
        next_x[:, length:, :] = jnp.zeros_like(next_x[:, length:, :])
        next_t[:, length:, :] = jnp.zeros_like(next_t[:, length:, :])

    params = (wx_ref[...], bx_ref[...], wt_ref[...], bt_ref[...], hp_ref[...])
    for q in range(seqs):
        offset = off_ref[0, q]
        conv_x, conv_t, raw, step, rate, decay_rate, cumul, spread, step_x, entry_x, end_x = (
            chunk_common(
                x_ref[0, q], xh_ref[0, q], tail_ref[0, q], tailh_ref[0, q], offset, params,
                ext_x.at[q], ext_t.at[q], width,
            )
        )
        sig_x = sigmoid(conv_x)
        xs = conv_x * sig_x
        slope_x = sig_x + xs * (1.0 - sig_x)
        sig_t = sigmoid(conv_t)
        act_t = conv_t * sig_t
        slope_t = sig_t + act_t * (1.0 - sig_t)
        bs = act_t[:, :STATE].astype(BF16)
        cs = act_t[:, STATE:].astype(BF16)
        scaled = xs * step_x
        scaled_low = scaled.astype(BF16)
        dy_low = dy_ref[0, q]
        dy = dy_low.astype(F32)
        scores = mm_tr(bs, cs)
        rows, cols = iota((length, length), 0), iota((length, length), 1)
        gap = cols - rows
        same = (gap >= 0) & (gap.astype(F32) <= offr_ref[0, q])
        strict = gap > 0
        upper = (rows >= cols).astype(BF16)
        cumul_t = cumul.T
        old = state_ref[0, q]
        grad_state = memory[q]
        state_low = grad_state.astype(BF16)
        grad_scores = jnp.zeros((length, length), F32)
        grad_scaled = []
        inside_rows = []
        for start, size, heads in head_tiles(width):
            dy_tile = masked_heads(dy_low[:, start : start + size], heads)
            grad_mix = mm_tr(scaled_low[:, start : start + size], dy_tile)
            mixing = []
            for place, head in enumerate(heads):
                spans = cumul_t[head : head + 1, :] - cumul[:, head : head + 1]
                decays = jnp.exp(jnp.where(same, spans, -1e30))
                weighted = grad_mix[:, place * length : (place + 1) * length] * decays
                grad_scores = grad_scores + weighted
                mixing.append((decays * scores).astype(BF16))
                terms = jnp.where(strict, weighted * scores, 0.0).astype(BF16)
                sums = jnp.dot(terms, upper, preferred_element_type=F32)
                inside_rows.append(
                    jnp.sum(jnp.where(strict, sums, 0.0), axis=0, keepdims=True)
                )
            mix = mixing[0] if len(heads) == 1 else jnp.concatenate(mixing, axis=1)
            grad_scaled.append(jnp.dot(mix, dy_tile, preferred_element_type=F32))
        inside_rows.append(jnp.zeros((LANES - len(inside_rows), length), F32))
        inside = jnp.concatenate(inside_rows, axis=0).T
        from_end = mm(bs, state_low) * end_x
        grad_scaled = jnp.concatenate(grad_scaled, axis=1) + from_end
        entry_dy = dy * entry_x
        entry_dy_low = entry_dy.astype(BF16)
        out_terms = mm(cs, old) * entry_dy
        end_terms = scaled * from_end
        grad_step = mm_ones_tr(xs * grad_scaled, spread, 2)
        out_terms = mm_ones_tr(out_terms, spread, 2)
        end_terms = mm_ones_tr(end_terms, spread, 2)
        keep_row = entry_x[length - 1 : length, :]
        carried = jnp.sum(grad_state * old.astype(F32), axis=0, keepdims=True) * keep_row
        carried = mm_ones_tr(jnp.broadcast_to(carried, (8, width)), spread, 2)[0:1, :]
        triu = (cols >= rows).astype(BF16)
        below = (rows > cols).astype(BF16)
        grad_rate = inside + ones_mm(triu, out_terms, 2) + ones_mm(below, end_terms, 2) + carried
        grad_step = grad_step - decay_rate * grad_rate
        grad_raw = grad_step * sigmoid(raw)
        grad_scores_low = grad_scores.astype(BF16)
        grad_b = mm(grad_scores_low, cs) + mm_tr(scaled * end_x, state_low)
        grad_c = tr_mm(grad_scores_low, bs) + mm_tr(entry_dy_low, old)
        memory[q] = grad_state * keep_row + tr_mm(cs, entry_dy_low)
        conv_grad_x = (skip_ref[...] * dy + step_x * grad_scaled) * slope_x
        conv_grad_t = jnp.concatenate([grad_b, grad_c], axis=1) * slope_t

        remain = rem_ref[0, q]
        for grad, ext, nxt, weight, out, sums, cols_of in (
            (conv_grad_x, ext_x.at[q], next_x.at[q], params[0], dx_ref, gx_ref, width),
            (conv_grad_t, ext_t.at[q], next_t.at[q], params[2], dtail_ref, gt_ref, 2 * STATE),
        ):
            current = ext[pl.ds(HALO, length), :]
            sums[KERNEL : KERNEL + 1, :] += jnp.sum(grad, axis=0, keepdims=True)
            sums[KERNEL - 1 : KERNEL, :] += jnp.sum(grad * current, axis=0, keepdims=True)
            nxt[0:length, :] = grad
            total = weight[KERNEL - 1 : KERNEL, :] * grad
            for back in range(1, KERNEL):
                tap = KERNEL - 1 - back
                shifted = jnp.where(offset >= back, ext[pl.ds(HALO - back, length), :], 0.0)
                sums[tap : tap + 1, :] += jnp.sum(grad * shifted, axis=0, keepdims=True)
                ahead = jnp.where(remain >= back, nxt[pl.ds(back, length), :], 0.0)
                total = total + weight[tap : tap + 1, :] * ahead
            nxt[length:, :] = grad[0:HALO, :]
            out[0, q, :, :cols_of] = total.astype(BF16)
        gx_ref[KERNEL + 1 : KERNEL + 2, :] += jnp.sum(dy * xs, axis=0, keepdims=True)
        dtail_ref[0, q, :, 2 * STATE :] = grad_raw.astype(BF16)
        gh_ref[0:1, :] += jnp.sum(grad_raw, axis=0, keepdims=True)
        gh_ref[1:2, :] += jnp.sum(grad_rate * rate, axis=0, keepdims=True)


def whole_spec(shape):
    return pl.BlockSpec(shape, lambda i: (0,) * len(shape))


def forward_mix(x, tail, off_col, wx, bx, wt, bt, heads_p, skip_x):
    steps, seqs, length, width = x.shape
    wide = tail.shape[3]

    def block(cols):
        return pl.BlockSpec((1, seqs, length, cols), lambda i: (i, 0, 0, 0))

    def before(cols):
        return pl.BlockSpec(
            (1, seqs, HALO, cols), lambda i: (jnp.maximum(i - 1, 0), 0, length // HALO - 1, 0)
        )

    return pl.pallas_call(
        forward_kernel,
        grid=(steps,),
        in_specs=[
            block(width), before(width), block(wide), before(wide), block(1),
            whole_spec(wx.shape), whole_spec(bx.shape), whole_spec(wt.shape), whole_spec(bt.shape),
            whole_spec(heads_p.shape), whole_spec(skip_x.shape),
        ],
        out_specs=[
            block(width),
            pl.BlockSpec((1, seqs, STATE, width), lambda i: (i, 0, 0, 0)),
        ],
        out_shape=[
            jax.ShapeDtypeStruct(x.shape, BF16),
            jax.ShapeDtypeStruct((steps, seqs, STATE, width), BF16),
        ],
        scratch_shapes=[
            pltpu.VMEM((seqs, STATE, width), F32),
            pltpu.VMEM((seqs, HALO + length, width), F32),
            pltpu.VMEM((seqs, HALO + length, 2 * STATE), F32),
        ],
        compiler_params=pltpu.CompilerParams(
            dimension_semantics=("arbitrary",), vmem_limit_bytes=32 << 20
        ),
        cost_estimate=pl.CostEstimate(
            flops=steps * seqs * 150_000_000, transcendentals=0, bytes_accessed=8_000_000
        ),
        name="mix_forward",
    )(x, x, tail, tail, off_col, wx, bx, wt, bt, heads_p, skip_x)


def backward_mix(x, tail, off_col, off_row, rem_col, dy, states, wx, bx, wt, bt, heads_p, skip_x):
    steps, seqs, length, width = x.shape
    wide = tail.shape[3]

    def block(cols):
        return pl.BlockSpec((1, seqs, length, cols), lambda i: (steps - 1 - i, 0, 0, 0))

    def before(cols):
        return pl.BlockSpec(
            (1, seqs, HALO, cols),
            lambda i: (jnp.maximum(steps - 2 - i, 0), 0, length // HALO - 1, 0),
        )

    return pl.pallas_call(
        backward_kernel,
        grid=(steps,),
        in_specs=[
            block(width), before(width), block(wide), before(wide), block(1),
            pl.BlockSpec((1, seqs, 1, length), lambda i: (steps - 1 - i, 0, 0, 0)),
            block(1), block(width),
            pl.BlockSpec((1, seqs, STATE, width), lambda i: (steps - 1 - i, 0, 0, 0)),
            whole_spec(wx.shape), whole_spec(bx.shape), whole_spec(wt.shape), whole_spec(bt.shape),
            whole_spec(heads_p.shape), whole_spec(skip_x.shape),
        ],
        out_specs=[
            block(width), block(wide),
            whole_spec((8, width)), whole_spec((8, 2 * STATE)), whole_spec((8, LANES)),
        ],
        out_shape=[
            jax.ShapeDtypeStruct(x.shape, BF16),
            jax.ShapeDtypeStruct(tail.shape, BF16),
            jax.ShapeDtypeStruct((8, width), F32),
            jax.ShapeDtypeStruct((8, 2 * STATE), F32),
            jax.ShapeDtypeStruct((8, LANES), F32),
        ],
        scratch_shapes=[
            pltpu.VMEM((seqs, STATE, width), F32),
            pltpu.VMEM((seqs, HALO + length, width), F32),
            pltpu.VMEM((seqs, HALO + length, 2 * STATE), F32),
            pltpu.VMEM((seqs, length + HALO, width), F32),
            pltpu.VMEM((seqs, length + HALO, 2 * STATE), F32),
        ],
        compiler_params=pltpu.CompilerParams(
            dimension_semantics=("arbitrary",), vmem_limit_bytes=40 << 20
        ),
        cost_estimate=pl.CostEstimate(
            flops=steps * seqs * 400_000_000, transcendentals=0, bytes_accessed=12_000_000
        ),
        name="mix_backward",
    )(x, x, tail, tail, off_col, off_row, rem_col, dy, states, wx, bx, wt, bt, heads_p, skip_x)


def chunked(per_token, steps, length):
    return per_token.reshape(per_token.shape[0], steps, length).transpose(1, 0, 2)


def spread_last(piece, start, whole):
    zeros_full = jnp.zeros(piece.shape[:-1] + (whole,), F32)
    return lax.dynamic_update_slice_in_dim(zeros_full, piece, start, piece.ndim - 1)


def local(
    tokens, segments, gain_in, w_in, conv_w, conv_b, dt_bias, a_log, skip, gain_out, w_out,
    cotangent,
):
    steps = lax.axis_size("seq")
    shards = lax.axis_size("fsdp")
    rank = lax.axis_index("seq")
    seqs, length, _ = tokens.shape
    width = INNER // steps
    heads = HEADS // steps
    rows_in = w_in.shape[0]

    def mine(array, size):
        return lax.dynamic_slice_in_dim(array, rank * size, size, array.ndim - 1)

    wide = tokens.astype(F32)
    scale_in = lax.rsqrt(jnp.mean(wide * wide, axis=-1, keepdims=True) + EPSILON)
    normed = (wide * scale_in * gain_in).astype(BF16)
    h_all = lax.all_gather(normed, "seq", axis=0)
    cot_all = lax.all_gather(cotangent, "seq", axis=0)

    zx_local = w_in[:, : 2 * INNER].reshape(rows_in, 2, steps, width).transpose(2, 0, 1, 3)
    zx_local = zx_local.reshape(steps, rows_in, 2 * width)
    zx = lax.all_to_all(zx_local, "seq", split_axis=0, concat_axis=0, tiled=True)
    zx = lax.all_gather(zx, "fsdp", axis=1, tiled=True).reshape(D, 2 * width)
    tail_w = lax.all_gather(w_in[:, 2 * INNER :], ("seq", "fsdp"), axis=0, tiled=True)
    tail_w = jnp.concatenate(
        [
            tail_w[:, : 2 * STATE],
            mine(tail_w[:, 2 * STATE :], heads),
            jnp.zeros((D, LANES - heads), BF16),
        ],
        axis=1,
    )
    out_w = lax.all_gather(w_out, "fsdp", axis=0, tiled=True)
    w_z, w_x = zx[:, :width], zx[:, width:]

    total = steps * length
    index = lax.broadcasted_iota(jnp.int32, (seqs, total), 1)
    starts = jnp.concatenate(
        [jnp.ones((seqs, 1), bool), segments[:, 1:] != segments[:, :-1]], axis=1
    )
    first = lax.cummax(jnp.where(starts, index, 0), axis=1)
    ends = jnp.concatenate([starts[:, 1:], jnp.ones((seqs, 1), bool)], axis=1)
    last = lax.cummin(jnp.where(ends, index, total), axis=1, reverse=True)
    off = chunked((index - first).astype(F32), steps, length)
    rem = chunked((last - index).astype(F32), steps, length)
    off_col, off_row, rem_col = off[..., None], off[:, :, None, :], rem[..., None]

    wx, bx = mine(conv_w[:, :INNER], width), mine(conv_b[None, :INNER], width)
    wt, bt = conv_w[:, INNER:], conv_b[None, INNER:]
    heads_p = jnp.stack([mine(dt_bias, heads), mine(a_log, heads)])
    heads_p = jnp.pad(heads_p, ((0, 6), (0, LANES - heads)))
    skip_x = jnp.repeat(mine(skip, heads), HEAD_DIM)[None]
    gain_mine = mine(gain_out, width)

    def dot(a, b):
        return lax.dot_general(a, b, (((3,), (0,)), ((), ())), preferred_element_type=F32)

    def dot_tr(a, b):
        return lax.dot_general(a, b, (((3,), (1,)), ((), ())), preferred_element_type=F32)

    def dot_tokens(a, b):
        dims = (0, 1, 2)
        return lax.dot_general(a, b, ((dims, dims), ((), ())), preferred_element_type=F32)

    z = dot(h_all, w_z).astype(BF16)
    x = dot(h_all, w_x).astype(BF16)
    tail = dot(h_all, tail_w).astype(BF16)
    y, states = forward_mix(x, tail, off_col, wx, bx, wt, bt, heads_p, skip_x)

    grad_yn = dot_tr(cot_all, out_w)
    z_wide, y_wide = z.astype(F32), y.astype(F32)
    sig = sigmoid(z_wide)
    silu_z = z_wide * sig
    gated = y_wide * silu_z
    sums = jnp.stack(
        [
            jnp.sum(gated * gated, axis=-1),
            jnp.sum(grad_yn * gain_mine * gated, axis=-1),
        ]
    )
    sums = lax.psum(sums, "seq")
    scale = lax.rsqrt(sums[0] / INNER + EPSILON)[..., None]
    slope = sums[1][..., None] * (scale * scale * scale / INNER)
    y_normed = (gated * scale * gain_mine).astype(BF16)
    mixed_part = dot(y_normed, out_w).astype(BF16)
    mixed = lax.psum_scatter(mixed_part, "seq", scatter_dimension=0)
    mixed = (wide + mixed.astype(F32)).astype(BF16)
    out_part = dot_tokens(y_normed, cot_all)
    w_out_grad = lax.psum_scatter(out_part, "fsdp", scatter_dimension=0, tiled=True)
    gain_out_part = jnp.sum(grad_yn * gated * scale, axis=(0, 1, 2))
    grad_gated = scale * gain_mine * grad_yn - gated * slope
    dy = (grad_gated * silu_z).astype(BF16)
    dz = (grad_gated * y_wide * (sig + silu_z * (1.0 - sig))).astype(BF16)

    dx, dtail, sums_x, sums_t, sums_h = backward_mix(
        x, tail, off_col, off_row, rem_col, dy, states, wx, bx, wt, bt, heads_p, skip_x
    )

    grad_h = (dot_tr(dz, w_z) + dot_tr(dx, w_x) + dot_tr(dtail, tail_w)).astype(BF16)
    grad_h = lax.psum_scatter(grad_h, "seq", scatter_dimension=0).astype(F32)
    part_z = dot_tokens(h_all, dz)
    part_x = dot_tokens(h_all, dx)
    part_t = dot_tokens(h_all, dtail)
    part = jnp.concatenate([part_z, part_x, part_t[:, 2 * STATE : 2 * STATE + heads]], axis=1)
    part = part.reshape(steps, shards, rows_in, 2 * width + heads)
    part = lax.psum_scatter(part, "fsdp", scatter_dimension=1)
    part = lax.all_to_all(part.astype(BF16), "seq", split_axis=0, concat_axis=0, tiled=True)
    part = part.astype(F32)
    bc_grad = lax.psum_scatter(
        part_t[:, : 2 * STATE], ("seq", "fsdp"), scatter_dimension=0, tiled=True
    )

    def columns(start, size):
        piece = part[:, :, start : start + size].transpose(1, 0, 2)
        return piece.reshape(rows_in, steps * size)

    w_in_grad = jnp.concatenate(
        [columns(0, width), columns(width, width), bc_grad, columns(2 * width, heads)], axis=1
    )

    scaled = grad_h * gain_in
    unit = wide * scale_in
    tokens_grad = cotangent.astype(F32) + scale_in * (
        scaled - unit * jnp.mean(scaled * unit, axis=-1, keepdims=True)
    )
    gain_in_part = jnp.sum(grad_h * unit, axis=(0, 1))

    skip_part = jnp.sum(sums_x[KERNEL + 1].reshape(heads, HEAD_DIM), axis=-1)
    reduced = lax.psum(
        (
            gain_in_part,
            spread_last(gain_out_part, rank * width, INNER),
            spread_last(sums_x[: KERNEL + 1], rank * width, INNER),
            sums_t[: KERNEL + 1],
            spread_last(sums_h[0, :heads], rank * heads, HEADS),
            spread_last(sums_h[1, :heads], rank * heads, HEADS),
            spread_last(skip_part, rank * heads, HEADS),
        ),
        ("seq", "fsdp"),
    )
    conv_grads = jnp.concatenate([reduced[2], reduced[3]], axis=1)
    return (
        mixed, tokens_grad, reduced[0], w_in_grad, conv_grads[:KERNEL], conv_grads[KERNEL],
        reduced[4], reduced[5], reduced[6], reduced[1], w_out_grad,
    )


def solution(mesh):
    by_token = P("fsdp", "seq", None)
    by_row = P(("seq", "fsdp"), None)
    placed = (
        by_token, P("fsdp", None), P(), by_row, P(), P(), P(), P(), P(), P(), by_row, by_token,
    )
    return jax.shard_map(
        local,
        mesh=mesh,
        in_specs=placed,
        out_specs=(by_token, by_token, P(), by_row, P(), P(), P(), P(), P(), P(), by_row),
        check_vma=False,
    )
```

time: 2270 us -> 924 us (0.41)
  waiting for transfers between devices: 1000 us -> 451 us
  local copies, waits for them, and re-layouts: 464 us -> 30.2 us
  matrix products: 337 us -> 93.1 us
  other arithmetic: 257 us -> 26.1 us
  blocking collectives: 105 us -> 258 us
  Pallas kernels: 0 us -> 46.3 us
  starting transfers between devices: 43.1 us -> 0.37 us
  loops' own time: 27.7 us -> 0 us
    reduce_scatter x4, waiting for transfers between devices: 682 us -> 188 us  [the longest x1 79 us: local(): grad_h = lax.psum_scatter(grad_h, 'seq', scatter_dimension=0).astype(F32)]
    dot_general x124 -> x12, matrix products: 337 us -> 93.1 us  [the longest x4 33.7 us: dot_tr(): lax.dot_general(a, b, (((3,), (1,)), ((), ())), preferred_element_type=F32)]
    dynamic_update_slice x48 -> x0, local copies, waits for them, and re-layouts: 180 us -> none  [state_mix(): final_state, outputs = lax.scan(jax.checkpoint(one_block), start, pieces)]
    another operation x68 -> x6, other arithmetic: 128 us -> 5.85 us
    unnamed x0 -> x1, blocking collectives: none -> 104 us
    all_gather x2 -> x4, waiting for transfers between devices: 213 us -> 132 us  [the longest x1 97.6 us: local(): cot_all = lax.all_gather(cotangent, 'seq', axis=0)]
    while x691 -> x0, local copies, waits for them, and re-layouts: 68.8 us -> none  [the longest x1 36.8 us: local(): lax.scan(layer, (big_start, small_start), (tokens, segments, cotangent))]
    another operation x136 -> x13, local copies, waits for them, and re-layouts: 56.8 us -> 0.71 us
  transfers between devices with their start and end apart: 17 -> 9, of which waited for: 12 -> 7; matrix products, arithmetic and copies ran while one was open for 4% -> 10% of each run, Pallas kernels for 0% -> 1%
where the time goes in v1:
time: 924 us; the launch traced here: 919 us
  waiting for transfers between devices  451 us (49%)
  blocking collectives  258 us (28%)
  matrix products  93.1 us (10%)
  Pallas kernels  46.3 us (5%)
  local copies, waits for them, and re-layouts  30.2 us (3%)
  other arithmetic  26.1 us (3%)
  between operations  14.7 us (2%)
    psum x1, waiting for transfers between devices, local(): lax.psum((gain_in_part, spread_last(gain_out_part, rank * width, INNER),...  129 us
    unnamed x1, blocking collectives  104 us
    all_gather x1, waiting for transfers between devices, local(): cot_all = lax.all_gather(cotangent, 'seq', axis=0)  97.6 us
    reduce_scatter x1, waiting for transfers between devices, local(): grad_h = lax.psum_scatter(grad_h, 'seq', scatter_dimension=0).astype(F32)  79 us
    reduce_scatter x1, waiting for transfers between devices, local(): mixed = lax.psum_scatter(mixed_part, 'seq', scatter_dimension=0)  76.1 us
    all_gather x1, blocking collectives, local(): lax.all_gather(w_in[:, 2 * INNER:], ('seq', 'fsdp'), axis=0, tiled=True)  56 us
    all_to_all x1, blocking collectives, local(): lax.all_to_all(part.astype(BF16), 'seq', split_axis=0, concat_axis=0, til...  41.3 us
    dot_general x4, matrix products, dot_tr(): lax.dot_general(a, b, (((3,), (1,)), ((), ())), preferred_element_type=F32)  33.7 us
  transfers between devices with their start and end apart: 9, of which 7 were waited for; matrix products, arithmetic and copies ran while one was open for 10% of the time, Pallas kernels for 1%

profile of v1, /device:TPU:1, one launch (start us, length us, event | category | flops | bytes accessed | tf_op | source)
XLA Modules:
  0.0 919.5 jit_solution(10659472943445390180)
XLA Ops:
  7.2 1.4 fusion.15
  8.7 2.3 fusion.12
  12.0 28.9 %all_to_all.10 = bf16[8,48,768]{2,1,0:T(8,128)(2,1)} all-to-all(bf16[8,48,768]{2,1,0:T(8,128)(2,1)S(1)} %reshape.124), channel_id=1, replica_groups=mesh['seq'=8,'fsdp'=4] {'seq'}, dimensions={0} | all-to-all | bytes 1179648 | tf_op jit(solution)/shard_map/all_to_all | solution.py:434
  42.4 56.0 %all_gather.24 = bf16[1536,304]{1,0:T(8,128)(2,1)S(1)} all-gather(bf16[48,304]{1,0:T(8,128)(2,1)S(1)} %slice-done.1), channel_id=1, replica_groups=mesh['seq'=8,'fsdp'=4] {'seq','fsdp'}, dimensions={0}, use_global_device_ids=true | all-gather | bytes 963072 | tf_op jit(solution)/shard_map/all_gather | solution.py:436
  99.8 4.9 reduce-window.16
  106.4 1.3 copy.83.rem_ref
  108.5 14.7 %all-gather.11.cloned.1.call-done = bf16[16,128,1536]{2,1,0:T(8,128)(2,1)} async-done(((bf16[2,128,1536]{2,1,0:T(8,128)(2,1)}), bf16[16,128,1536]{2,1,0:T(8,128)(2,1)}) %all-gather.11.cloned.1.call-update) | async-done | bytes 6291472 | tf_op jit(solution)/shard_map/all_gather | solution.py:429
  123.2 7.4 convolution_convert_fusion.2.tail_ref.tailh_ref
  130.6 19.7 %all-gather.7.cloned.1.call-done = bf16[8,192,768]{2,1,0:T(8,128)(2,1)} async-done(((bf16[8,48,768]{2,1,0:T(8,128)(2,1)}), bf16[8,192,768]{2,1,0:T(8,128)(2,1)}) %all-gather.7.cloned.1.call-update) | async-done | bytes 2359312 | tf_op jit(solution)/shard_map/all_gather | solution.py:435
  150.3 6.6 convolution_convert_fusion.3.x_ref.xh_ref
  156.9 12.7 %mix_forward.1 = (bf16[8,2,128,384]{3,2,1,0:T(8,128)(2,1)S(1)}, bf16[8,2,128,384]{3,2,1,0:T(8,128)(2,1)S(1)}) custom-call(bf16[8,2,128,384]{3,2,1,0:T(8,128)(2,1)S(1)} %convolution_convert_fusion.3.x_ref.xh_ref, bf16[8,2,128,384]{3,2,1,0:T(8,128)(2,1)S(1)} %convolution_convert_fusion.3.x_ref.xh_ref, bf16[8,2,128,384]{3,2,1,0:T(8,128)(2,1)S(1)} %copy-done.5, ...), custom_call_target="tpu_custom_call" | custom-call | flops 2400000000 | bytes 8000000 | tf_op jit(solution)/shard_map/mix_forward/pallas_call | solution.py:319
  169.7 1.1 copy-done.7
  170.8 1.2 copy-done.9
  171.9 97.6 %all-gather.13.cloned.1.call-done = bf16[16,128,1536]{2,1,0:T(8,128)(2,1)} async-done(((bf16[2,128,1536]{2,1,0:T(8,128)(2,1)}), bf16[16,128,1536]{2,1,0:T(8,128)(2,1)}) %all-gather.13.cloned.1.call-update) | async-done | bytes 6291472 | tf_op jit(solution)/shard_map/all_gather | solution.py:430
  269.5 6.3 fusion.19
  275.8 8.5 multiply_reduce_fusion.2
  284.3 27.8 %psum.56 = f32[2,8,2,128]{3,2,1,0:T(2,128)S(1)} all-reduce(f32[2,8,2,128]{3,2,1,0:T(2,128)S(1)} %pad_maximum_fusion.2), channel_id=1, replica_groups=mesh['seq'=8,'fsdp'=4] {'seq'}, use_global_device_ids=true, to_apply=%region_5.6 | all-reduce | flops 4096 | bytes 32768 | tf_op jit(solution)/shard_map/psum | solution.py:493
  312.2 3.5 multiply_reduce_fusion
  315.8 7.8 fusion.22
  323.6 33.6 %mix_backward.1 = (bf16[8,2,128,384]{3,2,1,0:T(8,128)(2,1)S(1)}, bf16[8,2,128,384]{3,2,1,0:T(8,128)(2,1)S(1)}, f32[8,384]{1,0:T(8,128)S(1)}, f32[8,256]{1,0:T(8,128)}, f32[8,128]{1,0:T(8,128)S(1)}) custom-call(bf16[8,2,128,384]{3,2,1,0:T(8,128)(2,1)S(1)} %copy-done.8, bf16[8,2,128,384]{3,2,1,0:T(8,128)(2,1)S(1)} %copy-done.8, ...), custom_call_target="tpu_custom_call" | custom-call | flops 6400000000 | bytes 12000000 | tf_op jit(solution)/shard_map/mix_backward/pallas_call | solution.py:363
  357.2 6.4 fusion.21
  363.7 13.2 %add_convert_fusion = bf16[8,2,128,1536]{3,2,1,0:T(8,128)(2,1)} fusion(f32[8,2,128,1536]{3,2,1,0:T(8,128)} %fusion.22, f32[8,2,128,1536]{3,2,1,0:T(8,128)} %fusion.21, bf16[8,2,128,384]{3,2,1,0:T(8,128)(2,1)S(1)} %get-tuple-element.21, bf16[1536,6]{1,0:T(8,128)(2,1)S(1)} %copy-done.19, bf16[1536,256]{1,0:T(8,128)(2,1)S(1)} %copy-done.17, ...), kind=kOutput, calls=%fused_computation | convolution fusion | flops 2428895232 | bytes 33835776 | tf_op jit(solution)/shard_map/dot_general | solution.py:471
  376.9 5.3 convolution_bitcast_fusion.1
  382.2 1.4 copy-done.22
  383.7 1.6 copy.111
  385.4 8.5 convolution_convert_fusion
  396.3 7.0 convolution_bitcast_fusion.2
  403.3 7.1 convolution_bitcast_fusion
  410.4 9.1 convolution_bitcast_fusion.3
  419.5 79.0 %reduce-scatter.10.cloned.1.call-done = bf16[1,2,128,1536]{3,2,1,0:T(8,128)(2,1)} async-done(((bf16[8,2,128,1536]{3,2,1,0:T(8,128)(2,1)}), bf16[1,2,128,1536]{3,2,1,0:T(8,128)(2,1)}) %reduce-scatter.10.cloned.1.call-update) | async-done | bytes 786448 | tf_op jit(solution)/shard_map/reduce_scatter | solution.py:512
  498.4 2.3 fusion.14
  500.8 4.8 pad_maximum_fusion
  505.6 5.9 copy.87
  511.6 104.0 %all-reduce.9 = bf16[8,4,48,774]{3,2,1,0:T(8,128)(2,1)} all-reduce(f32[8,4,48,774]{3,2,1,0:T(8,128)} %bitcast.150), channel_id=6, replica_groups=mesh['seq'=8,'fsdp'=4] {'fsdp'}, use_global_device_ids=true, to_apply=%region_13.14.clone | all-reduce | flops 1188864 | bytes 7133184
  615.6 1.8 fusion.23
  617.4 41.3 %all_to_all.11 = bf16[8,48,774]{2,1,0:T(8,128)(2,1)S(1)} all-to-all(bf16[8,48,774]{2,1,0:T(8,128)(2,1)S(1)} %fusion.23), channel_id=1, replica_groups=mesh['seq'=8,'fsdp'=4] {'seq'}, dimensions={0} | all-to-all | bytes 1188864 | tf_op jit(solution)/shard_map/all_to_all | solution.py:519
  659.2 0.9 copy.114
  660.1 2.2 pad_maximum_fusion.1
  662.3 76.1 %reduce-scatter.8.cloned.1.call-done = bf16[1,2,128,1536]{3,2,1,0:T(8,128)(2,1)} async-done(((bf16[8,2,128,1536]{3,2,1,0:T(8,128)(2,1)}), bf16[1,2,128,1536]{3,2,1,0:T(8,128)(2,1)}) %reduce-scatter.8.cloned.1.call-update) | async-done | bytes 786448 | tf_op jit(solution)/shard_map/reduce_scatter | solution.py:498
  738.4 3.2 fusion.11
  741.6 129.2 %all-reduce.8.cloned.1.call-done = (f32[1536]{0:T(1024)}, f32[5,3072]{1,0:T(8,128)}, f32[5,256]{1,0:T(8,128)}, f32[48]{0:T(128)}, f32[48]{0:T(128)}, /*index=5*/f32[48]{0:T(128)}, f32[3072]{0:T(1024)}) async-done(((f32[1536]{0:T(1024)}, f32[5,3072]{1,0:T(8,128)}, f32[5,256]{1,0:T(8,128)}, f32[48]{0:T(128)}, f32[48]{0:T(128)}, /*index=5*/f32[48]{0:T(128)}, f32[3072]{0:T(1024)}), (f32[1536]{0:T(1024)}, ...) | async-done | bytes 85584 | tf_op jit(solution)/shard_map/psum | solution.py:541
  870.8 0.9 constant_dynamic-update-slice_fusion.1
  873.7 33.1 %reduce-scatter.12.cloned.1.call-done = f32[96,1536]{1,0:T(8,128)} async-done(((f32[384,1536]{1,0:T(8,128)}), f32[96,1536]{1,0:T(8,128)}) %reduce-scatter.12.cloned.1.call-update) | async-done | bytes 589840 | tf_op jit(solution)/shard_map/reduce_scatter | solution.py:501
  906.8 1.3 copy.138
  908.1 1.1 copy.139
  909.2 1.2 copy.140
  910.3 1.1 copy.141
  911.5 1.3 copy.142
  (167 shorter events, 11.2 us)
Async XLA Ops:
  7.2 3.8 slice-start
  7.2 116.0 %all-gather.11.cloned.1.call-start = ((), (), s32[]{:S(2)}) async-start(), calls=%async_computation.11 | async-start | bytes 7077888 | tf_op jit(solution)/shard_map/all_gather | solution.py:429
  11.0 139.3 %all-gather.7.cloned.1.call-start = ((), (), s32[]{:S(2)}) async-start(), calls=%async_computation.6 | async-start | bytes 2949120 | tf_op jit(solution)/shard_map/all_gather | solution.py:435
  11.0 31.3 %copy-start.30 = (f32[3328]{0:T(1024)S(1)}, f32[3328]{0:T(1024)}, u32[]{:S(2)}) copy-start(f32[3328]{0:T(1024)} %param.17) | copy-start | bytes 39940
  11.0 31.3 %copy-start.27 = (f32[4,3328]{1,0:T(4,128)S(1)}, f32[4,3328]{1,0:T(4,128)}, u32[]{:S(2)}) copy-start(f32[4,3328]{1,0:T(4,128)} %param.16) | copy-start | bytes 159748
  11.0 31.3 %slice-start.1 = ((bf16[48,6448]{1,0:T(8,128)(2,1)}), bf16[48,304]{1,0:T(8,128)(2,1)S(1)}, s32[]{:S(2)}) async-start(bf16[48,6448]{1,0:T(8,128)(2,1)} %param.15), calls=%async_computation.16 | async-start | bytes 73728 | tf_op jit(solution)/shard_map/slice | solution.py:436
  12.0 86.6 %copy-start.36 = (f32[48]{0:T(128)S(1)}, f32[48]{0:T(128)}, u32[]{:S(2)}) copy-start(f32[48]{0:T(128)} %param.20) | copy-start | bytes 580
  12.0 87.6 %slice-start.4 = ((f32[3328]{0:T(1024)}), f32[3072]{0:T(1024)S(1)}, s32[]{:S(2)}) async-start(f32[3328]{0:T(1024)} %param.17), calls=%async_computation.19 | async-start | bytes 24576 | tf_op jit(solution)/shard_map/slice | solution.py:460
  12.0 87.7 %copy-start.29 = (s32[2,1024]{1,0:T(2,128)S(1)}, s32[2,1024]{1,0:T(2,128)}, u32[]{:S(2)}) copy-start(s32[2,1024]{1,0:T(2,128)} %param.13) | copy-start | bytes 24580
  40.9 131.0 %all-gather.9.cloned.1.call-start = ((), (), s32[]{:S(2)}) async-start(), calls=%async_computation.7 | async-start | bytes 1474560 | tf_op jit(solution)/shard_map/all_gather | solution.py:445
  41.7 227.8 %all-gather.13.cloned.1.call-start = ((), (), s32[]{:S(2)}) async-start(), calls=%async_computation.12 | async-start | bytes 7077888 | tf_op jit(solution)/shard_map/all_gather | solution.py:430
  42.2 65.9 %copy-start.34 = (f32[48]{0:T(128)S(1)}, f32[48]{0:T(128)}, u32[]{:S(2)}) copy-start(f32[48]{0:T(128)} %param.19) | copy-start | bytes 580
  42.3 65.9 %copy-start.35 = (f32[48]{0:T(128)S(1)}, f32[48]{0:T(128)}, u32[]{:S(2)}) copy-start(f32[48]{0:T(128)} %param.18) | copy-start | bytes 580
  42.3 66.0 %slice-start.3 = ((f32[4,3328]{1,0:T(4,128)}), f32[4,3072]{1,0:T(4,128)S(1)}, s32[]{:S(2)}) async-start(f32[4,3328]{1,0:T(4,128)} %param.16), calls=%async_computation.18 | async-start | bytes 98304 | tf_op jit(solution)/shard_map/slice | solution.py:460
  42.3 456.1 %reduce-scatter.10.cloned.1.call-start = ((), (), s32[]{:S(2)}) async-start(), calls=%async_computation.9 | async-start | bytes 7077888 | tf_op jit(solution)/shard_map/reduce_scatter | solution.py:512
  98.5 32.0 %copy-start.16 = (bf16[1536,256]{1,0:T(8,128)(2,1)}, bf16[1536,256]{1,0:T(8,128)(2,1)S(1)}, u32[]{:S(2)}) copy-start(bf16[1536,256]{1,0:T(8,128)(2,1)S(1)} %slice.121) | copy-start | bytes 2359300
  108.1 48.8 %copy-start.3 = (f32[8,2,128,1]{3,2,1,0:T(8,128)}, f32[8,2,128,1]{3,2,1,0:T(8,128)S(1)}, u32[]{:S(2)}) copy-start(f32[8,2,128,1]{3,2,1,0:T(8,128)S(1)} %copy.78.off_ref) | copy-start | bytes 24580
  108.5 22.1 %copy-start.18 = (bf16[1536,6]{1,0:T(8,128)(2,1)}, bf16[1536,6]{1,0:T(8,128)(2,1)S(1)}, u32[]{:S(2)}) copy-start(bf16[1536,6]{1,0:T(8,128)(2,1)S(1)} %constant_dynamic-slice_fusion.1) | copy-start | bytes 55300
  150.3 6.7 copy-start.5
  269.5 6.3 copy-start.23
  275.8 8.5 copy-start.12
  284.3 31.4 %copy-start.20 = (bf16[8,2,128,384]{3,2,1,0:T(8,128)(2,1)}, bf16[8,2,128,384]{3,2,1,0:T(8,128)(2,1)S(1)}, u32[]{:S(2)}) copy-start(bf16[8,2,128,384]{3,2,1,0:T(8,128)(2,1)S(1)} %get-tuple-element.46) | copy-start | bytes 4718596
  312.1 3.6 copy-start.13
  312.1 3.6 copy-start.24
  315.7 7.9 copy-start.2
  315.7 7.9 copy-start.4
  315.8 7.9 copy-start.6
  315.8 7.9 copy-start.8
  315.8 7.9 copy-start.10
  357.2 6.4 copy-start
  357.2 6.4 copy-start.17
  357.2 6.4 copy-start.19
  376.9 283.2 %reduce-scatter.14.cloned.1.call-start = ((), (), s32[]{:S(2)}) async-start(), calls=%async_computation.13 | async-start | bytes 1622016 | tf_op jit(solution)/shard_map/reduce_scatter | solution.py:521
  385.4 353.0 %reduce-scatter.8.cloned.1.call-start = ((), (), s32[]{:S(2)}) async-start(), calls=%async_computation.8 | async-start | bytes 7077888 | tf_op jit(solution)/shard_map/reduce_scatter | solution.py:498
  393.9 2.3 copy-start.1
  393.9 476.9 %all-reduce.8.cloned.1.call-start = ((), (), s32[]{:S(2)}) async-start(), calls=%async_computation.14 | async-start | bytes 257024 | tf_op jit(solution)/shard_map/psum | solution.py:541
  395.5 7.8 copy-start.28
  395.8 7.4 copy-start.32
  395.9 7.3 copy-start.33
  396.2 7.1 copy-start.31
  396.2 7.1 copy-start.25
  396.2 7.1 copy-start.21
  410.4 88.0 %copy-start.11 = (bf16[2,128,1536]{2,1,0:T(8,128)(2,1)S(1)}, bf16[2,128,1536]{2,1,0:T(8,128)(2,1)}, u32[]{:S(2)}) copy-start(bf16[2,128,1536]{2,1,0:T(8,128)(2,1)} %param.12) | copy-start | bytes 2359300
  410.4 88.0 %copy-start.26 = (f32[1536]{0:T(1024)S(1)}, f32[1536]{0:T(1024)}, u32[]{:S(2)}) copy-start(f32[1536]{0:T(1024)} %param.14) | copy-start | bytes 18436
  410.4 90.4 %slice-start.2 = ((f32[1536,384]{0,1:T(8,128)}), f32[1536,6]{0,1:T(8,128)S(1)}, s32[]{:S(2)}) async-start(f32[1536,384]{0,1:T(8,128)} %copy-done.22), calls=%async_computation.17 | async-start | bytes 98304 | tf_op jit(solution)/shard_map/slice | solution.py:516
  500.7 406.0 %reduce-scatter.12.cloned.1.call-start = ((), (), s32[]{:S(2)}) async-start(), calls=%async_computation.10 | async-start | bytes 2949120 | tf_op jit(solution)/shard_map/reduce_scatter | solution.py:501
  659.1 79.3 %copy-start.14 = (bf16[2,128,1536]{2,1,0:T(8,128)(2,1)S(1)}, bf16[2,128,1536]{2,1,0:T(8,128)(2,1)}, u32[]{:S(2)}) copy-start(bf16[2,128,1536]{2,1,0:T(8,128)(2,1)} %param.23) | copy-start | bytes 2359300
  659.2 79.2 %copy-start.15 = (bf16[1,2,128,1536]{3,2,1,0:T(8,128)(2,1)S(1)}, bf16[1,2,128,1536]{3,2,1,0:T(8,128)(2,1)}, u32[]{:S(2)}) copy-start(bf16[1,2,128,1536]{3,2,1,0:T(8,128)(2,1)} %reduce-scatter.10.cloned.1.call-done) | copy-start | bytes 2359300
  (4 other events, 4.3 us)
Sparse Core Ops, SparseCore 0:
  11.1 112.0 all-gather.10
  124.7 25.4 all-gather.6
  151.8 17.4 all-gather.8
  171.4 98.1 all-gather.12
  377.0 121.4 reduce-scatter.9
  503.5 98.3 reduce-scatter.13
  605.5 132.8 reduce-scatter.7
  745.9 124.8 all-reduce.7
  873.9 32.7 reduce-scatter.11

commit v2 on v1

v2 whole, which is shorter than its diff:
```python
import functools

import jax
import jax.numpy as jnp
import numpy as np
from jax import lax
from jax.experimental import pallas as pl
from jax.experimental.pallas import tpu as pltpu
from jax.sharding import PartitionSpec as P

D = 1536
HEADS = 48
HEAD_DIM = 64
STATE = 128
KERNEL = 4
INNER = 3072
LANES = 128
HALO = 16
EPSILON = 1e-05
F32 = jnp.float32
BF16 = jnp.bfloat16


def mm(a, b):
    return jnp.dot(a.astype(BF16), b.astype(BF16), preferred_element_type=F32)


def mm_tr(a, b):
    return lax.dot_general(
        a.astype(BF16), b.astype(BF16), (((1,), (1,)), ((), ())), preferred_element_type=F32
    )


def tr_mm(a, b):
    return lax.dot_general(
        a.astype(BF16), b.astype(BF16), (((0,), (0,)), ((), ())), preferred_element_type=F32
    )


def pieces(a, count):
    out = []
    for _ in range(count - 1):
        part = a.astype(BF16)
        out.append(part)
        a = a - part.astype(F32)
    out.append(a.astype(BF16))
    return out


def ones_mm(ones, a, count):
    return sum(jnp.dot(ones, part, preferred_element_type=F32) for part in pieces(a, count))


def mm_ones(a, ones, count):
    return sum(jnp.dot(part, ones, preferred_element_type=F32) for part in pieces(a, count))


def mm_ones_tr(a, ones, count):
    return sum(
        lax.dot_general(part, ones, (((1,), (1,)), ((), ())), preferred_element_type=F32)
        for part in pieces(a, count)
    )


def iota(shape, dim):
    return lax.broadcasted_iota(jnp.int32, shape, dim)


def softplus(v):
    return jnp.maximum(v, 0.0) + jnp.log1p(jnp.exp(-jnp.abs(v)))


def sigmoid(v):
    return 1.0 / (1.0 + jnp.exp(-v))


def causal_conv(ext, current, halo, weight, bias, offset):
    length = current.shape[0]
    ext[0:HALO, :] = halo
    ext[HALO : HALO + length, :] = current
    total = bias + weight[KERNEL - 1 : KERNEL, :] * current
    for back in range(1, KERNEL):
        shifted = jnp.where(offset >= back, ext[pl.ds(HALO - back, length), :], 0.0)
        total = total + weight[KERNEL - 1 - back : KERNEL - back, :] * shifted
    return total


def head_tiles(width):
    out = []
    for start in range(0, width, LANES):
        size = min(LANES, width - start)
        heads = [start // HEAD_DIM + i for i in range(size // HEAD_DIM)]
        out.append((start, size, heads))
    return out


def masked_heads(tile, heads):
    if len(heads) == 1:
        return tile
    lane = iota(tile.shape, 1) // HEAD_DIM
    return jnp.concatenate(
        [jnp.where(lane == i, tile, jnp.zeros_like(tile)) for i in range(len(heads))], axis=0
    )


def expander(width):
    return (iota((LANES, width), 1) // HEAD_DIM == iota((LANES, width), 0)).astype(BF16)


def chunk_common(x, xh, tail, tailh, offset, params, ext_x, ext_t, width):
    wx, bx, wt, bt, heads_p = params
    length = x.shape[0]
    conv_x = causal_conv(ext_x, x.astype(F32), xh.astype(F32), wx, bx, offset)
    conv_t = causal_conv(
        ext_t,
        tail[:, : 2 * STATE].astype(F32),
        tailh[:, : 2 * STATE].astype(F32),
        wt,
        bt,
        offset,
    )
    raw = tail[:, 2 * STATE :].astype(F32) + heads_p[0:1, :]
    step = softplus(raw)
    decay_rate = jnp.exp(heads_p[1:2, :])
    rate = -step * decay_rate
    tril = (iota((length, length), 0) >= iota((length, length), 1)).astype(BF16)
    cumul = ones_mm(tril, rate, 3)
    spread = expander(width)
    row = iota((length, 1), 0)
    entry = jnp.where(offset > row.astype(F32), jnp.exp(cumul), 0.0)
    last_off = offset[length - 1 : length, :]
    same_last = row.astype(F32) >= (length - 1) - last_off
    to_end = jnp.where(same_last, jnp.exp(cumul[length - 1 : length, :] - cumul), 0.0)
    step_x = mm_ones(step, spread, 2)
    entry_x = mm_ones(entry, spread, 2)
    end_x = mm_ones(to_end, spread, 2)
    return conv_x, conv_t, raw, step, rate, decay_rate, cumul, spread, step_x, entry_x, end_x


def forward_kernel(order_ref, *refs, seqs):
    del order_ref
    per_seq, refs = refs[: 5 * seqs], refs[5 * seqs :]
    (wx_ref, bx_ref, wt_ref, bt_ref, hp_ref, skip_ref, gain_ref), refs = refs[:7], refs[7:]
    outs, (state_ref, memory, ext_x, ext_t) = refs[: 3 * seqs], refs[3 * seqs :]
    length, width = per_seq[0].shape[1], per_seq[0].shape[2] // 2

    @pl.when(pl.program_id(0) == 0)
    def _():
        memory[...] = jnp.zeros_like(memory)

    params = (wx_ref[...], bx_ref[...], wt_ref[...], bt_ref[...], hp_ref[...])
    for q in range(seqs):
        zx_ref, zxh_ref, tail_ref, tailh_ref, off_ref = per_seq[5 * q : 5 * q + 5]
        y_ref, gated_ref, square_ref = outs[3 * q : 3 * q + 3]
        offset = off_ref[0]
        conv_x, conv_t, _, _, _, _, cumul, _, step_x, entry_x, end_x = chunk_common(
            zx_ref[0, :, width:], zxh_ref[0, :, width:], tail_ref[0], tailh_ref[0], offset, params,
            ext_x.at[q], ext_t.at[q], width,
        )
        xs = conv_x * sigmoid(conv_x)
        act_t = conv_t * sigmoid(conv_t)
        bs = act_t[:, :STATE].astype(BF16)
        cs = act_t[:, STATE:].astype(BF16)
        scaled = xs * step_x
        scores = mm_tr(cs, bs)
        gap = iota((length, length), 0) - iota((length, length), 1)
        same = (gap >= 0) & (gap.astype(F32) <= offset)
        cumul_t = cumul.T
        old = memory[q]
        old_low = old.astype(BF16)
        state_ref[0, q] = old_low
        outside = mm(cs, old_low) * entry_x + skip_ref[...] * xs
        squares = jnp.zeros((length, 1), F32)
        for start, size, heads in head_tiles(width):
            mixing = []
            for head in heads:
                spans = cumul[:, head : head + 1] - cumul_t[head : head + 1, :]
                decays = jnp.exp(jnp.where(same, spans, -1e30))
                mixing.append((decays * scores).astype(BF16))
            tile = masked_heads(scaled[:, start : start + size].astype(BF16), heads)
            mix = mixing[0] if len(heads) == 1 else jnp.concatenate(mixing, axis=1)
            inside = jnp.dot(mix, tile, preferred_element_type=F32)
            y_low = (inside + outside[:, start : start + size]).astype(BF16)
            y_ref[0, :, start : start + size] = y_low
            z = zx_ref[0, :, start : start + size].astype(F32)
            gated = y_low.astype(F32) * (z * sigmoid(z))
            gated_ref[0, :, start : start + size] = (
                gated * gain_ref[:, start : start + size]
            ).astype(BF16)
            squares = squares + jnp.sum(gated * gated, axis=1, keepdims=True)
        square_ref[0] = jnp.broadcast_to(squares, (length, LANES)).T[0:1, :]
        fresh = tr_mm(bs, scaled * end_x)
        memory[q] = old * entry_x[length - 1 : length, :] + fresh


def backward_kernel(order_ref, *refs, seqs):
    del order_ref
    per_seq, refs = refs[: 10 * seqs], refs[10 * seqs :]
    (state_ref, wx_ref, bx_ref, wt_ref, bt_ref, hp_ref, skip_ref, gain_ref), refs = (
        refs[:8], refs[8:],
    )
    outs, refs = refs[:seqs], refs[seqs:]
    gx_ref, gt_ref, gh_ref, memory, ext_x, ext_t, next_x, next_t = refs
    length, width = per_seq[0].shape[1], per_seq[0].shape[2] // 2

    @pl.when(pl.program_id(0) == 0)
    def _():
        memory[...] = jnp.zeros_like(memory)
        gx_ref[...] = jnp.zeros_like(gx_ref)
        gt_ref[...] = jnp.zeros_like(gt_ref)
        gh_ref[...] = jnp.zeros_like(gh_ref)
        next_x[:, length:, :] = jnp.zeros_like(next_x[:, length:, :])
        next_t[:, length:, :] = jnp.zeros_like(next_t[:, length:, :])

    params = (wx_ref[...], bx_ref[...], wt_ref[...], bt_ref[...], hp_ref[...])
    for q in range(seqs):
        (zx_ref, zxh_ref, tail_ref, tailh_ref, off_ref, offr_ref, rem_ref, y_ref, grad_ref,
         stat_ref) = per_seq[10 * q : 10 * q + 10]
        out_ref = outs[q]
        offset = off_ref[0]
        conv_x, conv_t, raw, step, rate, decay_rate, cumul, spread, step_x, entry_x, end_x = (
            chunk_common(
                zx_ref[0, :, width:], zxh_ref[0, :, width:], tail_ref[0], tailh_ref[0], offset,
                params, ext_x.at[q], ext_t.at[q], width,
            )
        )
        stats = jnp.broadcast_to(stat_ref[0, 0:1, :], (LANES, length)).T
        slopes = jnp.broadcast_to(stat_ref[0, 1:2, :], (LANES, length)).T
        scale, slope = stats[:, 0:1], slopes[:, 0:1]
        z = zx_ref[0, :, :width].astype(F32)
        sig_z = sigmoid(z)
        silu_z = z * sig_z
        y = y_ref[0].astype(F32)
        gated = y * silu_z
        scaled_grad = grad_ref[0].astype(F32) * scale
        gx_ref[KERNEL + 2 : KERNEL + 3, :] += jnp.sum(scaled_grad * gated, axis=0, keepdims=True)
        grad_gated = gain_ref[...] * scaled_grad - gated * slope
        dy_low = (grad_gated * silu_z).astype(BF16)
        dz = (grad_gated * y * (sig_z + silu_z * (1.0 - sig_z))).astype(BF16)
        dy = dy_low.astype(F32)

        sig_x = sigmoid(conv_x)
        xs = conv_x * sig_x
        slope_x = sig_x + xs * (1.0 - sig_x)
        sig_t = sigmoid(conv_t)
        act_t = conv_t * sig_t
        slope_t = sig_t + act_t * (1.0 - sig_t)
        bs = act_t[:, :STATE].astype(BF16)
        cs = act_t[:, STATE:].astype(BF16)
        scaled = xs * step_x
        scaled_low = scaled.astype(BF16)
        scores = mm_tr(bs, cs)
        rows, cols = iota((length, length), 0), iota((length, length), 1)
        gap = cols - rows
        same = (gap >= 0) & (gap.astype(F32) <= offr_ref[0])
        strict = gap > 0
        upper = (rows >= cols).astype(BF16)
        cumul_t = cumul.T
        old = state_ref[0, q]
        grad_state = memory[q]
        state_low = grad_state.astype(BF16)
        grad_scores = jnp.zeros((length, length), F32)
        grad_scaled = []
        inside_rows = []
        for start, size, heads in head_tiles(width):
            dy_tile = masked_heads(dy_low[:, start : start + size], heads)
            grad_mix = mm_tr(scaled_low[:, start : start + size], dy_tile)
            mixing = []
            for place, head in enumerate(heads):
                spans = cumul_t[head : head + 1, :] - cumul[:, head : head + 1]
                decays = jnp.exp(jnp.where(same, spans, -1e30))
                weighted = grad_mix[:, place * length : (place + 1) * length] * decays
                grad_scores = grad_scores + weighted
                mixing.append((decays * scores).astype(BF16))
                terms = jnp.where(strict, weighted * scores, 0.0).astype(BF16)
                sums = jnp.dot(terms, upper, preferred_element_type=F32)
                inside_rows.append(
                    jnp.sum(jnp.where(strict, sums, 0.0), axis=0, keepdims=True)
                )
            mix = mixing[0] if len(heads) == 1 else jnp.concatenate(mixing, axis=1)
            grad_scaled.append(jnp.dot(mix, dy_tile, preferred_element_type=F32))
        inside_rows.append(jnp.zeros((LANES - len(inside_rows), length), F32))
        inside = jnp.concatenate(inside_rows, axis=0).T
        from_end = mm(bs, state_low) * end_x
        grad_scaled = jnp.concatenate(grad_scaled, axis=1) + from_end
        entry_dy = dy * entry_x
        entry_dy_low = entry_dy.astype(BF16)
        out_terms = mm(cs, old) * entry_dy
        end_terms = scaled * from_end
        grad_step = mm_ones_tr(xs * grad_scaled, spread, 2)
        out_terms = mm_ones_tr(out_terms, spread, 2)
        end_terms = mm_ones_tr(end_terms, spread, 2)
        keep_row = entry_x[length - 1 : length, :]
        carried = jnp.sum(grad_state * old.astype(F32), axis=0, keepdims=True) * keep_row
        carried = mm_ones_tr(jnp.broadcast_to(carried, (8, width)), spread, 2)[0:1, :]
        triu = (cols >= rows).astype(BF16)
        below = (rows > cols).astype(BF16)
        grad_rate = inside + ones_mm(triu, out_terms, 2) + ones_mm(below, end_terms, 2) + carried
        grad_step = grad_step - decay_rate * grad_rate
        grad_raw = grad_step * sigmoid(raw)
        grad_scores_low = grad_scores.astype(BF16)
        grad_b = mm(grad_scores_low, cs) + mm_tr(scaled * end_x, state_low)
        grad_c = tr_mm(grad_scores_low, bs) + mm_tr(entry_dy_low, old)
        memory[q] = grad_state * keep_row + tr_mm(cs, entry_dy_low)
        conv_grad_x = (skip_ref[...] * dy + step_x * grad_scaled) * slope_x
        conv_grad_t = jnp.concatenate([grad_b, grad_c], axis=1) * slope_t

        remain = rem_ref[0]
        results = [dz]
        for grad, ext, nxt, weight, sums in (
            (conv_grad_x, ext_x.at[q], next_x.at[q], params[0], gx_ref),
            (conv_grad_t, ext_t.at[q], next_t.at[q], params[2], gt_ref),
        ):
            current = ext[pl.ds(HALO, length), :]
            sums[KERNEL : KERNEL + 1, :] += jnp.sum(grad, axis=0, keepdims=True)
            sums[KERNEL - 1 : KERNEL, :] += jnp.sum(grad * current, axis=0, keepdims=True)
            nxt[0:length, :] = grad
            total = weight[KERNEL - 1 : KERNEL, :] * grad
            for back in range(1, KERNEL):
                tap = KERNEL - 1 - back
                shifted = jnp.where(offset >= back, ext[pl.ds(HALO - back, length), :], 0.0)
                sums[tap : tap + 1, :] += jnp.sum(grad * shifted, axis=0, keepdims=True)
                ahead = jnp.where(remain >= back, nxt[pl.ds(back, length), :], 0.0)
                total = total + weight[tap : tap + 1, :] * ahead
            nxt[length:, :] = grad[0:HALO, :]
            results.append(total.astype(BF16))
        results.append(grad_raw.astype(BF16))
        gx_ref[KERNEL + 1 : KERNEL + 2, :] += jnp.sum(dy * xs, axis=0, keepdims=True)
        gh_ref[0:1, :] += jnp.sum(grad_raw, axis=0, keepdims=True)
        gh_ref[1:2, :] += jnp.sum(grad_rate * rate, axis=0, keepdims=True)
        out_ref[0, :, : 2 * width] = jnp.concatenate(results[:2], axis=1)
        out_ref[0, :, 2 * width : 2 * width + 2 * STATE] = results[2]
        out_ref[0, :, 2 * width + 2 * STATE :] = results[3]


TAIL = 2 * STATE + LANES


def whole_spec(shape):
    return pl.BlockSpec(shape, lambda i, order: (0,) * len(shape))


def chunk_specs(steps, length, width, reverse):
    def place(i):
        return steps - 1 - i if reverse else i

    def ordered(q, cols, column=0):
        return pl.BlockSpec(
            (1, length, cols), lambda i, order: (order[q, place(i)], 0, column)
        )

    def before(q, cols, column=0):
        return pl.BlockSpec(
            (1, HALO, cols),
            lambda i, order: (
                order[q, jnp.maximum(place(i) - 1, 0)], length // HALO - 1, column
            ),
        )

    def plain(q, rows, cols):
        return pl.BlockSpec(
            (pl.Squeezed(), 1, rows, cols), lambda i, order: (q, place(i), 0, 0)
        )

    def row(q, rows, cols):
        return pl.BlockSpec((1, rows, cols), lambda i, order: (order[q, place(i)], 0, 0))

    return ordered, before, plain, row, place


def forward_mix(order, proj, off_col, consts):
    seqs = len(proj)
    steps, length, cols = proj[0].shape
    width = (cols - TAIL) // 2
    ordered, before, plain, row, _ = chunk_specs(steps, length, width, False)
    tail_at = 2 * width // TAIL
    in_specs, args, out_specs, out_shape = [], [], [], []
    for q in range(seqs):
        in_specs += [
            ordered(q, 2 * width), before(q, 2 * width),
            ordered(q, TAIL, tail_at), before(q, TAIL, tail_at), plain(q, length, 1),
        ]
        args += [proj[q]] * 4 + [off_col]
        out_specs += [ordered(q, width), ordered(q, width), row(q, 1, length)]
        out_shape += [jax.ShapeDtypeStruct((steps, length, width), BF16)] * 2
        out_shape += [jax.ShapeDtypeStruct((steps, 1, length), F32)]
    outs = pl.pallas_call(
        functools.partial(forward_kernel, seqs=seqs),
        grid_spec=pltpu.PrefetchScalarGridSpec(
            num_scalar_prefetch=1,
            grid=(steps,),
            in_specs=in_specs + [whole_spec(v.shape) for v in consts],
            out_specs=out_specs
            + [pl.BlockSpec((1, seqs, STATE, width), lambda i, order: (i, 0, 0, 0))],
            scratch_shapes=[
                pltpu.VMEM((seqs, STATE, width), F32),
                pltpu.VMEM((seqs, HALO + length, width), F32),
                pltpu.VMEM((seqs, HALO + length, 2 * STATE), F32),
            ],
        ),
        out_shape=out_shape + [jax.ShapeDtypeStruct((steps, seqs, STATE, width), BF16)],
        compiler_params=pltpu.CompilerParams(
            dimension_semantics=("arbitrary",), vmem_limit_bytes=32 << 20
        ),
        cost_estimate=pl.CostEstimate(
            flops=steps * seqs * 900_000_000, transcendentals=0, bytes_accessed=10_000_000
        ),
        name="mix_forward",
    )(order, *args, *consts)
    return outs[0:-1:3], outs[1:-1:3], outs[2:-1:3], outs[-1]


def backward_mix(order, proj, off_col, off_row, rem_col, y, grad_yn, stats, states, consts):
    seqs = len(proj)
    steps, length, cols = proj[0].shape
    width = (cols - TAIL) // 2
    ordered, before, plain, row, place = chunk_specs(steps, length, width, True)
    tail_at = 2 * width // TAIL
    in_specs, args = [], []
    for q in range(seqs):
        in_specs += [
            ordered(q, 2 * width), before(q, 2 * width),
            ordered(q, TAIL, tail_at), before(q, TAIL, tail_at),
            plain(q, length, 1), plain(q, 1, length), plain(q, length, 1),
            ordered(q, width), ordered(q, width), row(q, 2, length),
        ]
        args += [proj[q]] * 4 + [off_col, off_row, rem_col, y[q], grad_yn[q], stats[q]]
    in_specs += [
        pl.BlockSpec((1, seqs, STATE, width), lambda i, order: (place(i), 0, 0, 0))
    ] + [whole_spec(v.shape) for v in consts]
    sums = [(8, width), (8, 2 * STATE), (8, LANES)]
    outs = pl.pallas_call(
        functools.partial(backward_kernel, seqs=seqs),
        grid_spec=pltpu.PrefetchScalarGridSpec(
            num_scalar_prefetch=1,
            grid=(steps,),
            in_specs=in_specs,
            out_specs=[ordered(q, cols) for q in range(seqs)] + [whole_spec(v) for v in sums],
            scratch_shapes=[
                pltpu.VMEM((seqs, STATE, width), F32),
                pltpu.VMEM((seqs, HALO + length, width), F32),
                pltpu.VMEM((seqs, HALO + length, 2 * STATE), F32),
                pltpu.VMEM((seqs, length + HALO, width), F32),
                pltpu.VMEM((seqs, length + HALO, 2 * STATE), F32),
            ],
        ),
        out_shape=[jax.ShapeDtypeStruct(proj[0].shape, BF16)] * seqs
        + [jax.ShapeDtypeStruct(v, F32) for v in sums],
        compiler_params=pltpu.CompilerParams(
            dimension_semantics=("arbitrary",), vmem_limit_bytes=40 << 20
        ),
        cost_estimate=pl.CostEstimate(
            flops=steps * seqs * 2_000_000_000, transcendentals=0, bytes_accessed=16_000_000
        ),
        name="mix_backward",
    )(order, *args, states, *consts)
    return outs[:seqs], outs[seqs], outs[seqs + 1], outs[seqs + 2]


AXES = ("seq", "fsdp")


class Group:
    def __init__(self):
        self.seq = lax.axis_size("seq")
        self.fsdp = lax.axis_size("fsdp")
        self.half = self.seq // 2
        s, f = lax.axis_index("seq"), lax.axis_index("fsdp")
        self.s, self.f = s, f
        self.top, self.low = s // self.half, s % self.half
        self.core, self.pair = f % 2, f // 2
        self.home = self.core == self.top
        self.head_group = self.core * self.half + self.low
        self.low_bits = [1 << i for i in range(self.half.bit_length() - 1)]
        self.pair_bits = [2 << i for i in range((self.fsdp // 2).bit_length() - 1)]

    def swap(self, value, seq_bit=0, fsdp_bit=0, away=False, home=False):
        perm = []
        for s in range(self.seq):
            for f in range(self.fsdp):
                at_home = f % 2 == s // self.half
                if (away and at_home) or (home and not at_home):
                    continue
                perm.append((s * self.fsdp + f, (s ^ seq_bit) * self.fsdp + (f ^ fsdp_bit)))
        return lax.ppermute(value, AXES, perm)

    def bits_for(self, q):
        return self.low_bits if q % 2 == 0 else self.low_bits[::-1]

    def gather_tokens(self, block):
        moved = self.swap(block, self.half, 1, away=True)
        block = jnp.where(self.home, block, moved)
        out = []
        for q in range(block.shape[0]):
            held = block[q][None]
            for bit in self.bits_for(q):
                held = jnp.concatenate([held, self.swap(held, bit)], axis=0)
            out.append(jnp.concatenate([held, self.swap(held, 0, 1)], axis=0))
        return out

    def order(self, seqs):
        chunk = np.arange(self.seq)
        rows = []
        for q in range(seqs):
            table = np.zeros(self.half, np.int32)
            for value in range(self.half):
                table[value] = sum(
                    1 << i for i, bit in enumerate(self.bits_for(q)) if value & bit
                )
            low = (chunk % self.half) ^ self.low
            rows.append(
                jnp.asarray(table)[low] + self.half * ((chunk // self.half) ^ self.core)
            )
        return jnp.stack(rows).astype(jnp.int32)

    def scatter_tokens(self, parts):
        out = []
        for q, held in enumerate(parts):
            for seq_bit, fsdp_bit in [(0, 1)] + [(bit, 0) for bit in self.bits_for(q)[::-1]]:
                count = held.shape[0] // 2
                got = self.swap(held[count:], seq_bit, fsdp_bit)
                held = (held[:count].astype(F32) + got.astype(F32)).astype(BF16)
            out.append(held)
        held = jnp.concatenate(out, axis=0)
        moved = self.swap(held, self.half, 1, away=True)
        return jnp.where(self.home, held, moved).astype(F32)

    def bit_of(self, seq_bit, fsdp_bit):
        return (self.s // seq_bit) % 2 if seq_bit else (self.f // fsdp_bit) % 2

    def ordered(self, value, got, seq_bit, fsdp_bit, axis):
        first = self.bit_of(seq_bit, fsdp_bit) == 0
        return jnp.stack([jnp.where(first, value, got), jnp.where(first, got, value)], axis=axis)

    def merge(self, value, seq_bit, fsdp_bit, axis):
        got = self.swap(value, seq_bit, fsdp_bit)
        first = self.bit_of(seq_bit, fsdp_bit) == 0
        return jnp.concatenate(
            [jnp.where(first, value, got), jnp.where(first, got, value)], axis=axis
        )

    def split(self, value, seq_bit, fsdp_bit, axis):
        bit = self.bit_of(seq_bit, fsdp_bit)
        count = value.shape[axis] // 2
        keep = lax.dynamic_slice_in_dim(value, bit * count, count, axis)
        give = lax.dynamic_slice_in_dim(value, (1 - bit) * count, count, axis)
        return keep, self.swap(give, seq_bit, fsdp_bit)

    def all_bits(self):
        return [(self.half, 0)] + [(b, 0) for b in self.low_bits] + [
            (0, b) for b in self.pair_bits
        ] + [(0, 1)]

    def total(self, value, bits):
        for seq_bit, fsdp_bit in bits:
            value = value + self.swap(value, seq_bit, fsdp_bit)
        return value

    def group_total(self, parts):
        out = []
        for q, value in enumerate(parts):
            shape = value.shape
            steps = [(bit, 0) for bit in self.bits_for(q)] + [(0, 1)]
            for i, (seq_bit, fsdp_bit) in enumerate(steps):
                got = self.swap(value, seq_bit, fsdp_bit)
                pairs = got.reshape((-1, 2, 1 << i) + shape[1:])
                value = value + pairs[:, ::-1].reshape(shape)
            out.append(value)
        return out

    def gather_columns(self, value):
        rows, cols = value.shape[1:]
        keep, got = self.split(value, 0, 1, 0)
        value = self.ordered(keep, got, 0, 1, 1)[:, None]
        for bit in self.low_bits[::-1]:
            keep, got = self.split(value, bit, 0, 0)
            value = self.ordered(keep, got, bit, 0, 2)
            value = value.reshape((keep.shape[0], -1, 2, rows, cols))
        value = self.merge(value[0], self.half, 0, 0)[:, None]
        for bit in self.pair_bits[::-1]:
            got = self.swap(value, 0, bit)
            value = self.ordered(value, got, 0, bit, 2)
            value = value.reshape((self.seq, -1, 2, rows, cols))
        return value.reshape(-1, cols)

    def scatter_columns(self, value):
        cols = value.shape[1]
        pairs = self.fsdp // 2
        rows = value.shape[0] // (self.seq * self.fsdp)
        value = value.reshape(2, self.half, pairs, 2, rows, cols)
        for bit in self.pair_bits[::-1]:
            value = self.halve(value, 0, bit, 2)
        value = self.halve(value[:, :, 0], self.half, 0, 0)
        for bit in self.low_bits[::-1]:
            keep, got = self.split(value, bit, 0, 1)
            value = self.ordered(keep, got, bit, 0, 1)
            value = value.reshape((-1,) + keep.shape[1:])
        keep, got = self.split(value[:, 0], 0, 1, 1)
        return self.ordered(keep[:, 0], got[:, 0], 0, 1, 0).reshape(self.seq, rows, cols)

    def halve(self, value, seq_bit, fsdp_bit, axis):
        keep, got = self.split(value, seq_bit, fsdp_bit, axis)
        return (keep.astype(F32) + got.astype(F32)).astype(BF16)

    def gather_rows(self, value):
        rows, cols = value.shape
        value = self.merge(value[None], self.half, 0, 0)
        for bits in (
            [(b, 0) for b in self.low_bits[::-1]] + [(0, b) for b in self.pair_bits[::-1]] + [(0, 1)]
        ):
            value = self.merge(value[:, None], *bits, 1).reshape(-1, rows, cols)
        return value.reshape(-1, cols)

    def scatter_rows(self, value):
        cols = value.shape[1]
        rows = value.shape[0] // (self.seq * self.fsdp)
        value = value.reshape(2, self.half, self.fsdp // 2, 2, rows, cols)
        for bit in self.pair_bits[::-1]:
            value = self.halve(value, 0, bit, 2)
        value = self.halve(value, self.half, 0, 0)
        for bit in self.low_bits[::-1]:
            value = self.halve(value, bit, 0, 1)
        value = self.halve(value, 0, 1, 3)
        return value.reshape(rows, cols).astype(F32)

    def gather_own_rows(self, value):
        rows, cols = value.shape
        value = self.merge(value[None], 0, 1, 0)
        moved = self.swap(value, self.half, 0, home=True)
        value = jnp.where(self.home, value, moved)[None]
        for bit in self.pair_bits[::-1]:
            value = self.merge(value[:, None], 0, bit, 1).reshape(-1, 2, rows, cols)
        return value.reshape(-1, cols)

    def scatter_own_rows(self, value):
        cols = value.shape[1]
        rows = value.shape[0] // self.fsdp
        value = value.reshape(self.fsdp // 2, 2, rows, cols)
        for bit in self.pair_bits[::-1]:
            value = self.halve(value, 0, bit, 0)
        value = value[0].astype(F32) + self.swap(value[0], self.half, 0, away=True).astype(F32)
        value = value.astype(BF16)
        keep = lax.dynamic_index_in_dim(value, self.core, 0, False)
        give = lax.dynamic_index_in_dim(value, 1 - self.core, 0, False)
        moved = self.swap(give, 0, 1, home=True)
        return jnp.where(self.home, keep, moved).astype(F32)


def spread_last(piece, start, whole):
    zeros_full = jnp.zeros(piece.shape[:-1] + (whole,), F32)
    return lax.dynamic_update_slice_in_dim(zeros_full, piece, start, piece.ndim - 1)


def chunked(per_token, steps, length):
    return per_token.reshape(per_token.shape[0], steps, length)


def local(
    tokens, segments, gain_in, w_in, conv_w, conv_b, dt_bias, a_log, skip, gain_out, w_out,
    cotangent,
):
    group = Group()
    steps = group.seq
    seqs, length, _ = tokens.shape
    width = INNER // steps
    heads = HEADS // steps
    rows_in = w_in.shape[0]
    number = group.head_group

    def mine(array, size):
        return lax.dynamic_slice_in_dim(array, number * size, size, array.ndim - 1)

    wide = tokens.astype(F32)
    scale_in = lax.rsqrt(jnp.mean(wide * wide, axis=-1, keepdims=True) + EPSILON)
    normed = (wide * scale_in * gain_in).astype(BF16)
    h_all = group.gather_tokens(normed)
    order = group.order(seqs)

    zx = w_in[:, : 2 * INNER].reshape(rows_in, 2, steps, width).transpose(2, 0, 1, 3)
    zx = group.gather_columns(zx.reshape(steps, rows_in, 2 * width))
    tail_w = group.gather_rows(w_in[:, 2 * INNER :])
    w_mine = jnp.concatenate(
        [
            zx,
            tail_w[:, : 2 * STATE],
            mine(tail_w[:, 2 * STATE :], heads),
            jnp.zeros((D, LANES - heads), BF16),
        ],
        axis=1,
    )
    cot_all = group.gather_tokens(cotangent)
    out_w = group.gather_own_rows(w_out)

    segs = jnp.where(group.home, segments, group.swap(segments, 0, 1))
    total = steps * length
    index = lax.broadcasted_iota(jnp.int32, (seqs, total), 1)
    starts = jnp.concatenate([jnp.ones((seqs, 1), bool), segs[:, 1:] != segs[:, :-1]], axis=1)
    first = lax.cummax(jnp.where(starts, index, 0), axis=1)
    ends = jnp.concatenate([starts[:, 1:], jnp.ones((seqs, 1), bool)], axis=1)
    last = lax.cummin(jnp.where(ends, index, total), axis=1, reverse=True)
    off = chunked((index - first).astype(F32), steps, length)
    rem = chunked((last - index).astype(F32), steps, length)
    off_col, off_row, rem_col = off[..., None], off[:, :, None, :], rem[..., None]

    heads_p = jnp.stack([mine(dt_bias, heads), mine(a_log, heads)])
    consts = (
        mine(conv_w[:, :INNER], width),
        mine(conv_b[None, :INNER], width),
        conv_w[:, INNER:],
        conv_b[None, INNER:],
        jnp.pad(heads_p, ((0, 6), (0, LANES - heads))),
        jnp.repeat(mine(skip, heads), HEAD_DIM)[None],
        mine(gain_out[None], width),
    )

    def dot(a, b):
        return lax.dot_general(a, b, (((2,), (0,)), ((), ())), preferred_element_type=F32)

    def dot_tr(a, b):
        return lax.dot_general(a, b, (((2,), (1,)), ((), ())), preferred_element_type=F32)

    def dot_tokens(a, b):
        dims = (0, 1)
        return sum(
            lax.dot_general(l, r, ((dims, dims), ((), ())), preferred_element_type=F32)
            for l, r in zip(a, b)
        )

    proj = [dot(h, w_mine).astype(BF16) for h in h_all]
    y, gated, squares, states = forward_mix(order, proj, off_col, consts)

    grad_yn = [dot_tr(cot, out_w) for cot in cot_all]
    sums = group.group_total(
        [
            jnp.stack([sq[:, 0], jnp.sum(g * gt.astype(F32), axis=-1)], axis=1)
            for sq, g, gt in zip(squares, grad_yn, gated)
        ]
    )
    stats, scales = [], []
    for value in sums:
        scale = lax.rsqrt(value[:, 0] / INNER + EPSILON)
        stats.append(jnp.stack([scale, value[:, 1] * (scale * scale * scale / INNER)], axis=1))
        scales.append(scale[..., None])
    mixed = group.scatter_tokens(
        [(dot(gt, out_w) * scale).astype(BF16) for gt, scale in zip(gated, scales)]
    )
    mixed = (wide + mixed).astype(BF16)
    y_normed = [(gt.astype(F32) * scale).astype(BF16) for gt, scale in zip(gated, scales)]
    w_out_grad = group.scatter_own_rows(dot_tokens(y_normed, cot_all).astype(BF16))

    grad_proj, sums_x, sums_t, sums_h = backward_mix(
        order, proj, off_col, off_row, rem_col, y, grad_yn, stats, states, consts
    )

    grad_h = group.scatter_tokens([dot_tr(g, w_mine).astype(BF16) for g in grad_proj])
    part = dot_tokens(h_all, grad_proj)
    gain_part = jnp.sum(part * w_mine.astype(F32), axis=1)
    tail_part = jnp.concatenate(
        [
            part[:, 2 * width : 2 * width + 2 * STATE],
            spread_last(
                part[:, 2 * width + 2 * STATE : 2 * width + 2 * STATE + heads],
                number * heads,
                HEADS,
            ),
        ],
        axis=1,
    )
    zx_grad = group.scatter_columns(part[:, : 2 * width].astype(BF16)).astype(F32)
    tail_grad = group.scatter_rows(tail_part.astype(BF16))
    zx_grad = zx_grad.reshape(steps, rows_in, 2, width).transpose(1, 2, 0, 3)
    w_in_grad = jnp.concatenate([zx_grad.reshape(rows_in, 2 * INNER), tail_grad], axis=1)

    scaled = grad_h * gain_in
    unit = wide * scale_in
    tokens_grad = cotangent.astype(F32) + scale_in * (
        scaled - unit * jnp.mean(scaled * unit, axis=-1, keepdims=True)
    )

    everywhere = group.total(
        jnp.concatenate([gain_part, sums_t[: KERNEL + 1].reshape(-1)]), group.all_bits()
    )
    gain_in_grad = everywhere[:D] / gain_in
    grouped = jnp.concatenate(
        [
            sums_x[: KERNEL + 1].reshape(-1),
            sums_x[KERNEL + 2],
            jnp.sum(sums_x[KERNEL + 1].reshape(heads, HEAD_DIM), axis=-1),
            sums_h[:2, :heads].reshape(-1),
        ]
    )
    grouped = group.total(grouped, [(group.half, 0)] + [(0, b) for b in group.pair_bits])[None]
    for bits in [(b, 0) for b in group.low_bits] + [(0, 1)]:
        grouped = group.merge(grouped, *bits, 0)
    conv_x = grouped[:, : (KERNEL + 1) * width].reshape(steps, KERNEL + 1, width)
    conv_x = conv_x.transpose(1, 0, 2).reshape(KERNEL + 1, INNER)
    conv_grads = jnp.concatenate([conv_x, everywhere[D:].reshape(KERNEL + 1, -1)], axis=1)
    rest = grouped[:, (KERNEL + 1) * width :]
    gain_out_grad = rest[:, :width].reshape(-1)
    per_head = rest[:, width:].reshape(steps, 3, heads).transpose(1, 0, 2).reshape(3, HEADS)
    return (
        mixed, tokens_grad, gain_in_grad, w_in_grad, conv_grads[:KERNEL], conv_grads[KERNEL],
        per_head[1], per_head[2], per_head[0], gain_out_grad, w_out_grad,
    )


def solution(mesh):
    by_token = P("fsdp", "seq", None)
    by_row = P(("seq", "fsdp"), None)
    placed = (
        by_token, P("fsdp", None), P(), by_row, P(), P(), P(), P(), P(), P(), by_row, by_token,
    )
    return jax.shard_map(
        local,
        mesh=mesh,
        in_specs=placed,
        out_specs=(by_token, by_token, P(), by_row, P(), P(), P(), P(), P(), P(), by_row),
        check_vma=False,
    )
```

time: 924 us -> 524 us (0.57)
  waiting for transfers between devices: 451 us -> 174 us
  blocking collectives: 258 us -> 0 us
  starting transfers between devices: 0.37 us -> 103 us
  local copies, waits for them, and re-layouts: 30.2 us -> 62.8 us
  other arithmetic: 26.1 us -> 57.7 us
  matrix products: 93.1 us -> 63.9 us
  between operations: 14.7 us -> 3.06 us
    reduce_scatter x4 -> x0, waiting for transfers between devices: 188 us -> none  [the longest x1 79 us: local(): grad_h = lax.psum_scatter(grad_h, 'seq', scatter_dimension=0).astype(F32)]
    ppermute x0 -> x71, waiting for transfers between devices: none -> 174 us  [swap(): return lax.ppermute(value, AXES, perm)]
    all_gather x4 -> x0, waiting for transfers between devices: 132 us -> none  [the longest x1 97.6 us: local(): cot_all = lax.all_gather(cotangent, 'seq', axis=0)]
    psum x1 -> x0, waiting for transfers between devices: 129 us -> none  [local(): lax.psum((gain_in_part, spread_last(gain_out_part, rank * width, INNER),...]
    unnamed x1 -> x0, blocking collectives: 104 us -> none
    ppermute x0 -> x71, starting transfers between devices: none -> 103 us  [swap(): return lax.ppermute(value, AXES, perm)]
    all_to_all x2 -> x0, blocking collectives: 70.2 us -> none  [the longest x1 41.3 us: local(): lax.all_to_all(part.astype(BF16), 'seq', split_axis=0, concat_axis=0, til...]
    all_gather x1 -> x0, blocking collectives: 56 us -> none  [local(): lax.all_gather(w_in[:, 2 * INNER:], ('seq', 'fsdp'), axis=0, tiled=True)]
  transfers between devices with their start and end apart: 9 -> 71, of which waited for: 7 -> 26; matrix products, arithmetic and copies ran while one was open for 10% -> 32% of each run, Pallas kernels for 1% -> 3%
where the time goes in v2:
time: 524 us; the launch traced here: 517 us
  waiting for transfers between devices  174 us (33%)
  starting transfers between devices  103 us (20%)
  matrix products  63.9 us (12%)
  local copies, waits for them, and re-layouts  62.8 us (12%)
  other arithmetic  57.7 us (11%)
  Pallas kernels  52.2 us (10%)
    ppermute x71, waiting for transfers between devices, swap(): return lax.ppermute(value, AXES, perm)  174 us
    ppermute x71, starting transfers between devices, swap(): return lax.ppermute(value, AXES, perm)  103 us
    pallas_call x1, Pallas kernels, backward_mix(): pl.pallas_call(functools.partial(backward_kernel, seqs=seqs), grid_spec=p...  36.8 us
    dot_general x4, matrix products, dot_tr(): lax.dot_general(a, b, (((2,), (1,)), ((), ())), preferred_element_type=F32)  24.8 us
    dot_general x4, matrix products, dot(): lax.dot_general(a, b, (((2,), (0,)), ((), ())), preferred_element_type=F32)  20.6 us
    dot_general x4, matrix products, dot_tokens(): lax.dot_general(l, r, ((dims, dims), ((), ())), preferred_element_type=F32)  18.6 us
    pallas_call x1, Pallas kernels, forward_mix(): pl.pallas_call(functools.partial(forward_kernel, seqs=seqs), grid_spec=pl...  15.5 us
    unnamed x200, local copies, waits for them, and re-layouts  14.8 us
  transfers between devices with their start and end apart: 71, of which 26 were waited for; matrix products, arithmetic and copies ran while one was open for 32% of the time, Pallas kernels for 3%

profile of v2, /device:TPU:1, one launch (start us, length us, event | category | flops | bytes accessed | tf_op | source)
XLA Modules:
  0.0 517.0 jit_solution(40618459719895706)
XLA Ops:
  2.1 3.1 collective-permute-start.9
  11.3 4.5 collective-permute-start.21
  20.7 4.7 reduce-window.16
  34.8 14.7 %collective-permute-done.10 = bf16[2,1,48,304]{3,2,1,0:T(8,128)(2,1)S(1)} collective-permute-done((bf16[2,1,48,304]{3,2,1,0:T(8,128)(2,1)S(1)}, bf16[2,1,48,304]{3,2,1,0:T(8,128)(2,1)S(1)}, u32[]{:S(2)}, u32[]{:S(2)}) %collective-permute-start.10) | collective-permute-done | bytes 58400 | tf_op jit(solution)/shard_map/ppermute | solution.py:485
  51.0 3.4 collective-permute-done.11
  61.9 3.1 collective-permute-start.13
  72.1 4.1 collective-permute-done.19
  78.8 10.7 %collective-permute-done.15 = bf16[1,128,1536]{2,1,0:T(8,128)(2,1)S(1)} collective-permute-done((bf16[1,128,1536]{2,1,0:T(8,128)(2,1)S(1)}, bf16[1,128,1536]{2,1,0:T(8,128)(2,1)S(1)}, u32[]{:S(2)}, u32[]{:S(2)}) %collective-permute-start.15) | collective-permute-done | bytes 393248 | tf_op jit(solution)/shard_map/ppermute | solution.py:485
  91.9 7.5 %collective-permute-done.31 = bf16[1,128,1536]{2,1,0:T(8,128)(2,1)S(1)} collective-permute-done((bf16[1,128,1536]{2,1,0:T(8,128)(2,1)S(1)}, bf16[1,128,1536]{2,1,0:T(8,128)(2,1)S(1)}, u32[]{:S(2)}, u32[]{:S(2)}) %collective-permute-start.31) | collective-permute-done | bytes 393248 | tf_op jit(solution)/shard_map/ppermute | solution.py:485
  100.1 2.2 collective-permute-start.8
  102.5 3.9 collective-permute-done.16
  107.9 9.9 %collective-permute-start.17 = (bf16[4,128,1536]{2,1,0:T(8,128)(2,1)}, bf16[4,128,1536]{2,1,0:T(8,128)(2,1)}, u32[]{:S(2)}, u32[]{:S(2)}) collective-permute-start(bf16[4,128,1536]{2,1,0:T(8,128)(2,1)} %pad_maximum_fusion.6), channel_id=1, source_target_pairs={{0,1},{1,0},{2,3},{3,2},{4,5},{5,4},{6,7},{7,6},{8,9},{9,8},{10,11... | collective-permute-start | bytes 4718600 | tf_op jit(solution)/shard_map/ppermute | solution.py:485
  120.5 4.2 collective-permute-start.3
  124.7 11.2 %collective-permute-done.23 = bf16[2,128,1536]{2,1,0:T(8,128)(2,1)S(1)} collective-permute-done((bf16[2,128,1536]{2,1,0:T(8,128)(2,1)S(1)}, bf16[2,128,1536]{2,1,0:T(8,128)(2,1)S(1)}, u32[]{:S(2)}, u32[]{:S(2)}) %collective-permute-start.23) | collective-permute-done | bytes 786464 | tf_op jit(solution)/shard_map/ppermute | solution.py:485
  137.4 2.3 collective-permute-start.24
  143.0 6.8 %concatenate.125 = bf16[1536,1152]{1,0:T(8,128)(2,1)} concatenate(bf16[1536,768]{1,0:T(8,128)(2,1)} %bitcast.247, bf16[1536,256]{1,0:T(8,128)(2,1)} %slice.280, bf16[1536,6]{1,0:T(8,128)(2,1)} %constant_dynamic-slice_fusion.9, bf16[1536,122]{1,0:T(8,128)(2,1)S(1)} %broadcast_in_dim.54), dimensions={1} | concatenate | bytes 7077888 | tf_op jit(solution)/shard_map/concatenate | solution.py:682
  149.8 7.2 %convolution_convert_fusion.refs_5_.refs_6_.refs_7_.refs_8_.refs_10_.refs_11_.refs_12_.refs_13_ = bf16[8,128,1152]{2,1,0:T(8,128)(2,1)S(1)} fusion(bf16[1536,1152]{1,0:T(8,128)(2,1)} %concatenate.125, bf16[4,128,1536]{2,1,0:T(8,128)(2,1)} %collective-permute-done.17, bf16[2,128,1536]{2,1,0:T(8,128)(2,1)} %copy-done.64, bf16[1,128,1536]{2,1,0:T(8,128)(2,1)} %copy-done.47, ...), kind=kOutput, calls=%fused_computation.8 | convolution fusion | flops 3629776896 | bytes 9043968 | tf_op jit(solution)/shard_map/dot_general | solution.py:717
  157.1 6.5 %convolution_convert_fusion.1.refs_0_.refs_1_.refs_2_.refs_3_ = bf16[8,128,1152]{2,1,0:T(8,128)(2,1)S(1)} fusion(bf16[1536,1152]{1,0:T(8,128)(2,1)S(1)} %copy-done.19, bf16[4,128,1536]{2,1,0:T(8,128)(2,1)} %collective-permute-done.3, bf16[2,128,1536]{2,1,0:T(8,128)(2,1)S(1)} %copy-done.59, bf16[1,128,1536]{2,1,0:T(8,128)(2,1)S(1)} %copy-done.45, ...), kind=kOutput, calls=%fused_computation.9 | convolution fusion | flops 3629776896 | bytes 9043968 | tf_op jit(solution)/shard_map/dot_general | solution.py:717
  163.6 15.5 %mix_forward.1 = (bf16[8,128,384]{2,1,0:T(8,128)(2,1)S(1)}, bf16[8,128,384]{2,1,0:T(8,128)(2,1)S(1)}, f32[8,1,128]{2,1,0:T(1,128)S(1)}, bf16[8,128,384]{2,1,0:T(...) custom-call(s32[2,8]{1,0:T(2,128)S(1)} %pad_add_fusion.order_ref, ...), custom_call_target="tpu_custom_call" | custom-call | flops 14400000000 | bytes 10000000 | tf_op jit(solution)/shard_map/mix_forward/pallas_call | solution.py:387
  179.2 5.7 %fusion.10 = (f32[8,128]{1,0:T(8,128)S(1)}, f32[8,128,384]{2,1,0:T(8,128)}) fusion(bf16[8,128,384]{2,1,0:T(8,128)(2,1)S(1)} %get-tuple-element.23, bf16[384,1536,1]{1,0,2:T(8,128)(2,1)S(1)} %bitcast.267, bf16[4,128,1536]{2,1,0:T(8,128)(2,1)} %collective-permute-done.24, bf16[2,128,1536]{2,1,0:T(8,128)(2,1)S(1)} %copy-done.56, ...), kind=kOutput, calls=%fused_computation.40 | convolution fusion | flops 1213856768 | bytes 6688768 | tf_op jit(solution)/shard_map/dot_general | solution.py:720
  185.2 4.4 fusion.12
  193.5 2.3 collective-permute-start.27
  205.4 36.8 %mix_backward.1 = (bf16[8,128,1152]{2,1,0:T(8,128)(2,1)S(1)}, bf16[8,128,1152]{2,1,0:T(8,128)(2,1)S(1)}, f32[8,384]{1,0:T(8,128)S(1)}, f32[8,256]{1,0:T(8,128)S(1)}, f32[8,128]{1,0:T(8,128)S(1)}) custom-call(s32[2,8]{1,0:T(2,128)S(1)} %pad_add_fusion.order_ref, bf16[8,128,1152]{2,1,0:T(8,128)(2,1)} %copy-done.9, bf16[8,128,1152]{2,1,0:T(8,128)(2,1)} %copy-done.9, ...), custom_call_target="tpu_custom_call" | custom-call | flops 32000000000 | bytes 16000000 | tf_op jit(solution)/shard_map/mix_backward/pallas_call | solution.py:432
  246.4 8.8 %convolution_convert_fusion.3 = bf16[8,128,1536]{2,1,0:T(8,128)(2,1)} fusion(bf16[8,128,1152]{2,1,0:T(8,128)(2,1)} %copy-done.6, bf16[1536,1152]{1,0:T(8,128)(2,1)} %concatenate.125), kind=kOutput, calls=%fused_computation.11 | convolution fusion | flops 3625451520 | bytes 9043968 | tf_op jit(solution)/shard_map/dot_general | solution.py:720
  255.3 5.9 %convolution_convert_fusion.2 = bf16[8,128,1536]{2,1,0:T(8,128)(2,1)} fusion(bf16[8,128,1152]{2,1,0:T(8,128)(2,1)S(1)} %copy-done.5, bf16[1536,1152]{1,0:T(8,128)(2,1)S(1)} %copy-done.20), kind=kOutput, calls=%fused_computation.10 | convolution fusion | flops 3625451520 | bytes 9043968 | tf_op jit(solution)/shard_map/dot_general | solution.py:720
  261.2 5.9 %convolution_bitcast_fusion = f32[1536,1152]{1,0:T(8,128)S(1)} fusion(bf16[8,128,1152]{2,1,0:T(8,128)(2,1)S(1)} %copy-done.5, bf16[4,128,1536]{2,1,0:T(8,128)(2,1)} %collective-permute-done.17, bf16[2,128,1536]{2,1,0:T(8,128)(2,1)S(1)} %copy-done.65, bf16[1,128,1536]{2,1,0:T(8,128)(2,1)S(1)} %copy-done.48, bf16[1,128,1536]{2,1,0:T(8,128)(2,1)S(1)} %copy-done.29), kind=kOutput, calls=%fused_computation.2 | convolution fusion | flops 3628597248 | bytes 12582912 | tf_op jit(solution)/shard_map/dot_general | solution.py:725
  267.2 6.5 %fusion.68 = (bf16[1536,1152]{1,0:T(8,128)(2,1)S(1)}, f32[1536]{0:T(1024)S(1)}, bf16[1536,1152]{1,0:T(8,128)(2,1)S(1)}) fusion(bf16[1536,1152]{1,0:T(8,128)(2,1)S(1)} %copy-done.20, f32[1536,1152]{1,0:T(8,128)S(1)} %convolution_bitcast_fusion, bf16[8,128,1152]{2,1,0:T(8,128)(2,1)S(1)} %copy-done.7, bf16[4,128,1536]{2,1,0:T(8,128)(2,1)} %collective-permute-done.3, ...), kind=kOutput, calls=%fused_computation.263 | convolution fusion | flops 3639212544 | bytes 23205888 | tf_op jit(solution)/shard_map/dot_general | solution.py:725
  275.2 3.5 multiply_convert_fusion.1
  278.7 3.4 multiply_convert_fusion
  282.2 3.2 convolution_bitcast_fusion.2
  285.4 2.9 fusion.6
  293.2 11.3 %collective-permute-done.64 = f32[2322]{0:T(1024)S(1)} collective-permute-done((f32[2322]{0:T(1024)S(1)}, f32[2322]{0:T(1024)S(1)}, u32[]{:S(2)}, u32[]{:S(2)}) %collective-permute-start.64) | collective-permute-done | bytes 9320 | tf_op jit(solution)/shard_map/ppermute | solution.py:485
  308.9 4.4 dynamic_update_slice.3
  319.3 2.9 slice.289
  328.4 5.1 collective-permute-done.51
  333.5 5.2 %collective-permute-start.28 = (bf16[4,128,1536]{2,1,0:T(8,128)(2,1)}, bf16[4,128,1536]{2,1,0:T(8,128)(2,1)}, u32[]{:S(2)}, u32[]{:S(2)}) collective-permute-start(bf16[4,128,1536]{2,1,0:T(8,128)(2,1)} %slice.289), channel_id=1, source_target_pairs={{0,1},{1,0},{2,3},{3,2},{4,5},{5,4},{6,7},{7,6},{8,9},{9,8},{10,11... | collective-permute-start | bytes 4718600 | tf_op jit(solution)/shard_map/ppermute | solution.py:485
  350.5 13.2 %collective-permute-done.59 = bf16[1,4,1,2,48,304]{5,4,3,2,1,0:T(8,128)(2,1)S(1)} collective-permute-done((bf16[1,4,1,2,48,304]{5,4,3,2,1,0:T(8,128)(2,1)S(1)}, bf16[1,4,1,2,48,304]{5,4,3,2,1,0:T(8,128)(2,1)S(1)}, u32[]{:S(2)}, u32[]{:S(2)}) %collective-permute-start.59) | collective-permute-done | bytes 233504 | tf_op jit(solution)/shard_map/ppermute | solution.py:485
  366.4 2.4 collective-permute-done.60
  370.7 4.4 collective-permute-start.69
  382.8 9.2 %collective-permute-start.44 = (bf16[4,128,1536]{2,1,0:T(8,128)(2,1)}, bf16[4,128,1536]{2,1,0:T(8,128)(2,1)S(1)}, u32[]{:S(2)}, u32[]{:S(2)}) collective-permute-start(bf16[4,128,1536]{2,1,0:T(8,128)(2,1)} %slice.312), channel_id=1, source_target_pairs={{0,1},{1,0},{2,3},{3,2},{4,5},{5,4},{6,7},{7,6},{8,9},{9,8},{10,11... | collective-permute-start | bytes 4718600 | tf_op jit(solution)/shard_map/ppermute | solution.py:485
  403.8 19.0 %collective-permute-done.54 = bf16[1,4,2,48,768]{4,3,2,1,0:T(8,128)(2,1)S(1)} collective-permute-done((bf16[1,4,2,48,768]{4,3,2,1,0:T(8,128)(2,1)S(1)}, bf16[1,4,2,48,768]{4,3,2,1,0:T(8,128)(2,1)S(1)}, u32[]{:S(2)}, u32[]{:S(2)}) %collective-permute-start.54) | collective-permute-done | bytes 589856 | tf_op jit(solution)/shard_map/ppermute | solution.py:485
  424.8 27.7 %collective-permute-done.55 = bf16[1,2,2,48,768]{4,3,2,1,0:T(8,128)(2,1)S(1)} collective-permute-done((bf16[1,2,2,48,768]{4,3,2,1,0:T(8,128)(2,1)S(1)}, bf16[1,2,2,48,768]{4,3,2,1,0:T(8,128)(2,1)S(1)}, u32[]{:S(2)}, u32[]{:S(2)}) %collective-permute-start.55) | collective-permute-done | bytes 294944 | tf_op jit(solution)/shard_map/ppermute | solution.py:485
  459.6 5.0 collective-permute-start.57
  466.8 2.7 convert_element_type.363
  473.2 4.0 collective-permute-start.40
  479.5 3.8 collective-permute-start.47
  484.4 28.2 %collective-permute-done.47 = bf16[2,128,1536]{2,1,0:T(8,128)(2,1)S(1)} collective-permute-done((bf16[2,128,1536]{2,1,0:T(8,128)(2,1)S(1)}, bf16[2,128,1536]{2,1,0:T(8,128)(2,1)S(1)}, u32[]{:S(2)}, u32[]{:S(2)}) %collective-permute-start.47) | collective-permute-done | bytes 786464 | tf_op jit(solution)/shard_map/ppermute | solution.py:485
  513.2 3.5 fusion.18
  (520 shorter events, 147.1 us)
Async XLA Ops:
  2.1 27.0 %collective-permute-start.9 = (bf16[1,48,304]{2,1,0:T(8,128)(2,1)}, bf16[1,48,304]{2,1,0:T(8,128)(2,1)}, u32[]{:S(2)}, u32[]{:S(2)}) collective-permute-start(bf16[1,48,304]{2,1,0:T(8,128)(2,1)} %slice_bitcast_fusion), channel_id=1, source_target_pairs={{0,16},{1,17},{2,18},{3,19},{4,20},{5,21},{6,22},{7,23},{8,24},{9,... | collective-permute-start | bytes 87560 | tf_op jit(solution)/shard_map/ppermute | solution.py:485
  7.0 48.9 %collective-permute-start.4 = (bf16[4,48,768]{2,1,0:T(8,128)(2,1)}, bf16[4,48,768]{2,1,0:T(8,128)(2,1)}, u32[]{:S(2)}, u32[]{:S(2)}) collective-permute-start(bf16[4,48,768]{2,1,0:T(8,128)(2,1)} %constant_dynamic-slice_fusion.10), channel_id=1, source_target_pairs={{0,1},{1,0},{2,3},{3,2},{4,5},{5,4},{6,7},{7,6},{8,9},{9,8},{10,11... | collective-permute-start | bytes 884744 | tf_op jit(solution)/shard_map/ppermute | solution.py:485
  9.4 57.0 %collective-permute-start = (bf16[2,128,1536]{2,1,0:T(8,128)(2,1)}, bf16[2,128,1536]{2,1,0:T(8,128)(2,1)}, u32[]{:S(2)}, u32[]{:S(2)}) collective-permute-start(bf16[2,128,1536]{2,1,0:T(8,128)(2,1)} %fusion.14), channel_id=1, source_target_pairs={{1,16},{3,18},{5,20},{7,22},{9,24},{11,26},{13,28},{15,30},{16,1},... | collective-permute-start | bytes 2359304 | tf_op jit(solution)/shard_map/ppermute | solution.py:485
  11.3 55.1 %collective-permute-start.21 = (bf16[2,128,1536]{2,1,0:T(8,128)(2,1)}, bf16[2,128,1536]{2,1,0:T(8,128)(2,1)}, u32[]{:S(2)}, u32[]{:S(2)}) collective-permute-start(bf16[2,128,1536]{2,1,0:T(8,128)(2,1)} %param.29), channel_id=1, source_target_pairs={{1,16},{3,18},{5,20},{7,22},{9,24},{11,26},{13,28},{15,30},{16,1},... | collective-permute-start | bytes 2359304 | tf_op jit(solution)/shard_map/ppermute | solution.py:485
  19.4 37.6 %collective-permute-start.18 = (bf16[1,96,1536]{2,1,0:T(8,128)(2,1)}, bf16[1,96,1536]{2,1,0:T(8,128)(2,1)}, u32[]{:S(2)}, u32[]{:S(2)}) collective-permute-start(bf16[1,96,1536]{2,1,0:T(8,128)(2,1)} %bitcast.31), channel_id=1, source_target_pairs={{0,1},{1,0},{2,3},{3,2},{4,5},{5,4},{6,7},{7,6},{8,9},{9,8},{10,11... | collective-permute-start | bytes 884744 | tf_op jit(solution)/shard_map/ppermute | solution.py:485
  29.9 19.6 %collective-permute-start.10 = (bf16[2,1,48,304]{3,2,1,0:T(8,128)(2,1)S(1)}, bf16[2,1,48,304]{3,2,1,0:T(8,128)(2,1)S(1)}, u32[]{:S(2)}, u32[]{:S(2)}) collective-permute-start(bf16[2,1,48,304]{3,2,1,0:T(8,128)(2,1)S(1)} %maximum_bitcast_fusion.1), channel_id=1, source_target_pairs={{0,8},{1,9},{2,10},{3,11},{4,12},{5,13},{6,14},{7,15},{8,0},{9,1},... | collective-permute-start | bytes 175112 | tf_op jit(solution)/shard_map/ppermute | solution.py:485
  58.2 18.0 %collective-permute-start.19 = (bf16[2,96,1536]{2,1,0:T(8,128)(2,1)S(1)}, bf16[2,96,1536]{2,1,0:T(8,128)(2,1)S(1)}, u32[]{:S(2)}, u32[]{:S(2)}) collective-permute-start(bf16[2,96,1536]{2,1,0:T(8,128)(2,1)S(1)} %pad_maximum_fusion.19), channel_id=1, source_target_pairs={{0,16},{2,18},{4,20},{6,22},{8,24},{10,26},{12,28},{14,30},{17,1},... | collective-permute-start | bytes 1769480 | tf_op jit(solution)/shard_map/ppermute | solution.py:485
  61.9 14.4 %collective-permute-start.13 = (bf16[16,1,48,304]{3,2,0,1:T(8,128)(2,1)S(1)}, bf16[16,1,48,304]{3,2,0,1:T(8,128)(2,1)S(1)}, u32[]{:S(2)}, u32[]{:S(2)}) collective-permute-start(bf16[16,1,48,304]{3,2,0,1:T(8,128)(2,1)S(1)} %bitcast.259), channel_id=1, source_target_pairs={{0,1},{1,0},{2,3},{3,2},{4,5},{5,4},{6,7},{7,6},{8,9},{9,8},{10,11... | collective-permute-start | bytes 1400840 | tf_op jit(solution)/shard_map/ppermute | solution.py:485
  68.4 21.1 %collective-permute-start.15 = (bf16[1,128,1536]{2,1,0:T(8,128)(2,1)S(1)}, bf16[1,128,1536]{2,1,0:T(8,128)(2,1)S(1)}, u32[]{:S(2)}, u32[]{:S(2)}) collective-permute-start(bf16[1,128,1536]{2,1,0:T(8,128)(2,1)S(1)} %get-tuple-element.64), channel_id=1, source_target_pairs={{0,8},{1,9},{2,10},{3,11},{4,12},{5,13},{6,14},{7,15},{8,0},{9,1},... | collective-permute-start | bytes 1179656 | tf_op jit(solution)/shard_map/ppermute | solution.py:485
  68.5 23.1 %collective-permute-start.1 = (bf16[1,128,1536]{2,1,0:T(8,128)(2,1)S(1)}, bf16[1,128,1536]{2,1,0:T(8,128)(2,1)S(1)}, u32[]{:S(2)}, u32[]{:S(2)}) collective-permute-start(bf16[1,128,1536]{2,1,0:T(8,128)(2,1)S(1)} %get-tuple-element.65), channel_id=1, source_target_pairs={{0,4},{1,5},{2,6},{3,7},{4,0},{5,1},{6,2},{7,3},{8,12},{9,13},{10,... | collective-permute-start | bytes 1179656 | tf_op jit(solution)/shard_map/ppermute | solution.py:485
  70.7 21.0 %collective-permute-start.22 = (bf16[1,128,1536]{2,1,0:T(8,128)(2,1)S(1)}, bf16[1,128,1536]{2,1,0:T(8,128)(2,1)S(1)}, u32[]{:S(2)}, u32[]{:S(2)}) collective-permute-start(bf16[1,128,1536]{2,1,0:T(8,128)(2,1)S(1)} %get-tuple-element.62), channel_id=1, source_target_pairs={{0,4},{1,5},{2,6},{3,7},{4,0},{5,1},{6,2},{7,3},{8,12},{9,13},{10,... | collective-permute-start | bytes 1179656 | tf_op jit(solution)/shard_map/ppermute | solution.py:485
  76.2 23.2 %collective-permute-start.31 = (bf16[1,128,1536]{2,1,0:T(8,128)(2,1)S(1)}, bf16[1,128,1536]{2,1,0:T(8,128)(2,1)S(1)}, u32[]{:S(2)}, u32[]{:S(2)}) collective-permute-start(bf16[1,128,1536]{2,1,0:T(8,128)(2,1)S(1)} %get-tuple-element.63), channel_id=1, source_target_pairs={{0,8},{1,9},{2,10},{3,11},{4,12},{5,13},{6,14},{7,15},{8,0},{9,1},... | collective-permute-start | bytes 1179656 | tf_op jit(solution)/shard_map/ppermute | solution.py:485
  76.3 23.2 %collective-permute-start.7 = (bf16[4,2,48,768]{3,2,1,0:T(8,128)(2,1)S(1)}, bf16[4,2,48,768]{3,2,1,0:T(8,128)(2,1)S(1)}, u32[]{:S(2)}, u32[]{:S(2)}) collective-permute-start(bf16[4,2,48,768]{3,2,1,0:T(8,128)(2,1)S(1)} %bitcast.260), channel_id=1, source_target_pairs={{0,16},{1,17},{2,18},{3,19},{4,20},{5,21},{6,22},{7,23},{8,24},{9,... | collective-permute-start | bytes 1769480 | tf_op jit(solution)/shard_map/ppermute | solution.py:485
  91.5 14.9 %collective-permute-start.16 = (bf16[2,128,1536]{2,1,0:T(8,128)(2,1)S(1)}, bf16[2,128,1536]{2,1,0:T(8,128)(2,1)S(1)}, u32[]{:S(2)}, u32[]{:S(2)}) collective-permute-start(bf16[2,128,1536]{2,1,0:T(8,128)(2,1)S(1)} %pad_maximum_fusion.12), channel_id=1, source_target_pairs={{0,4},{1,5},{2,6},{3,7},{4,0},{5,1},{6,2},{7,3},{8,12},{9,13},{10,... | collective-permute-start | bytes 2359304 | tf_op jit(solution)/shard_map/ppermute | solution.py:485
  91.7 27.4 %collective-permute-start.2 = (bf16[2,128,1536]{2,1,0:T(8,128)(2,1)S(1)}, bf16[2,128,1536]{2,1,0:T(8,128)(2,1)S(1)}, u32[]{:S(2)}, u32[]{:S(2)}) collective-permute-start(bf16[2,128,1536]{2,1,0:T(8,128)(2,1)S(1)} %pad_maximum_fusion.11), channel_id=1, source_target_pairs={{0,8},{1,9},{2,10},{3,11},{4,12},{5,13},{6,14},{7,15},{8,0},{9,1},... | collective-permute-start | bytes 2359304 | tf_op jit(solution)/shard_map/ppermute | solution.py:485
  99.4 36.6 %collective-permute-start.23 = (bf16[2,128,1536]{2,1,0:T(8,128)(2,1)S(1)}, bf16[2,128,1536]{2,1,0:T(8,128)(2,1)S(1)}, u32[]{:S(2)}, u32[]{:S(2)}) collective-permute-start(bf16[2,128,1536]{2,1,0:T(8,128)(2,1)S(1)} %pad_maximum_fusion.13), channel_id=1, source_target_pairs={{0,8},{1,9},{2,10},{3,11},{4,12},{5,13},{6,14},{7,15},{8,0},{9,1},... | collective-permute-start | bytes 2359304 | tf_op jit(solution)/shard_map/ppermute | solution.py:485
  99.5 40.2 %collective-permute-start.32 = (bf16[2,128,1536]{2,1,0:T(8,128)(2,1)S(1)}, bf16[2,128,1536]{2,1,0:T(8,128)(2,1)S(1)}, u32[]{:S(2)}, u32[]{:S(2)}) collective-permute-start(bf16[2,128,1536]{2,1,0:T(8,128)(2,1)S(1)} %pad_maximum_fusion.14), channel_id=1, source_target_pairs={{0,4},{1,5},{2,6},{3,7},{4,0},{5,1},{6,2},{7,3},{8,12},{9,13},{10,... | collective-permute-start | bytes 2359304 | tf_op jit(solution)/shard_map/ppermute | solution.py:485
  100.1 41.0 %collective-permute-start.8 = (bf16[8,1,2,48,768]{4,3,2,0,1:T(8,128)(2,1)S(1)}, bf16[8,1,2,48,768]{4,3,2,0,1:T(8,128)(2,1)S(1)}, u32[]{:S(2)}, u32[]{:S(2)}) collective-permute-start(bf16[8,1,2,48,768]{4,3,2,0,1:T(8,128)(2,1)S(1)} %maximum_bitcast_fusion), channel_id=1, source_target_pairs={{0,2},{1,3},{2,0},{3,1},{4,6},{5,7},{6,4},{7,5},{8,10},{9,11},{10,... | collective-permute-start | bytes 3538952 | tf_op jit(solution)/shard_map/ppermute | solution.py:485
  107.9 41.9 %collective-permute-start.17 = (bf16[4,128,1536]{2,1,0:T(8,128)(2,1)}, bf16[4,128,1536]{2,1,0:T(8,128)(2,1)}, u32[]{:S(2)}, u32[]{:S(2)}) collective-permute-start(bf16[4,128,1536]{2,1,0:T(8,128)(2,1)} %pad_maximum_fusion.6), channel_id=1, source_target_pairs={{0,1},{1,0},{2,3},{3,2},{4,5},{5,4},{6,7},{7,6},{8,9},{9,8},{10,11... | collective-permute-start | bytes 4718600 | tf_op jit(solution)/shard_map/ppermute | solution.py:485
  120.5 36.5 %collective-permute-start.3 = (bf16[4,128,1536]{2,1,0:T(8,128)(2,1)}, bf16[4,128,1536]{2,1,0:T(8,128)(2,1)}, u32[]{:S(2)}, u32[]{:S(2)}) collective-permute-start(bf16[4,128,1536]{2,1,0:T(8,128)(2,1)} %pad_maximum_fusion.5), channel_id=1, source_target_pairs={{0,1},{1,0},{2,3},{3,2},{4,5},{5,4},{6,7},{7,6},{8,9},{9,8},{10,11... | collective-permute-start | bytes 4718600 | tf_op jit(solution)/shard_map/ppermute | solution.py:485
  137.4 41.7 %collective-permute-start.24 = (bf16[4,128,1536]{2,1,0:T(8,128)(2,1)}, bf16[4,128,1536]{2,1,0:T(8,128)(2,1)}, u32[]{:S(2)}, u32[]{:S(2)}) collective-permute-start(bf16[4,128,1536]{2,1,0:T(8,128)(2,1)} %pad_maximum_fusion.7), channel_id=1, source_target_pairs={{0,1},{1,0},{2,3},{3,2},{4,5},{5,4},{6,7},{7,6},{8,9},{9,8},{10,11... | collective-permute-start | bytes 4718600 | tf_op jit(solution)/shard_map/ppermute | solution.py:485
  141.1 44.1 %collective-permute-start.33 = (bf16[4,128,1536]{2,1,0:T(8,128)(2,1)}, bf16[4,128,1536]{2,1,0:T(8,128)(2,1)}, u32[]{:S(2)}, u32[]{:S(2)}) collective-permute-start(bf16[4,128,1536]{2,1,0:T(8,128)(2,1)} %pad_maximum_fusion.8), channel_id=1, source_target_pairs={{0,1},{1,0},{2,3},{3,2},{4,5},{5,4},{6,7},{7,6},{8,9},{9,8},{10,11... | collective-permute-start | bytes 4718600 | tf_op jit(solution)/shard_map/ppermute | solution.py:485
  245.5 45.1 %collective-permute-start.63 = (f32[2322]{0:T(1024)S(1)}, f32[2322]{0:T(1024)S(1)}, u32[]{:S(2)}, u32[]{:S(2)}) collective-permute-start(f32[2322]{0:T(1024)S(1)} %concatenate.147), channel_id=1, source_target_pairs={{0,16},{1,17},{2,18},{3,19},{4,20},{5,21},{6,22},{7,23},{8,24},{9,... | collective-permute-start | bytes 27872 | tf_op jit(solution)/shard_map/ppermute | solution.py:485
  273.7 17.7 %collective-permute-start.48 = (f32[2816]{0:T(1024)S(1)}, f32[2816]{0:T(1024)S(1)}, u32[]{:S(2)}, u32[]{:S(2)}) collective-permute-start(f32[2816]{0:T(1024)S(1)} %pad_maximum_fusion.35), channel_id=1, source_target_pairs={{0,16},{1,17},{2,18},{3,19},{4,20},{5,21},{6,22},{7,23},{8,24},{9,... | collective-permute-start | bytes 33800 | tf_op jit(solution)/shard_map/ppermute | solution.py:485
  289.9 79.4 %collective-permute-start.68 = (bf16[1,2,96,1536]{3,2,1,0:T(8,128)(2,1)}, bf16[1,2,96,1536]{3,2,1,0:T(8,128)(2,1)}, u32[]{:S(2)}, u32[]{:S(2)}) collective-permute-start(bf16[1,2,96,1536]{3,2,1,0:T(8,128)(2,1)} %constant_dynamic-slice_fusion), channel_id=1, source_target_pairs={{0,2},{1,3},{2,0},{3,1},{4,6},{5,7},{6,4},{7,5},{8,10},{9,11},{10,... | collective-permute-start | bytes 1769480 | tf_op jit(solution)/shard_map/ppermute | solution.py:485
  290.6 13.9 %collective-permute-start.64 = (f32[2322]{0:T(1024)S(1)}, f32[2322]{0:T(1024)S(1)}, u32[]{:S(2)}, u32[]{:S(2)}) collective-permute-start(f32[2322]{0:T(1024)S(1)} %add.358), channel_id=1, source_target_pairs={{0,2},{1,3},{2,0},{3,1},{4,6},{5,7},{6,4},{7,5},{8,10},{9,11},{10,... | collective-permute-start | bytes 27872 | tf_op jit(solution)/shard_map/ppermute | solution.py:485
  292.0 21.3 %collective-permute-start.49 = (f32[2816]{0:T(1024)}, f32[2816]{0:T(1024)}, u32[]{:S(2)}, u32[]{:S(2)}) collective-permute-start(f32[2816]{0:T(1024)} %fusion.81), channel_id=1, source_target_pairs={{0,4},{1,5},{2,6},{3,7},{4,0},{5,1},{6,2},{7,3},{8,12},{9,13},{10,... | collective-permute-start | bytes 33800 | tf_op jit(solution)/shard_map/ppermute | solution.py:485
  307.4 84.8 %collective-permute-start.53 = (bf16[2,4,1,2,48,768]{5,4,3,2,1,0:T(8,128)(2,1)}, bf16[2,4,1,2,48,768]{5,4,3,2,1,0:T(8,128)(2,1)}, u32[]{:S(2)}, u32[]{:S(2)}) collective-permute-start(bf16[2,4,1,2,48,768]{5,4,3,2,1,0:T(8,128)(2,1)} %constant_dynamic-slice_fusion.7), channel_id=1, source_target_pairs={{0,2},{1,3},{2,0},{3,1},{4,6},{5,7},{6,4},{7,5},{8,10},{9,11},{10,... | collective-permute-start | bytes 3538952 | tf_op jit(solution)/shard_map/ppermute | solution.py:485
  316.0 22.7 %collective-permute-start.66 = (f32[2,2322]{1,0:T(2,128)S(1)}, f32[2,2322]{1,0:T(2,128)S(1)}, u32[]{:S(2)}, u32[]{:S(2)}) collective-permute-start(f32[2,2322]{1,0:T(2,128)S(1)} %pad_maximum_fusion.33), channel_id=1, source_target_pairs={{0,8},{1,9},{2,10},{3,11},{4,12},{5,13},{6,14},{7,15},{8,0},{9,1},... | collective-permute-start | bytes 55736 | tf_op jit(solution)/shard_map/ppermute | solution.py:485
  317.0 16.5 %collective-permute-start.51 = (f32[2816]{0:T(1024)S(1)}, f32[2816]{0:T(1024)S(1)}, u32[]{:S(2)}, u32[]{:S(2)}) collective-permute-start(f32[2816]{0:T(1024)S(1)} %add.342), channel_id=1, source_target_pairs={{0,2},{1,3},{2,0},{3,1},{4,6},{5,7},{6,4},{7,5},{8,10},{9,11},{10,... | collective-permute-start | bytes 33800 | tf_op jit(solution)/shard_map/ppermute | solution.py:485
  318.7 27.5 %collective-permute-start.58 = (bf16[2,4,1,2,48,304]{5,4,3,2,1,0:T(8,128)(2,1)}, bf16[2,4,1,2,48,304]{5,4,3,2,1,0:T(8,128)(2,1)}, u32[]{:S(2)}, u32[]{:S(2)}) collective-permute-start(bf16[2,4,1,2,48,304]{5,4,3,2,1,0:T(8,128)(2,1)} %fusion.27), channel_id=1, source_target_pairs={{0,2},{1,3},{2,0},{3,1},{4,6},{5,7},{6,4},{7,5},{8,10},{9,11},{10,... | collective-permute-start | bytes 1400840 | tf_op jit(solution)/shard_map/ppermute | solution.py:485
  333.5 63.0 %collective-permute-start.28 = (bf16[4,128,1536]{2,1,0:T(8,128)(2,1)}, bf16[4,128,1536]{2,1,0:T(8,128)(2,1)}, u32[]{:S(2)}, u32[]{:S(2)}) collective-permute-start(bf16[4,128,1536]{2,1,0:T(8,128)(2,1)} %slice.289), channel_id=1, source_target_pairs={{0,1},{1,0},{2,3},{3,2},{4,5},{5,4},{6,7},{7,6},{8,9},{9,8},{10,11... | collective-permute-start | bytes 4718600 | tf_op jit(solution)/shard_map/ppermute | solution.py:485
  343.7 55.9 %collective-permute-start.37 = (bf16[4,128,1536]{2,1,0:T(8,128)(2,1)}, bf16[4,128,1536]{2,1,0:T(8,128)(2,1)}, u32[]{:S(2)}, u32[]{:S(2)}) collective-permute-start(bf16[4,128,1536]{2,1,0:T(8,128)(2,1)} %slice.297), channel_id=1, source_target_pairs={{0,1},{1,0},{2,3},{3,2},{4,5},{5,4},{6,7},{7,6},{8,9},{9,8},{10,11... | collective-permute-start | bytes 4718600 | tf_op jit(solution)/shard_map/ppermute | solution.py:485
  348.2 15.5 %collective-permute-start.59 = (bf16[1,4,1,2,48,304]{5,4,3,2,1,0:T(8,128)(2,1)S(1)}, bf16[1,4,1,2,48,304]{5,4,3,2,1,0:T(8,128)(2,1)S(1)}, u32[]{:S(2)}, u32[]{:S(2)}) collective-permute-start(bf16[1,4,1,2,48,304]{5,4,3,2,1,0:T(8,128)(2,1)S(1)} %constant_dynamic-slice_fusion.4), channel_id=1, source_target_pairs={{0,16},{1,17},{2,18},{3,19},{4,20},{5,21},{6,22},{7,23},{8,24},{9,... | collective-permute-start | bytes 700424 | tf_op jit(solution)/shard_map/ppermute | solution.py:485
  381.4 21.5 %collective-permute-start.41 = (bf16[4,128,1536]{2,1,0:T(8,128)(2,1)}, bf16[4,128,1536]{2,1,0:T(8,128)(2,1)S(1)}, u32[]{:S(2)}, u32[]{:S(2)}) collective-permute-start(bf16[4,128,1536]{2,1,0:T(8,128)(2,1)} %slice.306), channel_id=1, source_target_pairs={{0,1},{1,0},{2,3},{3,2},{4,5},{5,4},{6,7},{7,6},{8,9},{9,8},{10,11... | collective-permute-start | bytes 4718600 | tf_op jit(solution)/shard_map/ppermute | solution.py:485
  382.8 40.3 %collective-permute-start.44 = (bf16[4,128,1536]{2,1,0:T(8,128)(2,1)}, bf16[4,128,1536]{2,1,0:T(8,128)(2,1)S(1)}, u32[]{:S(2)}, u32[]{:S(2)}) collective-permute-start(bf16[4,128,1536]{2,1,0:T(8,128)(2,1)} %slice.312), channel_id=1, source_target_pairs={{0,1},{1,0},{2,3},{3,2},{4,5},{5,4},{6,7},{7,6},{8,9},{9,8},{10,11... | collective-permute-start | bytes 4718600 | tf_op jit(solution)/shard_map/ppermute | solution.py:485
  395.7 27.2 %collective-permute-start.54 = (bf16[1,4,2,48,768]{4,3,2,1,0:T(8,128)(2,1)S(1)}, bf16[1,4,2,48,768]{4,3,2,1,0:T(8,128)(2,1)S(1)}, u32[]{:S(2)}, u32[]{:S(2)}) collective-permute-start(bf16[1,4,2,48,768]{4,3,2,1,0:T(8,128)(2,1)S(1)} %dynamic-slice_bitcast_fusion), channel_id=1, source_target_pairs={{0,16},{1,17},{2,18},{3,19},{4,20},{5,21},{6,22},{7,23},{8,24},{9,... | collective-permute-start | bytes 1769480 | tf_op jit(solution)/shard_map/ppermute | solution.py:485
  398.5 55.3 %collective-permute-start.29 = (bf16[2,128,1536]{2,1,0:T(8,128)(2,1)S(1)}, bf16[2,128,1536]{2,1,0:T(8,128)(2,1)S(1)}, u32[]{:S(2)}, u32[]{:S(2)}) collective-permute-start(bf16[2,128,1536]{2,1,0:T(8,128)(2,1)S(1)} %slice.291), channel_id=1, source_target_pairs={{0,8},{1,9},{2,10},{3,11},{4,12},{5,13},{6,14},{7,15},{8,0},{9,1},... | collective-permute-start | bytes 2359304 | tf_op jit(solution)/shard_map/ppermute | solution.py:485
  401.6 52.9 %collective-permute-start.38 = (bf16[2,128,1536]{2,1,0:T(8,128)(2,1)S(1)}, bf16[2,128,1536]{2,1,0:T(8,128)(2,1)S(1)}, u32[]{:S(2)}, u32[]{:S(2)}) collective-permute-start(bf16[2,128,1536]{2,1,0:T(8,128)(2,1)S(1)} %slice.299), channel_id=1, source_target_pairs={{0,4},{1,5},{2,6},{3,7},{4,0},{5,1},{6,2},{7,3},{8,12},{9,13},{10,... | collective-permute-start | bytes 2359304 | tf_op jit(solution)/shard_map/ppermute | solution.py:485
  403.3 52.1 %collective-permute-start.42 = (bf16[2,128,1536]{2,1,0:T(8,128)(2,1)S(1)}, bf16[2,128,1536]{2,1,0:T(8,128)(2,1)S(1)}, u32[]{:S(2)}, u32[]{:S(2)}) collective-permute-start(bf16[2,128,1536]{2,1,0:T(8,128)(2,1)S(1)} %slice.308), channel_id=1, source_target_pairs={{0,8},{1,9},{2,10},{3,11},{4,12},{5,13},{6,14},{7,15},{8,0},{9,1},... | collective-permute-start | bytes 2359304 | tf_op jit(solution)/shard_map/ppermute | solution.py:485
  423.0 29.5 %collective-permute-start.55 = (bf16[1,2,2,48,768]{4,3,2,1,0:T(8,128)(2,1)S(1)}, bf16[1,2,2,48,768]{4,3,2,1,0:T(8,128)(2,1)S(1)}, u32[]{:S(2)}, u32[]{:S(2)}) collective-permute-start(bf16[1,2,2,48,768]{4,3,2,1,0:T(8,128)(2,1)S(1)} %constant_dynamic-slice_fusion.6), channel_id=1, source_target_pairs={{0,8},{1,9},{2,10},{3,11},{4,12},{5,13},{6,14},{7,15},{8,0},{9,1},... | collective-permute-start | bytes 884744 | tf_op jit(solution)/shard_map/ppermute | solution.py:485
  423.6 41.0 %collective-permute-start.45 = (bf16[2,128,1536]{2,1,0:T(8,128)(2,1)S(1)}, bf16[2,128,1536]{2,1,0:T(8,128)(2,1)S(1)}, u32[]{:S(2)}, u32[]{:S(2)}) collective-permute-start(bf16[2,128,1536]{2,1,0:T(8,128)(2,1)S(1)} %slice.314), channel_id=1, source_target_pairs={{0,4},{1,5},{2,6},{3,7},{4,0},{5,1},{6,2},{7,3},{8,12},{9,13},{10,... | collective-permute-start | bytes 2359304 | tf_op jit(solution)/shard_map/ppermute | solution.py:485
  454.1 16.8 %collective-permute-start.30 = (bf16[1,128,1536]{2,1,0:T(8,128)(2,1)S(1)}, bf16[1,128,1536]{2,1,0:T(8,128)(2,1)}, u32[]{:S(2)}, u32[]{:S(2)}) collective-permute-start(bf16[1,128,1536]{2,1,0:T(8,128)(2,1)S(1)} %slice.293), channel_id=1, source_target_pairs={{0,4},{1,5},{2,6},{3,7},{4,0},{5,1},{6,2},{7,3},{8,12},{9,13},{10,... | collective-permute-start | bytes 1179656 | tf_op jit(solution)/shard_map/ppermute | solution.py:485
  455.4 16.5 %collective-permute-start.39 = (bf16[1,128,1536]{2,1,0:T(8,128)(2,1)}, bf16[1,128,1536]{2,1,0:T(8,128)(2,1)}, u32[]{:S(2)}, u32[]{:S(2)}) collective-permute-start(bf16[1,128,1536]{2,1,0:T(8,128)(2,1)} %slice.301), channel_id=1, source_target_pairs={{0,8},{1,9},{2,10},{3,11},{4,12},{5,13},{6,14},{7,15},{8,0},{9,1},... | collective-permute-start | bytes 1179656 | tf_op jit(solution)/shard_map/ppermute | solution.py:485
  456.4 20.7 %collective-permute-start.43 = (bf16[1,128,1536]{2,1,0:T(8,128)(2,1)}, bf16[1,128,1536]{2,1,0:T(8,128)(2,1)}, u32[]{:S(2)}, u32[]{:S(2)}) collective-permute-start(bf16[1,128,1536]{2,1,0:T(8,128)(2,1)} %slice.310), channel_id=1, source_target_pairs={{0,4},{1,5},{2,6},{3,7},{4,0},{5,1},{6,2},{7,3},{8,12},{9,13},{10,... | collective-permute-start | bytes 1179656 | tf_op jit(solution)/shard_map/ppermute | solution.py:485
  465.6 12.7 %collective-permute-start.46 = (bf16[1,128,1536]{2,1,0:T(8,128)(2,1)}, bf16[1,128,1536]{2,1,0:T(8,128)(2,1)}, u32[]{:S(2)}, u32[]{:S(2)}) collective-permute-start(bf16[1,128,1536]{2,1,0:T(8,128)(2,1)} %slice.316), channel_id=1, source_target_pairs={{0,8},{1,9},{2,10},{3,11},{4,12},{5,13},{6,14},{7,15},{8,0},{9,1},... | collective-permute-start | bytes 1179656 | tf_op jit(solution)/shard_map/ppermute | solution.py:485
  473.2 40.0 %collective-permute-start.40 = (bf16[2,128,1536]{2,1,0:T(8,128)(2,1)S(1)}, bf16[2,128,1536]{2,1,0:T(8,128)(2,1)S(1)}, u32[]{:S(2)}, u32[]{:S(2)}) collective-permute-start(bf16[2,128,1536]{2,1,0:T(8,128)(2,1)S(1)} %pad_maximum_fusion.15), channel_id=1, source_target_pairs={{1,16},{3,18},{5,20},{7,22},{9,24},{11,26},{13,28},{15,30},{16,1},... | collective-permute-start | bytes 2359304 | tf_op jit(solution)/shard_map/ppermute | solution.py:485
  479.5 33.2 %collective-permute-start.47 = (bf16[2,128,1536]{2,1,0:T(8,128)(2,1)S(1)}, bf16[2,128,1536]{2,1,0:T(8,128)(2,1)S(1)}, u32[]{:S(2)}, u32[]{:S(2)}) collective-permute-start(bf16[2,128,1536]{2,1,0:T(8,128)(2,1)S(1)} %pad_maximum_fusion.16), channel_id=1, source_target_pairs={{1,16},{3,18},{5,20},{7,22},{9,24},{11,26},{13,28},{15,30},{16,1},... | collective-permute-start | bytes 2359304 | tf_op jit(solution)/shard_map/ppermute | solution.py:485
  (123 other events, 1100.6 us)

commit v3 on v1

v3 whole, which is shorter than its diff:
```python
import functools

import jax
import jax.numpy as jnp
import numpy as np
from jax import lax
from jax.experimental import pallas as pl
from jax.experimental.pallas import tpu as pltpu
from jax.sharding import PartitionSpec as P

D = 1536
HEADS = 48
HEAD_DIM = 64
STATE = 128
KERNEL = 4
INNER = 3072
LANES = 128
HALO = 16
EPSILON = 1e-05
F32 = jnp.float32
BF16 = jnp.bfloat16


def mm(a, b):
    return jnp.dot(a.astype(BF16), b.astype(BF16), preferred_element_type=F32)


def mm_tr(a, b):
    return lax.dot_general(
        a.astype(BF16), b.astype(BF16), (((1,), (1,)), ((), ())), preferred_element_type=F32
    )


def tr_mm(a, b):
    return lax.dot_general(
        a.astype(BF16), b.astype(BF16), (((0,), (0,)), ((), ())), preferred_element_type=F32
    )


def pieces(a, count):
    out = []
    for _ in range(count - 1):
        part = a.astype(BF16)
        out.append(part)
        a = a - part.astype(F32)
    out.append(a.astype(BF16))
    return out


def ones_mm(ones, a, count):
    return sum(jnp.dot(ones, part, preferred_element_type=F32) for part in pieces(a, count))


def mm_ones(a, ones, count):
    return sum(jnp.dot(part, ones, preferred_element_type=F32) for part in pieces(a, count))


def mm_ones_tr(a, ones, count):
    return sum(
        lax.dot_general(part, ones, (((1,), (1,)), ((), ())), preferred_element_type=F32)
        for part in pieces(a, count)
    )


def iota(shape, dim):
    return lax.broadcasted_iota(jnp.int32, shape, dim)


def softplus(v):
    return jnp.maximum(v, 0.0) + jnp.log1p(jnp.exp(-jnp.abs(v)))


def sigmoid(v):
    return 1.0 / (1.0 + jnp.exp(-v))


def causal_conv(ext, current, halo, weight, bias, offset):
    length = current.shape[0]
    ext[0:HALO, :] = halo
    ext[HALO : HALO + length, :] = current
    total = bias + weight[KERNEL - 1 : KERNEL, :] * current
    for back in range(1, KERNEL):
        shifted = jnp.where(offset >= back, ext[pl.ds(HALO - back, length), :], 0.0)
        total = total + weight[KERNEL - 1 - back : KERNEL - back, :] * shifted
    return total


def head_tiles(width):
    out = []
    for start in range(0, width, LANES):
        size = min(LANES, width - start)
        heads = [start // HEAD_DIM + i for i in range(size // HEAD_DIM)]
        out.append((start, size, heads))
    return out


def masked_heads(tile, heads):
    if len(heads) == 1:
        return tile
    lane = iota(tile.shape, 1) // HEAD_DIM
    return jnp.concatenate(
        [jnp.where(lane == i, tile, jnp.zeros_like(tile)) for i in range(len(heads))], axis=0
    )


def expander(width):
    return (iota((LANES, width), 1) // HEAD_DIM == iota((LANES, width), 0)).astype(BF16)


def chunk_common(x, xh, tail, tailh, offset, params, ext_x, ext_t, width):
    wx, bx, wt, bt, heads_p, pick = params
    length = x.shape[0]
    conv_x = causal_conv(ext_x, x.astype(F32), xh.astype(F32), wx, bx, offset)
    conv_t = causal_conv(
        ext_t,
        tail[:, : 2 * STATE].astype(F32),
        tailh[:, : 2 * STATE].astype(F32),
        wt,
        bt,
        offset,
    )
    raw = jnp.dot(tail[:, 2 * STATE :], pick, preferred_element_type=F32) + heads_p[0:1, :]
    step = softplus(raw)
    decay_rate = jnp.exp(heads_p[1:2, :])
    rate = -step * decay_rate
    tril = (iota((length, length), 0) >= iota((length, length), 1)).astype(BF16)
    cumul = ones_mm(tril, rate, 3)
    spread = expander(width)
    row = iota((length, 1), 0)
    entry = jnp.where(offset > row.astype(F32), jnp.exp(cumul), 0.0)
    last_off = offset[length - 1 : length, :]
    same_last = row.astype(F32) >= (length - 1) - last_off
    to_end = jnp.where(same_last, jnp.exp(cumul[length - 1 : length, :] - cumul), 0.0)
    step_x = mm_ones(step, spread, 2)
    entry_x = mm_ones(entry, spread, 2)
    end_x = mm_ones(to_end, spread, 2)
    return conv_x, conv_t, raw, step, rate, decay_rate, cumul, spread, step_x, entry_x, end_x


def forward_kernel(
    zx_ref, zxh_ref, tail_ref, tailh_ref, off_ref,
    wx_ref, bx_ref, wt_ref, bt_ref, hp_ref, pick_ref, skip_ref, gain_ref,
    y_ref, gated_ref, square_ref, state_ref, memory, ext_x, ext_t,
):
    seqs, _, length, width = y_ref.shape

    @pl.when(pl.program_id(0) == 0)
    def _():
        memory[...] = jnp.zeros_like(memory)

    params = tuple(r[...] for r in (wx_ref, bx_ref, wt_ref, bt_ref, hp_ref, pick_ref))
    for q in range(seqs):
        offset = off_ref[q, 0]
        conv_x, conv_t, _, _, _, _, cumul, _, step_x, entry_x, end_x = chunk_common(
            zx_ref[q, 0, :, width:], zxh_ref[q, 0, :, width:], tail_ref[q, 0], tailh_ref[q, 0], offset, params,
            ext_x.at[q], ext_t.at[q], width,
        )
        xs = conv_x * sigmoid(conv_x)
        act_t = conv_t * sigmoid(conv_t)
        bs = act_t[:, :STATE].astype(BF16)
        cs = act_t[:, STATE:].astype(BF16)
        scaled = xs * step_x
        scores = mm_tr(cs, bs)
        gap = iota((length, length), 0) - iota((length, length), 1)
        same = (gap >= 0) & (gap.astype(F32) <= offset)
        cumul_t = cumul.T
        old = memory[q]
        old_low = old.astype(BF16)
        state_ref[q, 0] = old_low
        outside = mm(cs, old_low) * entry_x + skip_ref[...] * xs
        squares = jnp.zeros((length, 1), F32)
        for start, size, heads in head_tiles(width):
            mixing = []
            for head in heads:
                spans = cumul[:, head : head + 1] - cumul_t[head : head + 1, :]
                decays = jnp.exp(jnp.where(same, spans, -1e30))
                mixing.append((decays * scores).astype(BF16))
            tile = masked_heads(scaled[:, start : start + size].astype(BF16), heads)
            mix = mixing[0] if len(heads) == 1 else jnp.concatenate(mixing, axis=1)
            inside = jnp.dot(mix, tile, preferred_element_type=F32)
            y_low = (inside + outside[:, start : start + size]).astype(BF16)
            y_ref[q, 0, :, start : start + size] = y_low
            z = zx_ref[q, 0, :, start : start + size].astype(F32)
            gated = y_low.astype(F32) * (z * sigmoid(z))
            gated_ref[q, 0, :, start : start + size] = (
                gated * gain_ref[:, start : start + size]
            ).astype(BF16)
            squares = squares + jnp.sum(gated * gated, axis=1, keepdims=True)
        square_ref[q, 0] = jnp.broadcast_to(squares, (length, LANES)).T[0:1, :]
        fresh = tr_mm(bs, scaled * end_x)
        memory[q] = old * entry_x[length - 1 : length, :] + fresh


def backward_kernel(
    zx_ref, zxh_ref, tail_ref, tailh_ref, off_ref, offr_ref, rem_ref, y_ref, grad_ref, stat_ref,
    state_ref, wx_ref, bx_ref, wt_ref, bt_ref, hp_ref, pick_ref, skip_ref, gain_ref,
    out_ref, gx_ref, gt_ref, gh_ref,
    memory, ext_x, ext_t, next_x, next_t,
):
    seqs, _, length, width = y_ref.shape

    @pl.when(pl.program_id(0) == 0)
    def _():
        memory[...] = jnp.zeros_like(memory)
        gx_ref[...] = jnp.zeros_like(gx_ref)
        gt_ref[...] = jnp.zeros_like(gt_ref)
        gh_ref[...] = jnp.zeros_like(gh_ref)
        next_x[:, length:, :] = jnp.zeros_like(next_x[:, length:, :])
        next_t[:, length:, :] = jnp.zeros_like(next_t[:, length:, :])

    params = tuple(r[...] for r in (wx_ref, bx_ref, wt_ref, bt_ref, hp_ref, pick_ref))
    for q in range(seqs):
        offset = off_ref[q, 0]
        conv_x, conv_t, raw, step, rate, decay_rate, cumul, spread, step_x, entry_x, end_x = (
            chunk_common(
                zx_ref[q, 0, :, width:], zxh_ref[q, 0, :, width:], tail_ref[q, 0], tailh_ref[q, 0], offset,
                params, ext_x.at[q], ext_t.at[q], width,
            )
        )
        stats = jnp.broadcast_to(stat_ref[q, 0, 0:1, :], (LANES, length)).T
        slopes = jnp.broadcast_to(stat_ref[q, 0, 1:2, :], (LANES, length)).T
        scale, slope = stats[:, 0:1], slopes[:, 0:1]
        z = zx_ref[q, 0, :, :width].astype(F32)
        sig_z = sigmoid(z)
        silu_z = z * sig_z
        y = y_ref[q, 0].astype(F32)
        gated = y * silu_z
        scaled_grad = grad_ref[q, 0].astype(F32) * scale
        gx_ref[KERNEL + 2 : KERNEL + 3, :] += jnp.sum(scaled_grad * gated, axis=0, keepdims=True)
        grad_gated = gain_ref[...] * scaled_grad - gated * slope
        dy_low = (grad_gated * silu_z).astype(BF16)
        dz = (grad_gated * y * (sig_z + silu_z * (1.0 - sig_z))).astype(BF16)
        dy = dy_low.astype(F32)

        sig_x = sigmoid(conv_x)
        xs = conv_x * sig_x
        slope_x = sig_x + xs * (1.0 - sig_x)
        sig_t = sigmoid(conv_t)
        act_t = conv_t * sig_t
        slope_t = sig_t + act_t * (1.0 - sig_t)
        bs = act_t[:, :STATE].astype(BF16)
        cs = act_t[:, STATE:].astype(BF16)
        scaled = xs * step_x
        scaled_low = scaled.astype(BF16)
        scores = mm_tr(bs, cs)
        rows, cols = iota((length, length), 0), iota((length, length), 1)
        gap = cols - rows
        same = (gap >= 0) & (gap.astype(F32) <= offr_ref[q, 0])
        strict = gap > 0
        upper = (rows >= cols).astype(BF16)
        cumul_t = cumul.T
        old = state_ref[q, 0]
        grad_state = memory[q]
        state_low = grad_state.astype(BF16)
        grad_scores = jnp.zeros((length, length), F32)
        grad_scaled = []
        inside_rows = []
        for start, size, heads in head_tiles(width):
            dy_tile = masked_heads(dy_low[:, start : start + size], heads)
            grad_mix = mm_tr(scaled_low[:, start : start + size], dy_tile)
            mixing = []
            for place, head in enumerate(heads):
                spans = cumul_t[head : head + 1, :] - cumul[:, head : head + 1]
                decays = jnp.exp(jnp.where(same, spans, -1e30))
                weighted = grad_mix[:, place * length : (place + 1) * length] * decays
                grad_scores = grad_scores + weighted
                mixing.append((decays * scores).astype(BF16))
                terms = jnp.where(strict, weighted * scores, 0.0).astype(BF16)
                sums = jnp.dot(terms, upper, preferred_element_type=F32)
                inside_rows.append(
                    jnp.sum(jnp.where(strict, sums, 0.0), axis=0, keepdims=True)
                )
            mix = mixing[0] if len(heads) == 1 else jnp.concatenate(mixing, axis=1)
            grad_scaled.append(jnp.dot(mix, dy_tile, preferred_element_type=F32))
        inside_rows.append(jnp.zeros((LANES - len(inside_rows), length), F32))
        inside = jnp.concatenate(inside_rows, axis=0).T
        from_end = mm(bs, state_low) * end_x
        grad_scaled = jnp.concatenate(grad_scaled, axis=1) + from_end
        entry_dy = dy * entry_x
        entry_dy_low = entry_dy.astype(BF16)
        out_terms = mm(cs, old) * entry_dy
        end_terms = scaled * from_end
        grad_step = mm_ones_tr(xs * grad_scaled, spread, 2)
        out_terms = mm_ones_tr(out_terms, spread, 2)
        end_terms = mm_ones_tr(end_terms, spread, 2)
        keep_row = entry_x[length - 1 : length, :]
        carried = jnp.sum(grad_state * old.astype(F32), axis=0, keepdims=True) * keep_row
        carried = mm_ones_tr(jnp.broadcast_to(carried, (8, width)), spread, 2)[0:1, :]
        triu = (cols >= rows).astype(BF16)
        below = (rows > cols).astype(BF16)
        grad_rate = inside + ones_mm(triu, out_terms, 2) + ones_mm(below, end_terms, 2) + carried
        grad_step = grad_step - decay_rate * grad_rate
        grad_raw = grad_step * sigmoid(raw)
        grad_scores_low = grad_scores.astype(BF16)
        grad_b = mm(grad_scores_low, cs) + mm_tr(scaled * end_x, state_low)
        grad_c = tr_mm(grad_scores_low, bs) + mm_tr(entry_dy_low, old)
        memory[q] = grad_state * keep_row + tr_mm(cs, entry_dy_low)
        conv_grad_x = (skip_ref[...] * dy + step_x * grad_scaled) * slope_x
        conv_grad_t = jnp.concatenate([grad_b, grad_c], axis=1) * slope_t

        remain = rem_ref[q, 0]
        results = [dz]
        for grad, ext, nxt, weight, sums in (
            (conv_grad_x, ext_x.at[q], next_x.at[q], params[0], gx_ref),
            (conv_grad_t, ext_t.at[q], next_t.at[q], params[2], gt_ref),
        ):
            current = ext[pl.ds(HALO, length), :]
            sums[KERNEL : KERNEL + 1, :] += jnp.sum(grad, axis=0, keepdims=True)
            sums[KERNEL - 1 : KERNEL, :] += jnp.sum(grad * current, axis=0, keepdims=True)
            nxt[0:length, :] = grad
            total = weight[KERNEL - 1 : KERNEL, :] * grad
            for back in range(1, KERNEL):
                tap = KERNEL - 1 - back
                shifted = jnp.where(offset >= back, ext[pl.ds(HALO - back, length), :], 0.0)
                sums[tap : tap + 1, :] += jnp.sum(grad * shifted, axis=0, keepdims=True)
                ahead = jnp.where(remain >= back, nxt[pl.ds(back, length), :], 0.0)
                total = total + weight[tap : tap + 1, :] * ahead
            nxt[length:, :] = grad[0:HALO, :]
            results.append(total.astype(BF16))
        results.append(mm_tr(grad_raw, params[5]).astype(BF16))
        gx_ref[KERNEL + 1 : KERNEL + 2, :] += jnp.sum(dy * xs, axis=0, keepdims=True)
        gh_ref[0:1, :] += jnp.sum(grad_raw, axis=0, keepdims=True)
        gh_ref[1:2, :] += jnp.sum(grad_rate * rate, axis=0, keepdims=True)
        out_ref[q, 0, :, : 2 * width] = jnp.concatenate(results[:2], axis=1)
        out_ref[q, 0, :, 2 * width : 2 * width + 2 * STATE] = results[2]
        out_ref[q, 0, :, 2 * width + 2 * STATE :] = results[3]


TAIL = 2 * STATE + LANES
AXES = ("seq", "fsdp")
MESH = pl.DeviceIdType.MESH


def whole_spec(shape):
    return pl.BlockSpec(shape, lambda i: (0,) * len(shape))


def chunk_specs(seqs, steps, length, reverse):
    def place(i):
        return steps - 1 - i if reverse else i

    def block(cols, column=0, rows=length):
        return pl.BlockSpec((seqs, 1, rows, cols), lambda i: (0, place(i), 0, column))

    def before(cols, column=0):
        return pl.BlockSpec(
            (seqs, 1, HALO, cols),
            lambda i: (0, jnp.maximum(place(i) - 1, 0), length // HALO - 1, column),
        )

    return block, before


def forward_mix(proj, off_col, consts):
    seqs, steps, length, cols = proj.shape
    width = (cols - TAIL) // 2
    block, before = chunk_specs(seqs, steps, length, False)
    tail_at = 2 * width // TAIL
    shape = (seqs, steps, length, width)
    return pl.pallas_call(
        forward_kernel,
        grid=(steps,),
        in_specs=[
            block(2 * width), before(2 * width), block(TAIL, tail_at), before(TAIL, tail_at),
            block(1),
        ]
        + [whole_spec(v.shape) for v in consts],
        out_specs=[
            block(width), block(width), block(length, 0, 1), block(width, 0, STATE),
        ],
        out_shape=[
            jax.ShapeDtypeStruct(shape, BF16),
            jax.ShapeDtypeStruct(shape, BF16),
            jax.ShapeDtypeStruct((seqs, steps, 1, length), F32),
            jax.ShapeDtypeStruct((seqs, steps, STATE, width), BF16),
        ],
        scratch_shapes=[
            pltpu.VMEM((seqs, STATE, width), F32),
            pltpu.VMEM((seqs, HALO + length, width), F32),
            pltpu.VMEM((seqs, HALO + length, 2 * STATE), F32),
        ],
        compiler_params=pltpu.CompilerParams(
            dimension_semantics=("arbitrary",), vmem_limit_bytes=32 << 20
        ),
        cost_estimate=pl.CostEstimate(
            flops=steps * seqs * 900_000_000, transcendentals=0, bytes_accessed=10_000_000
        ),
        name="mix_forward",
    )(proj, proj, proj, proj, off_col, *consts)


def backward_mix(proj, off_col, off_row, rem_col, y, grad_yn, stats, states, consts):
    seqs, steps, length, cols = proj.shape
    width = (cols - TAIL) // 2
    block, before = chunk_specs(seqs, steps, length, True)
    tail_at = 2 * width // TAIL
    sums = [(8, width), (8, 2 * STATE), (8, LANES)]
    return pl.pallas_call(
        backward_kernel,
        grid=(steps,),
        in_specs=[
            block(2 * width), before(2 * width), block(TAIL, tail_at), before(TAIL, tail_at),
            block(1), block(length, 0, 1), block(1), block(width), block(width),
            block(length, 0, 2), block(width, 0, STATE),
        ]
        + [whole_spec(v.shape) for v in consts],
        out_specs=[block(cols)] + [whole_spec(v) for v in sums],
        scratch_shapes=[
            pltpu.VMEM((seqs, STATE, width), F32),
            pltpu.VMEM((seqs, HALO + length, width), F32),
            pltpu.VMEM((seqs, HALO + length, 2 * STATE), F32),
            pltpu.VMEM((seqs, length + HALO, width), F32),
            pltpu.VMEM((seqs, length + HALO, 2 * STATE), F32),
        ],
        out_shape=[jax.ShapeDtypeStruct(proj.shape, BF16)]
        + [jax.ShapeDtypeStruct(v, F32) for v in sums],
        compiler_params=pltpu.CompilerParams(
            dimension_semantics=("arbitrary",), vmem_limit_bytes=40 << 20
        ),
        cost_estimate=pl.CostEstimate(
            flops=steps * seqs * 2_000_000_000, transcendentals=0, bytes_accessed=16_000_000
        ),
        name="mix_backward",
    )(
        proj, proj, proj, proj, off_col, off_row, rem_col, y, grad_yn, stats, states, *consts
    )


class Place:
    def __init__(self, seq, fsdp):
        self.seq, self.fsdp = seq, fsdp
        self.half, self.pairs = seq // 2, fsdp // 2
        s, f = lax.axis_index("seq"), lax.axis_index("fsdp")
        self.s, self.f = s, f
        self.top, self.low = s // self.half, lax.rem(s, self.half)
        self.core, self.pair = lax.rem(f, 2), f // 2
        self.home = self.core == self.top
        self.away = self.core != self.top
        self.chunk = self.low + self.half * self.core
        self.low_bits = [1 << i for i in range(self.half.bit_length() - 1)]

    def at(self, top=0, low=0, pair=0, core=0):
        return (
            flip(self.top, top) * self.half + flip(self.low, low),
            flip(self.pair, pair) * 2 + flip(self.core, core),
        )

    def bits_for(self, q):
        return self.low_bits if q % 2 == 0 else self.low_bits[::-1]


def flip(index, bits):
    for i in range(bits.bit_length()):
        if bits >> i & 1:
            bit = lax.rem(index // (1 << i), 2)
            index = index + (1 << i) * (1 - 2 * bit)
    return index


class Links:
    def __init__(self, send, recv, near):
        self.send, self.recv, self.near = send, recv, near
        self.far_count = self.near_count = 0

    def far(self, src, dst, device):
        i = self.far_count
        self.far_count += 1
        return pltpu.make_async_remote_copy(
            src_ref=src, dst_ref=dst, send_sem=self.send.at[i], recv_sem=self.recv.at[i],
            device_id=device, device_id_type=MESH,
        )

    def local(self, src, dst):
        i = self.near_count
        self.near_count += 1
        return pltpu.make_async_copy(src, dst, self.near.at[i])


def meet(devices):
    barrier = pltpu.get_barrier_semaphore()
    for device in devices:
        pl.semaphore_signal(barrier, inc=1, device_id=device, device_id_type=MESH)
    pl.semaphore_wait(barrier, len(devices))


def started(copy):
    copy.start()
    return copy


class TokenGather:
    def __init__(self, place, links, src, dst):
        self.place, self.src, self.dst = place, src, dst
        self.links = links
        chunk = place.s
        self.cross = links.far(src, dst.at[:, chunk], place.at(top=1, core=1))
        self.stay = links.local(src, dst.at[:, chunk])
        self.held = None
        self.sent = []
        self.stage = 0

    def begin(self):
        @pl.when(self.place.away)
        def _():
            self.cross.start()

        @pl.when(self.place.home)
        def _():
            self.stay.start()

    def arrive(self):
        @pl.when(self.place.away)
        def _():
            self.cross.wait_recv()

        @pl.when(self.place.home)
        def _():
            self.stay.wait()

        self.held = [[0] for _ in range(self.src.shape[0])]
        self.pending = [[] for _ in self.held]
        self.across = []
        for q in range(len(self.held)):
            self.share(q, [0])

    def block(self, q, low):
        return self.dst.at[q, flip(self.place.low, low) + self.place.half * self.place.core]

    def share(self, q, lows):
        for low in lows:
            ref = self.block(q, low)
            self.across.append(started(self.links.far(ref, ref, self.place.at(core=1))))

    def send_stage(self):
        for q, held in enumerate(self.held):
            bit = self.place.bits_for(q)[self.stage]
            for low in held:
                ref = self.block(q, low)
                self.pending[q].append(started(self.links.far(ref, ref, self.place.at(low=bit))))

    def finish_stage(self):
        for q, held in enumerate(self.held):
            bit = self.place.bits_for(q)[self.stage]
            for copy in self.pending[q]:
                copy.wait_recv()
            self.sent += self.pending[q]
            self.pending[q] = []
            fresh = [low ^ bit for low in held]
            held += fresh
            self.share(q, fresh)
        self.stage += 1

    def finish(self):
        for copy in self.across:
            copy.wait()
        for copy in self.sent:
            copy.wait_send()

        @pl.when(self.place.away)
        def _():
            self.cross.wait_send()


def peers_of(place):
    out = []
    for top in (1, 0):
        for low in range(place.half):
            for core in (0, 1):
                if (top, low, core) != (0, 0, 0):
                    out.append((top, low, core))
    return out


def entry_kernel(
    seq, fsdp,
    h_ref, zx_ref, tail_ref, ow_ref, cot_ref, seg_ref,
    h_out, w_out, ow_out, cot_out, seg_out,
    send, recv, near,
):
    place = Place(seq, fsdp)
    links = Links(send, recv, near)
    cols = zx_ref.shape[2]
    peers = peers_of(place)
    pair_steps = range(1, place.pairs)
    meet(
        [place.at(top=t, low=l, core=c) for t, l, c in peers]
        + [place.at(pair=p) for p in pair_steps]
    )
    tokens = TokenGather(place, links, h_ref, h_out)
    tokens.begin()

    def columns(ref):
        return ref.at[:, pl.ds(0, cols)]

    def tail_of(ref):
        return ref.at[:, pl.ds(cols, TAIL)]

    own = w_out.at[place.s, place.pair, place.core]
    other = w_out.at[flip(place.s, place.half), place.pair, place.core]

    tail_cross = started(links.far(tail_ref, tail_of(own), place.at(top=1)))
    zx_copies = []
    for t, l, c in peers:
        group = flip(place.core, c) * place.half + flip(place.low, l)
        zx_copies.append(
            started(links.far(zx_ref.at[group], columns(own), place.at(top=t, low=l, core=c)))
        )
    locals_ = [
        started(links.local(zx_ref.at[place.chunk], columns(own))),
        started(links.local(tail_ref, tail_of(own))),
    ]
    near_peers = [(l, c) for t, l, c in peers if t == 0]
    tail_copies = [
        started(links.far(tail_ref, tail_of(own), place.at(low=l, core=c))) for l, c in near_peers
    ]
    swap_segments = started(links.far(seg_ref, seg_out, place.at(core=1)))

    tokens.arrive()
    tokens.send_stage()
    tail_cross.wait_recv()
    tail_more = [
        started(links.far(tail_of(other), tail_of(other), place.at(low=l, core=c)))
        for l, c in near_peers
    ]
    for copy in locals_:
        copy.wait()
    cot = TokenGather(place, links, cot_ref, cot_out)
    cot.begin()
    tokens.finish_stage()

    index = lax.rem(place.core, 2)
    rows_own = ow_out.at[place.pair, index]
    to_home = links.far(ow_ref, rows_own, place.at(core=1))
    stay = links.local(ow_ref, rows_own)
    to_near = links.far(ow_ref, rows_own, place.at(top=1))
    to_far = links.far(ow_ref, rows_own, place.at(top=1, core=1))

    stages = len(place.low_bits)
    for _ in range(1, stages):
        tokens.send_stage()

    blocks = [(0, 0, 0)] + [p for p in peers if p[0] == 0] + [p for p in peers if p[0] == 1]
    arrival = {p: copy for p, copy in zip(peers, zx_copies)}
    tails = dict(zip(near_peers, tail_copies))
    tails_more = dict(zip(near_peers, tail_more))
    forwards = []
    for t, l, c in blocks:
        if (t, l, c) != (0, 0, 0):
            arrival[t, l, c].wait_recv()
            if t == 0:
                tails[l, c].wait_recv()
            elif (l, c) != (0, 0):
                tails_more[l, c].wait_recv()
        s, f = place.at(top=t, low=l, core=c)
        ref = w_out.at[s, place.pair, lax.rem(f, 2)]
        for p in pair_steps:
            forwards.append(started(links.far(ref, ref, place.at(pair=p))))
    for i in range(1, stages):
        tokens.finish_stage()

    cot.arrive()
    cot.send_stage()

    @pl.when(place.home)
    def _():
        stay.start()
        to_near.start()

    @pl.when(place.away)
    def _():
        to_home.start()
        to_far.start()

    for i in range(stages):
        cot.finish_stage()
        if i + 1 < stages:
            cot.send_stage()

    @pl.when(place.home)
    def _():
        stay.wait()
        to_home.wait_recv()

    @pl.when(place.away)
    def _():
        to_near.wait_recv()
        to_far.wait_recv()

    out_forwards = []
    for c in (0, 1):
        ref = ow_out.at[place.pair, c]
        for p in pair_steps:
            out_forwards.append(started(links.far(ref, ref, place.at(pair=p))))
    tokens.finish()
    cot.finish()
    for copy in forwards + out_forwards:
        copy.wait()
    for copy in [tail_cross] + zx_copies + tail_copies + tail_more:
        copy.wait_send()
    swap_segments.wait()

    @pl.when(place.home)
    def _():
        to_near.wait_send()

    @pl.when(place.away)
    def _():
        to_home.wait_send()
        to_far.wait_send()


ANYWHERE = pl.BlockSpec(memory_space=pl.ANY)


def entry_gather(seq, fsdp, normed, zx, tail, out_w, cotangent, segments):
    seqs, length, depth = normed.shape
    rows = tail.shape[0]
    tokens = jax.ShapeDtypeStruct((seqs, seq, length, depth), BF16)
    pairs = fsdp // 2
    return pl.pallas_call(
        functools.partial(entry_kernel, seq, fsdp),
        in_specs=[ANYWHERE] * 6,
        out_specs=[ANYWHERE] * 5,
        out_shape=[
            tokens,
            jax.ShapeDtypeStruct((seq, pairs, 2, rows, zx.shape[2] + TAIL), BF16),
            jax.ShapeDtypeStruct((pairs, 2) + out_w.shape, BF16),
            tokens,
            jax.ShapeDtypeStruct(segments.shape, segments.dtype),
        ],
        scratch_shapes=[
            pltpu.SemaphoreType.DMA((512,)),
            pltpu.SemaphoreType.DMA((512,)),
            pltpu.SemaphoreType.DMA((16,)),
        ],
        compiler_params=pltpu.CompilerParams(collective_id=0, has_side_effects=True),
        cost_estimate=pl.CostEstimate(
            flops=0, transcendentals=0, bytes_accessed=200_000_000
        ),
        name="entry_gather",
    )(normed, zx, tail, out_w, cotangent, segments)


def add_rows(out, left, right, rows=32):
    total = left.shape[0]
    step = next((size for size in (rows, 16) if total % size == 0), total)

    if step == total:
        out[...] = (left[...].astype(F32) + right[...].astype(F32)).astype(out.dtype)
        return

    @pl.loop(0, total // step)
    def _(i):
        at = pl.ds(pl.multiple_of(i * step, step), step)
        out[at] = (left[at].astype(F32) + right[at].astype(F32)).astype(out.dtype)


class TokenScatter:
    def __init__(self, place, links, src, out, own, first, later):
        self.place, self.links = place, links
        self.src, self.out, self.own, self.first, self.later = src, out, own, first, later
        self.seqs = src.shape[0]
        self.sent = []

    def begin(self):
        half, core = self.place.half, self.place.core
        self.loads, self.cores = [], []
        for q in range(self.seqs):
            give = self.src.at[q, pl.ds(half * (1 - core), half)]
            self.cores.append(
                started(self.links.far(give, self.first.at[q], self.place.at(core=1)))
            )
            keep = self.src.at[q, pl.ds(half * core, half)]
            self.loads.append(started(self.links.local(keep, self.own.at[q])))

    def add_cores(self):
        place = self.place
        self.live = [list(range(place.half)) for _ in range(self.seqs)]
        self.slot = [0] * self.seqs
        self.pending = [None] * self.seqs
        for q in range(self.seqs):
            self.loads[q].wait()
            self.cores[q].wait_recv()
            self.sent.append(self.cores[q])
            for low in self.away_first(q, 0):
                at = flip(place.low, low)
                add_rows(self.own.at[q, at], self.own.at[q, at], self.first.at[q, at])
            self.send(q, 0)

    def away_first(self, q, stage):
        return self.live[q]

    def send(self, q, stage):
        place = self.place
        bit = place.bits_for(q)[::-1][stage]
        give = [low for low in self.live[q] if low & bit]
        self.live[q] = [low for low in self.live[q] if not low & bit]
        self.pending[q] = []
        for low in give:
            slot = self.slot[q]
            self.slot[q] += 1
            copy = started(
                self.links.far(
                    self.own.at[q, flip(place.low, low)], self.later.at[q, slot],
                    place.at(low=bit),
                )
            )
            self.pending[q].append((copy, low ^ bit, slot))

    def add_stage(self, stage):
        for q in range(self.seqs):
            for copy, low, slot in self.pending[q]:
                copy.wait_recv()
                at = flip(self.place.low, low)
                add_rows(self.own.at[q, at], self.own.at[q, at], self.later.at[q, slot])
                self.sent.append(copy)
            if stage + 1 < len(self.place.low_bits):
                self.send(q, stage + 1)

    def deliver(self):
        place = self.place
        self.last = []
        for q in range(self.seqs):
            ref = self.own.at[q, place.low]
            cross = self.links.far(ref, self.out.at[q], place.at(top=1, core=1))
            stay = self.links.local(ref, self.out.at[q])
            self.last.append((cross, stay))

            @pl.when(place.away)
            def _():
                cross.start()

            @pl.when(place.home)
            def _():
                stay.start()

    def finish(self):
        for cross, stay in self.last:

            @pl.when(self.place.away)
            def _():
                cross.wait()

            @pl.when(self.place.home)
            def _():
                stay.wait()

        for copy in self.sent:
            copy.wait_send()


def exit_kernel(
    seq, fsdp,
    dh_ref, mixed_ref, part_ref, pout_ref, vec_ref,
    dh_out, mixed_out, slots_out, rows_out, vec_out,
    dh_own, dh_first, dh_later, mix_own, mix_first, mix_later,
    part_own, part_first, part_top, pout_own, pout_first, vec_val, vec_got,
    send, recv, near,
):
    place = Place(seq, fsdp)
    links = Links(send, recv, near)
    peers = peers_of(place)
    pair_steps = list(range(1, place.pairs))
    near_peers = [(l, c) for t, l, c in peers if t == 0]
    meet(
        [place.at(top=t, low=l, core=c) for t, l, c in peers]
        + [place.at(pair=p) for p in pair_steps]
    )
    half = place.half
    dh = TokenScatter(place, links, dh_ref, dh_out, dh_own, dh_first, dh_later)
    mixed = TokenScatter(place, links, mixed_ref, mixed_out, mix_own, mix_first, mix_later)
    dh.begin()

    far_rows = pl.ds(half * (1 - place.top), half)
    near_rows = pl.ds(half * place.top, half)
    by_pair = {}
    for name, rows in (("far", far_rows), ("near", near_rows)):
        by_pair[name] = [
            started(
                links.far(
                    part_ref.at[rows, flip(place.pair, p)], part_first.at[p - 1, rows],
                    place.at(pair=p),
                )
            )
            for p in pair_steps
        ]
    part_load = started(links.local(part_ref.at[:, place.pair], part_own))
    pout_pairs = [
        started(
            links.far(pout_ref.at[flip(place.pair, p)], pout_first.at[p - 1], place.at(pair=p))
        )
        for p in pair_steps
    ]
    pout_load = started(links.local(pout_ref.at[place.pair], pout_own))

    hops = [dict(pair=1 << i) for i in range(place.pairs.bit_length() - 1)]
    hops += [dict(top=1)] + [dict(low=b) for b in place.low_bits] + [dict(core=1)]
    vec_load = started(links.local(vec_ref, vec_val.at[0]))
    vec_copies = []

    def vec_send():
        i = len(vec_copies)
        vec_copies.append(
            started(links.far(vec_val.at[i], vec_got.at[i], place.at(**hops[i])))
        )

    def vec_add():
        i = len(vec_copies) - 1
        vec_copies[i].wait_recv()
        vec_val[i + 1] = vec_val[i] + vec_got[i]

    vec_load.wait()
    vec_send()
    mixed.begin()
    dh.add_cores()
    vec_add()
    vec_send()
    mixed.add_cores()

    def add_pairs(rows_at, copies):
        for copy in copies:
            copy.wait_recv()
        for p in pair_steps:
            for i in range(half):
                for c in (0, 1):
                    at = rows_at + i
                    add_rows(
                        part_own.at[at, c], part_own.at[at, c], part_first.at[p - 1, at, c], 16
                    )

    part_load.wait()
    add_pairs(half * (1 - place.top), by_pair["far"])
    cross = started(links.far(part_own.at[far_rows], part_top, place.at(top=1)))
    dh.add_stage(0)
    vec_add()
    vec_send()
    mixed.add_stage(0)
    add_pairs(half * place.top, by_pair["near"])

    pout_load.wait()
    for copy in pout_pairs:
        copy.wait_recv()
    for p in pair_steps:
        for c in (0, 1):
            add_rows(pout_own.at[c], pout_own.at[c], pout_first.at[p - 1, c])
    row_copies = []
    for c in (0, 1):
        to_far = links.far(
            pout_own.at[flip(place.core, c)], rows_out.at[1], place.at(top=1, core=c)
        )
        row_copies.append(to_far)

        @pl.when(place.away)
        def _():
            to_far.start()

    row_home = links.far(pout_own.at[1 - place.core], rows_out.at[0], place.at(core=1))
    row_stay = links.local(pout_own.at[place.core], rows_out.at[0])

    @pl.when(place.home)
    def _():
        row_home.start()
        row_stay.start()

    for stage in range(1, len(place.low_bits)):
        dh.add_stage(stage)
    dh.deliver()
    vec_add()
    vec_send()
    for stage in range(1, len(place.low_bits)):
        mixed.add_stage(stage)
    mixed.deliver()

    cross.wait_recv()
    slots = []
    for l, c in near_peers + [(0, 0)]:
        low, core = flip(place.low, l), flip(place.core, c)
        ref = part_own.at[half * place.top + low, core]
        add_rows(ref, ref, part_top.at[low, core], 16)
        slot = slots_out.at[place.core, place.low]
        if (l, c) == (0, 0):
            slots.append(started(links.local(ref, slot)))
        else:
            slots.append(started(links.far(ref, slot, place.at(low=l, core=c))))
    while len(vec_copies) < len(hops):
        vec_add()
        vec_send()
    vec_add()
    vec_store = started(links.local(vec_val.at[len(hops)], vec_out))

    for copy in slots:
        copy.wait()
    vec_store.wait()
    dh.finish()
    mixed.finish()
    cross.wait_send()
    for copy in by_pair["far"] + by_pair["near"] + pout_pairs + vec_copies:
        copy.wait_send()

    @pl.when(place.home)
    def _():
        row_stay.wait()
        row_home.wait_send()
        row_copies[0].wait_recv()

    @pl.when(place.away)
    def _():
        row_home.wait_recv()
        row_copies[1].wait_recv()
        row_copies[0].wait_send()
        row_copies[1].wait_send()


def exit_scatter(seq, fsdp, grad_h, mixed, part, part_out, vector):
    seqs, _, length, depth = grad_h.shape
    half, pairs = seq // 2, fsdp // 2
    rows, cols = part.shape[3:]
    rows_out = part_out.shape[2]
    bits = (half.bit_length() - 1) + (pairs.bit_length() - 1) + 2
    token_own = pltpu.VMEM((seqs, half, length, depth), BF16)
    token_later = pltpu.VMEM((seqs, max(half - 1, 1), length, depth), BF16)
    tokens = jax.ShapeDtypeStruct((seqs, length, depth), BF16)
    return pl.pallas_call(
        functools.partial(exit_kernel, seq, fsdp),
        in_specs=[ANYWHERE] * 5,
        out_specs=[ANYWHERE] * 5,
        out_shape=[
            tokens,
            tokens,
            jax.ShapeDtypeStruct((2, half, rows, cols), BF16),
            jax.ShapeDtypeStruct((2, rows_out, depth), BF16),
            jax.ShapeDtypeStruct(vector.shape, F32),
        ],
        scratch_shapes=[
            token_own, token_own, token_later, token_own, token_own, token_later,
            pltpu.VMEM((seq, 2, rows, cols), BF16),
            pltpu.VMEM((max(pairs - 1, 1), seq, 2, rows, cols), BF16),
            pltpu.VMEM((half, 2, rows, cols), BF16),
            pltpu.VMEM((2, rows_out, depth), BF16),
            pltpu.VMEM((max(pairs - 1, 1), 2, rows_out, depth), BF16),
            pltpu.VMEM((bits + 1,) + vector.shape, F32),
            pltpu.VMEM((bits,) + vector.shape, F32),
            pltpu.SemaphoreType.DMA((128,)),
            pltpu.SemaphoreType.DMA((128,)),
            pltpu.SemaphoreType.DMA((32,)),
        ],
        compiler_params=pltpu.CompilerParams(
            collective_id=1, has_side_effects=True, vmem_limit_bytes=56 << 20
        ),
        cost_estimate=pl.CostEstimate(
            flops=0, transcendentals=0, bytes_accessed=200_000_000
        ),
        name="exit_scatter",
    )(grad_h, mixed, part, part_out, vector)


def local(
    tokens, segments, gain_in, w_in, conv_w, conv_b, dt_bias, a_log, skip, gain_out, w_out,
    cotangent,
):
    steps, shards = lax.axis_size("seq"), lax.axis_size("fsdp")
    place = Place(steps, shards)
    seqs, length, _ = tokens.shape
    width = INNER // steps
    heads = HEADS // steps
    rows_in = w_in.shape[0]
    number = place.chunk

    def mine(array, size):
        return lax.dynamic_slice_in_dim(array, number * size, size, array.ndim - 1)

    wide = tokens.astype(F32)
    scale_in = lax.rsqrt(jnp.mean(wide * wide, axis=-1, keepdims=True) + EPSILON)
    normed = (wide * scale_in * gain_in).astype(BF16)
    zx = w_in[:, : 2 * INNER].reshape(rows_in, 2, steps, width).transpose(2, 0, 1, 3)
    zx = zx.reshape(steps, rows_in, 2 * width)
    tail = jnp.pad(w_in[:, 2 * INNER :], ((0, 0), (0, LANES - HEADS)))
    h_all, w_mine, out_w, cot_all, segs = entry_gather(
        steps, shards, normed, zx, tail, w_out, cotangent, segments
    )
    w_mine = w_mine.reshape(D, 2 * width + TAIL)
    out_w = out_w.reshape(width, D)
    segs = jnp.where(place.home, segments, segs)

    total = steps * length
    index = lax.broadcasted_iota(jnp.int32, (seqs, total), 1)
    starts = jnp.concatenate([jnp.ones((seqs, 1), bool), segs[:, 1:] != segs[:, :-1]], axis=1)
    first = lax.cummax(jnp.where(starts, index, 0), axis=1)
    ends = jnp.concatenate([starts[:, 1:], jnp.ones((seqs, 1), bool)], axis=1)
    last = lax.cummin(jnp.where(ends, index, total), axis=1, reverse=True)
    off = (index - first).astype(F32).reshape(seqs, steps, length)
    rem = (last - index).astype(F32).reshape(seqs, steps, length)
    off_col, off_row, rem_col = off[..., None], off[:, :, None, :], rem[..., None]

    heads_p = jnp.stack([mine(dt_bias, heads), mine(a_log, heads)])
    lane = lax.broadcasted_iota(jnp.int32, (LANES, LANES), 1)
    source = lax.broadcasted_iota(jnp.int32, (LANES, LANES), 0)
    pick = ((lane < heads) & (source == lane + number * heads)).astype(BF16)
    consts = (
        mine(conv_w[:, :INNER], width),
        mine(conv_b[None, :INNER], width),
        conv_w[:, INNER:],
        conv_b[None, INNER:],
        jnp.pad(heads_p, ((0, 6), (0, LANES - heads))),
        pick,
        jnp.repeat(mine(skip, heads), HEAD_DIM)[None],
        mine(gain_out[None], width),
    )

    def dot(a, b):
        return lax.dot_general(a, b, (((3,), (0,)), ((), ())), preferred_element_type=F32)

    def dot_tr(a, b):
        return lax.dot_general(a, b, (((3,), (1,)), ((), ())), preferred_element_type=F32)

    def dot_tokens(a, b):
        dims = (0, 1, 2)
        return lax.dot_general(a, b, ((dims, dims), ((), ())), preferred_element_type=F32)

    proj = dot(h_all, w_mine).astype(BF16)
    y, gated, squares, states = forward_mix(proj, off_col, consts)

    grad_yn = dot_tr(cot_all, out_w)
    sums = jnp.stack(
        [squares[:, :, 0], jnp.sum(grad_yn * gated.astype(F32), axis=-1)], axis=2
    )
    for offsets in [dict(core=1)] + [dict(low=b) for b in place.low_bits]:
        sums = sums + exchange(sums, steps, shards, **offsets)
    scale = lax.rsqrt(sums[:, :, 0] / INNER + EPSILON)
    stats = jnp.stack([scale, sums[:, :, 1] * (scale * scale * scale / INNER)], axis=2)
    scale = scale[..., None]
    mixed = (dot(gated, out_w) * scale).astype(BF16)
    y_normed = (gated.astype(F32) * scale).astype(BF16)
    part_out = dot_tokens(y_normed, cot_all).astype(BF16)

    grad_proj, sums_x, sums_t, sums_h = backward_mix(
        proj, off_col, off_row, rem_col, y, grad_yn, stats, states, consts
    )

    grad_h = dot_tr(grad_proj, w_mine).astype(BF16)
    part = dot_tokens(h_all, grad_proj)
    gain_part = jnp.sum(part * w_mine.astype(F32), axis=1)
    part = part.astype(BF16).reshape(steps, shards // 2, 2, rows_in, 2 * width + TAIL)
    grouped = jnp.concatenate(
        [
            sums_x[: KERNEL + 1].reshape(-1),
            sums_x[KERNEL + 2],
            jnp.sum(sums_x[KERNEL + 1].reshape(heads, HEAD_DIM), axis=-1),
            sums_h[:2, :heads].reshape(-1),
        ]
    )
    size = -(-grouped.shape[0] // LANES) * LANES
    grouped = jnp.pad(grouped, (0, size - grouped.shape[0])).reshape(1, -1, LANES)
    grouped = lax.dynamic_update_slice_in_dim(
        jnp.zeros((steps,) + grouped.shape[1:], F32), grouped, number, 0
    )
    everywhere = jnp.concatenate([gain_part, sums_t[: KERNEL + 1].reshape(-1)])
    vector = jnp.concatenate([grouped.reshape(-1, LANES), everywhere.reshape(-1, LANES)])
    grad_h, mixed, slots, rows, vector = exit_scatter(
        steps, shards, grad_h, mixed, part,
        part_out.reshape((shards // 2, 2) + w_out.shape), vector,
    )

    mixed = (wide + mixed.astype(F32)).astype(BF16)
    w_out_grad = rows[0].astype(F32) + rows[1].astype(F32)
    slots = slots.reshape(steps, rows_in, 2 * width + TAIL).astype(F32)
    zx_grad = slots[:, :, : 2 * width].reshape(steps, rows_in, 2, width).transpose(1, 2, 0, 3)
    tail_grad = jnp.sum(slots[:, :, 2 * width : 2 * width + 2 * STATE + HEADS], axis=0)
    w_in_grad = jnp.concatenate([zx_grad.reshape(rows_in, 2 * INNER), tail_grad], axis=1)

    grad_h = grad_h.astype(F32)
    scaled = grad_h * gain_in
    unit = wide * scale_in
    tokens_grad = cotangent.astype(F32) + scale_in * (
        scaled - unit * jnp.mean(scaled * unit, axis=-1, keepdims=True)
    )

    edge = steps * size // LANES
    everywhere = vector[edge:].reshape(-1)
    grouped = vector[:edge].reshape(steps, size)
    gain_in_grad = everywhere[:D] / gain_in
    conv_x = grouped[:, : (KERNEL + 1) * width].reshape(steps, KERNEL + 1, width)
    conv_x = conv_x.transpose(1, 0, 2).reshape(KERNEL + 1, INNER)
    conv_grads = jnp.concatenate([conv_x, everywhere[D:].reshape(KERNEL + 1, -1)], axis=1)
    rest = grouped[:, (KERNEL + 1) * width :]
    gain_out_grad = rest[:, :width].reshape(-1)
    per_head = rest[:, width : width + 3 * heads].reshape(steps, 3, heads)
    per_head = per_head.transpose(1, 0, 2).reshape(3, HEADS)
    return (
        mixed, tokens_grad, gain_in_grad, w_in_grad, conv_grads[:KERNEL], conv_grads[KERNEL],
        per_head[1], per_head[2], per_head[0], gain_out_grad, w_out_grad,
    )


def exchange(value, seq, fsdp, low=0, core=0):
    perm = [
        (s * fsdp + f, (s ^ low) * fsdp + (f ^ core)) for s in range(seq) for f in range(fsdp)
    ]
    return lax.ppermute(value, AXES, perm)


def solution(mesh):
    by_token = P("fsdp", "seq", None)
    by_row = P(("seq", "fsdp"), None)
    placed = (
        by_token, P("fsdp", None), P(), by_row, P(), P(), P(), P(), P(), P(), by_row, by_token,
    )
    return jax.shard_map(
        local,
        mesh=mesh,
        in_specs=placed,
        out_specs=(by_token, by_token, P(), by_row, P(), P(), P(), P(), P(), P(), by_row),
        check_vma=False,
    )
```

time: 924 us -> 443 us (0.48)
  waiting for transfers between devices: 451 us -> 1.18 us
  Pallas kernels: 46.3 us -> 338 us
  blocking collectives: 258 us -> 0 us
  matrix products: 93.1 us -> 48.8 us
  between operations: 14.7 us -> 1.76 us
    pallas_call x2 -> x4, Pallas kernels: 46.3 us -> 338 us  [the longest x1 153 us: exit_scatter(): pl.pallas_call(functools.partial(exit_kernel, seq, fsdp), in_specs=[ANYWH...]
    reduce_scatter x4 -> x0, waiting for transfers between devices: 188 us -> none  [the longest x1 79 us: local(): grad_h = lax.psum_scatter(grad_h, 'seq', scatter_dimension=0).astype(F32)]
    all_gather x4 -> x0, waiting for transfers between devices: 132 us -> none  [the longest x1 97.6 us: local(): cot_all = lax.all_gather(cotangent, 'seq', axis=0)]
    psum x1 -> x0, waiting for transfers between devices: 129 us -> none  [local(): lax.psum((gain_in_part, spread_last(gain_out_part, rank * width, INNER),...]
    unnamed x1 -> x0, blocking collectives: 104 us -> none
    all_to_all x2 -> x0, blocking collectives: 70.2 us -> none  [the longest x1 41.3 us: local(): lax.all_to_all(part.astype(BF16), 'seq', split_axis=0, concat_axis=0, til...]
    all_gather x1 -> x0, blocking collectives: 56 us -> none  [local(): lax.all_gather(w_in[:, 2 * INNER:], ('seq', 'fsdp'), axis=0, tiled=True)]
    psum x1 -> x0, blocking collectives: 27.8 us -> none  [local(): sums = lax.psum(sums, 'seq')]
  transfers between devices with their start and end apart: 9 -> 3, of which waited for: 7 -> 1; matrix products, arithmetic and copies ran while one was open for 10% -> 2% of each run, Pallas kernels for 1% -> 0%
where the time goes in v3:
time: 443 us; the launch traced here: 438 us
  Pallas kernels  338 us (76%)
  matrix products  48.8 us (11%)
  local copies, waits for them, and re-layouts  24.5 us (6%)
  other arithmetic  18.9 us (4%)
  starting transfers between devices  4.74 us (1%)
    pallas_call x1, Pallas kernels, exit_scatter(): pl.pallas_call(functools.partial(exit_kernel, seq, fsdp), in_specs=[ANYWH...  153 us
    pallas_call x1, Pallas kernels, entry_gather(): pl.pallas_call(functools.partial(entry_kernel, seq, fsdp), in_specs=[ANYW...  133 us
    pallas_call x1, Pallas kernels, backward_mix(): pl.pallas_call(backward_kernel, grid=(steps,), in_specs=[block(2 * width)...  36.4 us
    dot_general x2, matrix products, dot(): lax.dot_general(a, b, (((3,), (0,)), ((), ())), preferred_element_type=F32)  16.7 us
    pallas_call x1, Pallas kernels, forward_mix(): pl.pallas_call(forward_kernel, grid=(steps,), in_specs=[block(2 * width),...  16.6 us
    dot_general x2, matrix products, dot_tokens(): lax.dot_general(a, b, ((dims, dims), ((), ())), preferred_element_type=F32)  16.2 us
    dot_general x2, matrix products, dot_tr(): lax.dot_general(a, b, (((3,), (1,)), ((), ())), preferred_element_type=F32)  15.8 us
  transfers between devices with their start and end apart: 3, of which 1 were waited for; matrix products, arithmetic and copies ran while one was open for 2% of the time, Pallas kernels for 0%

profile of v3, /device:TPU:1, one launch (start us, length us, event | category | flops | bytes accessed | tf_op | source)
XLA Modules:
  0.0 438.3 jit_solution(12856413300029902963)
XLA Ops:
  0.8 0.8 slice.126
  1.5 0.7 slice.125.wt_ref
  2.5 0.8 dynamic-slice.7
  3.7 0.5 copy.58
  4.2 1.2 reshape.232.zx_ref
  5.3 0.6 pad.14.tail_ref
  6.0 1.1 fusion.6.h_ref
  7.1 132.8 %entry_gather.1 = (bf16[2,8,128,1536]{3,2,1,0:T(8,128)(2,1)}, bf16[8,2,2,48,1152]{4,3,2,1,0:T(8,128)(2,1)}, bf16[2,2,96,1536]{3,2,1,0:T(8,128)(2,1)}, bf16[2,8,128,1536]{3,2,1,0:T(8,128)(2,1)}, s32[2,1024]{1,0:T(2,128)}) custom-call(bf16[2,128,1536]{2,1,0:T(8,128)(2,1)} %fusion.6.h_ref, bf16[8,48,768]{2,1,0:T(8,128)(2,1)} %reshape.232.zx_ref, ...), custom_call_target="tpu_custom_call" | custom-call | bytes 200000000 | tf_op jit(solution)/shard_map/entry_gather/pallas_call | solution.py:720
  139.9 0.7 broadcast_select_fusion
  140.8 0.8 reduce-window.14
  142.5 11.5 %convolution_convert_fusion.1.zx_ref.zxh_ref.tail_ref.tailh_ref = bf16[2,8,128,1152]{3,2,1,0:T(8,128)(2,1)S(1)} fusion(bf16[2,8,128,1536]{3,2,1,0:T(8,128)(2,1)} %get-tuple-element.29, bf16[1536,1152,1,1]{1,0,3,2:T(8,128)(2,1)} %bitcast.117), kind=kOutput, calls=%fused_computation.4 | convolution fusion | flops 7250116608 | bytes 14548992 | tf_op jit(solution)/shard_map/dot_general | solution.py:1111
  154.2 16.6 %mix_forward.1 = (bf16[2,8,128,384]{3,2,1,0:T(8,128)(2,1)S(1)}, bf16[2,8,128,384]{3,2,1,0:T(8,128)(2,1)S(1)}, f32[2,8,1,128]{3,2,1,0:T(1,128)S(1)}, bf16[2,8,128,384]{3,2,1,0:T(8,128)(2,1)S(1)}) custom-call(bf16[2,8,128,1152]{3,2,1,0:T(8,128)(2,1)S(1)} %convolution_convert_fusion.1.zx_ref.zxh_ref.tail_ref.tailh_ref, ...), custom_call_target="tpu_custom_call" | custom-call | flops 14400000000 | bytes 10000000 | tf_op jit(solution)/shard_map/mix_forward/pallas_call | solution.py:360
  170.9 5.1 %fusion = (f32[2,8,128]{2,1,0:T(8,128)S(1)}, f32[2,8,128,384]{3,2,1,0:T(8,128)}) fusion(bf16[2,8,128,384]{3,2,1,0:T(8,128)(2,1)S(1)} %get-tuple-element.36, bf16[2,8,128,1536]{3,2,1,0:T(8,128)(2,1)S(1)} %bitcast.114, bf16[384,1536,1,1]{1,0,3,2:T(8,128)(2,1)S(1)} %bitcast.119), kind=kOutput, calls=%fused_computation.7 | convolution fusion | flops 2418276352 | bytes 12197888 | tf_op jit(solution)/shard_map/dot_general | solution.py:1114
  176.0 1.9 collective-permute-start
  178.0 4.7 %reduce-window.16 = s32[2,8,128]{2,1,0:T(8,128)S(1)} reduce-window(s32[2,8,128]{2,1,0:T(8,128)S(1)} %get-tuple-element.63, s32[]{:T(128)} %constant.66.clone.1), window={size=1x1x128 pad=0_0x0_0x0_127}, to_apply=%region_3.4 | reduce-window | flops 260096 | bytes 16388 | tf_op jit(solution)/shard_map/reduce-window.2
  183.1 1.4 collective-permute-start.1
  184.5 1.2 collective-permute-done.1
  185.7 1.4 collective-permute-start.2
  187.2 1.3 copy.37
  188.6 1.3 convert_element_type.100.rem_ref
  190.0 1.9 copy-done.2
  191.9 1.4 copy-done.5
  193.3 1.4 copy-done.7
  194.7 36.4 %mix_backward.1 = (bf16[2,8,128,1152]{3,2,1,0:T(8,128)(2,1)S(1)}, f32[8,384]{1,0:T(8,128)S(1)}, f32[8,256]{1,0:T(8,128)S(1)}, f32[8,128]{1,0:T(8,128)S(1)}) custom-call(bf16[2,8,128,1152]{3,2,1,0:T(8,128)(2,1)} %copy-done.3, bf16[2,8,128,1152]{3,2,1,0:T(8,128)(2,1)} %copy-done.3, bf16[2,8,128,1152]{3,2,1,0:T(8,128)(2,1)} %copy-done.3, ...), custom_call_target="tpu_custom_call" | custom-call | flops 32000000000 | bytes 16000000 | tf_op jit(solution)/shard_map/mix_backward/pallas_call | solution.py:398
  231.2 12.5 %multiply_reduce_fusion = (f32[1536]{0:T(1024)S(1)}, bf16[1536,1152]{1,0:T(8,128)(2,1)}) fusion(bf16[8,2,2,48,1152]{4,3,2,1,0:T(8,128)(2,1)S(1)} %copy-done.19, bf16[2,8,128,1536]{3,2,1,0:T(8,128)(2,1)} %get-tuple-element.29, bf16[2,8,128,1152]{3,2,1,0:T(8,128)(2,1)S(1)} %get-tuple-element.38), kind=kOutput, calls=%fused_computation.2 | convolution fusion | flops 7254833664 | bytes 18094080 | tf_op jit(solution)/shard_map/dot_general | solution.py:1118
  243.6 10.7 %convolution_convert_fusion.dh_ref = bf16[2,8,128,1536]{3,2,1,0:T(8,128)(2,1)} fusion(bf16[2,8,128,1152]{3,2,1,0:T(8,128)(2,1)S(1)} %get-tuple-element.38, bf16[1536,1152,1,1]{1,0,3,2:T(8,128)(2,1)S(1)} %bitcast.118), kind=kOutput, calls=%fused_computation.3 | convolution fusion | flops 7250903040 | bytes 14548992 | tf_op jit(solution)/shard_map/dot_general | solution.py:1114
  254.4 3.8 fusion.2
  258.2 5.3 %multiply_convert_fusion.mixed_ref = bf16[2,8,128,1536]{3,2,1,0:T(8,128)(2,1)} fusion(bf16[2,8,128,384]{3,2,1,0:T(8,128)(2,1)S(1)} %copy-done.1, bf16[384,1536,1,1]{1,0,3,2:T(8,128)(2,1)S(1)} %bitcast.120, f32[2,8,128]{2,1,0:T(8,128)S(1)} %bitcast.110), kind=kOutput, calls=%fused_computation | convolution fusion | flops 2422210560 | bytes 9052160 | tf_op jit(solution)/shard_map/dot_general | solution.py:1111
  263.9 0.6 pad_maximum_fusion.1.vec_ref
  264.5 152.7 %exit_scatter.1 = (bf16[2,128,1536]{2,1,0:T(8,128)(2,1)}, bf16[2,128,1536]{2,1,0:T(8,128)(2,1)}, bf16[2,4,48,1152]{3,2,1,0:T(8,128)(2,1)}, bf16[2,96,1536]{2,1,0:T(8,128)(2,1)}, f32[174,128]{1,0:T(8,128)}) custom-call(bf16[2,8,128,1536]{3,2,1,0:T(8,128)(2,1)} %convolution_convert_fusion.dh_ref, bf16[2,8,128,1536]{3,2,1,0:T(8,128)(2,1)} %multiply_convert_fusion.mixed_ref, ...), custom_call_target="tpu_custom_call" | custom-call | bytes 200000000 | tf_op jit(solution)/shard_map/exit_scatter/pallas_call | solution.py:1023
  417.3 0.7 slice.140
  418.0 1.3 bitcast_divide_fusion
  419.3 0.9 slice.138
  420.3 0.6 slice_reduce_fusion.1
  420.9 0.6 slice.159
  421.5 1.3 bitcast_convert_fusion
  422.9 1.6 copy-done.11
  424.6 0.4 fusion.7
  425.2 0.6 squeeze.23
  425.8 0.6 squeeze.22
  426.3 0.6 squeeze.21
  426.9 0.6 reshape.257
  427.5 1.9 add_bitcast_fusion
  429.5 1.6 reshape.250
  431.1 2.0 copy.42
  433.5 0.7 copy-done.10
  434.7 2.1 fusion.10
  436.8 1.1 pad_maximum_fusion
  (125 shorter events, 4.3 us)
Async XLA Ops:
  0.6 2.9 slice-start.6
  0.7 2.9 slice-start.5
  0.7 2.9 slice-start.2
  0.7 1.5 copy-start.8
  0.7 2.6 copy-start.22
  3.6 1.8 slice-start.1
  3.6 2.4 copy-start.15
  7.1 132.8 %copy-start.16 = (s32[2,1024]{1,0:T(2,128)S(1)}, s32[2,1024]{1,0:T(2,128)}, u32[]{:S(2)}) copy-start(s32[2,1024]{1,0:T(2,128)} %seg_ref.1) | copy-start | bytes 24580
  7.1 135.2 %copy-start.17 = (f32[48]{0:T(128)S(1)}, f32[48]{0:T(128)}, u32[]{:S(2)}) copy-start(f32[48]{0:T(128)} %param.19) | copy-start | bytes 580
  7.1 135.2 %copy-start.18 = (f32[48]{0:T(128)S(1)}, f32[48]{0:T(128)}, u32[]{:S(2)}) copy-start(f32[48]{0:T(128)} %param.18) | copy-start | bytes 580
  153.9 16.9 %copy-start.3 = (bf16[2,8,128,1152]{3,2,1,0:T(8,128)(2,1)}, bf16[2,8,128,1152]{3,2,1,0:T(8,128)(2,1)S(1)}, u32[]{:S(2)}) copy-start(bf16[2,8,128,1152]{3,2,1,0:T(8,128)(2,1)S(1)} %convolution_convert_fusion.1.zx_ref.zxh_ref.tail_ref.tailh_ref) | copy-start | bytes 14155780
  153.9 16.9 %slice-start.7 = ((s8[6291456]{0:T(1024)(128)(4,1)}), s8[4194304]{0:T(1024)(128)(4,1)S(1)}, s32[]{:S(2)}) async-start(s8[6291456]{0:T(1024)(128)(4,1)} %bitcast.113), calls=%async_computation.7 | async-start | bytes 8388608
  154.2 16.6 %slice-start.8 = ((s8[6291456]{0:T(1024)(128)(4,1)}), s8[2097152]{0:T(1024)(128)(4,1)S(1)}, s32[]{:S(2)}) async-start(s8[6291456]{0:T(1024)(128)(4,1)} %bitcast.113), calls=%async_computation.8 | async-start | bytes 4194304
  154.2 16.6 %copy-start.20 = (bf16[2,2,96,1536]{3,2,1,0:T(8,128)(2,1)S(1)}, bf16[2,2,96,1536]{3,2,1,0:T(8,128)(2,1)}, u32[]{:S(2)}) copy-start(bf16[2,2,96,1536]{3,2,1,0:T(8,128)(2,1)} %get-tuple-element.34) | copy-start | bytes 3538948
  170.8 5.2 %copy-start = (bf16[2,8,128,384]{3,2,1,0:T(8,128)(2,1)}, bf16[2,8,128,384]{3,2,1,0:T(8,128)(2,1)S(1)}, u32[]{:S(2)}) copy-start(bf16[2,8,128,384]{3,2,1,0:T(8,128)(2,1)S(1)} %get-tuple-element.36) | copy-start | bytes 4718596
  170.8 5.2 %copy-start.4 = (bf16[2,8,128,384]{3,2,1,0:T(8,128)(2,1)}, bf16[2,8,128,384]{3,2,1,0:T(8,128)(2,1)S(1)}, u32[]{:S(2)}) copy-start(bf16[2,8,128,384]{3,2,1,0:T(8,128)(2,1)S(1)} %get-tuple-element.32.y_ref) | copy-start | bytes 4718596
  170.8 5.2 %copy-start.6 = (bf16[2,8,128,384]{3,2,1,0:T(8,128)(2,1)}, bf16[2,8,128,384]{3,2,1,0:T(8,128)(2,1)S(1)}, u32[]{:S(2)}) copy-start(bf16[2,8,128,384]{3,2,1,0:T(8,128)(2,1)S(1)} %get-tuple-element.37.state_ref) | copy-start | bytes 4718596
  176.0 7.0 %collective-permute-start = (f32[2,8,2,128]{3,2,1,0:T(2,128)S(1)}, f32[2,8,2,128]{3,2,1,0:T(2,128)S(1)}, u32[]{:S(2)}, u32[]{:S(2)}) collective-permute-start(f32[2,8,2,128]{3,2,1,0:T(2,128)S(1)} %pad_maximum_fusion.2), channel_id=1, source_target_pairs={{0,1},{1,0},{2,3},{3,2},{4,5},{5,4},{6,7},{7,6},{8,9},{9,8},{10,11... | collective-permute-start | bytes 49160 | tf_op jit(solution)/shard_map/ppermute | solution.py:1199
  183.1 2.7 collective-permute-start.1
  185.7 4.2 collective-permute-start.2
  190.0 1.9 copy-start.2
  191.9 1.4 copy-start.5
  193.3 1.4 copy-start.7
  194.7 36.4 %copy-start.19 = (bf16[8,2,2,48,1152]{4,3,2,1,0:T(8,128)(2,1)S(1)}, bf16[8,2,2,48,1152]{4,3,2,1,0:T(8,128)(2,1)}, u32[]{:S(2)}) copy-start(bf16[8,2,2,48,1152]{4,3,2,1,0:T(8,128)(2,1)} %get-tuple-element.30) | copy-start | bytes 10616836
  231.2 23.2 %slice-start.9 = ((s8[6291456]{0:T(1024)(128)(4,1)}), s8[4194304]{0:T(1024)(128)(4,1)S(1)}, s32[]{:S(2)}) async-start(s8[6291456]{0:T(1024)(128)(4,1)} %bitcast.115), calls=%async_computation.9 | async-start | bytes 8388608
  243.6 10.7 %copy-start.1 = (bf16[2,8,128,384]{3,2,1,0:T(8,128)(2,1)S(1)}, bf16[2,8,128,384]{3,2,1,0:T(8,128)(2,1)}, u32[]{:S(2)}) copy-start(bf16[2,8,128,384]{3,2,1,0:T(8,128)(2,1)} %copy-done) | copy-start | bytes 4718596
  243.6 10.7 %slice-start.10 = ((s8[6291456]{0:T(1024)(128)(4,1)}), s8[2097152]{0:T(1024)(128)(4,1)S(1)}, s32[]{:S(2)}) async-start(s8[6291456]{0:T(1024)(128)(4,1)} %bitcast.115), calls=%async_computation.10 | async-start | bytes 4194304
  254.4 3.8 copy-start.21
  420.2 2.7 copy-start.14
  422.8 2.2 copy-start.9
  422.9 1.7 copy-start.11
  422.9 2.1 slice-start.3
  422.9 4.0 slice-start.4
  425.0 4.4 %slice-start = ((f32[8,48,1152]{2,1,0:T(8,128)}), f32[8,48,768]{2,1,0:T(8,128)S(1)}, s32[]{:S(2)}) async-start(f32[8,48,1152]{2,1,0:T(8,128)} %copy-done.9), calls=%async_computation | async-start | bytes 2359296 | tf_op jit(solution)/shard_map/slice | solution.py:1167
  433.1 1.1 copy-start.10
  433.1 1.4 copy-start.12
  433.1 1.6 copy-start.13

commit v4 on v3

--- a/solution.py
+++ b/solution.py
@@ -138,21 +138,51 @@
 
 
 def forward_kernel(
-    zx_ref, zxh_ref, tail_ref, tailh_ref, off_ref,
+    seq, fsdp,
+    h_ref, w_ref, cot_ref, ow_ref, off_ref,
     wx_ref, bx_ref, wt_ref, bt_ref, hp_ref, pick_ref, skip_ref, gain_ref,
-    y_ref, gated_ref, square_ref, state_ref, memory, ext_x, ext_t,
+    proj_ref, y_ref, gated_ref, square_ref, state_ref, cot_out, ow_out,
+    memory, ext_x, ext_t, last_rows, send, recv, near,
 ):
     seqs, _, length, width = y_ref.shape
-
-    @pl.when(pl.program_id(0) == 0)
+    depth = h_ref.shape[3]
+    step_at = pl.program_id(0)
+
+    place = Place(seq, fsdp)
+    links = Links(send, recv, near)
+    cot = TokenGather(place, links, cot_ref, cot_out)
+    w_rows = RowGather(place, links, ow_ref, ow_out)
+    stages = len(place.low_bits)
+    arrive_at = max(seq // 2 - 1, 1)
+
+    @pl.when(step_at == 0)
     def _():
         memory[...] = jnp.zeros_like(memory)
-
+        last_rows[...] = jnp.zeros_like(last_rows)
+        meet_pair(place)
+        cot.begin()
+
+    @pl.when(step_at == 1)
+    def _():
+        w_rows.begin()
+
+    @pl.when(step_at == arrive_at)
+    def _():
+        cot.arrive()
+        cot.send_stage(0)
+
+    proj = jnp.dot(
+        h_ref[...].reshape(seqs * length, depth), w_ref[...], preferred_element_type=F32
+    ).astype(BF16)
+    proj_ref[...] = proj.reshape(proj_ref.shape)
     params = tuple(r[...] for r in (wx_ref, bx_ref, wt_ref, bt_ref, hp_ref, pick_ref))
     for q in range(seqs):
         offset = off_ref[q, 0]
+        chunk_rows = proj[q * length : (q + 1) * length]
+        zx, tail = chunk_rows[:, : 2 * width], chunk_rows[:, 2 * width :]
+        earlier = last_rows[q]
         conv_x, conv_t, _, _, _, _, cumul, _, step_x, entry_x, end_x = chunk_common(
-            zx_ref[q, 0, :, width:], zxh_ref[q, 0, :, width:], tail_ref[q, 0], tailh_ref[q, 0], offset, params,
+            zx[:, width:], earlier[:, width : 2 * width], tail, earlier[:, 2 * width :], offset, params,
             ext_x.at[q], ext_t.at[q], width,
         )
         xs = conv_x * sigmoid(conv_x)
@@ -180,7 +210,7 @@
             inside = jnp.dot(mix, tile, preferred_element_type=F32)
             y_low = (inside + outside[:, start : start + size]).astype(BF16)
             y_ref[q, 0, :, start : start + size] = y_low
-            z = zx_ref[q, 0, :, start : start + size].astype(F32)
+            z = zx[:, start : start + size].astype(F32)
             gated = y_low.astype(F32) * (z * sigmoid(z))
             gated_ref[q, 0, :, start : start + size] = (
                 gated * gain_ref[:, start : start + size]
@@ -189,15 +219,60 @@
         square_ref[q, 0] = jnp.broadcast_to(squares, (length, LANES)).T[0:1, :]
         fresh = tr_mm(bs, scaled * end_x)
         memory[q] = old * entry_x[length - 1 : length, :] + fresh
+        last_rows[q] = chunk_rows[length - HALO :]
+
+    @pl.when(step_at == pl.num_programs(0) - 2)
+    def _():
+        w_rows.forward()
+
+    @pl.when(step_at == pl.num_programs(0) - 1)
+    def _():
+        for stage in range(stages):
+            cot.finish_stage(stage)
+            if stage + 1 < stages:
+                cot.send_stage(stage + 1)
+        w_rows.finish()
+        cot.finish()
 
 
 def backward_kernel(
+    seq, fsdp,
     zx_ref, zxh_ref, tail_ref, tailh_ref, off_ref, offr_ref, rem_ref, y_ref, grad_ref, stat_ref,
-    state_ref, wx_ref, bx_ref, wt_ref, bt_ref, hp_ref, pick_ref, skip_ref, gain_ref,
-    out_ref, gx_ref, gt_ref, gh_ref,
+    state_ref, mixed_ref, pout_ref,
+    wx_ref, bx_ref, wt_ref, bt_ref, hp_ref, pick_ref, skip_ref, gain_ref,
+    out_ref, gx_ref, gt_ref, gh_ref, mixed_out, rows_out,
     memory, ext_x, ext_t, next_x, next_t,
+    mix_own, mix_first, mix_later, pout_own, pout_first, send, recv, near,
 ):
     seqs, _, length, width = y_ref.shape
+    step_at = pl.program_id(0)
+
+    place = Place(seq, fsdp)
+    links = Links(send, recv, near)
+    mixed = TokenScatter(place, links, mixed_ref, mixed_out, mix_own, mix_first, mix_later)
+    w_rows = RowScatter(place, links, pout_ref, rows_out, pout_own, pout_first)
+    stages = len(place.low_bits)
+
+    @pl.when(step_at == 0)
+    def _():
+        meet_pair(place)
+        mixed.begin()
+        w_rows.begin()
+
+    @pl.when(step_at == 2)
+    def _():
+        mixed.add_cores()
+        mixed.send_stage(0)
+
+    @pl.when(step_at == 4)
+    def _():
+        w_rows.add_pairs()
+
+    @pl.when(step_at == pl.num_programs(0) - 2)
+    def _():
+        mixed.add_stage(0)
+        if stages > 1:
+            mixed.send_stage(1)
 
     @pl.when(pl.program_id(0) == 0)
     def _():
@@ -325,6 +400,16 @@
         out_ref[q, 0, :, 2 * width : 2 * width + 2 * STATE] = results[2]
         out_ref[q, 0, :, 2 * width + 2 * STATE :] = results[3]
 
+    @pl.when(step_at == pl.num_programs(0) - 1)
+    def _():
+        for stage in range(1, stages):
+            mixed.add_stage(stage)
+            if stage + 1 < stages:
+                mixed.send_stage(stage + 1)
+        mixed.store()
+        w_rows.finish()
+        mixed.finish()
+
 
 TAIL = 2 * STATE + LANES
 AXES = ("seq", "fsdp")
@@ -351,78 +436,106 @@
     return block, before
 
 
-def forward_mix(proj, off_col, consts):
-    seqs, steps, length, cols = proj.shape
+def forward_mix(h_all, w_mine, cotangent, out_w, off_col, consts, seq, fsdp):
+    seqs, steps, length, depth = h_all.shape
+    cols = w_mine.shape[1]
     width = (cols - TAIL) // 2
-    block, before = chunk_specs(seqs, steps, length, False)
-    tail_at = 2 * width // TAIL
+    block, _ = chunk_specs(seqs, steps, length, False)
     shape = (seqs, steps, length, width)
     return pl.pallas_call(
-        forward_kernel,
+        functools.partial(forward_kernel, seq, fsdp),
         grid=(steps,),
         in_specs=[
-            block(2 * width), before(2 * width), block(TAIL, tail_at), before(TAIL, tail_at),
-            block(1),
+            block(depth),
+            pl.BlockSpec(w_mine.shape, lambda i: (0, 0), pipeline_mode=pl.Buffered(1)),
+            ANYWHERE, ANYWHERE, block(1),
         ]
         + [whole_spec(v.shape) for v in consts],
         out_specs=[
-            block(width), block(width), block(length, 0, 1), block(width, 0, STATE),
+            block(cols), block(width), block(width), block(length, 0, 1), block(width, 0, STATE),
+            ANYWHERE, ANYWHERE,
         ],
         out_shape=[
+            jax.ShapeDtypeStruct((seqs, steps, length, cols), BF16),
             jax.ShapeDtypeStruct(shape, BF16),
             jax.ShapeDtypeStruct(shape, BF16),
             jax.ShapeDtypeStruct((seqs, steps, 1, length), F32),
             jax.ShapeDtypeStruct((seqs, steps, STATE, width), BF16),
+            jax.ShapeDtypeStruct(h_all.shape, BF16),
+            jax.ShapeDtypeStruct((fsdp // 2, 2) + out_w.shape, BF16),
         ],
         scratch_shapes=[
             pltpu.VMEM((seqs, STATE, width), F32),
             pltpu.VMEM((seqs, HALO + length, width), F32),
             pltpu.VMEM((seqs, HALO + length, 2 * STATE), F32),
+            pltpu.VMEM((seqs, HALO, cols), BF16),
+            pltpu.SemaphoreType.DMA((64,)),
+            pltpu.SemaphoreType.DMA((64,)),
+            pltpu.SemaphoreType.DMA((8,)),
         ],
         compiler_params=pltpu.CompilerParams(
-            dimension_semantics=("arbitrary",), vmem_limit_bytes=32 << 20
+            dimension_semantics=("arbitrary",), vmem_limit_bytes=48 << 20, collective_id=2,
+            has_side_effects=True,
         ),
         cost_estimate=pl.CostEstimate(
             flops=steps * seqs * 900_000_000, transcendentals=0, bytes_accessed=10_000_000
         ),
         name="mix_forward",
-    )(proj, proj, proj, proj, off_col, *consts)
-
-
-def backward_mix(proj, off_col, off_row, rem_col, y, grad_yn, stats, states, consts):
+    )(h_all, w_mine, cotangent, out_w, off_col, *consts)
+
+
+def backward_mix(
+    proj, off_col, off_row, rem_col, y, grad_yn, stats, states, mixed, part_out, consts, seq, fsdp
+):
     seqs, steps, length, cols = proj.shape
+    depth = mixed.shape[3]
     width = (cols - TAIL) // 2
     block, before = chunk_specs(seqs, steps, length, True)
     tail_at = 2 * width // TAIL
+    half, pairs = seq // 2, fsdp // 2
+    rows_out = part_out.shape[2]
     sums = [(8, width), (8, 2 * STATE), (8, LANES)]
+    token_own = pltpu.VMEM((seqs, half, length, depth), BF16)
     return pl.pallas_call(
-        backward_kernel,
+        functools.partial(backward_kernel, seq, fsdp),
         grid=(steps,),
         in_specs=[
             block(2 * width), before(2 * width), block(TAIL, tail_at), before(TAIL, tail_at),
             block(1), block(length, 0, 1), block(1), block(width), block(width),
-            block(length, 0, 2), block(width, 0, STATE),
+            block(length, 0, 2), block(width, 0, STATE), ANYWHERE, ANYWHERE,
         ]
         + [whole_spec(v.shape) for v in consts],
-        out_specs=[block(cols)] + [whole_spec(v) for v in sums],
+        out_specs=[block(cols)] + [whole_spec(v) for v in sums] + [ANYWHERE, ANYWHERE],
         scratch_shapes=[
             pltpu.VMEM((seqs, STATE, width), F32),
             pltpu.VMEM((seqs, HALO + length, width), F32),
             pltpu.VMEM((seqs, HALO + length, 2 * STATE), F32),
             pltpu.VMEM((seqs, length + HALO, width), F32),
             pltpu.VMEM((seqs, length + HALO, 2 * STATE), F32),
+            token_own, token_own, pltpu.VMEM((seqs, max(half - 1, 1), length, depth), BF16),
+            pltpu.VMEM((2, rows_out, depth), BF16),
+            pltpu.VMEM((max(pairs - 1, 1), 2, rows_out, depth), BF16),
+            pltpu.SemaphoreType.DMA((64,)),
+            pltpu.SemaphoreType.DMA((64,)),
+            pltpu.SemaphoreType.DMA((16,)),
         ],
         out_shape=[jax.ShapeDtypeStruct(proj.shape, BF16)]
-        + [jax.ShapeDtypeStruct(v, F32) for v in sums],
+        + [jax.ShapeDtypeStruct(v, F32) for v in sums]
+        + [
+            jax.ShapeDtypeStruct((seqs, length, depth), BF16),
+            jax.ShapeDtypeStruct((2, rows_out, depth), BF16),
+        ],
         compiler_params=pltpu.CompilerParams(
-            dimension_semantics=("arbitrary",), vmem_limit_bytes=40 << 20
+            dimension_semantics=("arbitrary",), vmem_limit_bytes=56 << 20, collective_id=3,
+            has_side_effects=True,
         ),
         cost_estimate=pl.CostEstimate(
             flops=steps * seqs * 2_000_000_000, transcendentals=0, bytes_accessed=16_000_000
         ),
         name="mix_backward",
     )(
-        proj, proj, proj, proj, off_col, off_row, rem_col, y, grad_yn, stats, states, *consts
+        proj, proj, proj, proj, off_col, off_row, rem_col, y, grad_yn, stats, states, mixed,
+        part_out, *consts,
     )
 
 
@@ -457,23 +570,46 @@
     return index
 
 
+class Copy:
+    def __init__(self, make):
+        self.make = make
+
+    def start(self):
+        self.make().start()
+        return self
+
+    def wait(self):
+        self.make().wait()
+
+    def wait_send(self):
+        self.make().wait_send()
+
+    def wait_recv(self):
+        self.make().wait_recv()
+
+
 class Links:
     def __init__(self, send, recv, near):
         self.send, self.recv, self.near = send, recv, near
         self.far_count = self.near_count = 0
 
-    def far(self, src, dst, device):
+    def far(self, make):
         i = self.far_count
         self.far_count += 1
-        return pltpu.make_async_remote_copy(
-            src_ref=src, dst_ref=dst, send_sem=self.send.at[i], recv_sem=self.recv.at[i],
-            device_id=device, device_id_type=MESH,
-        )
-
-    def local(self, src, dst):
+
+        def build():
+            src, dst, device = make()
+            return pltpu.make_async_remote_copy(
+                src_ref=src, dst_ref=dst, send_sem=self.send.at[i], recv_sem=self.recv.at[i],
+                device_id=device, device_id_type=MESH,
+            )
+
+        return Copy(build)
+
+    def local(self, make):
         i = self.near_count
         self.near_count += 1
-        return pltpu.make_async_copy(src, dst, self.near.at[i])
+        return Copy(lambda: pltpu.make_async_copy(*make(), self.near.at[i]))
 
 
 def meet(devices):
@@ -483,87 +619,16 @@
     pl.semaphore_wait(barrier, len(devices))
 
 
-def started(copy):
-    copy.start()
-    return copy
-
-
-class TokenGather:
-    def __init__(self, place, links, src, dst):
-        self.place, self.src, self.dst = place, src, dst
-        self.links = links
-        chunk = place.s
-        self.cross = links.far(src, dst.at[:, chunk], place.at(top=1, core=1))
-        self.stay = links.local(src, dst.at[:, chunk])
-        self.held = None
-        self.sent = []
-        self.stage = 0
-
-    def begin(self):
-        @pl.when(self.place.away)
-        def _():
-            self.cross.start()
-
-        @pl.when(self.place.home)
-        def _():
-            self.stay.start()
-
-    def arrive(self):
-        @pl.when(self.place.away)
-        def _():
-            self.cross.wait_recv()
-
-        @pl.when(self.place.home)
-        def _():
-            self.stay.wait()
-
-        self.held = [[0] for _ in range(self.src.shape[0])]
-        self.pending = [[] for _ in self.held]
-        self.across = []
-        for q in range(len(self.held)):
-            self.share(q, [0])
-
-    def block(self, q, low):
-        return self.dst.at[q, flip(self.place.low, low) + self.place.half * self.place.core]
-
-    def share(self, q, lows):
-        for low in lows:
-            ref = self.block(q, low)
-            self.across.append(started(self.links.far(ref, ref, self.place.at(core=1))))
-
-    def send_stage(self):
-        for q, held in enumerate(self.held):
-            bit = self.place.bits_for(q)[self.stage]
-            for low in held:
-                ref = self.block(q, low)
-                self.pending[q].append(started(self.links.far(ref, ref, self.place.at(low=bit))))
-
-    def finish_stage(self):
-        for q, held in enumerate(self.held):
-            bit = self.place.bits_for(q)[self.stage]
-            for copy in self.pending[q]:
-                copy.wait_recv()
-            self.sent += self.pending[q]
-            self.pending[q] = []
-            fresh = [low ^ bit for low in held]
-            held += fresh
-            self.share(q, fresh)
-        self.stage += 1
-
-    def finish(self):
-        for copy in self.across:
-            copy.wait()
-        for copy in self.sent:
-            copy.wait_send()
-
-        @pl.when(self.place.away)
-        def _():
-            self.cross.wait_send()
+def meet_pair(place):
+    meet(
+        [place.at(top=t, low=l, core=c) for t, l, c in peers_of(place)]
+        + [place.at(pair=p) for p in range(1, place.pairs)]
+    )
 
 
 def peers_of(place):
     out = []
-    for top in (1, 0):
+    for top in (0, 1):
         for low in range(place.half):
             for core in (0, 1):
                 if (top, low, core) != (0, 0, 0):
@@ -571,23 +636,159 @@
     return out
 
 
+class TokenGather:
+    def __init__(self, place, links, src, dst):
+        self.place, self.src, self.dst = place, src, dst
+        seqs = src.shape[0]
+        self.cross = links.far(
+            lambda: (src, dst.at[:, place.s], place.at(top=1, core=1))
+        )
+        self.stay = links.local(lambda: (src, dst.at[:, place.s]))
+        self.share = [[] for _ in range(seqs)]
+        self.stages = []
+        held = [[0] for _ in range(seqs)]
+        for q in range(seqs):
+            self.share[q].append([self.copy(links, q, low, core=1) for low in held[q]])
+        for i in range(len(place.low_bits)):
+            stage = []
+            for q in range(seqs):
+                bit = place.bits_for(q)[i]
+                stage.append([self.copy(links, q, low, low_bit=bit) for low in held[q]])
+                fresh = [low ^ bit for low in held[q]]
+                held[q] = held[q] + fresh
+                self.share[q].append([self.copy(links, q, low, core=1) for low in fresh])
+            self.stages.append(stage)
+
+    def copy(self, links, q, low, low_bit=0, core=0):
+        def make():
+            place = self.place
+            ref = self.dst.at[q, flip(place.low, low) + place.half * place.core]
+            return ref, ref, place.at(low=low_bit, core=core)
+
+        return links.far(make)
+
+    def begin(self):
+        @pl.when(self.place.away)
+        def _():
+            self.cross.start()
+
+        @pl.when(self.place.home)
+        def _():
+            self.stay.start()
+
+    def arrive(self):
+        @pl.when(self.place.away)
+        def _():
+            self.cross.wait_recv()
+
+        @pl.when(self.place.home)
+        def _():
+            self.stay.wait()
+
+    def send_stage(self, i):
+        for copies in self.stages[i]:
+            for copy in copies:
+                copy.start()
+        for share in self.share:
+            for copy in share[i]:
+                copy.start()
+
+    def finish_stage(self, i):
+        for copies in self.stages[i]:
+            for copy in copies:
+                copy.wait_recv()
+        if i + 1 == len(self.stages):
+            for share in self.share:
+                for copy in share[i + 1]:
+                    copy.start()
+
+    def finish(self):
+        for share in self.share:
+            for copies in share:
+                for copy in copies:
+                    copy.wait()
+        for stage in self.stages:
+            for copies in stage:
+                for copy in copies:
+                    copy.wait_send()
+
+        @pl.when(self.place.away)
+        def _():
+            self.cross.wait_send()
+
+
+class RowGather:
+    def __init__(self, place, links, src, dst):
+        self.place = place
+        pairs = range(1, place.pairs)
+
+        def slot():
+            return dst.at[place.pair, place.core]
+
+        self.stay = links.local(lambda: (src, slot()))
+        self.to_home = links.far(lambda: (src, slot(), place.at(core=1)))
+        self.to_near = links.far(lambda: (src, slot(), place.at(top=1)))
+        self.to_far = links.far(lambda: (src, slot(), place.at(top=1, core=1)))
+
+        def forward(c, p):
+            return links.far(
+                lambda: (dst.at[place.pair, c], dst.at[place.pair, c], place.at(pair=p))
+            )
+
+        self.forwards = [forward(c, p) for c in (0, 1) for p in pairs]
+
+    def begin(self):
+        @pl.when(self.place.home)
+        def _():
+            self.stay.start()
+            self.to_near.start()
+
+        @pl.when(self.place.away)
+        def _():
+            self.to_home.start()
+            self.to_far.start()
+
+    def forward(self):
+        @pl.when(self.place.home)
+        def _():
+            self.stay.wait()
+            self.to_home.wait_recv()
+
+        @pl.when(self.place.away)
+        def _():
+            self.to_near.wait_recv()
+            self.to_far.wait_recv()
+
+        for copy in self.forwards:
+            copy.start()
+
+    def finish(self):
+        for copy in self.forwards:
+            copy.wait()
+
+        @pl.when(self.place.home)
+        def _():
+            self.to_near.wait_send()
+
+        @pl.when(self.place.away)
+        def _():
+            self.to_home.wait_send()
+            self.to_far.wait_send()
+
+
 def entry_kernel(
-    seq, fsdp,
-    h_ref, zx_ref, tail_ref, ow_ref, cot_ref, seg_ref,
-    h_out, w_out, ow_out, cot_out, seg_out,
-    send, recv, near,
+    seq, fsdp, h_ref, zx_ref, tail_ref, seg_ref, h_out, w_out, seg_out, send, recv, near
 ):
     place = Place(seq, fsdp)
     links = Links(send, recv, near)
     cols = zx_ref.shape[2]
     peers = peers_of(place)
-    pair_steps = range(1, place.pairs)
-    meet(
-        [place.at(top=t, low=l, core=c) for t, l, c in peers]
-        + [place.at(pair=p) for p in pair_steps]
-    )
+    others = range(1, place.pairs)
     tokens = TokenGather(place, links, h_ref, h_out)
-    tokens.begin()
+
+    def block(t=0, l=0, c=0):
+        s, f = place.at(top=t, low=l, core=c)
+        return w_out.at[s, place.pair, lax.rem(f, 2)]
 
     def columns(ref):
         return ref.at[:, pl.ds(0, cols)]
@@ -595,150 +796,114 @@
     def tail_of(ref):
         return ref.at[:, pl.ds(cols, TAIL)]
 
-    own = w_out.at[place.s, place.pair, place.core]
-    other = w_out.at[flip(place.s, place.half), place.pair, place.core]
-
-    tail_cross = started(links.far(tail_ref, tail_of(own), place.at(top=1)))
-    zx_copies = []
-    for t, l, c in peers:
+    def send_zx(t, l, c):
         group = flip(place.core, c) * place.half + flip(place.low, l)
-        zx_copies.append(
-            started(links.far(zx_ref.at[group], columns(own), place.at(top=t, low=l, core=c)))
-        )
-    locals_ = [
-        started(links.local(zx_ref.at[place.chunk], columns(own))),
-        started(links.local(tail_ref, tail_of(own))),
+        return zx_ref.at[group], columns(block()), place.at(top=t, low=l, core=c)
+
+    zx = {p: links.far(functools.partial(send_zx, *p)) for p in peers}
+    own = [
+        links.local(lambda: (zx_ref.at[place.chunk], columns(block()))),
+        links.local(lambda: (tail_ref, tail_of(block()))),
     ]
+    tail_cross = links.far(lambda: (tail_ref, tail_of(block()), place.at(top=1)))
     near_peers = [(l, c) for t, l, c in peers if t == 0]
-    tail_copies = [
-        started(links.far(tail_ref, tail_of(own), place.at(low=l, core=c))) for l, c in near_peers
-    ]
-    swap_segments = started(links.far(seg_ref, seg_out, place.at(core=1)))
+
+    def send_tail(l, c):
+        return tail_ref, tail_of(block()), place.at(low=l, core=c)
+
+    def send_other(l, c):
+        return tail_of(block(1)), tail_of(block(1)), place.at(low=l, core=c)
+
+    tails = {p: links.far(functools.partial(send_tail, *p)) for p in near_peers}
+    tails_more = {p: links.far(functools.partial(send_other, *p)) for p in near_peers}
+    swap_segments = links.far(lambda: (seg_ref, seg_out, place.at(core=1)))
+
+    def send_on(t, l, c, p):
+        return block(t, l, c), block(t, l, c), place.at(pair=p)
+
+    forwards = {
+        p: [links.far(functools.partial(send_on, *p, other)) for other in others]
+        for p in [(0, 0, 0)] + peers
+    }
+
+    meet_pair(place)
+    tokens.begin()
+    tail_cross.start()
+    for copy in own:
+        copy.start()
+    for p in near_peers:
+        zx[0, *p].start()
+        tails[p].start()
+    swap_segments.start()
+    for copy in own:
+        copy.wait()
+    for copy in forwards[0, 0, 0]:
+        copy.start()
+    tail_cross.wait_recv()
+    for p in near_peers:
+        tails_more[p].start()
+    for p in near_peers:
+        zx[0, *p].wait_recv()
+        tails[p].wait_recv()
+        for copy in forwards[0, *p]:
+            copy.start()
+    for p in peers:
+        if p[0] == 1:
+            zx[p].start()
 
     tokens.arrive()
-    tokens.send_stage()
-    tail_cross.wait_recv()
-    tail_more = [
-        started(links.far(tail_of(other), tail_of(other), place.at(low=l, core=c)))
-        for l, c in near_peers
-    ]
-    for copy in locals_:
-        copy.wait()
-    cot = TokenGather(place, links, cot_ref, cot_out)
-    cot.begin()
-    tokens.finish_stage()
-
-    index = lax.rem(place.core, 2)
-    rows_own = ow_out.at[place.pair, index]
-    to_home = links.far(ow_ref, rows_own, place.at(core=1))
-    stay = links.local(ow_ref, rows_own)
-    to_near = links.far(ow_ref, rows_own, place.at(top=1))
-    to_far = links.far(ow_ref, rows_own, place.at(top=1, core=1))
-
+    tokens.send_stage(0)
+    for p in near_peers:
+        tails_more[p].wait_recv()
     stages = len(place.low_bits)
-    for _ in range(1, stages):
-        tokens.send_stage()
-
-    blocks = [(0, 0, 0)] + [p for p in peers if p[0] == 0] + [p for p in peers if p[0] == 1]
-    arrival = {p: copy for p, copy in zip(peers, zx_copies)}
-    tails = dict(zip(near_peers, tail_copies))
-    tails_more = dict(zip(near_peers, tail_more))
-    forwards = []
-    for t, l, c in blocks:
-        if (t, l, c) != (0, 0, 0):
-            arrival[t, l, c].wait_recv()
-            if t == 0:
-                tails[l, c].wait_recv()
-            elif (l, c) != (0, 0):
-                tails_more[l, c].wait_recv()
-        s, f = place.at(top=t, low=l, core=c)
-        ref = w_out.at[s, place.pair, lax.rem(f, 2)]
-        for p in pair_steps:
-            forwards.append(started(links.far(ref, ref, place.at(pair=p))))
-    for i in range(1, stages):
-        tokens.finish_stage()
-
-    cot.arrive()
-    cot.send_stage()
-
-    @pl.when(place.home)
-    def _():
-        stay.start()
-        to_near.start()
-
-    @pl.when(place.away)
-    def _():
-        to_home.start()
-        to_far.start()
-
+    far_peers = [p for p in peers if p[0] == 1]
     for i in range(stages):
-        cot.finish_stage()
+        tokens.finish_stage(i)
         if i + 1 < stages:
-            cot.send_stage()
-
-    @pl.when(place.home)
-    def _():
-        stay.wait()
-        to_home.wait_recv()
-
-    @pl.when(place.away)
-    def _():
-        to_near.wait_recv()
-        to_far.wait_recv()
-
-    out_forwards = []
-    for c in (0, 1):
-        ref = ow_out.at[place.pair, c]
-        for p in pair_steps:
-            out_forwards.append(started(links.far(ref, ref, place.at(pair=p))))
+            tokens.send_stage(i + 1)
+        at, to = (len(far_peers) * k // stages for k in (i, i + 1))
+        for p in far_peers[at:to]:
+            zx[p].wait_recv()
+            for copy in forwards[p]:
+                copy.start()
+
     tokens.finish()
-    cot.finish()
-    for copy in forwards + out_forwards:
-        copy.wait()
-    for copy in [tail_cross] + zx_copies + tail_copies + tail_more:
-        copy.wait_send()
+    for p in forwards:
+        for copy in forwards[p]:
+            copy.wait()
+    tail_cross.wait_send()
+    for group in (zx, tails, tails_more):
+        for copy in group.values():
+            copy.wait_send()
     swap_segments.wait()
 
-    @pl.when(place.home)
-    def _():
-        to_near.wait_send()
-
-    @pl.when(place.away)
-    def _():
-        to_home.wait_send()
-        to_far.wait_send()
-
 
 ANYWHERE = pl.BlockSpec(memory_space=pl.ANY)
 
 
-def entry_gather(seq, fsdp, normed, zx, tail, out_w, cotangent, segments):
+def entry_gather(seq, fsdp, normed, zx, tail, segments):
     seqs, length, depth = normed.shape
     rows = tail.shape[0]
-    tokens = jax.ShapeDtypeStruct((seqs, seq, length, depth), BF16)
-    pairs = fsdp // 2
     return pl.pallas_call(
         functools.partial(entry_kernel, seq, fsdp),
-        in_specs=[ANYWHERE] * 6,
-        out_specs=[ANYWHERE] * 5,
+        in_specs=[ANYWHERE] * 4,
+        out_specs=[ANYWHERE] * 3,
         out_shape=[
-            tokens,
-            jax.ShapeDtypeStruct((seq, pairs, 2, rows, zx.shape[2] + TAIL), BF16),
-            jax.ShapeDtypeStruct((pairs, 2) + out_w.shape, BF16),
-            tokens,
+            jax.ShapeDtypeStruct((seqs, seq, length, depth), BF16),
+            jax.ShapeDtypeStruct((seq, fsdp // 2, 2, rows, zx.shape[2] + TAIL), BF16),
             jax.ShapeDtypeStruct(segments.shape, segments.dtype),
         ],
         scratch_shapes=[
-            pltpu.SemaphoreType.DMA((512,)),
-            pltpu.SemaphoreType.DMA((512,)),
-            pltpu.SemaphoreType.DMA((16,)),
+            pltpu.SemaphoreType.DMA((256,)),
+            pltpu.SemaphoreType.DMA((256,)),
+            pltpu.SemaphoreType.DMA((8,)),
         ],
         compiler_params=pltpu.CompilerParams(collective_id=0, has_side_effects=True),
         cost_estimate=pl.CostEstimate(
             flops=0, transcendentals=0, bytes_accessed=200_000_000
         ),
         name="entry_gather",
-    )(normed, zx, tail, out_w, cotangent, segments)
+    )(normed, zx, tail, segments)
 
 
 def add_rows(out, left, right, rows=32):
@@ -757,292 +922,311 @@
 
 class TokenScatter:
     def __init__(self, place, links, src, out, own, first, later):
-        self.place, self.links = place, links
-        self.src, self.out, self.own, self.first, self.later = src, out, own, first, later
+        self.place = place
+        self.out, self.own, self.first, self.later = out, own, first, later
         self.seqs = src.shape[0]
-        self.sent = []
+        half = place.half
+
+        def give(q):
+            return links.far(
+                lambda: (
+                    src.at[q, pl.ds(half * (1 - place.core), half)], first.at[q],
+                    place.at(core=1),
+                )
+            )
+
+        def keep(q):
+            return links.local(
+                lambda: (src.at[q, pl.ds(half * place.core, half)], own.at[q])
+            )
+
+        self.cores = [give(q) for q in range(self.seqs)]
+        self.loads = [keep(q) for q in range(self.seqs)]
+        self.stages = [[] for _ in place.low_bits]
+        for q in range(self.seqs):
+            live, slot = list(range(half)), 0
+            for i, bit in enumerate(place.bits_for(q)[::-1]):
+                for low in [low for low in live if low & bit]:
+                    self.stages[i].append((self.copy(links, q, low, slot, bit), q, low ^ bit, slot))
+                    slot += 1
+                live = [low for low in live if not low & bit]
+        self.stay = links.local(lambda: (own.at[:, place.low], out))
+
+    def copy(self, links, q, low, slot, bit):
+        return links.far(
+            lambda: (
+                self.own.at[q, flip(self.place.low, low)], self.later.at[q, slot],
+                self.place.at(low=bit),
+            )
+        )
 
     def begin(self):
-        half, core = self.place.half, self.place.core
-        self.loads, self.cores = [], []
         for q in range(self.seqs):
-            give = self.src.at[q, pl.ds(half * (1 - core), half)]
-            self.cores.append(
-                started(self.links.far(give, self.first.at[q], self.place.at(core=1)))
-            )
-            keep = self.src.at[q, pl.ds(half * core, half)]
-            self.loads.append(started(self.links.local(keep, self.own.at[q])))
+            self.cores[q].start()
+            self.loads[q].start()
 
     def add_cores(self):
-        place = self.place
-        self.live = [list(range(place.half)) for _ in range(self.seqs)]
-        self.slot = [0] * self.seqs
-        self.pending = [None] * self.seqs
         for q in range(self.seqs):
             self.loads[q].wait()
             self.cores[q].wait_recv()
-            self.sent.append(self.cores[q])
-            for low in self.away_first(q, 0):
-                at = flip(place.low, low)
-                add_rows(self.own.at[q, at], self.own.at[q, at], self.first.at[q, at])
-            self.send(q, 0)
-
-    def away_first(self, q, stage):
-        return self.live[q]
-
-    def send(self, q, stage):
-        place = self.place
-        bit = place.bits_for(q)[::-1][stage]
-        give = [low for low in self.live[q] if low & bit]
-        self.live[q] = [low for low in self.live[q] if not low & bit]
-        self.pending[q] = []
-        for low in give:
-            slot = self.slot[q]
-            self.slot[q] += 1
-            copy = started(
-                self.links.far(
-                    self.own.at[q, flip(place.low, low)], self.later.at[q, slot],
-                    place.at(low=bit),
-                )
+            for low in range(self.place.half):
+                add_rows(self.own.at[q, low], self.own.at[q, low], self.first.at[q, low])
+
+    def send_stage(self, i):
+        for copy, _, _, _ in self.stages[i]:
+            copy.start()
+
+    def add_stage(self, i):
+        for copy, q, low, slot in self.stages[i]:
+            copy.wait_recv()
+            ref = self.own.at[q, flip(self.place.low, low)]
+            add_rows(ref, ref, self.later.at[q, slot])
+
+    def store(self):
+        self.stay.start()
+        self.stay.wait()
+
+    def finish(self):
+        for copy in self.cores:
+            copy.wait_send()
+        for stage in self.stages:
+            for copy, _, _, _ in stage:
+                copy.wait_send()
+
+
+class RowScatter:
+    def __init__(self, place, links, src, out, own, first):
+        self.place, self.own, self.first = place, own, first
+
+        def over(p):
+            return links.far(
+                lambda: (src.at[flip(place.pair, p)], first.at[p - 1], place.at(pair=p))
             )
-            self.pending[q].append((copy, low ^ bit, slot))
-
-    def add_stage(self, stage):
-        for q in range(self.seqs):
-            for copy, low, slot in self.pending[q]:
-                copy.wait_recv()
-                at = flip(self.place.low, low)
-                add_rows(self.own.at[q, at], self.own.at[q, at], self.later.at[q, slot])
-                self.sent.append(copy)
-            if stage + 1 < len(self.place.low_bits):
-                self.send(q, stage + 1)
-
-    def deliver(self):
-        place = self.place
-        self.last = []
-        for q in range(self.seqs):
-            ref = self.own.at[q, place.low]
-            cross = self.links.far(ref, self.out.at[q], place.at(top=1, core=1))
-            stay = self.links.local(ref, self.out.at[q])
-            self.last.append((cross, stay))
-
-            @pl.when(place.away)
-            def _():
-                cross.start()
-
-            @pl.when(place.home)
-            def _():
-                stay.start()
+
+        def far(c):
+            return links.far(
+                lambda: (own.at[flip(place.core, c)], out.at[1], place.at(top=1, core=c))
+            )
+
+        self.over = [over(p) for p in range(1, place.pairs)]
+        self.load = links.local(lambda: (src.at[place.pair], own))
+        self.far = [far(0), far(1)]
+        self.near = links.far(lambda: (own.at[1 - place.core], out.at[0], place.at(core=1)))
+        self.stay = links.local(lambda: (own.at[place.core], out.at[0]))
+
+    def begin(self):
+        self.load.start()
+        for copy in self.over:
+            copy.start()
+
+    def add_pairs(self):
+        self.load.wait()
+        for i, copy in enumerate(self.over):
+            copy.wait_recv()
+            for c in (0, 1):
+                add_rows(self.own.at[c], self.own.at[c], self.first.at[i, c])
+
+        @pl.when(self.place.away)
+        def _():
+            for copy in self.far:
+                copy.start()
+
+        @pl.when(self.place.home)
+        def _():
+            self.near.start()
+            self.stay.start()
 
     def finish(self):
-        for cross, stay in self.last:
-
-            @pl.when(self.place.away)
-            def _():
-                cross.wait()
-
-            @pl.when(self.place.home)
-            def _():
-                stay.wait()
-
-        for copy in self.sent:
+        for copy in self.over:
             copy.wait_send()
+
+        @pl.when(self.place.home)
+        def _():
+            self.stay.wait()
+            self.near.wait_send()
+            self.far[0].wait_recv()
+
+        @pl.when(self.place.away)
+        def _():
+            self.near.wait_recv()
+            self.far[1].wait_recv()
+            for copy in self.far:
+                copy.wait_send()
+
+
+class Deliver:
+    def __init__(self, place, links, src, out):
+        self.place = place
+        self.cross = links.far(lambda: (src(), out, place.at(top=1, core=1)))
+        self.stay = links.local(lambda: (src(), out))
+
+    def begin(self):
+        @pl.when(self.place.away)
+        def _():
+            self.cross.start()
+
+        @pl.when(self.place.home)
+        def _():
+            self.stay.start()
+
+    def finish(self):
+        @pl.when(self.place.away)
+        def _():
+            self.cross.wait()
+
+        @pl.when(self.place.home)
+        def _():
+            self.stay.wait()
 
 
 def exit_kernel(
     seq, fsdp,
-    dh_ref, mixed_ref, part_ref, pout_ref, vec_ref,
-    dh_out, mixed_out, slots_out, rows_out, vec_out,
-    dh_own, dh_first, dh_later, mix_own, mix_first, mix_later,
-    part_own, part_first, part_top, pout_own, pout_first, vec_val, vec_got,
+    dh_ref, mixed_ref, part_ref, vec_ref,
+    dh_out, mixed_out, slots_out, vec_out,
+    dh_own, dh_first, dh_later, part_own, part_first, part_top, vec_val, vec_got,
     send, recv, near,
 ):
     place = Place(seq, fsdp)
     links = Links(send, recv, near)
-    peers = peers_of(place)
-    pair_steps = list(range(1, place.pairs))
-    near_peers = [(l, c) for t, l, c in peers if t == 0]
-    meet(
-        [place.at(top=t, low=l, core=c) for t, l, c in peers]
-        + [place.at(pair=p) for p in pair_steps]
-    )
     half = place.half
+    others = list(range(1, place.pairs))
     dh = TokenScatter(place, links, dh_ref, dh_out, dh_own, dh_first, dh_later)
-    mixed = TokenScatter(place, links, mixed_ref, mixed_out, mix_own, mix_first, mix_later)
-    dh.begin()
-
-    far_rows = pl.ds(half * (1 - place.top), half)
-    near_rows = pl.ds(half * place.top, half)
-    by_pair = {}
-    for name, rows in (("far", far_rows), ("near", near_rows)):
-        by_pair[name] = [
-            started(
-                links.far(
-                    part_ref.at[rows, flip(place.pair, p)], part_first.at[p - 1, rows],
-                    place.at(pair=p),
-                )
+    dh_last = Deliver(place, links, lambda: dh_own.at[:, place.low], dh_out)
+    mixed = Deliver(place, links, lambda: mixed_ref, mixed_out)
+
+    def rows_of(top):
+        return pl.ds(half * flip(place.top, top), half)
+
+    def over(top, p):
+        return links.far(
+            lambda: (
+                part_ref.at[rows_of(top), flip(place.pair, p)],
+                part_first.at[p - 1, rows_of(top)],
+                place.at(pair=p),
             )
-            for p in pair_steps
-        ]
-    part_load = started(links.local(part_ref.at[:, place.pair], part_own))
-    pout_pairs = [
-        started(
-            links.far(pout_ref.at[flip(place.pair, p)], pout_first.at[p - 1], place.at(pair=p))
         )
-        for p in pair_steps
-    ]
-    pout_load = started(links.local(pout_ref.at[place.pair], pout_own))
+
+    over_pairs = [[over(top, p) for p in others] for top in (0, 1)]
+    part_load = links.local(lambda: (part_ref.at[:, place.pair], part_own))
+    cross = links.far(lambda: (part_own.at[rows_of(1)], part_top, place.at(top=1)))
+
+    def row_block(l, c):
+        return part_own.at[half * place.top + flip(place.low, l), flip(place.core, c)]
+
+    def spread(l, c):
+        return links.far(
+            lambda: (
+                row_block(l, c), slots_out.at[place.core, place.low], place.at(low=l, core=c)
+            )
+        )
+
+    near_peers = [(l, c) for t, l, c in peers_of(place) if t == 0]
+    slots = {p: spread(*p) for p in near_peers}
+    slots[0, 0] = links.local(lambda: (row_block(0, 0), slots_out.at[place.core, place.low]))
 
     hops = [dict(pair=1 << i) for i in range(place.pairs.bit_length() - 1)]
     hops += [dict(top=1)] + [dict(low=b) for b in place.low_bits] + [dict(core=1)]
-    vec_load = started(links.local(vec_ref, vec_val.at[0]))
-    vec_copies = []
-
-    def vec_send():
-        i = len(vec_copies)
-        vec_copies.append(
-            started(links.far(vec_val.at[i], vec_got.at[i], place.at(**hops[i])))
-        )
-
-    def vec_add():
-        i = len(vec_copies) - 1
-        vec_copies[i].wait_recv()
-        vec_val[i + 1] = vec_val[i] + vec_got[i]
-
+
+    def hop(i):
+        return links.far(lambda: (vec_val.at[i], vec_got.at[i], place.at(**hops[i])))
+
+    vec = [hop(i) for i in range(len(hops))]
+    vec_load = links.local(lambda: (vec_ref, vec_val.at[0]))
+    vec_store = links.local(lambda: (vec_val.at[len(hops)], vec_out))
+    state = {"at": 0}
+
+    def vec_next():
+        i = state["at"]
+        state["at"] += 1
+        if i < len(hops):
+            vec[i].wait_recv()
+            vec_val[i + 1] = vec_val[i] + vec_got[i]
+            if i + 1 < len(hops):
+                vec[i + 1].start()
+            else:
+                vec_store.start()
+
+    def add_pairs(top):
+        for i, copy in enumerate(over_pairs[top]):
+            copy.wait_recv()
+            for low in range(half):
+                for c in (0, 1):
+                    ref = part_own.at[half * flip(place.top, top) + low, c]
+                    got = part_first.at[i, half * flip(place.top, top) + low, c]
+                    add_rows(ref, ref, got, 16)
+
+    meet_pair(place)
+    for copy in over_pairs[1]:
+        copy.start()
+    mixed.begin()
+    dh.begin()
+    part_load.start()
+    vec_load.start()
+    for copy in over_pairs[0]:
+        copy.start()
     vec_load.wait()
-    vec_send()
-    mixed.begin()
+    vec[0].start()
     dh.add_cores()
-    vec_add()
-    vec_send()
-    mixed.add_cores()
-
-    def add_pairs(rows_at, copies):
-        for copy in copies:
-            copy.wait_recv()
-        for p in pair_steps:
-            for i in range(half):
-                for c in (0, 1):
-                    at = rows_at + i
-                    add_rows(
-                        part_own.at[at, c], part_own.at[at, c], part_first.at[p - 1, at, c], 16
-                    )
-
+    dh.send_stage(0)
+    vec_next()
     part_load.wait()
-    add_pairs(half * (1 - place.top), by_pair["far"])
-    cross = started(links.far(part_own.at[far_rows], part_top, place.at(top=1)))
-    dh.add_stage(0)
-    vec_add()
-    vec_send()
-    mixed.add_stage(0)
-    add_pairs(half * place.top, by_pair["near"])
-
-    pout_load.wait()
-    for copy in pout_pairs:
-        copy.wait_recv()
-    for p in pair_steps:
-        for c in (0, 1):
-            add_rows(pout_own.at[c], pout_own.at[c], pout_first.at[p - 1, c])
-    row_copies = []
-    for c in (0, 1):
-        to_far = links.far(
-            pout_own.at[flip(place.core, c)], rows_out.at[1], place.at(top=1, core=c)
-        )
-        row_copies.append(to_far)
-
-        @pl.when(place.away)
-        def _():
-            to_far.start()
-
-    row_home = links.far(pout_own.at[1 - place.core], rows_out.at[0], place.at(core=1))
-    row_stay = links.local(pout_own.at[place.core], rows_out.at[0])
-
-    @pl.when(place.home)
-    def _():
-        row_home.start()
-        row_stay.start()
-
-    for stage in range(1, len(place.low_bits)):
-        dh.add_stage(stage)
-    dh.deliver()
-    vec_add()
-    vec_send()
-    for stage in range(1, len(place.low_bits)):
-        mixed.add_stage(stage)
-    mixed.deliver()
-
+    add_pairs(1)
+    cross.start()
+    stages = len(place.low_bits)
+    for i in range(stages):
+        dh.add_stage(i)
+        if i + 1 < stages:
+            dh.send_stage(i + 1)
+        else:
+            dh_last.begin()
+        vec_next()
+    add_pairs(0)
+    vec_next()
     cross.wait_recv()
-    slots = []
     for l, c in near_peers + [(0, 0)]:
-        low, core = flip(place.low, l), flip(place.core, c)
-        ref = part_own.at[half * place.top + low, core]
-        add_rows(ref, ref, part_top.at[low, core], 16)
-        slot = slots_out.at[place.core, place.low]
-        if (l, c) == (0, 0):
-            slots.append(started(links.local(ref, slot)))
-        else:
-            slots.append(started(links.far(ref, slot, place.at(low=l, core=c))))
-    while len(vec_copies) < len(hops):
-        vec_add()
-        vec_send()
-    vec_add()
-    vec_store = started(links.local(vec_val.at[len(hops)], vec_out))
-
-    for copy in slots:
+        ref = row_block(l, c)
+        add_rows(ref, ref, part_top.at[flip(place.low, l), flip(place.core, c)], 16)
+        slots[l, c].start()
+    while state["at"] < len(hops):
+        vec_next()
+    for copy in slots.values():
         copy.wait()
     vec_store.wait()
+    mixed.finish()
+    dh_last.finish()
     dh.finish()
-    mixed.finish()
     cross.wait_send()
-    for copy in by_pair["far"] + by_pair["near"] + pout_pairs + vec_copies:
+    for copy in over_pairs[0] + over_pairs[1] + vec:
         copy.wait_send()
 
-    @pl.when(place.home)
-    def _():
-        row_stay.wait()
-        row_home.wait_send()
-        row_copies[0].wait_recv()
-
-    @pl.when(place.away)
-    def _():
-        row_home.wait_recv()
-        row_copies[1].wait_recv()
-        row_copies[0].wait_send()
-        row_copies[1].wait_send()
-
-
-def exit_scatter(seq, fsdp, grad_h, mixed, part, part_out, vector):
+
+def exit_scatter(seq, fsdp, grad_h, mixed, part, vector):
     seqs, _, length, depth = grad_h.shape
     half, pairs = seq // 2, fsdp // 2
     rows, cols = part.shape[3:]
-    rows_out = part_out.shape[2]
     bits = (half.bit_length() - 1) + (pairs.bit_length() - 1) + 2
     token_own = pltpu.VMEM((seqs, half, length, depth), BF16)
-    token_later = pltpu.VMEM((seqs, max(half - 1, 1), length, depth), BF16)
     tokens = jax.ShapeDtypeStruct((seqs, length, depth), BF16)
     return pl.pallas_call(
         functools.partial(exit_kernel, seq, fsdp),
-        in_specs=[ANYWHERE] * 5,
-        out_specs=[ANYWHERE] * 5,
+        in_specs=[ANYWHERE] * 4,
+        out_specs=[ANYWHERE] * 4,
         out_shape=[
             tokens,
             tokens,
             jax.ShapeDtypeStruct((2, half, rows, cols), BF16),
-            jax.ShapeDtypeStruct((2, rows_out, depth), BF16),
             jax.ShapeDtypeStruct(vector.shape, F32),
         ],
         scratch_shapes=[
-            token_own, token_own, token_later, token_own, token_own, token_later,
+            token_own, token_own, pltpu.VMEM((seqs, max(half - 1, 1), length, depth), BF16),
             pltpu.VMEM((seq, 2, rows, cols), BF16),
             pltpu.VMEM((max(pairs - 1, 1), seq, 2, rows, cols), BF16),
             pltpu.VMEM((half, 2, rows, cols), BF16),
-            pltpu.VMEM((2, rows_out, depth), BF16),
-            pltpu.VMEM((max(pairs - 1, 1), 2, rows_out, depth), BF16),
             pltpu.VMEM((bits + 1,) + vector.shape, F32),
             pltpu.VMEM((bits,) + vector.shape, F32),
-            pltpu.SemaphoreType.DMA((128,)),
-            pltpu.SemaphoreType.DMA((128,)),
-            pltpu.SemaphoreType.DMA((32,)),
+            pltpu.SemaphoreType.DMA((96,)),
+            pltpu.SemaphoreType.DMA((96,)),
+            pltpu.SemaphoreType.DMA((16,)),
         ],
         compiler_params=pltpu.CompilerParams(
             collective_id=1, has_side_effects=True, vmem_limit_bytes=56 << 20
@@ -1051,7 +1235,7 @@
             flops=0, transcendentals=0, bytes_accessed=200_000_000
         ),
         name="exit_scatter",
-    )(grad_h, mixed, part, part_out, vector)
+    )(grad_h, mixed, part, vector)
 
 
 def local(
@@ -1075,11 +1259,8 @@
     zx = w_in[:, : 2 * INNER].reshape(rows_in, 2, steps, width).transpose(2, 0, 1, 3)
     zx = zx.reshape(steps, rows_in, 2 * width)
     tail = jnp.pad(w_in[:, 2 * INNER :], ((0, 0), (0, LANES - HEADS)))
-    h_all, w_mine, out_w, cot_all, segs = entry_gather(
-        steps, shards, normed, zx, tail, w_out, cotangent, segments
-    )
+    h_all, w_mine, segs = entry_gather(steps, shards, normed, zx, tail, segments)
     w_mine = w_mine.reshape(D, 2 * width + TAIL)
-    out_w = out_w.reshape(width, D)
     segs = jnp.where(place.home, segments, segs)
 
     total = steps * length
@@ -1117,8 +1298,10 @@
         dims = (0, 1, 2)
         return lax.dot_general(a, b, ((dims, dims), ((), ())), preferred_element_type=F32)
 
-    proj = dot(h_all, w_mine).astype(BF16)
-    y, gated, squares, states = forward_mix(proj, off_col, consts)
+    proj, y, gated, squares, states, cot_all, out_w = forward_mix(
+        h_all, w_mine, cotangent, w_out, off_col, consts, steps, shards
+    )
+    out_w = out_w.reshape(width, D)
 
     grad_yn = dot_tr(cot_all, out_w)
     sums = jnp.stack(
@@ -1133,8 +1316,10 @@
     y_normed = (gated.astype(F32) * scale).astype(BF16)
     part_out = dot_tokens(y_normed, cot_all).astype(BF16)
 
-    grad_proj, sums_x, sums_t, sums_h = backward_mix(
-        proj, off_col, off_row, rem_col, y, grad_yn, stats, states, consts
+    part_out = part_out.reshape((shards // 2, 2) + w_out.shape)
+    grad_proj, sums_x, sums_t, sums_h, mixed, rows = backward_mix(
+        proj, off_col, off_row, rem_col, y, grad_yn, stats, states, mixed, part_out, consts,
+        steps, shards,
     )
 
     grad_h = dot_tr(grad_proj, w_mine).astype(BF16)
@@ -1156,10 +1341,7 @@
     )
     everywhere = jnp.concatenate([gain_part, sums_t[: KERNEL + 1].reshape(-1)])
     vector = jnp.concatenate([grouped.reshape(-1, LANES), everywhere.reshape(-1, LANES)])
-    grad_h, mixed, slots, rows, vector = exit_scatter(
-        steps, shards, grad_h, mixed, part,
-        part_out.reshape((shards // 2, 2) + w_out.shape), vector,
-    )
+    grad_h, mixed, slots, vector = exit_scatter(steps, shards, grad_h, mixed, part, vector)
 
     mixed = (wide + mixed.astype(F32)).astype(BF16)
     w_out_grad = rows[0].astype(F32) + rows[1].astype(F32)

time: 443 us -> 409 us (0.923)
  Pallas kernels: 338 us -> 310 us
    pallas_call x2, Pallas kernels: 53 us -> 122 us  [the longest x1 69.8 us: forward_mix(): pl.pallas_call(functools.partial(forward_kernel, seq, fsdp), grid=(steps,...]
    pallas_call x1, Pallas kernels: 133 us -> 77.2 us  [entry_gather(): pl.pallas_call(functools.partial(entry_kernel, seq, fsdp), in_specs=[ANYW...]
    pallas_call x1, Pallas kernels: 153 us -> 111 us  [exit_scatter(): pl.pallas_call(functools.partial(exit_kernel, seq, fsdp), in_specs=[ANYWH...]
    dot_general x2 -> x1, matrix products: 16.7 us -> 5.23 us  [dot(): lax.dot_general(a, b, (((3,), (0,)), ((), ())), preferred_element_type=F32)]
    unnamed x58 -> x66, local copies, waits for them, and re-layouts: 8.1 us -> 1.55 us
    dot_general x2, matrix products: 15.8 us -> 22.1 us  [dot_tr(): lax.dot_general(a, b, (((3,), (1,)), ((), ())), preferred_element_type=F32)]
    dot_general x2, matrix products: 16.2 us -> 21.2 us  [dot_tokens(): lax.dot_general(a, b, ((dims, dims), ((), ())), preferred_element_type=F32)]
where the time goes in v4:
time: 409 us; the launch traced here: 406 us
  Pallas kernels  310 us (76%)
  matrix products  48.5 us (12%)
  other arithmetic  21.1 us (5%)
  local copies, waits for them, and re-layouts  20.4 us (5%)
    pallas_call x1, Pallas kernels, exit_scatter(): pl.pallas_call(functools.partial(exit_kernel, seq, fsdp), in_specs=[ANYWH...  111 us
    pallas_call x1, Pallas kernels, entry_gather(): pl.pallas_call(functools.partial(entry_kernel, seq, fsdp), in_specs=[ANYW...  77.2 us
    pallas_call x1, Pallas kernels, forward_mix(): pl.pallas_call(functools.partial(forward_kernel, seq, fsdp), grid=(steps,...  69.8 us
    pallas_call x1, Pallas kernels, backward_mix(): pl.pallas_call(functools.partial(backward_kernel, seq, fsdp), grid=(steps...  52.3 us
    dot_general x2, matrix products, dot_tr(): lax.dot_general(a, b, (((3,), (1,)), ((), ())), preferred_element_type=F32)  22.1 us
    dot_general x2, matrix products, dot_tokens(): lax.dot_general(a, b, ((dims, dims), ((), ())), preferred_element_type=F32)  21.2 us
  transfers between devices with their start and end apart: 3, of which 1 were waited for; matrix products, arithmetic and copies ran while one was open for 2% of the time, Pallas kernels for 0%

profile of v4, /device:TPU:1, one launch (start us, length us, event | category | flops | bytes accessed | tf_op | source)
XLA Modules:
  0.0 406.0 jit_solution(9175321115963472127)
XLA Ops:
  0.7 0.8 slice.123.wt_ref
  1.5 0.7 slice.124
  2.6 0.5 copy.58
  3.0 1.2 reshape.232.zx_ref
  4.2 1.1 fusion.6.h_ref
  5.4 0.6 pad.14.tail_ref
  6.0 77.2 %entry_gather.1 = (bf16[2,8,128,1536]{3,2,1,0:T(8,128)(2,1)}, bf16[8,2,2,48,1152]{4,3,2,1,0:T(8,128)(2,1)}, s32[2,1024]{1,0:T(2,128)}) custom-call(bf16[2,128,1536]{2,1,0:T(8,128)(2,1)} %fusion.6.h_ref, bf16[8,48,768]{2,1,0:T(8,128)(2,1)} %reshape.232.zx_ref, bf16[48,384]{1,0:T(8,128)(2,1)} %pad.14.tail_ref, s32[2,1024]{1,0:T(2,128)} %seg_ref.1), custom_call_target="tpu_custom_call" | custom-call | bytes 200000000 | tf_op jit(solution)/shard_map/entry_gather/pallas_call | solution.py:887
  83.2 0.7 broadcast_select_fusion
  84.1 0.8 reduce-window.14
  86.0 0.8 dynamic-slice.7
  87.2 69.8 %mix_forward.1 = (bf16[2,8,128,1152]{3,2,1,0:T(8,128)(2,1)}, bf16[2,8,128,384]{3,2,1,0:T(8,128)(2,1)S(1)}, bf16[2,8,128,384]{3,2,1,0:T(8,128)(2,1)}, f32[2,8,1,1...) custom-call(bf16[2,8,128,1536]{3,2,1,0:T(8,128)(2,1)} %get-tuple-ele, ...), custom_call_target="tpu_custom_call" | custom-call | flops 14400000000 | bytes 10000000 | tf_op jit(solution)/shard_map/mix_forward/pallas_call | solution.py:445
  157.2 8.9 %fusion = (f32[2,8,128]{2,1,0:T(8,128)S(1)}, f32[2,8,128,384]{3,2,1,0:T(8,128)}) fusion(bf16[2,8,128,384]{3,2,1,0:T(8,128)(2,1)} %get-tuple-element.39, bf16[2,8,128,1536]{3,2,1,0:T(8,128)(2,1)} %get-tuple-element.36, bf16[384,1536,1,1]{1,0,3,2:T(8,128)(2,1)S(1)} %bitcast.89), kind=kOutput, calls=%fused_computation.6 | convolution fusion | flops 2418276352 | bytes 12197888 | tf_op jit(solution)/shard_map/dot_general | solution.py:1295
  166.6 4.9 %reduce-window.16 = s32[2,8,128]{2,1,0:T(8,128)S(1)} reduce-window(s32[2,8,128]{2,1,0:T(8,128)S(1)} %get-tuple-element.67, s32[]{:T(128)} %constant.71.clone.1), window={size=1x1x128 pad=0_0x0_0x0_127}, to_apply=%region_3.4 | reduce-window | flops 260096 | bytes 16388 | tf_op jit(solution)/shard_map/reduce-window.2
  171.9 1.2 collective-permute-start.1
  173.2 1.4 collective-permute-done.1
  174.5 1.2 collective-permute-start.2
  175.7 0.7 subtract_convert_fusion.1.offr_ref
  176.8 1.1 convert_element_type.97.rem_ref
  177.9 7.1 %fusion.2 = bf16[384,1536]{1,0:T(8,128)(2,1)} fusion(bf16[2,8,128,1536]{3,2,1,0:T(8,128)(2,1)} %get-tuple-element.36, bf16[2,8,128,384]{3,2,1,0:T(8,128)(2,1)} %get-tuple-element.39, f32[2,8,128]{2,1,0:T(8,128)S(1)} %bitcast.106), kind=kOutput, calls=%fused_computation.9 | convolution fusion | flops 2418868224 | bytes 9052160 | tf_op jit(solution)/shard_map/dot_general | solution.py:1299
  185.1 5.2 %multiply_convert_fusion.mixed_ref = bf16[2,8,128,1536]{3,2,1,0:T(8,128)(2,1)} fusion(bf16[2,8,128,384]{3,2,1,0:T(8,128)(2,1)S(1)} %copy-done.30, bf16[384,1536,1,1]{1,0,3,2:T(8,128)(2,1)S(1)} %bitcast.90, f32[2,8,128]{2,1,0:T(8,128)S(1)} %bitcast.107), kind=kOutput, calls=%fused_computation | convolution fusion | flops 2422210560 | bytes 9052160 | tf_op jit(solution)/shard_map/dot_general | solution.py:1292
  190.3 0.6 pad_maximum_fusion.3.stat_ref
  190.9 52.3 %mix_backward.1 = (bf16[2,8,128,1152]{3,2,1,0:T(8,128)(2,1)}, f32[8,384]{1,0:T(8,128)}, f32[8,256]{1,0:T(8,128)}, f32[8,128]{1,0:T(8,128)}, bf16[2,128,1536]{2,1,0:T(8,128)(2,1)}, /*index=5*/bf16[2,96,1536]{2,1,0:T(8,128)(2,1)}) custom-call(bf16[2,8,128,1152]{3,2,1,0:T(8,128)(2,1)} %get-tuple-element.34.zx_ref.zxh_ref.tail_ref.tailh_ref, ...), custom_call_target="tpu_custom_call" | custom-call | flops 32000000000 | bytes 16000000 | tf_op jit(solution)/shard_map/mix_backward/pallas_call | solution.py:499
  243.2 0.8 slice_reduce_fusion.7
  244.1 0.7 reshape.244
  244.8 0.7 slice.132
  245.8 14.1 %multiply_reduce_fusion = (f32[1536]{0:T(1024)S(1)}, bf16[1536,1152]{1,0:T(8,128)(2,1)}) fusion(bf16[8,2,2,48,1152]{4,3,2,1,0:T(8,128)(2,1)} %get-tuple-element.32, bf16[2,8,128,1536]{3,2,1,0:T(8,128)(2,1)} %get-tuple-element.31.h_ref, bf16[2,8,128,1152]{3,2,1,0:T(8,128)(2,1)} %get-tuple-element.41), kind=kOutput, calls=%fused_computation.2 | convolution fusion | flops 7254833664 | bytes 18094080 | tf_op jit(solution)/shard_map/dot_general | solution.py:1299
  259.9 13.2 %convolution_convert_fusion.dh_ref = bf16[2,8,128,1536]{3,2,1,0:T(8,128)(2,1)} fusion(bf16[2,8,128,1152]{3,2,1,0:T(8,128)(2,1)} %get-tuple-element.41, bf16[1536,1152,1,1]{1,0,3,2:T(8,128)(2,1)} %bitcast.113), kind=kOutput, calls=%fused_computation.3 | convolution fusion | flops 7250903040 | bytes 14548992 | tf_op jit(solution)/shard_map/dot_general | solution.py:1295
  273.1 0.6 pad_maximum_fusion.1.vec_ref
  273.8 111.1 %exit_scatter.1 = (bf16[2,128,1536]{2,1,0:T(8,128)(2,1)}, bf16[2,128,1536]{2,1,0:T(8,128)(2,1)}, bf16[2,4,48,1152]{3,2,1,0:T(8,128)(2,1)}, f32[174,128]{1,0:T(8,128)}) custom-call(bf16[2,8,128,1536]{3,2,1,0:T(8,128)(2,1)} %convolution_convert_fusion.dh_ref, bf16[2,128,1536]{2,1,0:T(8,128)(2,1)} %get-tuple-element.42.mixed_ref, ...), custom_call_target="tpu_custom_call" | custom-call | bytes 200000000 | tf_op jit(solution)/shard_map/exit_scatter/pallas_call | solution.py:1210
  384.9 1.0 slice.138
  385.9 0.7 slice.140
  386.7 0.6 slice.159
  387.3 0.6 slice_reduce_fusion.1
  388.3 0.7 slice_reduce_fusion
  388.9 1.3 bitcast_divide_fusion
  390.2 0.6 reshape.250
  390.9 0.7 copy.42
  392.0 0.7 copy-done.13
  393.4 0.6 broadcast_multiply_fusion
  394.0 0.7 reshape.256
  394.7 1.5 slice_reduce_fusion.4
  396.1 1.3 squeeze.21
  397.4 1.3 squeeze.22
  398.7 0.6 squeeze.23
  399.3 0.6 reshape.257
  399.9 2.0 add_bitcast_fusion
  401.9 2.0 pad_maximum_fusion
  403.9 2.1 fusion.10
  (129 shorter events, 5.3 us)
Async XLA Ops:
  0.6 1.8 slice-start
  0.7 1.6 copy-start.12
  1.5 85.7 %copy-start.5 = (f32[4,256]{1,0:T(4,128)}, f32[4,256]{1,0:T(4,128)S(1)}, u32[]{:S(2)}) copy-start(f32[4,256]{1,0:T(4,128)S(1)} %slice.123.wt_ref) | copy-start | bytes 12292
  2.2 85.0 %copy-start.9 = (f32[256]{0:T(256)}, f32[256]{0:T(256)S(1)}, u32[]{:S(2)}) copy-start(f32[256]{0:T(256)S(1)} %slice.124) | copy-start | bytes 3076
  2.5 1.8 copy-start.22
  2.5 1.8 copy-start.18
  3.0 2.3 slice-start.1
  4.2 79.0 %copy-start.21 = (s32[2,1024]{1,0:T(2,128)S(1)}, s32[2,1024]{1,0:T(2,128)}, u32[]{:S(2)}) copy-start(s32[2,1024]{1,0:T(2,128)} %seg_ref.1) | copy-start | bytes 24580
  5.4 80.3 %copy-start.29 = (f32[48]{0:T(128)S(1)}, f32[48]{0:T(128)}, u32[]{:S(2)}) copy-start(f32[48]{0:T(128)} %param.20) | copy-start | bytes 580
  5.4 80.5 %slice-start.4 = ((f32[4,3328]{1,0:T(4,128)}), f32[4,3072]{1,0:T(4,128)S(1)}, s32[]{:S(2)}) async-start(f32[4,3328]{1,0:T(4,128)} %param.16), calls=%async_computation.4 | async-start | bytes 98304 | tf_op jit(solution)/shard_map/slice | solution.py:1281
  5.4 80.5 %slice-start.5 = ((f32[3328]{0:T(1024)}), f32[3072]{0:T(1024)S(1)}, s32[]{:S(2)}) async-start(f32[3328]{0:T(1024)} %param.17), calls=%async_computation.5 | async-start | bytes 24576 | tf_op jit(solution)/shard_map/slice | solution.py:1282
  5.4 81.4 %copy-start.27 = (f32[48]{0:T(128)S(1)}, f32[48]{0:T(128)}, u32[]{:S(2)}) copy-start(f32[48]{0:T(128)} %param.19) | copy-start | bytes 580
  5.4 81.4 %copy-start.28 = (f32[48]{0:T(128)S(1)}, f32[48]{0:T(128)}, u32[]{:S(2)}) copy-start(f32[48]{0:T(128)} %param.18) | copy-start | bytes 580
  85.1 2.1 copy-start.1
  85.1 2.1 copy-start.10
  85.9 71.2 %copy-start.8 = (f32[1,384]{1,0:T(1,128)}, f32[1,384]{1,0:T(1,128)S(1)}, u32[]{:S(2)}) copy-start(f32[1,384]{1,0:T(1,128)S(1)} %broadcast_in_dim_reshape.2.skip_ref) | copy-start | bytes 4612
  85.9 71.2 %copy-start.3 = (f32[4,384]{1,0:T(4,128)}, f32[4,384]{1,0:T(4,128)S(1)}, u32[]{:S(2)}) copy-start(f32[4,384]{1,0:T(4,128)S(1)} %constant_dynamic-slice_fusion.wx_ref) | copy-start | bytes 18436
  86.0 71.1 %copy-start.6 = (f32[1,384]{1,0:T(1,128)}, f32[1,384]{1,0:T(1,128)S(1)}, u32[]{:S(2)}) copy-start(f32[1,384]{1,0:T(1,128)S(1)} %dynamic_slice.19.bx_ref) | copy-start | bytes 4612
  86.8 70.3 %copy-start.7 = (f32[1,384]{1,0:T(1,128)}, f32[1,384]{1,0:T(1,128)S(1)}, u32[]{:S(2)}) copy-start(f32[1,384]{1,0:T(1,128)S(1)} %dynamic_slice.23.gain_ref) | copy-start | bytes 4612
  86.9 70.3 %copy-start.4 = (f32[8,128]{1,0:T(8,128)}, f32[8,128]{1,0:T(8,128)S(1)}, u32[]{:S(2)}) copy-start(f32[8,128]{1,0:T(8,128)S(1)} %select_maximum_fusion.hp_ref) | copy-start | bytes 12292
  86.9 70.2 %copy-start.2 = (bf16[128,128]{1,0:T(8,128)(2,1)}, bf16[128,128]{1,0:T(8,128)(2,1)S(1)}, u32[]{:S(2)}) copy-start(bf16[128,128]{1,0:T(8,128)(2,1)S(1)} %fusion.16.pick_ref) | copy-start | bytes 98308
  87.2 70.0 %copy-start = (f32[2,8,128,1]{3,2,1,0:T(8,128)}, f32[2,8,128,1]{3,2,1,0:T(8,128)S(1)}, u32[]{:S(2)}) copy-start(f32[2,8,128,1]{3,2,1,0:T(8,128)S(1)} %subtract_convert_fusion.off_ref) | copy-start | bytes 24580
  157.2 8.9 %copy-start.11 = (bf16[2,8,128,384]{3,2,1,0:T(8,128)(2,1)}, bf16[2,8,128,384]{3,2,1,0:T(8,128)(2,1)S(1)}, u32[]{:S(2)}) copy-start(bf16[2,8,128,384]{3,2,1,0:T(8,128)(2,1)S(1)} %get-tuple-element.35.y_ref) | copy-start | bytes 4718596
  166.1 5.7 %collective-permute-start = (f32[2,8,2,128]{3,2,1,0:T(2,128)S(1)}, f32[2,8,2,128]{3,2,1,0:T(2,128)S(1)}, u32[]{:S(2)}, u32[]{:S(2)}) collective-permute-start(f32[2,8,2,128]{3,2,1,0:T(2,128)S(1)} %pad_maximum_fusion.2), channel_id=1, source_target_pairs={{0,1},{1,0},{2,3},{3,2},{4,5},{5,4},{6,7},{7,6},{8,9},{9,8},{10,11... | collective-permute-start | bytes 49160 | tf_op jit(solution)/shard_map/ppermute | solution.py:1381
  171.9 2.7 collective-permute-start.1
  174.5 3.3 collective-permute-start.2
  177.9 7.1 %copy-start.30 = (bf16[2,8,128,384]{3,2,1,0:T(8,128)(2,1)S(1)}, bf16[2,8,128,384]{3,2,1,0:T(8,128)(2,1)}, u32[]{:S(2)}) copy-start(bf16[2,8,128,384]{3,2,1,0:T(8,128)(2,1)} %get-tuple-element.39) | copy-start | bytes 4718596
  245.8 14.1 %copy-start.25 = (f32[8,256]{1,0:T(8,128)S(1)}, f32[8,256]{1,0:T(8,128)}, u32[]{:S(2)}) copy-start(f32[8,256]{1,0:T(8,128)} %get-tuple-element.45) | copy-start | bytes 24580
  384.9 3.1 copy-start.15
  386.6 2.3 copy-start.17
  391.6 1.1 copy-start.13
  391.6 1.4 copy-start.14
  391.6 1.4 copy-start.19
  391.6 1.3 copy-start.23
  391.6 2.4 slice-start.2
  391.6 7.6 %slice-start.3 = ((f32[8,2432]{1,0:T(8,128)}), f32[8,384]{1,0:T(8,128)S(1)}, s32[]{:S(2)}) async-start(f32[8,2432]{1,0:T(8,128)} %copy-done.17), calls=%async_computation.3 | async-start | bytes 24576 | tf_op jit(solution)/shard_map/slice | solution.py:1368
  399.9 4.0 copy-start.16
  399.9 4.0 copy-start.20
  399.9 4.0 copy-start.24
  399.9 4.0 copy-start.26

commit v5 on v4

--- a/solution.py
+++ b/solution.py
@@ -153,7 +153,6 @@
     cot = TokenGather(place, links, cot_ref, cot_out)
     w_rows = RowGather(place, links, ow_ref, ow_out)
     stages = len(place.low_bits)
-    arrive_at = max(seq // 2 - 1, 1)
 
     @pl.when(step_at == 0)
     def _():
@@ -166,10 +165,20 @@
     def _():
         w_rows.begin()
 
-    @pl.when(step_at == arrive_at)
+    last = pl.num_programs(0) - 1
+    for i in range(stages):
+
+        @pl.when(step_at == min(2 + 2 * i, seq - 2))
+        def _():
+            cot.pass_on(i, "home")
+
+    @pl.when(step_at == last - 3)
     def _():
         cot.arrive()
-        cot.send_stage(0)
+
+    @pl.when(step_at == last - 1)
+    def _():
+        cot.pass_on(0, "away")
 
     proj = jnp.dot(
         h_ref[...].reshape(seqs * length, depth), w_ref[...], preferred_element_type=F32
@@ -221,16 +230,14 @@
         memory[q] = old * entry_x[length - 1 : length, :] + fresh
         last_rows[q] = chunk_rows[length - HALO :]
 
-    @pl.when(step_at == pl.num_programs(0) - 2)
+    @pl.when(step_at == last - 1)
     def _():
         w_rows.forward()
 
-    @pl.when(step_at == pl.num_programs(0) - 1)
+    @pl.when(step_at == last)
     def _():
-        for stage in range(stages):
-            cot.finish_stage(stage)
-            if stage + 1 < stages:
-                cot.send_stage(stage + 1)
+        for i in range(1, stages):
+            cot.pass_on(i, "away")
         w_rows.finish()
         cot.finish()
 
@@ -640,9 +647,13 @@
     def __init__(self, place, links, src, dst):
         self.place, self.src, self.dst = place, src, dst
         seqs = src.shape[0]
-        self.cross = links.far(
-            lambda: (src, dst.at[:, place.s], place.at(top=1, core=1))
-        )
+
+        def over(q):
+            return links.far(
+                lambda: (src.at[q], dst.at[q, place.s], place.at(top=1, core=1))
+            )
+
+        self.cross = [over(q) for q in range(seqs)]
         self.stay = links.local(lambda: (src, dst.at[:, place.s]))
         self.share = [[] for _ in range(seqs)]
         self.stages = []
@@ -670,36 +681,36 @@
     def begin(self):
         @pl.when(self.place.away)
         def _():
-            self.cross.start()
+            for copy in self.cross:
+                copy.start()
 
         @pl.when(self.place.home)
         def _():
             self.stay.start()
+            self.stay.wait()
+            self.send_stage(0)
 
     def arrive(self):
         @pl.when(self.place.away)
         def _():
-            self.cross.wait_recv()
-
-        @pl.when(self.place.home)
-        def _():
-            self.stay.wait()
+            for copy in self.cross:
+                copy.wait_recv()
+            self.send_stage(0)
 
     def send_stage(self, i):
-        for copies in self.stages[i]:
-            for copy in copies:
+        for q in range(len(self.share)):
+            for copy in self.stages[i][q] + self.share[q][i]:
                 copy.start()
-        for share in self.share:
-            for copy in share[i]:
-                copy.start()
-
-    def finish_stage(self, i):
-        for copies in self.stages[i]:
-            for copy in copies:
-                copy.wait_recv()
-        if i + 1 == len(self.stages):
-            for share in self.share:
-                for copy in share[i + 1]:
+
+    def pass_on(self, i, role):
+        @pl.when(self.place.home if role == "home" else self.place.away)
+        def _():
+            for q in range(len(self.share)):
+                for copy in self.stages[i][q]:
+                    copy.wait_recv()
+                for copy in (self.stages[i + 1][q] if i + 1 < len(self.stages) else []):
+                    copy.start()
+                for copy in self.share[q][i + 1]:
                     copy.start()
 
     def finish(self):
@@ -714,7 +725,8 @@
 
         @pl.when(self.place.away)
         def _():
-            self.cross.wait_send()
+            for copy in self.cross:
+                copy.wait_send()
 
 
 class RowGather:
@@ -827,6 +839,8 @@
     }
 
     meet_pair(place)
+    stages = len(place.low_bits)
+    far_peers = [p for p in peers if p[0] == 1]
     tokens.begin()
     tail_cross.start()
     for copy in own:
@@ -842,25 +856,22 @@
     tail_cross.wait_recv()
     for p in near_peers:
         tails_more[p].start()
+    tokens.pass_on(0, "home")
     for p in near_peers:
         zx[0, *p].wait_recv()
         tails[p].wait_recv()
         for copy in forwards[0, *p]:
             copy.start()
-    for p in peers:
-        if p[0] == 1:
-            zx[p].start()
+    for p in far_peers:
+        zx[p].start()
+    for i in range(1, stages):
+        tokens.pass_on(i, "home")
 
     tokens.arrive()
-    tokens.send_stage(0)
     for p in near_peers:
         tails_more[p].wait_recv()
-    stages = len(place.low_bits)
-    far_peers = [p for p in peers if p[0] == 1]
     for i in range(stages):
-        tokens.finish_stage(i)
-        if i + 1 < stages:
-            tokens.send_stage(i + 1)
+        tokens.pass_on(i, "away")
         at, to = (len(far_peers) * k // stages for k in (i, i + 1))
         for p in far_peers[at:to]:
             zx[p].wait_recv()
@@ -921,19 +932,18 @@
 
 
 class TokenScatter:
-    def __init__(self, place, links, src, out, own, first, later):
+    def __init__(self, place, links, src, out, own, first, later, loads=True):
         self.place = place
         self.out, self.own, self.first, self.later = out, own, first, later
         self.seqs = src.shape[0]
         half = place.half
 
         def give(q):
-            return links.far(
-                lambda: (
-                    src.at[q, pl.ds(half * (1 - place.core), half)], first.at[q],
-                    place.at(core=1),
-                )
-            )
+            def make():
+                part = src.at[q, pl.ds(half * (1 - place.core), half)] if loads else src.at[q]
+                return part, first.at[q], place.at(core=1)
+
+            return links.far(make)
 
         def keep(q):
             return links.local(
@@ -941,7 +951,7 @@
             )
 
         self.cores = [give(q) for q in range(self.seqs)]
-        self.loads = [keep(q) for q in range(self.seqs)]
+        self.loads = [keep(q) for q in range(self.seqs)] if loads else []
         self.stages = [[] for _ in place.low_bits]
         for q in range(self.seqs):
             live, slot = list(range(half)), 0
@@ -961,13 +971,13 @@
         )
 
     def begin(self):
-        for q in range(self.seqs):
-            self.cores[q].start()
-            self.loads[q].start()
+        for copy in self.cores + self.loads:
+            copy.start()
 
     def add_cores(self):
         for q in range(self.seqs):
-            self.loads[q].wait()
+            if self.loads:
+                self.loads[q].wait()
             self.cores[q].wait_recv()
             for low in range(self.place.half):
                 add_rows(self.own.at[q, low], self.own.at[q, low], self.first.at[q, low])
@@ -1079,20 +1089,34 @@
             self.stay.wait()
 
 
+TILE = 384
+ROWS = 256
+
+
 def exit_kernel(
     seq, fsdp,
-    dh_ref, mixed_ref, part_ref, vec_ref,
+    h_ref, grad_ref, w_ref, mixed_ref, vec_ref,
     dh_out, mixed_out, slots_out, vec_out,
-    dh_own, dh_first, dh_later, part_own, part_first, part_top, vec_val, vec_got,
+    h_all, grads, weights, part,
+    dh_give, dh_own, dh_first, dh_later, part_first, part_top, vec_val, vec_got,
     send, recv, near,
 ):
     place = Place(seq, fsdp)
     links = Links(send, recv, near)
     half = place.half
     others = list(range(1, place.pairs))
-    dh = TokenScatter(place, links, dh_ref, dh_out, dh_own, dh_first, dh_later)
+    seqs, _, length, depth = dh_own.shape
+    rows = part.shape[3]
+    dh = TokenScatter(
+        place, links, dh_give, dh_out, dh_own, dh_first, dh_later, loads=False
+    )
     dh_last = Deliver(place, links, lambda: dh_own.at[:, place.low], dh_out)
     mixed = Deliver(place, links, lambda: mixed_ref, mixed_out)
+    loads = [
+        links.local(lambda: (h_ref, h_all)),
+        links.local(lambda: (grad_ref, grads)),
+        links.local(lambda: (w_ref, weights)),
+    ]
 
     def rows_of(top):
         return pl.ds(half * flip(place.top, top), half)
@@ -1100,18 +1124,19 @@
     def over(top, p):
         return links.far(
             lambda: (
-                part_ref.at[rows_of(top), flip(place.pair, p)],
+                part.at[rows_of(top), flip(place.pair, p)],
                 part_first.at[p - 1, rows_of(top)],
                 place.at(pair=p),
             )
         )
 
     over_pairs = [[over(top, p) for p in others] for top in (0, 1)]
-    part_load = links.local(lambda: (part_ref.at[:, place.pair], part_own))
-    cross = links.far(lambda: (part_own.at[rows_of(1)], part_top, place.at(top=1)))
+    cross = links.far(lambda: (part.at[rows_of(1), place.pair], part_top, place.at(top=1)))
 
     def row_block(l, c):
-        return part_own.at[half * place.top + flip(place.low, l), flip(place.core, c)]
+        return part.at[
+            half * place.top + flip(place.low, l), place.pair, flip(place.core, c)
+        ]
 
     def spread(l, c):
         return links.far(
@@ -1151,27 +1176,66 @@
             copy.wait_recv()
             for low in range(half):
                 for c in (0, 1):
-                    ref = part_own.at[half * flip(place.top, top) + low, c]
-                    got = part_first.at[i, half * flip(place.top, top) + low, c]
-                    add_rows(ref, ref, got, 16)
-
+                    at = half * flip(place.top, top) + low
+                    ref = part.at[at, place.pair, c]
+                    add_rows(ref, ref, part_first.at[i, at, c], 16)
+
+    tiles = depth // 2 // TILE
+    blocks = TILE // rows
+    per_seq = fsdp
+
+    def weight_rows(top):
+        @pl.loop(0, tiles)
+        def _(k):
+            t = tiles * flip(place.top, top) + k
+            lanes = pl.ds(pl.multiple_of(t * TILE, LANES), TILE)
+            term = tr_mm(h_all[:, lanes], grads[...])
+            for b in range(blocks):
+                at = t * (blocks // per_seq) + b // per_seq if blocks >= per_seq else None
+                part[at, b % per_seq // 2, b % 2] = term[b * rows : (b + 1) * rows].astype(BF16)
+            sums = jnp.sum(term * weights[lanes, :].astype(F32), axis=1, keepdims=True)
+            wide = jnp.broadcast_to(sums, (TILE, LANES))
+            for i in range(TILE // LANES):
+                vec_val[0, pl.ds(t * (TILE // LANES) + i, 1), :] = (
+                    wide[i * LANES : (i + 1) * LANES].T[0:1, :]
+                )
+
+    def token_rows(out, side):
+        per_chunk = ROWS // length
+        count = half // per_chunk
+        for q in range(seqs):
+
+            @pl.loop(0, count)
+            def _(k):
+                at = (q * seq + half * side + k * per_chunk) * length
+                term = mm_tr(grads[pl.ds(pl.multiple_of(at, LANES), ROWS), :], weights[...])
+                out[q, pl.ds(k * per_chunk, per_chunk)] = term.astype(BF16).reshape(
+                    per_chunk, length, depth
+                )
+
+    for copy in loads:
+        copy.start()
+    vec_load.start()
     meet_pair(place)
+    mixed.begin()
+    for copy in loads:
+        copy.wait()
+    vec_load.wait()
+    weight_rows(1)
     for copy in over_pairs[1]:
         copy.start()
-    mixed.begin()
+    token_rows(dh_give, 1 - place.core)
     dh.begin()
-    part_load.start()
-    vec_load.start()
+    weight_rows(0)
     for copy in over_pairs[0]:
         copy.start()
-    vec_load.wait()
     vec[0].start()
+    token_rows(dh_own, place.core)
     dh.add_cores()
     dh.send_stage(0)
-    vec_next()
-    part_load.wait()
     add_pairs(1)
     cross.start()
+    vec_next()
     stages = len(place.low_bits)
     for i in range(stages):
         dh.add_stage(i)
@@ -1200,16 +1264,18 @@
         copy.wait_send()
 
 
-def exit_scatter(seq, fsdp, grad_h, mixed, part, vector):
-    seqs, _, length, depth = grad_h.shape
+def exit_scatter(seq, fsdp, h_all, grad_proj, w_mine, mixed, vector):
+    seqs, _, length, depth = h_all.shape
     half, pairs = seq // 2, fsdp // 2
-    rows, cols = part.shape[3:]
+    cols = w_mine.shape[1]
+    rows = depth // (seq * fsdp)
+    count = seqs * seq * length
     bits = (half.bit_length() - 1) + (pairs.bit_length() - 1) + 2
     token_own = pltpu.VMEM((seqs, half, length, depth), BF16)
     tokens = jax.ShapeDtypeStruct((seqs, length, depth), BF16)
     return pl.pallas_call(
         functools.partial(exit_kernel, seq, fsdp),
-        in_specs=[ANYWHERE] * 4,
+        in_specs=[ANYWHERE] * 5,
         out_specs=[ANYWHERE] * 4,
         out_shape=[
             tokens,
@@ -1218,8 +1284,12 @@
             jax.ShapeDtypeStruct(vector.shape, F32),
         ],
         scratch_shapes=[
-            token_own, token_own, pltpu.VMEM((seqs, max(half - 1, 1), length, depth), BF16),
-            pltpu.VMEM((seq, 2, rows, cols), BF16),
+            pltpu.VMEM((count, depth), BF16),
+            pltpu.VMEM((count, cols), BF16),
+            pltpu.VMEM((depth, cols), BF16),
+            pltpu.VMEM((seq, pairs, 2, rows, cols), BF16),
+            token_own, token_own, token_own,
+            pltpu.VMEM((seqs, max(half - 1, 1), length, depth), BF16),
             pltpu.VMEM((max(pairs - 1, 1), seq, 2, rows, cols), BF16),
             pltpu.VMEM((half, 2, rows, cols), BF16),
             pltpu.VMEM((bits + 1,) + vector.shape, F32),
@@ -1229,13 +1299,54 @@
             pltpu.SemaphoreType.DMA((16,)),
         ],
         compiler_params=pltpu.CompilerParams(
-            collective_id=1, has_side_effects=True, vmem_limit_bytes=56 << 20
+            collective_id=1, has_side_effects=True, vmem_limit_bytes=60 << 20
         ),
         cost_estimate=pl.CostEstimate(
             flops=0, transcendentals=0, bytes_accessed=200_000_000
         ),
         name="exit_scatter",
-    )(grad_h, mixed, part, vector)
+    )(h_all.reshape(count, depth), grad_proj.reshape(count, cols), w_mine, mixed, vector)
+
+
+def finish_kernel(
+    tok_ref, cot_ref, gain_ref, dh_ref, mixed_ref, slots_ref, rows_ref,
+    mixed_out, tokens_out, w_in_out, w_out_out,
+):
+    gain = gain_ref[...]
+    for q in range(tok_ref.shape[0]):
+        wide = tok_ref[q].astype(F32)
+        mixed_out[q] = (wide + mixed_ref[q].astype(F32)).astype(BF16)
+        scale = lax.rsqrt(jnp.mean(wide * wide, axis=-1, keepdims=True) + EPSILON)
+        unit = wide * scale
+        scaled = dh_ref[q].astype(F32) * gain
+        tokens_out[q] = cot_ref[q].astype(F32) + scale * (
+            scaled - unit * jnp.mean(scaled * unit, axis=-1, keepdims=True)
+        )
+    groups, _, cols = slots_ref.shape
+    width = (cols - TAIL) // 2
+    tail = jnp.zeros((slots_ref.shape[1], TAIL), F32)
+    for g in range(groups):
+        w_in_out[:, g * width : (g + 1) * width] = slots_ref[g, :, :width].astype(F32)
+        w_in_out[:, INNER + g * width : INNER + (g + 1) * width] = (
+            slots_ref[g, :, width : 2 * width].astype(F32)
+        )
+        tail = tail + slots_ref[g, :, 2 * width :].astype(F32)
+    w_in_out[:, 2 * INNER :] = tail[:, : 2 * STATE + HEADS]
+    w_out_out[...] = rows_ref[0].astype(F32) + rows_ref[1].astype(F32)
+
+
+def finish(tokens, cotangent, gain_in, grad_h, mixed, slots, rows, shapes):
+    return pl.pallas_call(
+        finish_kernel,
+        out_shape=[
+            jax.ShapeDtypeStruct(tokens.shape, BF16),
+            jax.ShapeDtypeStruct(tokens.shape, F32),
+            jax.ShapeDtypeStruct(shapes[0], F32),
+            jax.ShapeDtypeStruct(shapes[1], F32),
+        ],
+        compiler_params=pltpu.CompilerParams(vmem_limit_bytes=32 << 20),
+        name="finish",
+    )(tokens, cotangent, gain_in[None], grad_h, mixed, slots, rows)
 
 
 def local(
@@ -1322,10 +1433,6 @@
         steps, shards,
     )
 
-    grad_h = dot_tr(grad_proj, w_mine).astype(BF16)
-    part = dot_tokens(h_all, grad_proj)
-    gain_part = jnp.sum(part * w_mine.astype(F32), axis=1)
-    part = part.astype(BF16).reshape(steps, shards // 2, 2, rows_in, 2 * width + TAIL)
     grouped = jnp.concatenate(
         [
             sums_x[: KERNEL + 1].reshape(-1),
@@ -1339,27 +1446,24 @@
     grouped = lax.dynamic_update_slice_in_dim(
         jnp.zeros((steps,) + grouped.shape[1:], F32), grouped, number, 0
     )
-    everywhere = jnp.concatenate([gain_part, sums_t[: KERNEL + 1].reshape(-1)])
-    vector = jnp.concatenate([grouped.reshape(-1, LANES), everywhere.reshape(-1, LANES)])
-    grad_h, mixed, slots, vector = exit_scatter(steps, shards, grad_h, mixed, part, vector)
-
-    mixed = (wide + mixed.astype(F32)).astype(BF16)
-    w_out_grad = rows[0].astype(F32) + rows[1].astype(F32)
-    slots = slots.reshape(steps, rows_in, 2 * width + TAIL).astype(F32)
-    zx_grad = slots[:, :, : 2 * width].reshape(steps, rows_in, 2, width).transpose(1, 2, 0, 3)
-    tail_grad = jnp.sum(slots[:, :, 2 * width : 2 * width + 2 * STATE + HEADS], axis=0)
-    w_in_grad = jnp.concatenate([zx_grad.reshape(rows_in, 2 * INNER), tail_grad], axis=1)
-
-    grad_h = grad_h.astype(F32)
-    scaled = grad_h * gain_in
-    unit = wide * scale_in
-    tokens_grad = cotangent.astype(F32) + scale_in * (
-        scaled - unit * jnp.mean(scaled * unit, axis=-1, keepdims=True)
-    )
-
-    edge = steps * size // LANES
-    everywhere = vector[edge:].reshape(-1)
-    grouped = vector[:edge].reshape(steps, size)
+    vector = jnp.concatenate(
+        [
+            jnp.zeros((D // LANES, LANES), F32),
+            sums_t[: KERNEL + 1].reshape(-1, LANES),
+            grouped.reshape(-1, LANES),
+        ]
+    )
+    grad_h, mixed, slots, vector = exit_scatter(
+        steps, shards, h_all, grad_proj, w_mine, mixed, vector
+    )
+    mixed, tokens_grad, w_in_grad, w_out_grad = finish(
+        tokens, cotangent, gain_in, grad_h, mixed,
+        slots.reshape(steps, rows_in, 2 * width + TAIL), rows, (w_in.shape, w_out.shape),
+    )
+
+    edge = vector.shape[0] - steps * size // LANES
+    everywhere = vector[:edge].reshape(-1)
+    grouped = vector[edge:].reshape(steps, size)
     gain_in_grad = everywhere[:D] / gain_in
     conv_x = grouped[:, : (KERNEL + 1) * width].reshape(steps, KERNEL + 1, width)
     conv_x = conv_x.transpose(1, 0, 2).reshape(KERNEL + 1, INNER)

time: 409 us -> 370 us (0.905)
  matrix products: 48.5 us -> 21.8 us
  other arithmetic: 21.1 us -> 13.3 us
  Pallas kernels: 310 us -> 304 us
    pallas_call x1, Pallas kernels: 77.2 us -> 95.9 us  [entry_gather(): pl.pallas_call(functools.partial(entry_kernel, seq, fsdp), in_specs=[ANYW...]
    pallas_call x1, Pallas kernels: 111 us -> 96.2 us  [exit_scatter(): pl.pallas_call(functools.partial(exit_kernel, seq, fsdp), in_specs=[ANYWH...]
    dot_general x2 -> x1, matrix products: 21.2 us -> 7.14 us  [dot_tokens(): lax.dot_general(a, b, ((dims, dims), ((), ())), preferred_element_type=F32)]
    pallas_call x1, Pallas kernels: 69.8 us -> 55.9 us  [forward_mix(): pl.pallas_call(functools.partial(forward_kernel, seq, fsdp), grid=(steps,...]
    dot_general x2 -> x1, matrix products: 22.1 us -> 9.38 us  [dot_tr(): lax.dot_general(a, b, (((3,), (1,)), ((), ())), preferred_element_type=F32)]
    add x2 -> x0, other arithmetic: 4.1 us -> none  [the longest x1 2.09 us: local(): cotangent.astype(F32)]
where the time goes in v5:
time: 370 us; the launch traced here: 365 us
  Pallas kernels  304 us (82%)
  matrix products  21.8 us (6%)
  local copies, waits for them, and re-layouts  17.2 us (5%)
  other arithmetic  13.3 us (4%)
  starting transfers between devices  5.76 us (2%)
    pallas_call x1, Pallas kernels, exit_scatter(): pl.pallas_call(functools.partial(exit_kernel, seq, fsdp), in_specs=[ANYWH...  96.2 us
    pallas_call x1, Pallas kernels, entry_gather(): pl.pallas_call(functools.partial(entry_kernel, seq, fsdp), in_specs=[ANYW...  95.9 us
    pallas_call x1, Pallas kernels, forward_mix(): pl.pallas_call(functools.partial(forward_kernel, seq, fsdp), grid=(steps,...  55.9 us
    pallas_call x1, Pallas kernels, backward_mix(): pl.pallas_call(functools.partial(backward_kernel, seq, fsdp), grid=(steps...  53 us
    dot_general x1, matrix products, dot_tr(): lax.dot_general(a, b, (((3,), (1,)), ((), ())), preferred_element_type=F32)  9.38 us
  transfers between devices with their start and end apart: 3, of which 1 were waited for; matrix products, arithmetic and copies ran while one was open for 2% of the time, Pallas kernels for 0%

profile of v5, /device:TPU:1, one launch (start us, length us, event | category | flops | bytes accessed | tf_op | source)
XLA Modules:
  0.0 364.8 jit_solution(5054088626987627110)
XLA Ops:
  0.7 0.7 slice.111.wt_ref
  1.5 0.7 slice.112
  2.2 0.5 copy.48
  2.7 1.2 reshape.219.zx_ref
  3.9 0.2 fusion.3
  4.2 1.1 fusion.5.h_ref
  5.3 0.6 pad.14.tail_ref
  6.0 95.9 %entry_gather.1 = (bf16[2,8,128,1536]{3,2,1,0:T(8,128)(2,1)}, bf16[8,2,2,48,1152]{4,3,2,1,0:T(8,128)(2,1)}, s32[2,1024]{1,0:T(2,128)}) custom-call(bf16[2,128,1536]{2,1,0:T(8,128)(2,1)} %fusion.5.h_ref, bf16[8,48,768]{2,1,0:T(8,128)(2,1)} %reshape.219.zx_ref, bf16[48,384]{1,0:T(8,128)(2,1)} %pad.14.tail_ref, s32[2,1024]{1,0:T(2,128)} %seg_ref.1), custom_call_target="tpu_custom_call" | custom-call | bytes 200000000 | tf_op jit(solution)/shard_map/entry_gather/pallas_call | solution.py:898
  101.9 0.7 broadcast_select_fusion
  102.8 0.8 reduce-window.14
  103.5 0.2 slice_reduce_fusion.2
  103.8 0.4 copy.30
  104.1 0.2 reduce-window.15
  104.7 0.8 dynamic-slice.7
  105.6 0.3 subtract_convert_fusion.off_ref
  105.9 55.9 %mix_forward.1 = (bf16[2,8,128,1152]{3,2,1,0:T(8,128)(2,1)}, bf16[2,8,128,384]{3,2,1,0:T(8,128)(2,1)S(1)}, bf16[2,8,128,384]{3,2,1,0:T(8,128)(2,1)}, f32[2,8,1,1...) custom-call(bf16[2,8,128,1536]{3,2,1,0:T(8,128)(2,1)} %get-tuple-ele, ...), custom_call_target="tpu_custom_call" | custom-call | flops 14400000000 | bytes 10000000 | tf_op jit(solution)/shard_map/mix_forward/pallas_call | solution.py:452
  162.0 9.4 %fusion = (f32[2,8,128]{2,1,0:T(8,128)S(1)}, f32[2,8,128,384]{3,2,1,0:T(8,128)}) fusion(bf16[2,8,128,384]{3,2,1,0:T(8,128)(2,1)} %get-tuple-element.43, bf16[2,8,128,1536]{3,2,1,0:T(8,128)(2,1)} %get-tuple-element.40, bf16[384,1536,1,1]{1,0,3,2:T(8,128)(2,1)S(1)} %bitcast.68), kind=kOutput, calls=%fused_computation.3 | convolution fusion | flops 2418276352 | bytes 12197888 | tf_op jit(solution)/shard_map/dot_general | solution.py:1406
  171.4 0.4 collective-permute-start
  171.8 4.9 %reduce-window.16 = s32[2,8,128]{2,1,0:T(8,128)S(1)} reduce-window(s32[2,8,128]{2,1,0:T(8,128)S(1)} %get-tuple-element.70, s32[]{:T(128)} %constant.71.clone.1), window={size=1x1x128 pad=0_0x0_0x0_127}, to_apply=%region_3.4 | reduce-window | flops 260096 | bytes 16388 | tf_op jit(solution)/shard_map/reduce-window.2
  176.8 0.2 reduce-window.19
  177.1 1.0 collective-permute-start.1
  178.2 1.6 collective-permute-done.1
  179.8 4.3 %collective-permute-start.2 = (f32[2,8,2,128]{3,2,1,0:T(2,128)S(1)}, f32[2,8,2,128]{3,2,1,0:T(2,128)S(1)}, u32[]{:S(2)}, u32[]{:S(2)}) collective-permute-start(f32[2,8,2,128]{3,2,1,0:T(2,128)S(1)} %fusion.23), channel_id=1, source_target_pairs={{0,8},{1,9},{2,10},{3,11},{4,12},{5,13},{6,14},{7,15},{8,0},{9,1},... | collective-permute-start | bytes 49160 | tf_op jit(solution)/shard_map/ppermute | solution.py:1485
  184.1 0.7 subtract_convert_fusion.1.offr_ref
  184.8 0.4 copy.33
  185.2 1.1 convert_element_type.62.rem_ref
  186.4 7.1 %fusion.2 = bf16[384,1536]{1,0:T(8,128)(2,1)} fusion(bf16[2,8,128,1536]{3,2,1,0:T(8,128)(2,1)} %get-tuple-element.40, bf16[2,8,128,384]{3,2,1,0:T(8,128)(2,1)} %get-tuple-element.43, f32[2,8,128]{2,1,0:T(8,128)S(1)} %bitcast.86), kind=kOutput, calls=%fused_computation.6 | convolution fusion | flops 2418868224 | bytes 9052160 | tf_op jit(solution)/shard_map/dot_general | solution.py:1410
  193.5 5.3 %multiply_convert_fusion.mixed_ref = bf16[2,8,128,1536]{3,2,1,0:T(8,128)(2,1)} fusion(bf16[2,8,128,384]{3,2,1,0:T(8,128)(2,1)S(1)} %copy-done.24, bf16[384,1536,1,1]{1,0,3,2:T(8,128)(2,1)S(1)} %bitcast.69, f32[2,8,128]{2,1,0:T(8,128)S(1)} %bitcast.87), kind=kOutput, calls=%fused_computation | convolution fusion | flops 2422210560 | bytes 9052160 | tf_op jit(solution)/shard_map/dot_general | solution.py:1403
  198.8 0.6 pad_maximum_fusion.2.stat_ref
  199.4 53.0 %mix_backward.1 = (bf16[2,8,128,1152]{3,2,1,0:T(8,128)(2,1)}, f32[8,384]{1,0:T(8,128)}, f32[8,256]{1,0:T(8,128)}, f32[8,128]{1,0:T(8,128)}, bf16[2,128,1536]{2,1,0:T(8,128)(2,1)}, /*index=5*/bf16[2,96,1536]{2,1,0:T(8,128)(2,1)}) custom-call(bf16[2,8,128,1152]{3,2,1,0:T(8,128)(2,1)} %get-tuple-element.38.zx_ref.zxh_ref.tail_ref.tailh_ref, ...), custom_call_target="tpu_custom_call" | custom-call | flops 32000000000 | bytes 16000000 | tf_op jit(solution)/shard_map/mix_backward/pallas_call | solution.py:506
  252.4 0.8 slice_reduce_fusion.6
  253.4 0.7 reshape.233
  254.2 0.7 slice.121
  255.0 0.7 reshape.232
  255.7 0.7 pad_maximum_fusion.vec_ref
  256.5 96.2 %exit_scatter.1 = (bf16[2,128,1536]{2,1,0:T(8,128)(2,1)}, bf16[2,128,1536]{2,1,0:T(8,128)(2,1)}, bf16[2,4,48,1152]{3,2,1,0:T(8,128)(2,1)}, f32[174,128]{1,0:T(8,128)}) custom-call(bf16[2048,1536]{1,0:T(8,128)(2,1)} %bitcast.70, bf16[2048,1152]{1,0:T(8,128)(2,1)} %bitcast.71, bf16[1536,1152]{1,0:T(8,128)(2,1)} %bitcast.73, ...), custom_call_target="tpu_custom_call" | custom-call | bytes 200000000 | tf_op jit(solution)/shard_map/exit_scatter/pallas_call | solution.py:1276
  352.7 1.0 slice.124
  353.7 0.7 slice.126
  354.5 0.6 slice.141
  355.1 0.6 slice_reduce_fusion
  355.7 1.3 bitcast_divide_fusion
  357.2 0.6 squeeze.19
  357.8 0.6 squeeze.20
  358.4 0.6 squeeze.21
  358.9 0.6 reshape.243
  359.6 1.1 copy-done.4
  360.7 1.1 copy-done.5
  361.8 2.9 finish.1
  (105 shorter events, 1.8 us)
Async XLA Ops:
  0.6 1.5 slice-start
  1.5 104.4 %copy-start.10 = (f32[4,256]{1,0:T(4,128)}, f32[4,256]{1,0:T(4,128)S(1)}, u32[]{:S(2)}) copy-start(f32[4,256]{1,0:T(4,128)S(1)} %slice.111.wt_ref) | copy-start | bytes 12292
  2.1 103.7 %copy-start.14 = (f32[256]{0:T(256)}, f32[256]{0:T(256)S(1)}, u32[]{:S(2)}) copy-start(f32[256]{0:T(256)S(1)} %slice.112) | copy-start | bytes 3076
  2.2 1.8 copy-start
  2.2 1.9 copy-start.19
  2.7 2.6 slice-start.1
  4.1 97.7 %copy-start.20 = (s32[2,1024]{1,0:T(2,128)S(1)}, s32[2,1024]{1,0:T(2,128)}, u32[]{:S(2)}) copy-start(s32[2,1024]{1,0:T(2,128)} %seg_ref.1) | copy-start | bytes 24580
  5.3 99.0 %copy-start.23 = (f32[48]{0:T(128)S(1)}, f32[48]{0:T(128)}, u32[]{:S(2)}) copy-start(f32[48]{0:T(128)} %param.20) | copy-start | bytes 580
  5.3 99.2 %slice-start.2 = ((f32[4,3328]{1,0:T(4,128)}), f32[4,3072]{1,0:T(4,128)S(1)}, s32[]{:S(2)}) async-start(f32[4,3328]{1,0:T(4,128)} %param.16), calls=%async_computation.2 | async-start | bytes 98304 | tf_op jit(solution)/shard_map/slice | solution.py:1392
  5.3 99.2 %slice-start.3 = ((f32[3328]{0:T(1024)}), f32[3072]{0:T(1024)S(1)}, s32[]{:S(2)}) async-start(f32[3328]{0:T(1024)} %param.17), calls=%async_computation.3 | async-start | bytes 24576 | tf_op jit(solution)/shard_map/slice | solution.py:1393
  5.3 100.1 %copy-start.21 = (f32[48]{0:T(128)S(1)}, f32[48]{0:T(128)}, u32[]{:S(2)}) copy-start(f32[48]{0:T(128)} %param.19) | copy-start | bytes 580
  5.3 100.1 %copy-start.22 = (f32[48]{0:T(128)S(1)}, f32[48]{0:T(128)}, u32[]{:S(2)}) copy-start(f32[48]{0:T(128)} %param.18) | copy-start | bytes 580
  103.7 2.1 copy-start.3
  103.8 2.1 copy-start.15
  104.5 57.3 %copy-start.13 = (f32[1,384]{1,0:T(1,128)}, f32[1,384]{1,0:T(1,128)S(1)}, u32[]{:S(2)}) copy-start(f32[1,384]{1,0:T(1,128)S(1)} %broadcast_in_dim_reshape.2.skip_ref) | copy-start | bytes 4612
  104.6 57.3 %copy-start.8 = (f32[4,384]{1,0:T(4,128)}, f32[4,384]{1,0:T(4,128)S(1)}, u32[]{:S(2)}) copy-start(f32[4,384]{1,0:T(4,128)S(1)} %constant_dynamic-slice_fusion.wx_ref) | copy-start | bytes 18436
  104.7 57.2 %copy-start.11 = (f32[1,384]{1,0:T(1,128)}, f32[1,384]{1,0:T(1,128)S(1)}, u32[]{:S(2)}) copy-start(f32[1,384]{1,0:T(1,128)S(1)} %dynamic_slice.19.bx_ref) | copy-start | bytes 4612
  105.5 56.4 %copy-start.12 = (f32[1,384]{1,0:T(1,128)}, f32[1,384]{1,0:T(1,128)S(1)}, u32[]{:S(2)}) copy-start(f32[1,384]{1,0:T(1,128)S(1)} %dynamic_slice.23.gain_ref) | copy-start | bytes 4612
  105.5 56.4 %copy-start.9 = (f32[8,128]{1,0:T(8,128)}, f32[8,128]{1,0:T(8,128)S(1)}, u32[]{:S(2)}) copy-start(f32[8,128]{1,0:T(8,128)S(1)} %select_maximum_fusion.hp_ref) | copy-start | bytes 12292
  105.6 56.3 %copy-start.7 = (bf16[128,128]{1,0:T(8,128)(2,1)}, bf16[128,128]{1,0:T(8,128)(2,1)S(1)}, u32[]{:S(2)}) copy-start(bf16[128,128]{1,0:T(8,128)(2,1)S(1)} %fusion.9.pick_ref) | copy-start | bytes 98308
  105.9 56.1 %copy-start.1 = (f32[2,8,128,1]{3,2,1,0:T(8,128)}, f32[2,8,128,1]{3,2,1,0:T(8,128)S(1)}, u32[]{:S(2)}) copy-start(f32[2,8,128,1]{3,2,1,0:T(8,128)S(1)} %subtract_convert_fusion.off_ref) | copy-start | bytes 24580
  161.9 9.4 %copy-start.16 = (bf16[2,2,96,1536]{3,2,1,0:T(8,128)(2,1)}, bf16[2,2,96,1536]{3,2,1,0:T(8,128)(2,1)S(1)}, u32[]{:S(2)}) copy-start(bf16[2,2,96,1536]{3,2,1,0:T(8,128)(2,1)S(1)} %get-tuple-element.41) | copy-start | bytes 3538948
  161.9 9.4 %copy-start.18 = (bf16[2,8,128,384]{3,2,1,0:T(8,128)(2,1)}, bf16[2,8,128,384]{3,2,1,0:T(8,128)(2,1)S(1)}, u32[]{:S(2)}) copy-start(bf16[2,8,128,384]{3,2,1,0:T(8,128)(2,1)S(1)} %get-tuple-element.39.y_ref) | copy-start | bytes 4718596
  171.4 5.7 %collective-permute-start = (f32[2,8,2,128]{3,2,1,0:T(2,128)S(1)}, f32[2,8,2,128]{3,2,1,0:T(2,128)S(1)}, u32[]{:S(2)}, u32[]{:S(2)}) collective-permute-start(f32[2,8,2,128]{3,2,1,0:T(2,128)S(1)} %pad_maximum_fusion.1), channel_id=1, source_target_pairs={{0,1},{1,0},{2,3},{3,2},{4,5},{5,4},{6,7},{7,6},{8,9},{9,8},{10,11... | collective-permute-start | bytes 49160 | tf_op jit(solution)/shard_map/ppermute | solution.py:1485
  177.1 2.7 collective-permute-start.1
  179.8 6.5 %collective-permute-start.2 = (f32[2,8,2,128]{3,2,1,0:T(2,128)S(1)}, f32[2,8,2,128]{3,2,1,0:T(2,128)S(1)}, u32[]{:S(2)}, u32[]{:S(2)}) collective-permute-start(f32[2,8,2,128]{3,2,1,0:T(2,128)S(1)} %fusion.23), channel_id=1, source_target_pairs={{0,8},{1,9},{2,10},{3,11},{4,12},{5,13},{6,14},{7,15},{8,0},{9,1},... | collective-permute-start | bytes 49160 | tf_op jit(solution)/shard_map/ppermute | solution.py:1485
  186.3 7.2 %copy-start.17 = (bf16[2,2,96,1536]{3,2,1,0:T(8,128)(2,1)S(1)}, bf16[2,2,96,1536]{3,2,1,0:T(8,128)(2,1)}, u32[]{:S(2)}) copy-start(bf16[2,2,96,1536]{3,2,1,0:T(8,128)(2,1)} %copy-done.16) | copy-start | bytes 3538948
  186.4 7.2 %copy-start.24 = (bf16[2,8,128,384]{3,2,1,0:T(8,128)(2,1)S(1)}, bf16[2,8,128,384]{3,2,1,0:T(8,128)(2,1)}, u32[]{:S(2)}) copy-start(bf16[2,8,128,384]{3,2,1,0:T(8,128)(2,1)} %get-tuple-element.43) | copy-start | bytes 4718596
  256.5 103.1 %copy-start.6 = (bf16[2,96,1536]{2,1,0:T(8,128)(2,1)S(1)}, bf16[2,96,1536]{2,1,0:T(8,128)(2,1)}, u32[]{:S(2)}) copy-start(bf16[2,96,1536]{2,1,0:T(8,128)(2,1)} %get-tuple-element.53.rows_ref) | copy-start | bytes 1769476
  352.7 6.9 %copy-start.2 = (bf16[2,4,48,1152]{3,2,1,0:T(8,128)(2,1)S(1)}, bf16[2,4,48,1152]{3,2,1,0:T(8,128)(2,1)}, u32[]{:S(2)}) copy-start(bf16[2,4,48,1152]{3,2,1,0:T(8,128)(2,1)} %get-tuple-element.52) | copy-start | bytes 2654212
  359.5 1.1 copy-start.4
  360.7 1.1 copy-start.5

commit v6 on v5

--- a/solution.py
+++ b/solution.py
@@ -137,109 +137,215 @@
     return conv_x, conv_t, raw, step, rate, decay_rate, cumul, spread, step_x, entry_x, end_x
 
 
+def positions(segments, chunk, length):
+    here = jnp.zeros((1, length), F32)
+    total = segments.shape[1] // length
+    rows = [segments[:, i * length : (i + 1) * length].astype(F32) for i in range(total)]
+    for i in range(total):
+        here = here + jnp.where(chunk == i, rows[i], 0.0)
+    own = jnp.broadcast_to(here, (length, length)).T
+    less = jnp.zeros((length, length), F32)
+    upto = jnp.zeros((length, length), F32)
+    for row in rows:
+        less = less + jnp.where(row < own, 1.0, 0.0)
+        upto = upto + jnp.where(row <= own, 1.0, 0.0)
+    index = (chunk * length + iota((length, 1), 0)).astype(F32)
+    offset = index - jnp.sum(less, axis=1, keepdims=True)
+    return offset, jnp.sum(upto, axis=1, keepdims=True) - 1.0 - index
+
+
+def flat_rows(ref, flat):
+    rows, cols = ref.shape[-2:]
+    if rows % HALO == 0:
+        return ref[...].reshape(-1, cols)
+    shape = ref.shape[:-2]
+    for i, at in enumerate(np.ndindex(*shape)):
+        flat[i * rows : (i + 1) * rows, :] = ref[at]
+    return flat[...]
+
+
 def forward_kernel(
     seq, fsdp,
-    h_ref, w_ref, cot_ref, ow_ref, off_ref,
+    h_ref, zx_ref, tail_ref, seg_ref, cot_ref, ow_ref,
     wx_ref, bx_ref, wt_ref, bt_ref, hp_ref, pick_ref, skip_ref, gain_ref,
-    proj_ref, y_ref, gated_ref, square_ref, state_ref, cot_out, ow_out,
-    memory, ext_x, ext_t, last_rows, send, recv, near,
+    proj_ref, y_ref, state_ref, off_ref, rem_ref, offr_ref,
+    h_out, w_out, grad_out, stat_out, mixed_out, pout_out,
+    h_v, w_v, w_flat, seg_v, cot_v, ow_v, ow_flat, gated_v, sums_v, sums_got, grad_v, mixed_v,
+    pout_v, memory, ext_x, ext_t, last_rows, send, recv, near,
 ):
     seqs, _, length, width = y_ref.shape
-    depth = h_ref.shape[3]
+    depth = h_v.shape[3]
+    cols = proj_ref.shape[3]
     step_at = pl.program_id(0)
-
     place = Place(seq, fsdp)
     links = Links(send, recv, near)
-    cot = TokenGather(place, links, cot_ref, cot_out)
-    w_rows = RowGather(place, links, ow_ref, ow_out)
+    peers = peers_of(place)
+    near_peers = [(l, c) for t, l, c in peers if t == 0]
+    entry = Entry(place, links, h_ref, zx_ref, tail_ref, seg_ref, h_v, w_v, seg_v)
+    cot = TokenGather(place, links, cot_ref, cot_v)
+    w_rows = RowGather(place, links, ow_ref, ow_v)
+    keep = [links.local(lambda: (h_v, h_out)), links.local(lambda: (w_v, w_out))]
     stages = len(place.low_bits)
+
+    def send_sums(i):
+        l, c = near_peers[i]
+        return links.far(lambda: (sums_v, sums_got.at[i], place.at(low=l, core=c)))
+
+    sums = [send_sums(i) for i in range(len(near_peers))]
 
     @pl.when(step_at == 0)
     def _():
         memory[...] = jnp.zeros_like(memory)
         last_rows[...] = jnp.zeros_like(last_rows)
         meet_pair(place)
-        cot.begin()
+        entry.run(cot.cross_over)
+        if w_v.shape[-2] % HALO:
+            flat_rows(w_v, w_flat)
 
     @pl.when(step_at == 1)
     def _():
+        for copy in keep:
+            copy.start()
+        cot.begin_home()
         w_rows.begin()
 
-    last = pl.num_programs(0) - 1
     for i in range(stages):
 
-        @pl.when(step_at == min(2 + 2 * i, seq - 2))
+        @pl.when(step_at == min(3 + 2 * i, seq - 1))
         def _():
             cot.pass_on(i, "home")
 
-    @pl.when(step_at == last - 3)
+    @pl.when(step_at == 2)
     def _():
         cot.arrive()
 
-    @pl.when(step_at == last - 1)
-    def _():
-        cot.pass_on(0, "away")
-
-    proj = jnp.dot(
-        h_ref[...].reshape(seqs * length, depth), w_ref[...], preferred_element_type=F32
-    ).astype(BF16)
-    proj_ref[...] = proj.reshape(proj_ref.shape)
-    params = tuple(r[...] for r in (wx_ref, bx_ref, wt_ref, bt_ref, hp_ref, pick_ref))
-    for q in range(seqs):
-        offset = off_ref[q, 0]
-        chunk_rows = proj[q * length : (q + 1) * length]
-        zx, tail = chunk_rows[:, : 2 * width], chunk_rows[:, 2 * width :]
-        earlier = last_rows[q]
-        conv_x, conv_t, _, _, _, _, cumul, _, step_x, entry_x, end_x = chunk_common(
-            zx[:, width:], earlier[:, width : 2 * width], tail, earlier[:, 2 * width :], offset, params,
-            ext_x.at[q], ext_t.at[q], width,
-        )
-        xs = conv_x * sigmoid(conv_x)
-        act_t = conv_t * sigmoid(conv_t)
-        bs = act_t[:, :STATE].astype(BF16)
-        cs = act_t[:, STATE:].astype(BF16)
-        scaled = xs * step_x
-        scores = mm_tr(cs, bs)
-        gap = iota((length, length), 0) - iota((length, length), 1)
-        same = (gap >= 0) & (gap.astype(F32) <= offset)
-        cumul_t = cumul.T
-        old = memory[q]
-        old_low = old.astype(BF16)
-        state_ref[q, 0] = old_low
-        outside = mm(cs, old_low) * entry_x + skip_ref[...] * xs
-        squares = jnp.zeros((length, 1), F32)
-        for start, size, heads in head_tiles(width):
-            mixing = []
-            for head in heads:
-                spans = cumul[:, head : head + 1] - cumul_t[head : head + 1, :]
-                decays = jnp.exp(jnp.where(same, spans, -1e30))
-                mixing.append((decays * scores).astype(BF16))
-            tile = masked_heads(scaled[:, start : start + size].astype(BF16), heads)
-            mix = mixing[0] if len(heads) == 1 else jnp.concatenate(mixing, axis=1)
-            inside = jnp.dot(mix, tile, preferred_element_type=F32)
-            y_low = (inside + outside[:, start : start + size]).astype(BF16)
-            y_ref[q, 0, :, start : start + size] = y_low
-            z = zx[:, start : start + size].astype(F32)
-            gated = y_low.astype(F32) * (z * sigmoid(z))
-            gated_ref[q, 0, :, start : start + size] = (
-                gated * gain_ref[:, start : start + size]
-            ).astype(BF16)
-            squares = squares + jnp.sum(gated * gated, axis=1, keepdims=True)
-        square_ref[q, 0] = jnp.broadcast_to(squares, (length, LANES)).T[0:1, :]
-        fresh = tr_mm(bs, scaled * end_x)
-        memory[q] = old * entry_x[length - 1 : length, :] + fresh
-        last_rows[q] = chunk_rows[length - HALO :]
-
-    @pl.when(step_at == last - 1)
+    for i in range(stages):
+
+        @pl.when(step_at == min(4 + 2 * i, seq - 1))
+        def _():
+            cot.pass_on(i, "away")
+
+    @pl.when(step_at == seq - 2)
     def _():
         w_rows.forward()
 
-    @pl.when(step_at == last)
+    @pl.when(step_at < seq)
     def _():
-        for i in range(1, stages):
-            cot.pass_on(i, "away")
+        weights = flat_rows(w_v, w_flat) if w_v.shape[-2] % HALO == 0 else w_flat[...]
+        proj = jnp.dot(
+            h_v[:, step_at].reshape(seqs * length, depth), weights, preferred_element_type=F32
+        ).astype(BF16)
+        proj_ref[...] = proj.reshape(proj_ref.shape)
+        params = tuple(r[...] for r in (wx_ref, bx_ref, wt_ref, bt_ref, hp_ref, pick_ref))
+        for q in range(seqs):
+            offset, remain = positions(seg_v[q : q + 1, :], step_at, length)
+            off_ref[q, 0] = offset
+            rem_ref[q, 0] = remain
+            offr_ref[q, 0] = jnp.broadcast_to(offset, (length, LANES)).T[0:1, :]
+            chunk_rows = proj[q * length : (q + 1) * length]
+            zx, tail = chunk_rows[:, : 2 * width], chunk_rows[:, 2 * width :]
+            earlier = last_rows[q]
+            here = pl.ds(pl.multiple_of((q * seq + step_at) * length, length), length)
+            conv_x, conv_t, _, _, _, _, cumul, _, step_x, entry_x, end_x = chunk_common(
+                zx[:, width:], earlier[:, width : 2 * width], tail, earlier[:, 2 * width :], offset, params,
+                ext_x.at[q], ext_t.at[q], width,
+            )
+            xs = conv_x * sigmoid(conv_x)
+            act_t = conv_t * sigmoid(conv_t)
+            bs = act_t[:, :STATE].astype(BF16)
+            cs = act_t[:, STATE:].astype(BF16)
+            scaled = xs * step_x
+            scores = mm_tr(cs, bs)
+            gap = iota((length, length), 0) - iota((length, length), 1)
+            same = (gap >= 0) & (gap.astype(F32) <= offset)
+            cumul_t = cumul.T
+            old = memory[q]
+            old_low = old.astype(BF16)
+            state_ref[q, 0] = old_low
+            outside = mm(cs, old_low) * entry_x + skip_ref[...] * xs
+            squares = jnp.zeros((length, 1), F32)
+            for start, size, heads in head_tiles(width):
+                mixing = []
+                for head in heads:
+                    spans = cumul[:, head : head + 1] - cumul_t[head : head + 1, :]
+                    decays = jnp.exp(jnp.where(same, spans, -1e30))
+                    mixing.append((decays * scores).astype(BF16))
+                tile = masked_heads(scaled[:, start : start + size].astype(BF16), heads)
+                mix = mixing[0] if len(heads) == 1 else jnp.concatenate(mixing, axis=1)
+                inside = jnp.dot(mix, tile, preferred_element_type=F32)
+                y_low = (inside + outside[:, start : start + size]).astype(BF16)
+                y_ref[q, 0, :, start : start + size] = y_low
+                z = zx[:, start : start + size].astype(F32)
+                gated = y_low.astype(F32) * (z * sigmoid(z))
+                gated_v[here, start : start + size] = (
+                    gated * gain_ref[:, start : start + size]
+                ).astype(BF16)
+                squares = squares + jnp.sum(gated * gated, axis=1, keepdims=True)
+            sums_v[pl.ds(2 * (q * seq + step_at), 1), :] = jnp.broadcast_to(
+                squares, (length, LANES)
+            ).T[0:1, :]
+            fresh = tr_mm(bs, scaled * end_x)
+            memory[q] = old * entry_x[length - 1 : length, :] + fresh
+            last_rows[q] = chunk_rows[length - HALO :]
+
+    @pl.when(step_at == seq)
+    def _():
         w_rows.finish()
         cot.finish()
+        rows_out = flat_rows(ow_v, ow_flat)
+        tile = 2 * length
+        tiles = seqs * seq // 2
+
+        @pl.loop(0, tiles)
+        def _(k):
+            at = pl.ds(pl.multiple_of(k * tile, tile), tile)
+            cots = cot_v[k // (seq // 2), pl.ds(lax.rem(k, seq // 2) * 2, 2)].reshape(tile, depth)
+            grad = mm_tr(cots, rows_out)
+            grad_v[at, :] = grad
+            part = jnp.sum(grad * gated_v[at, :].astype(F32), axis=1, keepdims=True)
+            part = jnp.broadcast_to(part, (tile, LANES))
+            for i in (0, 1):
+                sums_v[pl.ds(4 * k + 2 * i + 1, 1), :] = (
+                    part[i * length : (i + 1) * length].T[0:1, :]
+                )
+
+        grad_store = links.local(lambda: (grad_v, grad_out))
+        grad_store.start()
+        for copy in sums:
+            copy.start()
+        for copy in sums:
+            copy.wait_recv()
+        total = sums_v[...]
+        for i in range(len(near_peers)):
+            total = total + sums_got[i]
+        is_square = lax.rem(iota(total.shape, 0), 2) == 0
+        scale = lax.rsqrt(total / INNER + EPSILON)
+        other = pltpu.roll(scale, 1, 0)
+        stat_out[...] = jnp.where(is_square, scale, total * (other * other * other / INNER))
+
+        @pl.loop(0, tiles)
+        def _(k):
+            at = pl.ds(pl.multiple_of(k * tile, tile), tile)
+            scales = [
+                jnp.broadcast_to(stat_out[pl.ds(4 * k + 2 * i, 1), :], (LANES, length)).T[:, 0:1]
+                for i in (0, 1)
+            ]
+            scale_col = jnp.concatenate(scales, axis=0)
+            gated = gated_v[at, :]
+            mixed = jnp.dot(gated, rows_out, preferred_element_type=F32)
+            mixed_v[at, :] = (mixed * scale_col).astype(BF16)
+            gated_v[at, :] = (gated.astype(F32) * scale_col).astype(BF16)
+
+        mixed_store = links.local(lambda: (mixed_v, mixed_out))
+        mixed_store.start()
+        pout_v[...] = tr_mm(gated_v[...], cot_v[...].reshape(-1, depth)).astype(BF16)
+        pout_store = links.local(lambda: (pout_v, pout_out))
+        pout_store.start()
+        for copy in [grad_store, mixed_store, pout_store] + keep:
+            copy.wait()
+        for copy in sums:
+            copy.wait_send()
+        entry.finish()
 
 
 def backward_kernel(
@@ -421,6 +527,7 @@
 TAIL = 2 * STATE + LANES
 AXES = ("seq", "fsdp")
 MESH = pl.DeviceIdType.MESH
+ANYWHERE = pl.BlockSpec(memory_space=pl.ANY)
 
 
 def whole_spec(shape):
@@ -443,52 +550,83 @@
     return block, before
 
 
-def forward_mix(h_all, w_mine, cotangent, out_w, off_col, consts, seq, fsdp):
-    seqs, steps, length, depth = h_all.shape
-    cols = w_mine.shape[1]
-    width = (cols - TAIL) // 2
-    block, _ = chunk_specs(seqs, steps, length, False)
-    shape = (seqs, steps, length, width)
-    return pl.pallas_call(
+def forward_mix(normed, zx, tail, segments, cotangent, out_w, consts, seq, fsdp):
+    seqs, length, depth = normed.shape
+    rows = tail.shape[0]
+    cols = zx.shape[2] + TAIL
+    width = zx.shape[2] // 2
+    pairs = fsdp // 2
+    count = seqs * seq * length
+
+    def block(columns, height=length):
+        return pl.BlockSpec(
+            (seqs, 1, height, columns), lambda i: (0, jnp.minimum(i, seq - 1), 0, 0)
+        )
+
+    def blocks(columns, kind, height=length):
+        return jax.ShapeDtypeStruct((seqs, seq, height, columns), kind)
+
+    w_shape = (seq, pairs, 2, rows, cols)
+    out_shape = (pairs, 2) + out_w.shape
+    sums = (seqs * seq * 2, length)
+    flat = 8 if rows % HALO == 0 else depth
+    flat_out = 8 if out_w.shape[0] % HALO == 0 else width
+    outs = pl.pallas_call(
         functools.partial(forward_kernel, seq, fsdp),
-        grid=(steps,),
-        in_specs=[
-            block(depth),
-            pl.BlockSpec(w_mine.shape, lambda i: (0, 0), pipeline_mode=pl.Buffered(1)),
-            ANYWHERE, ANYWHERE, block(1),
-        ]
-        + [whole_spec(v.shape) for v in consts],
+        grid=(seq + 1,),
+        in_specs=[ANYWHERE] * 6 + [whole_spec(v.shape) for v in consts],
         out_specs=[
-            block(cols), block(width), block(width), block(length, 0, 1), block(width, 0, STATE),
-            ANYWHERE, ANYWHERE,
+            block(cols), block(width), block(width, STATE), block(1), block(1), block(length, 1),
+            ANYWHERE, ANYWHERE, ANYWHERE, whole_spec(sums), ANYWHERE, ANYWHERE,
         ],
         out_shape=[
-            jax.ShapeDtypeStruct((seqs, steps, length, cols), BF16),
-            jax.ShapeDtypeStruct(shape, BF16),
-            jax.ShapeDtypeStruct(shape, BF16),
-            jax.ShapeDtypeStruct((seqs, steps, 1, length), F32),
-            jax.ShapeDtypeStruct((seqs, steps, STATE, width), BF16),
-            jax.ShapeDtypeStruct(h_all.shape, BF16),
-            jax.ShapeDtypeStruct((fsdp // 2, 2) + out_w.shape, BF16),
+            blocks(cols, BF16), blocks(width, BF16), blocks(width, BF16, STATE),
+            blocks(1, F32), blocks(1, F32), blocks(length, F32, 1),
+            blocks(depth, BF16),
+            jax.ShapeDtypeStruct(w_shape, BF16),
+            jax.ShapeDtypeStruct((count, width), F32),
+            jax.ShapeDtypeStruct(sums, F32),
+            jax.ShapeDtypeStruct((count, depth), BF16),
+            jax.ShapeDtypeStruct((width, depth), BF16),
         ],
         scratch_shapes=[
+            pltpu.VMEM((seqs, seq, length, depth), BF16),
+            pltpu.VMEM(w_shape, BF16),
+            pltpu.VMEM((flat, cols), BF16),
+            pltpu.VMEM(segments.shape, segments.dtype),
+            pltpu.VMEM((seqs, seq, length, depth), BF16),
+            pltpu.VMEM(out_shape, BF16),
+            pltpu.VMEM((flat_out, depth), BF16),
+            pltpu.VMEM((count, width), BF16),
+            pltpu.VMEM(sums, F32),
+            pltpu.VMEM((seq - 1,) + sums, F32),
+            pltpu.VMEM((count, width), F32),
+            pltpu.VMEM((count, depth), BF16),
+            pltpu.VMEM((width, depth), BF16),
             pltpu.VMEM((seqs, STATE, width), F32),
             pltpu.VMEM((seqs, HALO + length, width), F32),
             pltpu.VMEM((seqs, HALO + length, 2 * STATE), F32),
             pltpu.VMEM((seqs, HALO, cols), BF16),
-            pltpu.SemaphoreType.DMA((64,)),
-            pltpu.SemaphoreType.DMA((64,)),
-            pltpu.SemaphoreType.DMA((8,)),
+            pltpu.SemaphoreType.DMA((320,)),
+            pltpu.SemaphoreType.DMA((320,)),
+            pltpu.SemaphoreType.DMA((24,)),
         ],
         compiler_params=pltpu.CompilerParams(
-            dimension_semantics=("arbitrary",), vmem_limit_bytes=48 << 20, collective_id=2,
+            dimension_semantics=("arbitrary",), vmem_limit_bytes=60 << 20, collective_id=0,
             has_side_effects=True,
         ),
         cost_estimate=pl.CostEstimate(
-            flops=steps * seqs * 900_000_000, transcendentals=0, bytes_accessed=10_000_000
+            flops=30_000_000_000, transcendentals=0, bytes_accessed=60_000_000
         ),
         name="mix_forward",
-    )(h_all, w_mine, cotangent, out_w, off_col, *consts)
+    )(normed, zx, tail, segments, cotangent, out_w, *consts)
+    proj, y, states, off_col, rem_col, off_row, h_all, w_mine, grad_yn, stats, mixed, part = outs
+    shape = (seqs, seq, length)
+    return (
+        proj, y, states, off_col, rem_col, off_row, h_all, w_mine.reshape(depth, cols),
+        grad_yn.reshape(shape + (width,)), stats.reshape(seqs, seq, 2, length),
+        mixed.reshape(shape + (depth,)), part.reshape(out_shape),
+    )
 
 
 def backward_mix(
@@ -679,11 +817,16 @@
         return links.far(make)
 
     def begin(self):
+        self.cross_over()
+        self.begin_home()
+
+    def cross_over(self):
         @pl.when(self.place.away)
         def _():
             for copy in self.cross:
                 copy.start()
 
+    def begin_home(self):
         @pl.when(self.place.home)
         def _():
             self.stay.start()
@@ -788,133 +931,122 @@
             self.to_far.wait_send()
 
 
-def entry_kernel(
-    seq, fsdp, h_ref, zx_ref, tail_ref, seg_ref, h_out, w_out, seg_out, send, recv, near
-):
-    place = Place(seq, fsdp)
-    links = Links(send, recv, near)
-    cols = zx_ref.shape[2]
-    peers = peers_of(place)
-    others = range(1, place.pairs)
-    tokens = TokenGather(place, links, h_ref, h_out)
-
-    def block(t=0, l=0, c=0):
-        s, f = place.at(top=t, low=l, core=c)
-        return w_out.at[s, place.pair, lax.rem(f, 2)]
-
-    def columns(ref):
-        return ref.at[:, pl.ds(0, cols)]
-
-    def tail_of(ref):
-        return ref.at[:, pl.ds(cols, TAIL)]
-
-    def send_zx(t, l, c):
-        group = flip(place.core, c) * place.half + flip(place.low, l)
-        return zx_ref.at[group], columns(block()), place.at(top=t, low=l, core=c)
-
-    zx = {p: links.far(functools.partial(send_zx, *p)) for p in peers}
-    own = [
-        links.local(lambda: (zx_ref.at[place.chunk], columns(block()))),
-        links.local(lambda: (tail_ref, tail_of(block()))),
-    ]
-    tail_cross = links.far(lambda: (tail_ref, tail_of(block()), place.at(top=1)))
-    near_peers = [(l, c) for t, l, c in peers if t == 0]
-
-    def send_tail(l, c):
-        return tail_ref, tail_of(block()), place.at(low=l, core=c)
-
-    def send_other(l, c):
-        return tail_of(block(1)), tail_of(block(1)), place.at(low=l, core=c)
-
-    tails = {p: links.far(functools.partial(send_tail, *p)) for p in near_peers}
-    tails_more = {p: links.far(functools.partial(send_other, *p)) for p in near_peers}
-    swap_segments = links.far(lambda: (seg_ref, seg_out, place.at(core=1)))
-
-    def send_on(t, l, c, p):
-        return block(t, l, c), block(t, l, c), place.at(pair=p)
-
-    forwards = {
-        p: [links.far(functools.partial(send_on, *p, other)) for other in others]
-        for p in [(0, 0, 0)] + peers
-    }
-
-    meet_pair(place)
-    stages = len(place.low_bits)
-    far_peers = [p for p in peers if p[0] == 1]
-    tokens.begin()
-    tail_cross.start()
-    for copy in own:
-        copy.start()
-    for p in near_peers:
-        zx[0, *p].start()
-        tails[p].start()
-    swap_segments.start()
-    for copy in own:
-        copy.wait()
-    for copy in forwards[0, 0, 0]:
-        copy.start()
-    tail_cross.wait_recv()
-    for p in near_peers:
-        tails_more[p].start()
-    tokens.pass_on(0, "home")
-    for p in near_peers:
-        zx[0, *p].wait_recv()
-        tails[p].wait_recv()
-        for copy in forwards[0, *p]:
+class Entry:
+    def __init__(self, place, links, h_ref, zx_ref, tail_ref, seg_ref, h_v, w_v, seg_v):
+        self.place = place
+        cols = zx_ref.shape[2]
+        self.peers = peers = peers_of(place)
+        others = range(1, place.pairs)
+        self.tokens = TokenGather(place, links, h_ref, h_v)
+
+        def block(t=0, l=0, c=0):
+            s, f = place.at(top=t, low=l, core=c)
+            return w_v.at[s, place.pair, lax.rem(f, 2)]
+
+        def columns(ref):
+            return ref.at[:, pl.ds(0, cols)]
+
+        def tail_of(ref):
+            return ref.at[:, pl.ds(cols, TAIL)]
+
+        def send_zx(t, l, c):
+            group = flip(place.core, c) * place.half + flip(place.low, l)
+            return zx_ref.at[group], columns(block()), place.at(top=t, low=l, core=c)
+
+        self.zx = {p: links.far(functools.partial(send_zx, *p)) for p in peers}
+        self.own = [
+            links.local(lambda: (zx_ref.at[place.chunk], columns(block()))),
+            links.local(lambda: (tail_ref, tail_of(block()))),
+        ]
+        self.tail_cross = links.far(lambda: (tail_ref, tail_of(block()), place.at(top=1)))
+        self.near_peers = [(l, c) for t, l, c in peers if t == 0]
+
+        def send_tail(l, c):
+            return tail_ref, tail_of(block()), place.at(low=l, core=c)
+
+        def send_other(l, c):
+            return tail_of(block(1)), tail_of(block(1)), place.at(low=l, core=c)
+
+        self.tails = {p: links.far(functools.partial(send_tail, *p)) for p in self.near_peers}
+        self.tails_more = {
+            p: links.far(functools.partial(send_other, *p)) for p in self.near_peers
+        }
+        self.seg_send = links.far(lambda: (seg_ref, seg_v, place.at(core=1)))
+        self.seg_keep = links.local(lambda: (seg_ref, seg_v))
+
+        def send_on(t, l, c, p):
+            return block(t, l, c), block(t, l, c), place.at(pair=p)
+
+        self.forwards = {
+            p: [links.far(functools.partial(send_on, *p, other)) for other in others]
+            for p in [(0, 0, 0)] + peers
+        }
+
+    def run(self, then):
+        tokens, zx, forwards = self.tokens, self.zx, self.forwards
+        stages = len(self.place.low_bits)
+        far_peers = [p for p in self.peers if p[0] == 1]
+        tokens.begin()
+        self.tail_cross.start()
+        for copy in self.own:
             copy.start()
-    for p in far_peers:
-        zx[p].start()
-    for i in range(1, stages):
-        tokens.pass_on(i, "home")
-
-    tokens.arrive()
-    for p in near_peers:
-        tails_more[p].wait_recv()
-    for i in range(stages):
-        tokens.pass_on(i, "away")
-        at, to = (len(far_peers) * k // stages for k in (i, i + 1))
-        for p in far_peers[at:to]:
-            zx[p].wait_recv()
+        for p in self.near_peers:
+            zx[0, *p].start()
+            self.tails[p].start()
+
+        @pl.when(self.place.home)
+        def _():
+            self.seg_send.start()
+            self.seg_keep.start()
+
+        for copy in self.own:
+            copy.wait()
+        for copy in forwards[0, 0, 0]:
+            copy.start()
+        self.tail_cross.wait_recv()
+        for p in self.near_peers:
+            self.tails_more[p].start()
+        tokens.pass_on(0, "home")
+        for p in self.near_peers:
+            zx[0, *p].wait_recv()
+            self.tails[p].wait_recv()
+            for copy in forwards[0, *p]:
+                copy.start()
+        for p in far_peers:
+            zx[p].start()
+        for i in range(1, stages):
+            tokens.pass_on(i, "home")
+        tokens.arrive()
+        for p in self.near_peers:
+            self.tails_more[p].wait_recv()
+        for i in range(stages):
+            tokens.pass_on(i, "away")
+            at, to = (len(far_peers) * k // stages for k in (i, i + 1))
+            for p in far_peers[at:to]:
+                zx[p].wait_recv()
+                for copy in forwards[p]:
+                    copy.start()
+        then()
+
+        @pl.when(self.place.home)
+        def _():
+            self.seg_keep.wait()
+            self.seg_send.wait_send()
+
+        @pl.when(self.place.away)
+        def _():
+            self.seg_send.wait_recv()
+
+        tokens.finish()
+        for p in forwards:
             for copy in forwards[p]:
-                copy.start()
-
-    tokens.finish()
-    for p in forwards:
-        for copy in forwards[p]:
-            copy.wait()
-    tail_cross.wait_send()
-    for group in (zx, tails, tails_more):
-        for copy in group.values():
-            copy.wait_send()
-    swap_segments.wait()
-
-
-ANYWHERE = pl.BlockSpec(memory_space=pl.ANY)
-
-
-def entry_gather(seq, fsdp, normed, zx, tail, segments):
-    seqs, length, depth = normed.shape
-    rows = tail.shape[0]
-    return pl.pallas_call(
-        functools.partial(entry_kernel, seq, fsdp),
-        in_specs=[ANYWHERE] * 4,
-        out_specs=[ANYWHERE] * 3,
-        out_shape=[
-            jax.ShapeDtypeStruct((seqs, seq, length, depth), BF16),
-            jax.ShapeDtypeStruct((seq, fsdp // 2, 2, rows, zx.shape[2] + TAIL), BF16),
-            jax.ShapeDtypeStruct(segments.shape, segments.dtype),
-        ],
-        scratch_shapes=[
-            pltpu.SemaphoreType.DMA((256,)),
-            pltpu.SemaphoreType.DMA((256,)),
-            pltpu.SemaphoreType.DMA((8,)),
-        ],
-        compiler_params=pltpu.CompilerParams(collective_id=0, has_side_effects=True),
-        cost_estimate=pl.CostEstimate(
-            flops=0, transcendentals=0, bytes_accessed=200_000_000
-        ),
-        name="entry_gather",
-    )(normed, zx, tail, segments)
+                copy.wait()
+
+    def finish(self):
+        self.tail_cross.wait_send()
+        for group in (self.zx, self.tails, self.tails_more):
+            for copy in group.values():
+                copy.wait_send()
 
 
 def add_rows(out, left, right, rows=32):
@@ -1370,20 +1502,6 @@
     zx = w_in[:, : 2 * INNER].reshape(rows_in, 2, steps, width).transpose(2, 0, 1, 3)
     zx = zx.reshape(steps, rows_in, 2 * width)
     tail = jnp.pad(w_in[:, 2 * INNER :], ((0, 0), (0, LANES - HEADS)))
-    h_all, w_mine, segs = entry_gather(steps, shards, normed, zx, tail, segments)
-    w_mine = w_mine.reshape(D, 2 * width + TAIL)
-    segs = jnp.where(place.home, segments, segs)
-
-    total = steps * length
-    index = lax.broadcasted_iota(jnp.int32, (seqs, total), 1)
-    starts = jnp.concatenate([jnp.ones((seqs, 1), bool), segs[:, 1:] != segs[:, :-1]], axis=1)
-    first = lax.cummax(jnp.where(starts, index, 0), axis=1)
-    ends = jnp.concatenate([starts[:, 1:], jnp.ones((seqs, 1), bool)], axis=1)
-    last = lax.cummin(jnp.where(ends, index, total), axis=1, reverse=True)
-    off = (index - first).astype(F32).reshape(seqs, steps, length)
-    rem = (last - index).astype(F32).reshape(seqs, steps, length)
-    off_col, off_row, rem_col = off[..., None], off[:, :, None, :], rem[..., None]
-
     heads_p = jnp.stack([mine(dt_bias, heads), mine(a_log, heads)])
     lane = lax.broadcasted_iota(jnp.int32, (LANES, LANES), 1)
     source = lax.broadcasted_iota(jnp.int32, (LANES, LANES), 0)
@@ -1399,35 +1517,9 @@
         mine(gain_out[None], width),
     )
 
-    def dot(a, b):
-        return lax.dot_general(a, b, (((3,), (0,)), ((), ())), preferred_element_type=F32)
-
-    def dot_tr(a, b):
-        return lax.dot_general(a, b, (((3,), (1,)), ((), ())), preferred_element_type=F32)
-
-    def dot_tokens(a, b):
-        dims = (0, 1, 2)
-        return lax.dot_general(a, b, ((dims, dims), ((), ())), preferred_element_type=F32)
-
-    proj, y, gated, squares, states, cot_all, out_w = forward_mix(
-        h_all, w_mine, cotangent, w_out, off_col, consts, steps, shards
-    )
-    out_w = out_w.reshape(width, D)
-
-    grad_yn = dot_tr(cot_all, out_w)
-    sums = jnp.stack(
-        [squares[:, :, 0], jnp.sum(grad_yn * gated.astype(F32), axis=-1)], axis=2
-    )
-    for offsets in [dict(core=1)] + [dict(low=b) for b in place.low_bits]:
-        sums = sums + exchange(sums, steps, shards, **offsets)
-    scale = lax.rsqrt(sums[:, :, 0] / INNER + EPSILON)
-    stats = jnp.stack([scale, sums[:, :, 1] * (scale * scale * scale / INNER)], axis=2)
-    scale = scale[..., None]
-    mixed = (dot(gated, out_w) * scale).astype(BF16)
-    y_normed = (gated.astype(F32) * scale).astype(BF16)
-    part_out = dot_tokens(y_normed, cot_all).astype(BF16)
-
-    part_out = part_out.reshape((shards // 2, 2) + w_out.shape)
+    (
+        proj, y, states, off_col, rem_col, off_row, h_all, w_mine, grad_yn, stats, mixed, part_out,
+    ) = forward_mix(normed, zx, tail, segments, cotangent, w_out, consts, steps, shards)
     grad_proj, sums_x, sums_t, sums_h, mixed, rows = backward_mix(
         proj, off_col, off_row, rem_col, y, grad_yn, stats, states, mixed, part_out, consts,
         steps, shards,
@@ -1478,13 +1570,6 @@
     )
 
 
-def exchange(value, seq, fsdp, low=0, core=0):
-    perm = [
-        (s * fsdp + f, (s ^ low) * fsdp + (f ^ core)) for s in range(seq) for f in range(fsdp)
-    ]
-    return lax.ppermute(value, AXES, perm)
-
-
 def solution(mesh):
     by_token = P("fsdp", "seq", None)
     by_row = P(("seq", "fsdp"), None)

time: 370 us -> 343 us (0.927)
  matrix products: 21.8 us -> 0 us
  Pallas kernels: 304 us -> 313 us
  other arithmetic: 13.3 us -> 4.77 us
  starting transfers between devices: 5.76 us -> 0 us
  local copies, waits for them, and re-layouts: 17.2 us -> 22.2 us
    dot_general x3 -> x0, matrix products: 21.8 us -> none  [the longest x1 9.38 us: dot_tr(): lax.dot_general(a, b, (((3,), (1,)), ((), ())), preferred_element_type=F32)]
    pallas_call x2 -> x1, Pallas kernels: 152 us -> 159 us  [forward_mix(): pl.pallas_call(functools.partial(forward_kernel, seq, fsdp), grid=(seq +...]
    another operation x6 -> x0, other arithmetic: 6.63 us -> none
    ppermute x3 -> x0, starting transfers between devices: 5.76 us -> none  [exchange(): return lax.ppermute(value, AXES, perm)]
    pallas_call x1, Pallas kernels: 96.2 us -> 101 us  [exit_scatter(): pl.pallas_call(functools.partial(exit_kernel, seq, fsdp), in_specs=[ANYWH...]
  transfers between devices with their start and end apart: 3 -> 0, of which waited for: 1 -> 0; matrix products, arithmetic and copies ran while one was open for 2% -> 0% of each run, Pallas kernels for 0% -> 0%
where the time goes in v6:
time: 343 us; the launch traced here: 341 us
  Pallas kernels  313 us (91%)
  local copies, waits for them, and re-layouts  22.2 us (6%)
  other arithmetic  4.77 us (1%)
    pallas_call x1, Pallas kernels, forward_mix(): pl.pallas_call(functools.partial(forward_kernel, seq, fsdp), grid=(seq +...  159 us
    pallas_call x1, Pallas kernels, exit_scatter(): pl.pallas_call(functools.partial(exit_kernel, seq, fsdp), in_specs=[ANYWH...  101 us
    pallas_call x1, Pallas kernels, backward_mix(): pl.pallas_call(functools.partial(backward_kernel, seq, fsdp), grid=(steps...  50.5 us

profile of v6, /device:TPU:1, one launch (start us, length us, event | category | flops | bytes accessed | tf_op | source)
XLA Modules:
  0.0 340.7 jit_solution(17902854317731755788)
XLA Ops:
  0.6 0.0 slice-start
  0.7 0.8 dynamic-slice_bitcast_fusion
  1.5 0.6 select_maximum_fusion.hp_ref
  2.1 0.8 slice.81
  2.9 0.6 constant_dynamic-slice_fusion.wx_ref
  3.5 0.7 slice.82
  4.2 0.1 dynamic-slice.6
  4.3 0.6 dynamic_slice.19.bx_ref
  4.8 0.7 dynamic_slice.22
  5.6 0.1 broadcast_in_dim.21
  5.6 0.7 broadcast_in_dim_reshape.3.skip_ref
  6.3 0.8 dynamic-slice.7
  7.1 0.6 dynamic_slice.23.gain_ref
  7.7 0.6 fusion.4.pick_ref
  8.3 1.3 slice.83.wt_ref
  9.6 1.2 slice.84
  10.8 0.1 copy.25
  10.9 0.5 copy.28
  11.3 0.0 slice-start.1
  11.4 1.2 reshape.108.zx_ref
  12.6 0.2 fusion
  12.8 1.1 fusion.2.h_ref
  13.9 0.6 pad.12.tail_ref
  14.6 158.7 %mix_forward.1 = (bf16[2,8,128,1152]{3,2,1,0:T(8,128)(2,1)}, bf16[2,8,128,384]{3,2,1,0:T(8,128)(2,1)}, bf16[2,8,128,384]{3,2,1,0:T(8,128)(2,1)}, f32[2,8,128,1]{...) custom-call(bf16[2,128,1536]{2,1,0:T(8,128)(2,1)} %fusion.2.h_ref, ...), custom_call_target="tpu_custom_call" | custom-call | flops 30000001024 | bytes 60000000 | tf_op jit(solution)/shard_map/mix_forward/pallas_call | solution.py:574
  173.3 50.5 %mix_backward.1 = (bf16[2,8,128,1152]{3,2,1,0:T(8,128)(2,1)}, f32[8,384]{1,0:T(8,128)}, f32[8,256]{1,0:T(8,128)}, f32[8,128]{1,0:T(8,128)}, bf16[2,128,1536]{2,1,0:T(8,128)(2,1)}, /*index=5*/bf16[2,96,1536]{2,1,0:T(8,128)(2,1)}) custom-call(bf16[2,8,128,1152]{3,2,1,0:T(8,128)(2,1)} %get-tuple-element.38.zx_ref.zxh_ref.tail_ref.tailh_ref, ...), custom_call_target="tpu_custom_call" | custom-call | flops 32000000000 | bytes 16000000 | tf_op jit(solution)/shard_map/mix_backward/pallas_call | solution.py:644
  223.8 0.8 slice_reduce_fusion.4
  224.6 0.1 reshape_squeeze.3
  224.6 0.1 reduce_sum.19
  224.8 0.7 reshape.117
  225.5 0.7 slice.89
  226.1 0.1 reshape.118
  226.2 0.1 concatenate.9
  226.3 0.7 reshape.116
  227.1 0.7 pad_maximum_fusion.vec_ref
  227.8 100.8 %exit_scatter.1 = (bf16[2,128,1536]{2,1,0:T(8,128)(2,1)}, bf16[2,128,1536]{2,1,0:T(8,128)(2,1)}, bf16[2,4,48,1152]{3,2,1,0:T(8,128)(2,1)}, f32[174,128]{1,0:T(8,128)}) custom-call(bf16[2048,1536]{1,0:T(8,128)(2,1)} %bitcast.32, bf16[2048,1152]{1,0:T(8,128)(2,1)} %bitcast.33, bf16[1536,1152]{1,0:T(8,128)(2,1)} %bitcast.34, ...), custom_call_target="tpu_custom_call" | custom-call | bytes 200000000 | tf_op jit(solution)/shard_map/exit_scatter/pallas_call | solution.py:1408
  328.7 1.0 slice.92
  329.7 0.7 slice.94
  330.4 0.6 slice.103
  331.1 0.6 slice_reduce_fusion
  331.7 1.1 copy-done.3
  332.9 1.1 copy-done.4
  334.0 2.9 finish.1
  336.9 0.1 reshape.126
  337.1 0.6 squeeze.17
  337.7 0.6 squeeze.18
  338.2 0.6 squeeze.19
  338.8 0.6 reshape.127
  339.4 1.3 bitcast_divide_fusion
  (32 shorter events, 0.2 us)
Async XLA Ops:
  0.6 10.1 %slice-start = ((bf16[48,6448]{1,0:T(8,128)(2,1)}), bf16[48,6144]{1,0:T(8,128)(2,1)S(1)}, s32[]{:S(2)}) async-start(bf16[48,6448]{1,0:T(8,128)(2,1)} %param.15), calls=%async_computation | async-start | bytes 1179648 | tf_op jit(solution)/shard_map/slice | solution.py:1502
  10.8 1.8 copy-start
  10.9 1.9 copy-start.6
  11.3 2.6 slice-start.1
  227.8 103.9 %copy-start.2 = (bf16[2,128,1536]{2,1,0:T(8,128)(2,1)S(1)}, bf16[2,128,1536]{2,1,0:T(8,128)(2,1)}, u32[]{:S(2)}) copy-start(bf16[2,128,1536]{2,1,0:T(8,128)(2,1)} %cot_ref.3) | copy-start | bytes 2359300
  227.8 103.9 %copy-start.5 = (bf16[2,96,1536]{2,1,0:T(8,128)(2,1)S(1)}, bf16[2,96,1536]{2,1,0:T(8,128)(2,1)}, u32[]{:S(2)}) copy-start(bf16[2,96,1536]{2,1,0:T(8,128)(2,1)} %get-tuple-element.57.rows_ref) | copy-start | bytes 1769476
  328.6 3.1 copy-start.1
  331.7 1.1 copy-start.3
  332.9 1.1 copy-start.4

commit v7 on v6

--- a/solution.py
+++ b/solution.py
@@ -414,7 +414,7 @@
         y = y_ref[q, 0].astype(F32)
         gated = y * silu_z
         scaled_grad = grad_ref[q, 0].astype(F32) * scale
-        gx_ref[KERNEL + 2 : KERNEL + 3, :] += jnp.sum(scaled_grad * gated, axis=0, keepdims=True)
+        gx_ref[KERNEL + 2 : KERNEL + 3, :width] += jnp.sum(scaled_grad * gated, axis=0, keepdims=True)
         grad_gated = gain_ref[...] * scaled_grad - gated * slope
         dy_low = (grad_gated * silu_z).astype(BF16)
         dz = (grad_gated * y * (sig_z + silu_z * (1.0 - sig_z))).astype(BF16)
@@ -492,21 +492,22 @@
             (conv_grad_x, ext_x.at[q], next_x.at[q], params[0], gx_ref),
             (conv_grad_t, ext_t.at[q], next_t.at[q], params[2], gt_ref),
         ):
+            columns = grad.shape[1]
             current = ext[pl.ds(HALO, length), :]
-            sums[KERNEL : KERNEL + 1, :] += jnp.sum(grad, axis=0, keepdims=True)
-            sums[KERNEL - 1 : KERNEL, :] += jnp.sum(grad * current, axis=0, keepdims=True)
+            sums[KERNEL : KERNEL + 1, :columns] += jnp.sum(grad, axis=0, keepdims=True)
+            sums[KERNEL - 1 : KERNEL, :columns] += jnp.sum(grad * current, axis=0, keepdims=True)
             nxt[0:length, :] = grad
             total = weight[KERNEL - 1 : KERNEL, :] * grad
             for back in range(1, KERNEL):
                 tap = KERNEL - 1 - back
                 shifted = jnp.where(offset >= back, ext[pl.ds(HALO - back, length), :], 0.0)
-                sums[tap : tap + 1, :] += jnp.sum(grad * shifted, axis=0, keepdims=True)
+                sums[tap : tap + 1, :columns] += jnp.sum(grad * shifted, axis=0, keepdims=True)
                 ahead = jnp.where(remain >= back, nxt[pl.ds(back, length), :], 0.0)
                 total = total + weight[tap : tap + 1, :] * ahead
             nxt[length:, :] = grad[0:HALO, :]
             results.append(total.astype(BF16))
         results.append(mm_tr(grad_raw, params[5]).astype(BF16))
-        gx_ref[KERNEL + 1 : KERNEL + 2, :] += jnp.sum(dy * xs, axis=0, keepdims=True)
+        gx_ref[KERNEL + 1 : KERNEL + 2, :width] += jnp.sum(dy * xs, axis=0, keepdims=True)
         gh_ref[0:1, :] += jnp.sum(grad_raw, axis=0, keepdims=True)
         gh_ref[1:2, :] += jnp.sum(grad_rate * rate, axis=0, keepdims=True)
         out_ref[q, 0, :, : 2 * width] = jnp.concatenate(results[:2], axis=1)
@@ -528,6 +529,16 @@
 AXES = ("seq", "fsdp")
 MESH = pl.DeviceIdType.MESH
 ANYWHERE = pl.BlockSpec(memory_space=pl.ANY)
+
+
+def lane_rows(width):
+    return -(-width // LANES)
+
+
+def sum_rows(width, seq):
+    shared = D // LANES + (KERNEL + 1) * 2 * STATE // LANES
+    group = (KERNEL + 3) * lane_rows(width) + 2
+    return shared, group, -(-(shared + seq * group) // 8) * 8
 
 
 def whole_spec(shape):
@@ -639,7 +650,7 @@
     tail_at = 2 * width // TAIL
     half, pairs = seq // 2, fsdp // 2
     rows_out = part_out.shape[2]
-    sums = [(8, width), (8, 2 * STATE), (8, LANES)]
+    sums = [(8, lane_rows(width) * LANES), (8, 2 * STATE), (8, LANES)]
     token_own = pltpu.VMEM((seqs, half, length, depth), BF16)
     return pl.pallas_call(
         functools.partial(backward_kernel, seq, fsdp),
@@ -1227,7 +1238,7 @@
 
 def exit_kernel(
     seq, fsdp,
-    h_ref, grad_ref, w_ref, mixed_ref, vec_ref,
+    h_ref, grad_ref, w_ref, mixed_ref, gx_ref, gt_ref, gh_ref,
     dh_out, mixed_out, slots_out, vec_out,
     h_all, grads, weights, part,
     dh_give, dh_own, dh_first, dh_later, part_first, part_top, vec_val, vec_got,
@@ -1239,6 +1250,7 @@
     others = list(range(1, place.pairs))
     seqs, _, length, depth = dh_own.shape
     rows = part.shape[3]
+    width = (weights.shape[1] - TAIL) // 2
     dh = TokenScatter(
         place, links, dh_give, dh_out, dh_own, dh_first, dh_later, loads=False
     )
@@ -1250,20 +1262,31 @@
         links.local(lambda: (w_ref, weights)),
     ]
 
-    def rows_of(top):
-        return pl.ds(half * flip(place.top, top), half)
-
-    def over(top, p):
+    tiles = depth // 2 // TILE
+    high = half // tiles
+
+    def rows_of(top, k):
+        return pl.ds(half * flip(place.top, top) + k * high, high)
+
+    def over(top, k, p):
         return links.far(
             lambda: (
-                part.at[rows_of(top), flip(place.pair, p)],
-                part_first.at[p - 1, rows_of(top)],
+                part.at[rows_of(top, k), flip(place.pair, p)],
+                part_first.at[p - 1, rows_of(top, k)],
                 place.at(pair=p),
             )
         )
 
-    over_pairs = [[over(top, p) for p in others] for top in (0, 1)]
-    cross = links.far(lambda: (part.at[rows_of(1), place.pair], part_top, place.at(top=1)))
+    def crossing(k):
+        return links.far(
+            lambda: (
+                part.at[rows_of(1, k), place.pair], part_top.at[pl.ds(k * high, high)],
+                place.at(top=1),
+            )
+        )
+
+    over_pairs = [[[over(top, k, p) for p in others] for k in range(tiles)] for top in (0, 1)]
+    cross = [crossing(k) for k in range(tiles)]
 
     def row_block(l, c):
         return part.at[
@@ -1288,7 +1311,6 @@
         return links.far(lambda: (vec_val.at[i], vec_got.at[i], place.at(**hops[i])))
 
     vec = [hop(i) for i in range(len(hops))]
-    vec_load = links.local(lambda: (vec_ref, vec_val.at[0]))
     vec_store = links.local(lambda: (vec_val.at[len(hops)], vec_out))
     state = {"at": 0}
 
@@ -1303,34 +1325,51 @@
             else:
                 vec_store.start()
 
-    def add_pairs(top):
-        for i, copy in enumerate(over_pairs[top]):
+    def add_pairs(top, k):
+        for i, copy in enumerate(over_pairs[top][k]):
             copy.wait_recv()
-            for low in range(half):
+            for low in range(high):
                 for c in (0, 1):
-                    at = half * flip(place.top, top) + low
+                    at = half * flip(place.top, top) + k * high + low
                     ref = part.at[at, place.pair, c]
                     add_rows(ref, ref, part_first.at[i, at, c], 16)
 
-    tiles = depth // 2 // TILE
     blocks = TILE // rows
-    per_seq = fsdp
-
-    def weight_rows(top):
-        @pl.loop(0, tiles)
-        def _(k):
-            t = tiles * flip(place.top, top) + k
-            lanes = pl.ds(pl.multiple_of(t * TILE, LANES), TILE)
-            term = tr_mm(h_all[:, lanes], grads[...])
-            for b in range(blocks):
-                at = t * (blocks // per_seq) + b // per_seq if blocks >= per_seq else None
-                part[at, b % per_seq // 2, b % 2] = term[b * rows : (b + 1) * rows].astype(BF16)
-            sums = jnp.sum(term * weights[lanes, :].astype(F32), axis=1, keepdims=True)
-            wide = jnp.broadcast_to(sums, (TILE, LANES))
-            for i in range(TILE // LANES):
-                vec_val[0, pl.ds(t * (TILE // LANES) + i, 1), :] = (
-                    wide[i * LANES : (i + 1) * LANES].T[0:1, :]
-                )
+
+    def weight_rows(top, k):
+        t = tiles * flip(place.top, top) + k
+        lanes = pl.ds(pl.multiple_of(t * TILE, LANES), TILE)
+        term = tr_mm(h_all[:, lanes], grads[...])
+        for b in range(blocks):
+            at = t * (blocks // fsdp) + b // fsdp
+            part[at, b % fsdp // 2, b % 2] = term[b * rows : (b + 1) * rows].astype(BF16)
+        sums = jnp.sum(term * weights[lanes, :].astype(F32), axis=1, keepdims=True)
+        wide = jnp.broadcast_to(sums, (TILE, LANES))
+        for i in range(TILE // LANES):
+            vec_val[0, pl.ds(t * (TILE // LANES) + i, 1), :] = (
+                wide[i * LANES : (i + 1) * LANES].T[0:1, :]
+            )
+        for copy in over_pairs[top][k]:
+            copy.start()
+
+    def place_sums():
+        shared, group, _ = sum_rows(width, seq)
+        vec_val[0] = jnp.zeros_like(vec_val[0])
+        at = D // LANES
+        for tap in range(KERNEL + 1):
+            for j in range(2 * STATE // LANES):
+                vec_val[0, at : at + 1, :] = gt_ref[
+                    tap : tap + 1, j * LANES : (j + 1) * LANES
+                ]
+                at += 1
+        at = shared + place.chunk * group
+        pieces_of = [
+            gx_ref[line : line + 1, j * LANES : (j + 1) * LANES]
+            for line in range(KERNEL + 3)
+            for j in range(lane_rows(width))
+        ] + [gh_ref[0:1, :], gh_ref[1:2, :]]
+        for i, piece in enumerate(pieces_of):
+            vec_val[0, pl.ds(at + i, 1), :] = piece
 
     def token_rows(out, side):
         per_chunk = ROWS // length
@@ -1347,27 +1386,26 @@
 
     for copy in loads:
         copy.start()
-    vec_load.start()
+    place_sums()
     meet_pair(place)
     mixed.begin()
     for copy in loads:
         copy.wait()
-    vec_load.wait()
-    weight_rows(1)
-    for copy in over_pairs[1]:
-        copy.start()
     token_rows(dh_give, 1 - place.core)
     dh.begin()
-    weight_rows(0)
-    for copy in over_pairs[0]:
-        copy.start()
-    vec[0].start()
+    for k in range(tiles):
+        weight_rows(1, k)
     token_rows(dh_own, place.core)
     dh.add_cores()
     dh.send_stage(0)
-    add_pairs(1)
-    cross.start()
-    vec_next()
+    add_pairs(1, 0)
+    cross[0].start()
+    for k in range(tiles):
+        weight_rows(0, k)
+    vec[0].start()
+    for k in range(1, tiles):
+        add_pairs(1, k)
+        cross[k].start()
     stages = len(place.low_bits)
     for i in range(stages):
         dh.add_stage(i)
@@ -1376,9 +1414,11 @@
         else:
             dh_last.begin()
         vec_next()
-    add_pairs(0)
+    for k in range(tiles):
+        add_pairs(0, k)
     vec_next()
-    cross.wait_recv()
+    for copy in cross:
+        copy.wait_recv()
     for l, c in near_peers + [(0, 0)]:
         ref = row_block(l, c)
         add_rows(ref, ref, part_top.at[flip(place.low, l), flip(place.core, c)], 16)
@@ -1391,29 +1431,29 @@
     mixed.finish()
     dh_last.finish()
     dh.finish()
-    cross.wait_send()
-    for copy in over_pairs[0] + over_pairs[1] + vec:
+    for copy in cross + vec + [c for top in over_pairs for tile in top for c in tile]:
         copy.wait_send()
 
 
-def exit_scatter(seq, fsdp, h_all, grad_proj, w_mine, mixed, vector):
+def exit_scatter(seq, fsdp, h_all, grad_proj, w_mine, mixed, sums):
     seqs, _, length, depth = h_all.shape
     half, pairs = seq // 2, fsdp // 2
     cols = w_mine.shape[1]
     rows = depth // (seq * fsdp)
     count = seqs * seq * length
+    vector = (sum_rows((cols - TAIL) // 2, seq)[2], LANES)
     bits = (half.bit_length() - 1) + (pairs.bit_length() - 1) + 2
     token_own = pltpu.VMEM((seqs, half, length, depth), BF16)
     tokens = jax.ShapeDtypeStruct((seqs, length, depth), BF16)
     return pl.pallas_call(
         functools.partial(exit_kernel, seq, fsdp),
-        in_specs=[ANYWHERE] * 5,
+        in_specs=[ANYWHERE] * 4 + [pl.BlockSpec(memory_space=pltpu.VMEM)] * 3,
         out_specs=[ANYWHERE] * 4,
         out_shape=[
             tokens,
             tokens,
             jax.ShapeDtypeStruct((2, half, rows, cols), BF16),
-            jax.ShapeDtypeStruct(vector.shape, F32),
+            jax.ShapeDtypeStruct(vector, F32),
         ],
         scratch_shapes=[
             pltpu.VMEM((count, depth), BF16),
@@ -1424,8 +1464,8 @@
             pltpu.VMEM((seqs, max(half - 1, 1), length, depth), BF16),
             pltpu.VMEM((max(pairs - 1, 1), seq, 2, rows, cols), BF16),
             pltpu.VMEM((half, 2, rows, cols), BF16),
-            pltpu.VMEM((bits + 1,) + vector.shape, F32),
-            pltpu.VMEM((bits,) + vector.shape, F32),
+            pltpu.VMEM((bits + 1,) + vector, F32),
+            pltpu.VMEM((bits,) + vector, F32),
             pltpu.SemaphoreType.DMA((96,)),
             pltpu.SemaphoreType.DMA((96,)),
             pltpu.SemaphoreType.DMA((16,)),
@@ -1437,12 +1477,14 @@
             flops=0, transcendentals=0, bytes_accessed=200_000_000
         ),
         name="exit_scatter",
-    )(h_all.reshape(count, depth), grad_proj.reshape(count, cols), w_mine, mixed, vector)
+    )(h_all.reshape(count, depth), grad_proj.reshape(count, cols), w_mine, mixed, *sums)
 
 
 def finish_kernel(
-    tok_ref, cot_ref, gain_ref, dh_ref, mixed_ref, slots_ref, rows_ref,
-    mixed_out, tokens_out, w_in_out, w_out_out,
+    seq,
+    tok_ref, cot_ref, gain_ref, dh_ref, mixed_ref, slots_ref, rows_ref, vec_ref,
+    mixed_out, tokens_out, gain_in_out, w_in_out, conv_w_out, conv_b_out, heads_out, gain_out_out,
+    w_out_out,
 ):
     gain = gain_ref[...]
     for q in range(tok_ref.shape[0]):
@@ -1466,19 +1508,57 @@
     w_in_out[:, 2 * INNER :] = tail[:, : 2 * STATE + HEADS]
     w_out_out[...] = rows_ref[0].astype(F32) + rows_ref[1].astype(F32)
 
-
-def finish(tokens, cotangent, gain_in, grad_h, mixed, slots, rows, shapes):
+    shared, size, _ = sum_rows(width, seq)
+    heads = HEADS // seq
+    for j in range(D // LANES):
+        at = slice(j * LANES, (j + 1) * LANES)
+        gain_in_out[:, at] = vec_ref[j : j + 1, :] / gain_ref[:, at]
+    row = D // LANES
+    targets = [conv_w_out.at[k : k + 1] for k in range(KERNEL)] + [conv_b_out]
+    for out in targets:
+        for j in range(2 * STATE // LANES):
+            out[:, INNER + j * LANES : INNER + (j + 1) * LANES] = vec_ref[row : row + 1, :]
+            row += 1
+    across = lane_rows(width)
+    lane = iota((8, LANES), 1)
+    per_head = jnp.zeros((8, LANES), F32)
+    fold = expander(across * LANES)
+    for g in range(groups):
+        row = shared + g * size
+
+        def lanes_of(line):
+            first = row + line * across
+            return jnp.concatenate(
+                [vec_ref[first + j : first + j + 1, :] for j in range(across)], axis=1
+            )
+
+        at = slice(g * width, (g + 1) * width)
+        for line, out in enumerate(targets):
+            out[:, at] = lanes_of(line)[:, :width]
+        gain_out_out[:, at] = lanes_of(KERNEL + 2)[:, :width]
+        skip = mm_ones_tr(jnp.broadcast_to(lanes_of(KERNEL + 1), (8, across * LANES)), fold, 3)
+        last = row + (KERNEL + 3) * across
+        lines = jnp.concatenate(
+            [skip[0:1, :], vec_ref[last : last + 2, :], jnp.zeros((5, LANES), F32)], axis=0
+        )
+        lines = jnp.where(lane < heads, lines, 0.0)
+        per_head = per_head + (pltpu.roll(lines, g * heads, 1) if g else lines)
+    heads_out[...] = per_head
+
+
+def finish(seq, tokens, cotangent, gain_in, grad_h, mixed, slots, rows, vector, shapes):
+    columns = INNER + 2 * STATE
+    kinds = [
+        (tokens.shape, BF16), (tokens.shape, F32), ((1, D), F32), (shapes[0], F32),
+        ((KERNEL, columns), F32), ((1, columns), F32), ((8, LANES), F32), ((1, INNER), F32),
+        (shapes[1], F32),
+    ]
     return pl.pallas_call(
-        finish_kernel,
-        out_shape=[
-            jax.ShapeDtypeStruct(tokens.shape, BF16),
-            jax.ShapeDtypeStruct(tokens.shape, F32),
-            jax.ShapeDtypeStruct(shapes[0], F32),
-            jax.ShapeDtypeStruct(shapes[1], F32),
-        ],
+        functools.partial(finish_kernel, seq),
+        out_shape=[jax.ShapeDtypeStruct(*kind) for kind in kinds],
         compiler_params=pltpu.CompilerParams(vmem_limit_bytes=32 << 20),
         name="finish",
-    )(tokens, cotangent, gain_in[None], grad_h, mixed, slots, rows)
+    )(tokens, cotangent, gain_in[None], grad_h, mixed, slots, rows, vector)
 
 
 def local(
@@ -1525,48 +1605,20 @@
         steps, shards,
     )
 
-    grouped = jnp.concatenate(
-        [
-            sums_x[: KERNEL + 1].reshape(-1),
-            sums_x[KERNEL + 2],
-            jnp.sum(sums_x[KERNEL + 1].reshape(heads, HEAD_DIM), axis=-1),
-            sums_h[:2, :heads].reshape(-1),
-        ]
+    grad_h, mixed, slots, vector = exit_scatter(
+        steps, shards, h_all, grad_proj, w_mine, mixed, (sums_x, sums_t, sums_h)
     )
-    size = -(-grouped.shape[0] // LANES) * LANES
-    grouped = jnp.pad(grouped, (0, size - grouped.shape[0])).reshape(1, -1, LANES)
-    grouped = lax.dynamic_update_slice_in_dim(
-        jnp.zeros((steps,) + grouped.shape[1:], F32), grouped, number, 0
+    (
+        mixed, tokens_grad, gain_in_grad, w_in_grad, conv_w_grad, conv_b_grad, per_head,
+        gain_out_grad, w_out_grad,
+    ) = finish(
+        steps, tokens, cotangent, gain_in, grad_h, mixed,
+        slots.reshape(steps, rows_in, 2 * width + TAIL), rows, vector, (w_in.shape, w_out.shape),
     )
-    vector = jnp.concatenate(
-        [
-            jnp.zeros((D // LANES, LANES), F32),
-            sums_t[: KERNEL + 1].reshape(-1, LANES),
-            grouped.reshape(-1, LANES),
-        ]
-    )
-    grad_h, mixed, slots, vector = exit_scatter(
-        steps, shards, h_all, grad_proj, w_mine, mixed, vector
-    )
-    mixed, tokens_grad, w_in_grad, w_out_grad = finish(
-        tokens, cotangent, gain_in, grad_h, mixed,
-        slots.reshape(steps, rows_in, 2 * width + TAIL), rows, (w_in.shape, w_out.shape),
-    )
-
-    edge = vector.shape[0] - steps * size // LANES
-    everywhere = vector[:edge].reshape(-1)
-    grouped = vector[edge:].reshape(steps, size)
-    gain_in_grad = everywhere[:D] / gain_in
-    conv_x = grouped[:, : (KERNEL + 1) * width].reshape(steps, KERNEL + 1, width)
-    conv_x = conv_x.transpose(1, 0, 2).reshape(KERNEL + 1, INNER)
-    conv_grads = jnp.concatenate([conv_x, everywhere[D:].reshape(KERNEL + 1, -1)], axis=1)
-    rest = grouped[:, (KERNEL + 1) * width :]
-    gain_out_grad = rest[:, :width].reshape(-1)
-    per_head = rest[:, width : width + 3 * heads].reshape(steps, 3, heads)
-    per_head = per_head.transpose(1, 0, 2).reshape(3, HEADS)
     return (
-        mixed, tokens_grad, gain_in_grad, w_in_grad, conv_grads[:KERNEL], conv_grads[KERNEL],
-        per_head[1], per_head[2], per_head[0], gain_out_grad, w_out_grad,
+        mixed, tokens_grad, gain_in_grad[0], w_in_grad, conv_w_grad, conv_b_grad[0],
+        per_head[1, :HEADS], per_head[2, :HEADS], per_head[0, :HEADS], gain_out_grad[0],
+        w_out_grad,
     )
 
 

time: 343 us -> 330 us (0.962)
  local copies, waits for them, and re-layouts: 22.2 us -> 16.1 us
  Pallas kernels: 313 us -> 308 us
    pallas_call x1, Pallas kernels: 101 us -> 95.5 us  [exit_scatter(): pl.pallas_call(functools.partial(exit_kernel, seq, fsdp), in_specs=[ANYWH...]
    slice x10 -> x0, local copies, waits for them, and re-layouts: 4.48 us -> none  [the longest x1 0.97 us: local(): grouped = vector[edge:].reshape(steps, size)]
where the time goes in v7:
time: 330 us; the launch traced here: 328 us
  Pallas kernels  308 us (93%)
  local copies, waits for them, and re-layouts  16.1 us (5%)
  other arithmetic  3.87 us (1%)
    pallas_call x1, Pallas kernels, forward_mix(): pl.pallas_call(functools.partial(forward_kernel, seq, fsdp), grid=(seq +...  159 us
    pallas_call x1, Pallas kernels, exit_scatter(): pl.pallas_call(functools.partial(exit_kernel, seq, fsdp), in_specs=[ANYWH...  95.5 us
    pallas_call x1, Pallas kernels, backward_mix(): pl.pallas_call(functools.partial(backward_kernel, seq, fsdp), grid=(steps...  50.4 us

profile of v7, /device:TPU:1, one launch (start us, length us, event | category | flops | bytes accessed | tf_op | source)
XLA Modules:
  0.0 328.3 jit_solution(13220664783939265509)
XLA Ops:
  0.6 0.0 slice-start
  0.7 0.8 dynamic-slice_bitcast_fusion
  1.5 0.6 select_maximum_fusion.hp_ref
  2.1 0.8 slice.29
  2.9 0.6 constant_dynamic-slice_fusion.wx_ref
  3.5 0.7 slice.30
  4.2 0.1 dynamic-slice.6
  4.3 0.6 dynamic_slice.19.bx_ref
  4.8 0.7 dynamic_slice.22
  5.6 0.1 broadcast_in_dim.15
  5.6 0.6 broadcast_in_dim_reshape.3.skip_ref
  6.2 0.8 dynamic-slice.7
  7.0 0.6 dynamic_slice.23.gain_ref
  7.6 0.6 fusion.4.pick_ref
  8.2 1.3 slice.31.wt_ref
  9.5 1.3 slice.32
  10.8 0.0 slice-done
  10.8 0.0 copy-start
  10.8 0.1 copy.24
  10.9 0.0 copy-start.7
  10.9 0.5 copy.26
  11.4 0.0 slice-start.1
  11.4 1.2 reshape.64.zx_ref
  12.6 0.0 copy-done
  12.6 0.2 fusion
  12.8 0.0 copy-done.7
  12.8 1.1 fusion.2.h_ref
  13.9 0.0 slice-done.1
  13.9 0.6 pad.8.tail_ref
  14.6 158.7 %mix_forward.1 = (bf16[2,8,128,1152]{3,2,1,0:T(8,128)(2,1)}, bf16[2,8,128,384]{3,2,1,0:T(8,128)(2,1)}, bf16[2,8,128,384]{3,2,1,0:T(8,128)(2,1)}, f32[2,8,128,1]{...) custom-call(bf16[2,128,1536]{2,1,0:T(8,128)(2,1)} %fusion.2.h_ref, ...), custom_call_target="tpu_custom_call" | custom-call | flops 30000001024 | bytes 60000000 | tf_op jit(solution)/shard_map/mix_forward/pallas_call | solution.py:585
  173.2 50.4 %mix_backward.1 = (bf16[2,8,128,1152]{3,2,1,0:T(8,128)(2,1)}, f32[8,384]{1,0:T(8,128)}, f32[8,256]{1,0:T(8,128)}, f32[8,128]{1,0:T(8,128)}, bf16[2,128,1536]{2,1,0:T(8,128)(2,1)}, /*index=5*/bf16[2,96,1536]{2,1,0:T(8,128)(2,1)}) custom-call(bf16[2,8,128,1152]{3,2,1,0:T(8,128)(2,1)} %get-tuple-element.43.zx_ref.zxh_ref.tail_ref.tailh_ref, ...), custom_call_target="tpu_custom_call" | custom-call | flops 32000000000 | bytes 16000000 | tf_op jit(solution)/shard_map/mix_backward/pallas_call | solution.py:655
  223.7 0.0 copy-start.2
  223.7 0.0 copy-start.5
  223.7 95.5 %exit_scatter.1 = (bf16[2,128,1536]{2,1,0:T(8,128)(2,1)}, bf16[2,128,1536]{2,1,0:T(8,128)(2,1)}, bf16[2,4,48,1152]{3,2,1,0:T(8,128)(2,1)}, f32[208,128]{1,0:T(8,128)}) custom-call(bf16[2048,1536]{1,0:T(8,128)(2,1)} %bitcast.27, bf16[2048,1152]{1,0:T(8,128)(2,1)} %bitcast.28, bf16[1536,1152]{1,0:T(8,128)(2,1)} %bitcast.29, ...), custom_call_target="tpu_custom_call" | custom-call | bytes 200000000 | tf_op jit(solution)/shard_map/exit_scatter/pallas_call | solution.py:1448
  319.2 0.0 copy-done.2
  319.2 0.0 copy-done.5
  319.2 0.0 copy-start.1
  319.2 1.2 copy-done.1
  320.4 0.0 copy-start.3
  320.4 1.1 copy-done.3
  321.5 0.0 copy-start.4
  321.5 1.1 copy-done.4
  322.7 0.0 copy-start.6
  322.7 0.9 copy-done.6
  323.5 3.0 finish.1
  326.5 0.6 reduce.1
  327.2 0.6 reduce
  327.8 0.5 slice_bitcast_fusion
  (4 shorter events, 0.0 us)
Async XLA Ops:
  0.6 10.2 %slice-start = ((bf16[48,6448]{1,0:T(8,128)(2,1)}), bf16[48,6144]{1,0:T(8,128)(2,1)S(1)}, s32[]{:S(2)}) async-start(bf16[48,6448]{1,0:T(8,128)(2,1)} %param.15), calls=%async_computation | async-start | bytes 1179648 | tf_op jit(solution)/shard_map/slice | solution.py:1582
  10.8 1.8 copy-start
  10.9 1.9 copy-start.7
  11.4 2.6 slice-start.1
  223.7 95.5 %copy-start.2 = (bf16[2,128,1536]{2,1,0:T(8,128)(2,1)S(1)}, bf16[2,128,1536]{2,1,0:T(8,128)(2,1)}, u32[]{:S(2)}) copy-start(bf16[2,128,1536]{2,1,0:T(8,128)(2,1)} %cot_ref.3) | copy-start | bytes 2359300
  223.7 95.5 %copy-start.5 = (bf16[2,96,1536]{2,1,0:T(8,128)(2,1)S(1)}, bf16[2,96,1536]{2,1,0:T(8,128)(2,1)}, u32[]{:S(2)}) copy-start(bf16[2,96,1536]{2,1,0:T(8,128)(2,1)} %get-tuple-element.62.rows_ref) | copy-start | bytes 1769476
  319.2 1.2 copy-start.1
  320.4 1.1 copy-start.3
  321.5 1.1 copy-start.4
  322.7 0.9 copy-start.6

commit v8 on v7

--- a/solution.py
+++ b/solution.py
@@ -164,14 +164,31 @@
     return flat[...]
 
 
+def pick_params(place, pack_ref, cx_ref, hp_ref, pick_ref):
+    width = cx_ref.shape[1]
+    heads = width // HEAD_DIM
+    mine = jnp.zeros((8, width), F32)
+    for g in range(INNER // width):
+        mine = mine + jnp.where(place.chunk == g, pack_ref[:, g * width : (g + 1) * width], 0.0)
+    lane, source = iota((LANES, LANES), 1), iota((LANES, LANES), 0)
+    pick = ((lane < heads) & (source == lane + place.chunk * heads)).astype(BF16)
+    pick_ref[...] = pick
+    lines = [pack_ref[6:7, i * LANES : (i + 1) * LANES] for i in range(3)]
+    lines = jnp.concatenate(lines + [jnp.zeros((5, LANES), F32)], axis=0)
+    lines = mm_ones(lines, pick, 3)
+    hp_ref[...] = lines
+    cx_ref[...] = mine
+    cx_ref[6:7, :] = mm_ones(lines, expander(width), 3)[2:3, :]
+
+
 def forward_kernel(
     seq, fsdp,
     h_ref, zx_ref, tail_ref, seg_ref, cot_ref, ow_ref,
-    wx_ref, bx_ref, wt_ref, bt_ref, hp_ref, pick_ref, skip_ref, gain_ref,
+    pack_ref,
     proj_ref, y_ref, state_ref, off_ref, rem_ref, offr_ref,
-    h_out, w_out, grad_out, stat_out, mixed_out, pout_out,
-    h_v, w_v, w_flat, seg_v, cot_v, ow_v, ow_flat, gated_v, sums_v, sums_got, grad_v, mixed_v,
-    pout_v, memory, ext_x, ext_t, last_rows, send, recv, near,
+    h_out, w_out, grad_out, stat_out, mixed_out, pout_out, cx_ref, hp_ref, pick_ref,
+    h_v, w_v, w_flat, seg_v, cot_v, ow_v, ow_flat, gated_v, sums_v, sums_got, grad_v, mix_give,
+    mix_own, mix_first, pout_v, memory, ext_x, ext_t, last_rows, send, recv, near,
 ):
     seqs, _, length, width = y_ref.shape
     depth = h_v.shape[3]
@@ -193,10 +210,16 @@
 
     sums = [send_sums(i) for i in range(len(near_peers))]
 
+    def send_core(q):
+        return links.far(lambda: (mix_give.at[q], mix_first.at[q], place.at(core=1)))
+
+    cores = [send_core(q) for q in range(seqs)]
+
     @pl.when(step_at == 0)
     def _():
         memory[...] = jnp.zeros_like(memory)
         last_rows[...] = jnp.zeros_like(last_rows)
+        pick_params(place, pack_ref, cx_ref, hp_ref, pick_ref)
         meet_pair(place)
         entry.run(cot.cross_over)
         if w_v.shape[-2] % HALO:
@@ -236,7 +259,12 @@
             h_v[:, step_at].reshape(seqs * length, depth), weights, preferred_element_type=F32
         ).astype(BF16)
         proj_ref[...] = proj.reshape(proj_ref.shape)
-        params = tuple(r[...] for r in (wx_ref, bx_ref, wt_ref, bt_ref, hp_ref, pick_ref))
+        params = (
+            cx_ref[:KERNEL, :], cx_ref[KERNEL : KERNEL + 1, :],
+            pack_ref[:KERNEL, INNER:], pack_ref[KERNEL : KERNEL + 1, INNER:],
+            hp_ref[...], pick_ref[...],
+        )
+        gain_row, skip_row = cx_ref[KERNEL + 1 : KERNEL + 2, :], cx_ref[KERNEL + 2 : KERNEL + 3, :]
         for q in range(seqs):
             offset, remain = positions(seg_v[q : q + 1, :], step_at, length)
             off_ref[q, 0] = offset
@@ -262,7 +290,7 @@
             old = memory[q]
             old_low = old.astype(BF16)
             state_ref[q, 0] = old_low
-            outside = mm(cs, old_low) * entry_x + skip_ref[...] * xs
+            outside = mm(cs, old_low) * entry_x + skip_row * xs
             squares = jnp.zeros((length, 1), F32)
             for start, size, heads in head_tiles(width):
                 mixing = []
@@ -278,7 +306,7 @@
                 z = zx[:, start : start + size].astype(F32)
                 gated = y_low.astype(F32) * (z * sigmoid(z))
                 gated_v[here, start : start + size] = (
-                    gated * gain_ref[:, start : start + size]
+                    gated * gain_row[:, start : start + size]
                 ).astype(BF16)
                 squares = squares + jnp.sum(gated * gated, axis=1, keepdims=True)
             sums_v[pl.ds(2 * (q * seq + step_at), 1), :] = jnp.broadcast_to(
@@ -313,6 +341,22 @@
         grad_store.start()
         for copy in sums:
             copy.start()
+
+        def mixed_rows(out, side):
+            per_side = seq // 2 // 2
+            for q in range(seqs):
+
+                @pl.loop(0, per_side)
+                def _(k):
+                    at = (q * seq + seq // 2 * side + 2 * k) * length
+                    rows = gated_v[pl.ds(pl.multiple_of(at, tile), tile), :]
+                    mixed = jnp.dot(rows, rows_out, preferred_element_type=F32)
+                    out[q, pl.ds(2 * k, 2)] = mixed.astype(BF16).reshape(2, length, depth)
+
+        mixed_rows(mix_give, 1 - place.core)
+        for copy in cores:
+            copy.start()
+        mixed_rows(mix_own, place.core)
         for copy in sums:
             copy.wait_recv()
         total = sums_v[...]
@@ -331,18 +375,21 @@
                 for i in (0, 1)
             ]
             scale_col = jnp.concatenate(scales, axis=0)
-            gated = gated_v[at, :]
-            mixed = jnp.dot(gated, rows_out, preferred_element_type=F32)
-            mixed_v[at, :] = (mixed * scale_col).astype(BF16)
-            gated_v[at, :] = (gated.astype(F32) * scale_col).astype(BF16)
-
-        mixed_store = links.local(lambda: (mixed_v, mixed_out))
-        mixed_store.start()
+            gated_v[at, :] = (gated_v[at, :].astype(F32) * scale_col).astype(BF16)
+
         pout_v[...] = tr_mm(gated_v[...], cot_v[...].reshape(-1, depth)).astype(BF16)
         pout_store = links.local(lambda: (pout_v, pout_out))
         pout_store.start()
+        for q in range(seqs):
+            cores[q].wait_recv()
+            for low in range(seq // 2):
+                add_rows(mix_own.at[q, low], mix_own.at[q, low], mix_first.at[q, low])
+        mixed_store = links.local(lambda: (mix_own, mixed_out))
+        mixed_store.start()
         for copy in [grad_store, mixed_store, pout_store] + keep:
             copy.wait()
+        for copy in cores:
+            copy.wait_send()
         for copy in sums:
             copy.wait_send()
         entry.finish()
@@ -351,18 +398,18 @@
 def backward_kernel(
     seq, fsdp,
     zx_ref, zxh_ref, tail_ref, tailh_ref, off_ref, offr_ref, rem_ref, y_ref, grad_ref, stat_ref,
-    state_ref, mixed_ref, pout_ref,
-    wx_ref, bx_ref, wt_ref, bt_ref, hp_ref, pick_ref, skip_ref, gain_ref,
+    state_ref, all_stat_ref, mixed_ref, pout_ref,
+    cx_ref, ct_ref, hp_ref, pick_ref,
     out_ref, gx_ref, gt_ref, gh_ref, mixed_out, rows_out,
     memory, ext_x, ext_t, next_x, next_t,
-    mix_own, mix_first, mix_later, pout_own, pout_first, send, recv, near,
+    mix_own, mix_later, pout_own, pout_first, send, recv, near,
 ):
     seqs, _, length, width = y_ref.shape
     step_at = pl.program_id(0)
 
     place = Place(seq, fsdp)
     links = Links(send, recv, near)
-    mixed = TokenScatter(place, links, mixed_ref, mixed_out, mix_own, mix_first, mix_later)
+    mixed = TokenScatter(place, links, mixed_ref, mixed_out, mix_own, None, mix_later, "halves")
     w_rows = RowScatter(place, links, pout_ref, rows_out, pout_own, pout_first)
     stages = len(place.low_bits)
 
@@ -372,16 +419,16 @@
         mixed.begin()
         w_rows.begin()
 
-    @pl.when(step_at == 2)
+    @pl.when(step_at == 1)
     def _():
         mixed.add_cores()
         mixed.send_stage(0)
 
-    @pl.when(step_at == 4)
+    @pl.when(step_at == 3)
     def _():
         w_rows.add_pairs()
 
-    @pl.when(step_at == pl.num_programs(0) - 2)
+    @pl.when(step_at == pl.num_programs(0) - 3)
     def _():
         mixed.add_stage(0)
         if stages > 1:
@@ -396,7 +443,12 @@
         next_x[:, length:, :] = jnp.zeros_like(next_x[:, length:, :])
         next_t[:, length:, :] = jnp.zeros_like(next_t[:, length:, :])
 
-    params = tuple(r[...] for r in (wx_ref, bx_ref, wt_ref, bt_ref, hp_ref, pick_ref))
+    params = (
+        cx_ref[:KERNEL, :], cx_ref[KERNEL : KERNEL + 1, :],
+        ct_ref[:KERNEL, :], ct_ref[KERNEL : KERNEL + 1, :],
+        hp_ref[...], pick_ref[...],
+    )
+    gain_row, skip_row = cx_ref[KERNEL + 1 : KERNEL + 2, :], cx_ref[KERNEL + 2 : KERNEL + 3, :]
     for q in range(seqs):
         offset = off_ref[q, 0]
         conv_x, conv_t, raw, step, rate, decay_rate, cumul, spread, step_x, entry_x, end_x = (
@@ -415,7 +467,7 @@
         gated = y * silu_z
         scaled_grad = grad_ref[q, 0].astype(F32) * scale
         gx_ref[KERNEL + 2 : KERNEL + 3, :width] += jnp.sum(scaled_grad * gated, axis=0, keepdims=True)
-        grad_gated = gain_ref[...] * scaled_grad - gated * slope
+        grad_gated = gain_row * scaled_grad - gated * slope
         dy_low = (grad_gated * silu_z).astype(BF16)
         dz = (grad_gated * y * (sig_z + silu_z * (1.0 - sig_z))).astype(BF16)
         dy = dy_low.astype(F32)
@@ -447,10 +499,10 @@
             dy_tile = masked_heads(dy_low[:, start : start + size], heads)
             grad_mix = mm_tr(scaled_low[:, start : start + size], dy_tile)
             mixing = []
-            for place, head in enumerate(heads):
+            for i, head in enumerate(heads):
                 spans = cumul_t[head : head + 1, :] - cumul[:, head : head + 1]
                 decays = jnp.exp(jnp.where(same, spans, -1e30))
-                weighted = grad_mix[:, place * length : (place + 1) * length] * decays
+                weighted = grad_mix[:, i * length : (i + 1) * length] * decays
                 grad_scores = grad_scores + weighted
                 mixing.append((decays * scores).astype(BF16))
                 terms = jnp.where(strict, weighted * scores, 0.0).astype(BF16)
@@ -483,7 +535,7 @@
         grad_b = mm(grad_scores_low, cs) + mm_tr(scaled * end_x, state_low)
         grad_c = tr_mm(grad_scores_low, bs) + mm_tr(entry_dy_low, old)
         memory[q] = grad_state * keep_row + tr_mm(cs, entry_dy_low)
-        conv_grad_x = (skip_ref[...] * dy + step_x * grad_scaled) * slope_x
+        conv_grad_x = (skip_row * dy + step_x * grad_scaled) * slope_x
         conv_grad_t = jnp.concatenate([grad_b, grad_c], axis=1) * slope_t
 
         remain = rem_ref[q, 0]
@@ -520,6 +572,11 @@
             mixed.add_stage(stage)
             if stage + 1 < stages:
                 mixed.send_stage(stage + 1)
+        for q in range(seqs):
+            row = all_stat_ref[pl.ds(2 * (q * seq + place.chunk), 1), :]
+            column = jnp.broadcast_to(row, (LANES, length)).T[:, 0:1]
+            done = mix_own.at[q, place.low]
+            done[...] = (done[...].astype(F32) * column).astype(BF16)
         mixed.store()
         w_rows.finish()
         mixed.finish()
@@ -561,7 +618,7 @@
     return block, before
 
 
-def forward_mix(normed, zx, tail, segments, cotangent, out_w, consts, seq, fsdp):
+def forward_mix(normed, zx, tail, segments, cotangent, out_w, packed, seq, fsdp):
     seqs, length, depth = normed.shape
     rows = tail.shape[0]
     cols = zx.shape[2] + TAIL
@@ -585,10 +642,11 @@
     outs = pl.pallas_call(
         functools.partial(forward_kernel, seq, fsdp),
         grid=(seq + 1,),
-        in_specs=[ANYWHERE] * 6 + [whole_spec(v.shape) for v in consts],
+        in_specs=[ANYWHERE] * 6 + [whole_spec(packed.shape)],
         out_specs=[
             block(cols), block(width), block(width, STATE), block(1), block(1), block(length, 1),
             ANYWHERE, ANYWHERE, ANYWHERE, whole_spec(sums), ANYWHERE, ANYWHERE,
+            whole_spec((8, width)), whole_spec((8, LANES)), whole_spec((LANES, LANES)),
         ],
         out_shape=[
             blocks(cols, BF16), blocks(width, BF16), blocks(width, BF16, STATE),
@@ -597,8 +655,11 @@
             jax.ShapeDtypeStruct(w_shape, BF16),
             jax.ShapeDtypeStruct((count, width), F32),
             jax.ShapeDtypeStruct(sums, F32),
-            jax.ShapeDtypeStruct((count, depth), BF16),
+            jax.ShapeDtypeStruct((seqs, seq // 2, length, depth), BF16),
             jax.ShapeDtypeStruct((width, depth), BF16),
+            jax.ShapeDtypeStruct((8, width), F32),
+            jax.ShapeDtypeStruct((8, LANES), F32),
+            jax.ShapeDtypeStruct((LANES, LANES), BF16),
         ],
         scratch_shapes=[
             pltpu.VMEM((seqs, seq, length, depth), BF16),
@@ -612,7 +673,9 @@
             pltpu.VMEM(sums, F32),
             pltpu.VMEM((seq - 1,) + sums, F32),
             pltpu.VMEM((count, width), F32),
-            pltpu.VMEM((count, depth), BF16),
+            pltpu.VMEM((seqs, seq // 2, length, depth), BF16),
+            pltpu.VMEM((seqs, seq // 2, length, depth), BF16),
+            pltpu.VMEM((seqs, seq // 2, length, depth), BF16),
             pltpu.VMEM((width, depth), BF16),
             pltpu.VMEM((seqs, STATE, width), F32),
             pltpu.VMEM((seqs, HALO + length, width), F32),
@@ -630,18 +693,17 @@
             flops=30_000_000_000, transcendentals=0, bytes_accessed=60_000_000
         ),
         name="mix_forward",
-    )(normed, zx, tail, segments, cotangent, out_w, *consts)
-    proj, y, states, off_col, rem_col, off_row, h_all, w_mine, grad_yn, stats, mixed, part = outs
+    )(normed, zx, tail, segments, cotangent, out_w, packed)
+    proj, y, states, off_col, rem_col, off_row, h_all, w_mine, grad_yn, stats, mixed, part = outs[:12]
     shape = (seqs, seq, length)
     return (
         proj, y, states, off_col, rem_col, off_row, h_all, w_mine.reshape(depth, cols),
-        grad_yn.reshape(shape + (width,)), stats.reshape(seqs, seq, 2, length),
-        mixed.reshape(shape + (depth,)), part.reshape(out_shape),
+        grad_yn.reshape(shape + (width,)), stats, mixed, part.reshape(out_shape), outs[12:],
     )
 
 
 def backward_mix(
-    proj, off_col, off_row, rem_col, y, grad_yn, stats, states, mixed, part_out, consts, seq, fsdp
+    proj, off_col, off_row, rem_col, y, grad_yn, stats, states, mixed, part_out, packed, consts, seq, fsdp
 ):
     seqs, steps, length, cols = proj.shape
     depth = mixed.shape[3]
@@ -658,9 +720,11 @@
         in_specs=[
             block(2 * width), before(2 * width), block(TAIL, tail_at), before(TAIL, tail_at),
             block(1), block(length, 0, 1), block(1), block(width), block(width),
-            block(length, 0, 2), block(width, 0, STATE), ANYWHERE, ANYWHERE,
-        ]
-        + [whole_spec(v.shape) for v in consts],
+            block(length, 0, 2), block(width, 0, STATE), whole_spec(stats.shape),
+            ANYWHERE, ANYWHERE, whole_spec(consts[0].shape),
+            pl.BlockSpec((8, 2 * STATE), lambda i: (0, INNER // (2 * STATE))),
+            whole_spec(consts[1].shape), whole_spec(consts[2].shape),
+        ],
         out_specs=[block(cols)] + [whole_spec(v) for v in sums] + [ANYWHERE, ANYWHERE],
         scratch_shapes=[
             pltpu.VMEM((seqs, STATE, width), F32),
@@ -668,7 +732,7 @@
             pltpu.VMEM((seqs, HALO + length, 2 * STATE), F32),
             pltpu.VMEM((seqs, length + HALO, width), F32),
             pltpu.VMEM((seqs, length + HALO, 2 * STATE), F32),
-            token_own, token_own, pltpu.VMEM((seqs, max(half - 1, 1), length, depth), BF16),
+            token_own, pltpu.VMEM((seqs, max(half - 1, 1), length, depth), BF16),
             pltpu.VMEM((2, rows_out, depth), BF16),
             pltpu.VMEM((max(pairs - 1, 1), 2, rows_out, depth), BF16),
             pltpu.SemaphoreType.DMA((64,)),
@@ -690,8 +754,9 @@
         ),
         name="mix_backward",
     )(
-        proj, proj, proj, proj, off_col, off_row, rem_col, y, grad_yn, stats, states, mixed,
-        part_out, *consts,
+        proj, proj, proj, proj, off_col, off_row, rem_col, y, grad_yn,
+        stats.reshape(seqs, steps, 2, length), states, stats, mixed, part_out, consts[0], packed,
+        consts[1], consts[2],
     )
 
 
@@ -1075,26 +1140,17 @@
 
 
 class TokenScatter:
-    def __init__(self, place, links, src, out, own, first, later, loads=True):
+    def __init__(self, place, links, src, out, own, first, later, held):
         self.place = place
         self.out, self.own, self.first, self.later = out, own, first, later
         self.seqs = src.shape[0]
         half = place.half
 
         def give(q):
-            def make():
-                part = src.at[q, pl.ds(half * (1 - place.core), half)] if loads else src.at[q]
-                return part, first.at[q], place.at(core=1)
-
-            return links.far(make)
-
-        def keep(q):
-            return links.local(
-                lambda: (src.at[q, pl.ds(half * place.core, half)], own.at[q])
-            )
-
-        self.cores = [give(q) for q in range(self.seqs)]
-        self.loads = [keep(q) for q in range(self.seqs)] if loads else []
+            return links.far(lambda: (src.at[q], first.at[q], place.at(core=1)))
+
+        self.cores = [give(q) for q in range(self.seqs)] if held == "give" else []
+        self.loads = [links.local(lambda: (src, own))] if held == "halves" else []
         self.stages = [[] for _ in place.low_bits]
         for q in range(self.seqs):
             live, slot = list(range(half)), 0
@@ -1118,10 +1174,10 @@
             copy.start()
 
     def add_cores(self):
-        for q in range(self.seqs):
-            if self.loads:
-                self.loads[q].wait()
-            self.cores[q].wait_recv()
+        for copy in self.loads:
+            copy.wait()
+        for q, copy in enumerate(self.cores):
+            copy.wait_recv()
             for low in range(self.place.half):
                 add_rows(self.own.at[q, low], self.own.at[q, low], self.first.at[q, low])
 
@@ -1252,7 +1308,7 @@
     rows = part.shape[3]
     width = (weights.shape[1] - TAIL) // 2
     dh = TokenScatter(
-        place, links, dh_give, dh_out, dh_own, dh_first, dh_later, loads=False
+        place, links, dh_give, dh_out, dh_own, dh_first, dh_later, "give"
     )
     dh_last = Deliver(place, links, lambda: dh_own.at[:, place.low], dh_out)
     mixed = Deliver(place, links, lambda: mixed_ref, mixed_out)
@@ -1569,12 +1625,7 @@
     place = Place(steps, shards)
     seqs, length, _ = tokens.shape
     width = INNER // steps
-    heads = HEADS // steps
     rows_in = w_in.shape[0]
-    number = place.chunk
-
-    def mine(array, size):
-        return lax.dynamic_slice_in_dim(array, number * size, size, array.ndim - 1)
 
     wide = tokens.astype(F32)
     scale_in = lax.rsqrt(jnp.mean(wide * wide, axis=-1, keepdims=True) + EPSILON)
@@ -1582,27 +1633,27 @@
     zx = w_in[:, : 2 * INNER].reshape(rows_in, 2, steps, width).transpose(2, 0, 1, 3)
     zx = zx.reshape(steps, rows_in, 2 * width)
     tail = jnp.pad(w_in[:, 2 * INNER :], ((0, 0), (0, LANES - HEADS)))
-    heads_p = jnp.stack([mine(dt_bias, heads), mine(a_log, heads)])
-    lane = lax.broadcasted_iota(jnp.int32, (LANES, LANES), 1)
-    source = lax.broadcasted_iota(jnp.int32, (LANES, LANES), 0)
-    pick = ((lane < heads) & (source == lane + number * heads)).astype(BF16)
-    consts = (
-        mine(conv_w[:, :INNER], width),
-        mine(conv_b[None, :INNER], width),
-        conv_w[:, INNER:],
-        conv_b[None, INNER:],
-        jnp.pad(heads_p, ((0, 6), (0, LANES - heads))),
-        pick,
-        jnp.repeat(mine(skip, heads), HEAD_DIM)[None],
-        mine(gain_out[None], width),
+    columns = INNER + 2 * STATE
+
+    def line(*arrays):
+        arrays = [jnp.pad(v, (0, -v.shape[0] % LANES)) for v in arrays]
+        return jnp.pad(jnp.concatenate(arrays), (0, columns - sum(v.shape[0] for v in arrays)))
+
+    packed = jnp.concatenate(
+        [
+            conv_w,
+            jnp.stack(
+                [conv_b, line(gain_out), line(dt_bias, a_log, skip), jnp.zeros((columns,), F32)]
+            ),
+        ]
     )
-
     (
         proj, y, states, off_col, rem_col, off_row, h_all, w_mine, grad_yn, stats, mixed, part_out,
-    ) = forward_mix(normed, zx, tail, segments, cotangent, w_out, consts, steps, shards)
+        consts,
+    ) = forward_mix(normed, zx, tail, segments, cotangent, w_out, packed, steps, shards)
     grad_proj, sums_x, sums_t, sums_h, mixed, rows = backward_mix(
-        proj, off_col, off_row, rem_col, y, grad_yn, stats, states, mixed, part_out, consts,
-        steps, shards,
+        proj, off_col, off_row, rem_col, y, grad_yn, stats, states, mixed, part_out,
+        packed, consts, steps, shards,
     )
 
     grad_h, mixed, slots, vector = exit_scatter(

time: 330 us -> 323 us (0.979)
  local copies, waits for them, and re-layouts: 16.1 us -> 10.2 us
    slice x4 -> x0, local copies, waits for them, and re-layouts: 4.07 us -> none  [the longest x1 1.28 us: local(): conv_b[None, INNER:]]
where the time goes in v8:
time: 323 us
  Pallas kernels  308 us (95%)
  local copies, waits for them, and re-layouts  10.2 us (3%)
  other arithmetic  3.39 us (1%)
    pallas_call x1, Pallas kernels, forward_mix(): pl.pallas_call(functools.partial(forward_kernel, seq, fsdp), grid=(seq +...  158 us
    pallas_call x1, Pallas kernels, exit_scatter(): pl.pallas_call(functools.partial(exit_kernel, seq, fsdp), in_specs=[ANYWH...  96.8 us
    pallas_call x1, Pallas kernels, backward_mix(): pl.pallas_call(functools.partial(backward_kernel, seq, fsdp), grid=(steps...  50.8 us

profile of v8, /device:TPU:1, one launch (start us, length us, event | category | flops | bytes accessed | tf_op | source)
XLA Modules:
  0.0 322.7 jit_solution(10411829352846399144)
XLA Ops:
  0.6 0.0 slice-start
  0.7 0.8 select_maximum_fusion
  1.4 0.7 pad.23
  2.2 0.7 stack.9
  2.9 1.5 concatenate.7.pack_ref.ct_ref
  4.5 0.0 slice-done
  4.5 0.0 copy-start
  4.5 0.1 copy.24
  4.5 0.0 copy-start.7
  4.6 0.5 copy.26
  5.0 0.0 slice-start.1
  5.0 1.2 reshape.59.zx_ref
  6.2 0.0 copy-done
  6.2 0.2 fusion
  6.5 0.0 copy-done.7
  6.5 1.1 fusion.2.h_ref
  7.6 0.0 slice-done.1
  7.6 0.6 pad.22.tail_ref
  8.2 157.6 %mix_forward.1 = (bf16[2,8,128,1152]{3,2,1,0:T(8,128)(2,1)}, bf16[2,8,128,384]{3,2,1,0:T(8,128)(2,1)}, bf16[2,8,128,384]{3,2,1,0:T(8,128)(2,1)}, f32[2,8,128,1]{...) custom-call(bf16[2,128,1536]{2,1,0:T(8,128)(2,1)} %fusion.2.h_ref, ...), custom_call_target="tpu_custom_call" | custom-call | flops 30000001024 | bytes 60000000 | tf_op jit(solution)/shard_map/mix_forward/pallas_call | solution.py:642
  165.8 50.8 %mix_backward.1 = (bf16[2,8,128,1152]{3,2,1,0:T(8,128)(2,1)}, f32[8,384]{1,0:T(8,128)}, f32[8,256]{1,0:T(8,128)}, f32[8,128]{1,0:T(8,128)}, bf16[2,128,1536]{2,1,0:T(8,128)(2,1)}, /*index=5*/bf16[2,96,1536]{2,1,0:T(8,128)(2,1)}) custom-call(bf16[2,8,128,1152]{3,2,1,0:T(8,128)(2,1)} %get-tuple-element.46.zx_ref.zxh_ref.tail_ref.tailh_ref, ...), custom_call_target="tpu_custom_call" | custom-call | flops 32000000000 | bytes 16000000 | tf_op jit(solution)/shard_map/mix_backward/pallas_call | solution.py:717
  216.7 0.0 copy-start.2
  216.7 0.0 copy-start.5
  216.7 96.8 %exit_scatter.1 = (bf16[2,128,1536]{2,1,0:T(8,128)(2,1)}, bf16[2,128,1536]{2,1,0:T(8,128)(2,1)}, bf16[2,4,48,1152]{3,2,1,0:T(8,128)(2,1)}, f32[208,128]{1,0:T(8,128)}) custom-call(bf16[2048,1536]{1,0:T(8,128)(2,1)} %bitcast.21, bf16[2048,1152]{1,0:T(8,128)(2,1)} %bitcast.22, bf16[1536,1152]{1,0:T(8,128)(2,1)} %bitcast.23, ...), custom_call_target="tpu_custom_call" | custom-call | bytes 200000000 | tf_op jit(solution)/shard_map/exit_scatter/pallas_call | solution.py:1504
  313.5 0.0 copy-done.2
  313.6 0.0 copy-done.5
  313.6 0.0 copy-start.1
  313.6 1.2 copy-done.1
  314.7 0.0 copy-start.3
  314.7 1.1 copy-done.3
  315.9 0.0 copy-start.4
  315.9 1.1 copy-done.4
  317.0 0.0 copy-start.6
  317.0 0.9 copy-done.6
  317.9 3.0 finish.1
  320.9 0.6 reduce.1
  321.5 0.6 reduce
  322.1 0.5 slice_bitcast_fusion
  (6 shorter events, 0.1 us)
Async XLA Ops:
  0.6 3.8 %slice-start = ((bf16[48,6448]{1,0:T(8,128)(2,1)}), bf16[48,6144]{1,0:T(8,128)(2,1)S(1)}, s32[]{:S(2)}) async-start(bf16[48,6448]{1,0:T(8,128)(2,1)} %param.15), calls=%async_computation | async-start | bytes 1179648 | tf_op jit(solution)/shard_map/slice | solution.py:1633
  4.5 1.8 copy-start
  4.5 1.9 copy-start.7
  5.0 2.6 slice-start.1
  216.7 96.9 %copy-start.2 = (bf16[2,128,1536]{2,1,0:T(8,128)(2,1)S(1)}, bf16[2,128,1536]{2,1,0:T(8,128)(2,1)}, u32[]{:S(2)}) copy-start(bf16[2,128,1536]{2,1,0:T(8,128)(2,1)} %cot_ref.3) | copy-start | bytes 2359300
  216.7 96.9 %copy-start.5 = (bf16[2,96,1536]{2,1,0:T(8,128)(2,1)S(1)}, bf16[2,96,1536]{2,1,0:T(8,128)(2,1)}, u32[]{:S(2)}) copy-start(bf16[2,96,1536]{2,1,0:T(8,128)(2,1)} %get-tuple-element.68.rows_ref) | copy-start | bytes 1769476
  313.6 1.2 copy-start.1
  314.7 1.1 copy-start.3
  315.9 1.1 copy-start.4
  317.0 0.9 copy-start.6

commit v9 on v8

--- a/solution.py
+++ b/solution.py
@@ -17,6 +17,7 @@
 LANES = 128
 HALO = 16
 EPSILON = 1e-05
+TILE = 384
 F32 = jnp.float32
 BF16 = jnp.bfloat16
 
@@ -185,14 +186,14 @@
     seq, fsdp,
     h_ref, zx_ref, tail_ref, seg_ref, cot_ref, ow_ref,
     pack_ref,
-    proj_ref, y_ref, state_ref, off_ref, rem_ref, offr_ref,
-    h_out, w_out, grad_out, stat_out, mixed_out, pout_out, cx_ref, hp_ref, pick_ref,
-    h_v, w_v, w_flat, seg_v, cot_v, ow_v, ow_flat, gated_v, sums_v, sums_got, grad_v, mix_give,
-    mix_own, mix_first, pout_v, memory, ext_x, ext_t, last_rows, send, recv, near,
+    proj_ref, state_ref, off_ref, rem_ref, offr_ref,
+    h_out, w_out, dz_out, dy_out, stat_out, mixed_out, mixed_got, pout_out, pz_out, gain_out_ref, gain_in_ref,
+    cx_ref, hp_ref, pick_ref,
+    h_v, w_v, w_flat, seg_v, cot_v, ow_v, ow_flat, gated_v, sums_v, sums_got, grad_v, z_v, y_v,
+    mix_give, mix_own, pout_v, pz_v, memory, ext_x, ext_t, last_rows, send, recv, near,
 ):
-    seqs, _, length, width = y_ref.shape
-    depth = h_v.shape[3]
-    cols = proj_ref.shape[3]
+    seqs, _, length, depth = h_v.shape
+    width = cx_ref.shape[1]
     step_at = pl.program_id(0)
     place = Place(seq, fsdp)
     links = Links(send, recv, near)
@@ -211,7 +212,7 @@
     sums = [send_sums(i) for i in range(len(near_peers))]
 
     def send_core(q):
-        return links.far(lambda: (mix_give.at[q], mix_first.at[q], place.at(core=1)))
+        return links.far(lambda: (mix_give.at[q], mixed_got.at[q], place.at(core=1)))
 
     cores = [send_core(q) for q in range(seqs)]
 
@@ -273,7 +274,9 @@
             chunk_rows = proj[q * length : (q + 1) * length]
             zx, tail = chunk_rows[:, : 2 * width], chunk_rows[:, 2 * width :]
             earlier = last_rows[q]
+            z_rows = zx[:, :width]
             here = pl.ds(pl.multiple_of((q * seq + step_at) * length, length), length)
+            z_v[here, :] = z_rows
             conv_x, conv_t, _, _, _, _, cumul, _, step_x, entry_x, end_x = chunk_common(
                 zx[:, width:], earlier[:, width : 2 * width], tail, earlier[:, 2 * width :], offset, params,
                 ext_x.at[q], ext_t.at[q], width,
@@ -302,7 +305,7 @@
                 mix = mixing[0] if len(heads) == 1 else jnp.concatenate(mixing, axis=1)
                 inside = jnp.dot(mix, tile, preferred_element_type=F32)
                 y_low = (inside + outside[:, start : start + size]).astype(BF16)
-                y_ref[q, 0, :, start : start + size] = y_low
+                y_v[here, start : start + size] = y_low
                 z = zx[:, start : start + size].astype(F32)
                 gated = y_low.astype(F32) * (z * sigmoid(z))
                 gated_v[here, start : start + size] = (
@@ -337,8 +340,6 @@
                     part[i * length : (i + 1) * length].T[0:1, :]
                 )
 
-        grad_store = links.local(lambda: (grad_v, grad_out))
-        grad_store.start()
         for copy in sums:
             copy.start()
 
@@ -357,6 +358,8 @@
         for copy in cores:
             copy.start()
         mixed_rows(mix_own, place.core)
+        mixed_store = links.local(lambda: (mix_own, mixed_out))
+        mixed_store.start()
         for copy in sums:
             copy.wait_recv()
         total = sums_v[...]
@@ -367,29 +370,66 @@
         other = pltpu.roll(scale, 1, 0)
         stat_out[...] = jnp.where(is_square, scale, total * (other * other * other / INNER))
 
+        gain_out_ref[...] = jnp.zeros_like(gain_out_ref)
+        gain_row = cx_ref[KERNEL + 1 : KERNEL + 2, :]
+
         @pl.loop(0, tiles)
         def _(k):
             at = pl.ds(pl.multiple_of(k * tile, tile), tile)
-            scales = [
-                jnp.broadcast_to(stat_out[pl.ds(4 * k + 2 * i, 1), :], (LANES, length)).T[:, 0:1]
-                for i in (0, 1)
-            ]
-            scale_col = jnp.concatenate(scales, axis=0)
-            gated_v[at, :] = (gated_v[at, :].astype(F32) * scale_col).astype(BF16)
-
+
+            def column(line):
+                rows = [
+                    jnp.broadcast_to(stat_out[pl.ds(4 * k + 2 * i + line, 1), :], (LANES, length))
+                    for i in (0, 1)
+                ]
+                return jnp.concatenate([row.T[:, 0:1] for row in rows], axis=0)
+
+            scale, slope = column(0), column(1)
+            gated_v[at, :] = (gated_v[at, :].astype(F32) * scale).astype(BF16)
+            z = z_v[at, :].astype(F32)
+            y = y_v[at, :].astype(F32)
+            sig = sigmoid(z)
+            silu_z = z * sig
+            gated = y * silu_z
+            scaled = grad_v[at, :] * scale
+            gain_out_ref[0:1, :width] += jnp.sum(scaled * gated, axis=0, keepdims=True)
+            grad_gated = gain_row * scaled - gated * slope
+            y_v[at, :] = (grad_gated * silu_z).astype(BF16)
+            z_v[at, :] = (grad_gated * y * (sig + silu_z * (1.0 - sig))).astype(BF16)
+
+        dz_store = links.local(lambda: (z_v, dz_out))
+        dy_store = links.local(lambda: (y_v, dy_out))
+        dz_store.start()
+        dy_store.start()
+
+        rows_in = w_v.shape[3]
+        blocks = TILE // rows_in
+        high = blocks // fsdp
+        h_flat = h_v[...].reshape(-1, depth)
+        for t in range(depth // TILE):
+            term = tr_mm(h_flat[:, t * TILE : (t + 1) * TILE], z_v[...])
+            for i in range(blocks):
+                pz_v[t * high + i // fsdp, i % fsdp // 2, i % 2] = term[
+                    i * rows_in : (i + 1) * rows_in
+                ].astype(BF16)
+            if rows_in % HALO:
+                some = w_flat[t * TILE : (t + 1) * TILE, :width]
+            else:
+                some = w_v[t * high : (t + 1) * high, :, :, :, :width].reshape(TILE, width)
+            line = jnp.sum(term * some.astype(F32), axis=1, keepdims=True)
+            wide = jnp.broadcast_to(line, (TILE, LANES))
+            for i in range(TILE // LANES):
+                row = t * (TILE // LANES) + i
+                gain_in_ref[row : row + 1, :] = wide[i * LANES : (i + 1) * LANES].T[0:1, :]
+        pz_store = links.local(lambda: (pz_v, pz_out))
+        pz_store.start()
         pout_v[...] = tr_mm(gated_v[...], cot_v[...].reshape(-1, depth)).astype(BF16)
         pout_store = links.local(lambda: (pout_v, pout_out))
         pout_store.start()
-        for q in range(seqs):
-            cores[q].wait_recv()
-            for low in range(seq // 2):
-                add_rows(mix_own.at[q, low], mix_own.at[q, low], mix_first.at[q, low])
-        mixed_store = links.local(lambda: (mix_own, mixed_out))
-        mixed_store.start()
-        for copy in [grad_store, mixed_store, pout_store] + keep:
+        for copy in [dz_store, dy_store, pz_store, mixed_store, pout_store] + keep:
             copy.wait()
         for copy in cores:
-            copy.wait_send()
+            copy.wait()
         for copy in sums:
             copy.wait_send()
         entry.finish()
@@ -397,36 +437,70 @@
 
 def backward_kernel(
     seq, fsdp,
-    zx_ref, zxh_ref, tail_ref, tailh_ref, off_ref, offr_ref, rem_ref, y_ref, grad_ref, stat_ref,
-    state_ref, all_stat_ref, mixed_ref, pout_ref,
+    x_ref, xh_ref, tail_ref, tailh_ref, off_ref, offr_ref, rem_ref, dy_ref, dz_ref, state_ref,
+    w_ref,    all_stat_ref, mixed_ref, got_ref, pout_ref, pz_ref,
     cx_ref, ct_ref, hp_ref, pick_ref,
-    out_ref, gx_ref, gt_ref, gh_ref, mixed_out, rows_out,
+    out_ref, gx_ref, gt_ref, gh_ref, mixed_out, rows_out, slots_out, dh_out,
     memory, ext_x, ext_t, next_x, next_t,
-    mix_own, mix_later, pout_own, pout_first, send, recv, near,
+    mix_own, mix_first, mix_later, pout_own, pout_first, pz_own, pz_first, pz_top,
+    dh_give, dh_own, dh_first, send, recv, near,
 ):
-    seqs, _, length, width = y_ref.shape
+    seqs, _, length, width = dy_ref.shape
+    x_at = x_ref.shape[3] - width
     step_at = pl.program_id(0)
 
     place = Place(seq, fsdp)
     links = Links(send, recv, near)
-    mixed = TokenScatter(place, links, mixed_ref, mixed_out, mix_own, None, mix_later, "halves")
+    mixed = TokenScatter(
+        place, links, (mixed_ref, got_ref), mixed_out, mix_own, mix_first, mix_later, "halves"
+    )
     w_rows = RowScatter(place, links, pout_ref, rows_out, pout_own, pout_first)
+    z_part = PartScatter(
+        place, links, pz_ref, lambda s, c: pz_own.at[s, c], pz_first, pz_top, slots_out, 1
+    )
+    pz_load = links.local(lambda: (pz_ref.at[:, place.pair], pz_own))
+    half = seq // 2
+
+    def give_chunk(low):
+        return links.far(
+            lambda: (dh_give.at[:, low], dh_first.at[:, low], place.at(core=1))
+        )
+
+    dh_chunks = [give_chunk(low) for low in range(half)]
+    dh_store = links.local(lambda: (dh_own, dh_out))
     stages = len(place.low_bits)
 
     @pl.when(step_at == 0)
     def _():
+        mixed.begin()
+        pz_load.start()
         meet_pair(place)
-        mixed.begin()
-        w_rows.begin()
+        z_part.send_pairs(1, 0)
 
     @pl.when(step_at == 1)
     def _():
         mixed.add_cores()
         mixed.send_stage(0)
-
-    @pl.when(step_at == 3)
+        z_part.send_pairs(0, 0)
+
+    @pl.when(step_at == 2)
+    def _():
+        pz_load.wait()
+        z_part.add_pairs(1, 0)
+        z_part.send_cross(0)
+        w_rows.begin()
+
+    @pl.when(step_at == 4)
+    def _():
+        z_part.add_pairs(0, 0)
+
+    @pl.when(step_at == 5)
     def _():
         w_rows.add_pairs()
+
+    @pl.when(step_at == pl.num_programs(0) - 1)
+    def _():
+        z_part.spread()
 
     @pl.when(step_at == pl.num_programs(0) - 3)
     def _():
@@ -448,28 +522,16 @@
         ct_ref[:KERNEL, :], ct_ref[KERNEL : KERNEL + 1, :],
         hp_ref[...], pick_ref[...],
     )
-    gain_row, skip_row = cx_ref[KERNEL + 1 : KERNEL + 2, :], cx_ref[KERNEL + 2 : KERNEL + 3, :]
+    skip_row = cx_ref[KERNEL + 2 : KERNEL + 3, :]
     for q in range(seqs):
         offset = off_ref[q, 0]
         conv_x, conv_t, raw, step, rate, decay_rate, cumul, spread, step_x, entry_x, end_x = (
             chunk_common(
-                zx_ref[q, 0, :, width:], zxh_ref[q, 0, :, width:], tail_ref[q, 0], tailh_ref[q, 0], offset,
+                x_ref[q, 0, :, x_at:], xh_ref[q, 0, :, x_at:], tail_ref[q, 0], tailh_ref[q, 0], offset,
                 params, ext_x.at[q], ext_t.at[q], width,
             )
         )
-        stats = jnp.broadcast_to(stat_ref[q, 0, 0:1, :], (LANES, length)).T
-        slopes = jnp.broadcast_to(stat_ref[q, 0, 1:2, :], (LANES, length)).T
-        scale, slope = stats[:, 0:1], slopes[:, 0:1]
-        z = zx_ref[q, 0, :, :width].astype(F32)
-        sig_z = sigmoid(z)
-        silu_z = z * sig_z
-        y = y_ref[q, 0].astype(F32)
-        gated = y * silu_z
-        scaled_grad = grad_ref[q, 0].astype(F32) * scale
-        gx_ref[KERNEL + 2 : KERNEL + 3, :width] += jnp.sum(scaled_grad * gated, axis=0, keepdims=True)
-        grad_gated = gain_row * scaled_grad - gated * slope
-        dy_low = (grad_gated * silu_z).astype(BF16)
-        dz = (grad_gated * y * (sig_z + silu_z * (1.0 - sig_z))).astype(BF16)
+        dy_low = dy_ref[q, 0]
         dy = dy_low.astype(F32)
 
         sig_x = sigmoid(conv_x)
@@ -539,7 +601,7 @@
         conv_grad_t = jnp.concatenate([grad_b, grad_c], axis=1) * slope_t
 
         remain = rem_ref[q, 0]
-        results = [dz]
+        results = []
         for grad, ext, nxt, weight, sums in (
             (conv_grad_x, ext_x.at[q], next_x.at[q], params[0], gx_ref),
             (conv_grad_t, ext_t.at[q], next_t.at[q], params[2], gt_ref),
@@ -562,9 +624,25 @@
         gx_ref[KERNEL + 1 : KERNEL + 2, :width] += jnp.sum(dy * xs, axis=0, keepdims=True)
         gh_ref[0:1, :] += jnp.sum(grad_raw, axis=0, keepdims=True)
         gh_ref[1:2, :] += jnp.sum(grad_rate * rate, axis=0, keepdims=True)
-        out_ref[q, 0, :, : 2 * width] = jnp.concatenate(results[:2], axis=1)
-        out_ref[q, 0, :, 2 * width : 2 * width + 2 * STATE] = results[2]
-        out_ref[q, 0, :, 2 * width + 2 * STATE :] = results[3]
+        out_ref[q, 0] = jnp.concatenate(results, axis=1)
+
+    depth = w_ref.shape[0]
+    grad_h = mm_tr(dz_ref[...].reshape(seqs * length, width), w_ref[:, :width])
+    grad_h = grad_h + mm_tr(
+        out_ref[...].reshape(seqs * length, out_ref.shape[3]), w_ref[:, width:]
+    )
+    grad_h = grad_h.astype(BF16).reshape(seqs, length, depth)
+    for i in range(seq):
+        chunk = seq - 1 - i
+
+        @pl.when((step_at == i) & (place.core == chunk // half))
+        def _():
+            dh_own[:, chunk % half] = grad_h
+
+        @pl.when((step_at == i) & (place.core != chunk // half))
+        def _():
+            dh_give[:, chunk % half] = grad_h
+            dh_chunks[chunk % half].start()
 
     @pl.when(step_at == pl.num_programs(0) - 1)
     def _():
@@ -578,6 +656,14 @@
             done = mix_own.at[q, place.low]
             done[...] = (done[...].astype(F32) * column).astype(BF16)
         mixed.store()
+        z_part.finish()
+        for copy in dh_chunks:
+            copy.wait()
+        for q in range(seqs):
+            for low in range(half):
+                add_rows(dh_own.at[q, low], dh_own.at[q, low], dh_first.at[q, low])
+        dh_store.start()
+        dh_store.wait()
         w_rows.finish()
         mixed.finish()
 
@@ -592,10 +678,10 @@
     return -(-width // LANES)
 
 
-def sum_rows(width, seq):
-    shared = D // LANES + (KERNEL + 1) * 2 * STATE // LANES
-    group = (KERNEL + 3) * lane_rows(width) + 2
-    return shared, group, -(-(shared + seq * group) // 8) * 8
+def sum_rows(width):
+    shared = D // LANES
+    group = shared + (KERNEL + 1) * 2 * STATE // LANES
+    return shared, group, -(-(group + (KERNEL + 3) * lane_rows(width) + 2) // 8) * 8
 
 
 def whole_spec(shape):
@@ -644,19 +730,25 @@
         grid=(seq + 1,),
         in_specs=[ANYWHERE] * 6 + [whole_spec(packed.shape)],
         out_specs=[
-            block(cols), block(width), block(width, STATE), block(1), block(1), block(length, 1),
-            ANYWHERE, ANYWHERE, ANYWHERE, whole_spec(sums), ANYWHERE, ANYWHERE,
+            block(cols), block(width, STATE), block(1), block(1), block(length, 1),
+            ANYWHERE, ANYWHERE, ANYWHERE, ANYWHERE, whole_spec(sums), ANYWHERE, ANYWHERE, ANYWHERE, ANYWHERE,
+            whole_spec((8, lane_rows(width) * LANES)), whole_spec((depth // LANES, LANES)),
             whole_spec((8, width)), whole_spec((8, LANES)), whole_spec((LANES, LANES)),
         ],
         out_shape=[
-            blocks(cols, BF16), blocks(width, BF16), blocks(width, BF16, STATE),
+            blocks(cols, BF16), blocks(width, BF16, STATE),
             blocks(1, F32), blocks(1, F32), blocks(length, F32, 1),
             blocks(depth, BF16),
             jax.ShapeDtypeStruct(w_shape, BF16),
-            jax.ShapeDtypeStruct((count, width), F32),
+            jax.ShapeDtypeStruct((count, width), BF16),
+            jax.ShapeDtypeStruct((count, width), BF16),
             jax.ShapeDtypeStruct(sums, F32),
             jax.ShapeDtypeStruct((seqs, seq // 2, length, depth), BF16),
+            jax.ShapeDtypeStruct((seqs, seq // 2, length, depth), BF16),
             jax.ShapeDtypeStruct((width, depth), BF16),
+            jax.ShapeDtypeStruct(w_shape[:4] + (width,), BF16),
+            jax.ShapeDtypeStruct((8, lane_rows(width) * LANES), F32),
+            jax.ShapeDtypeStruct((depth // LANES, LANES), F32),
             jax.ShapeDtypeStruct((8, width), F32),
             jax.ShapeDtypeStruct((8, LANES), F32),
             jax.ShapeDtypeStruct((LANES, LANES), BF16),
@@ -673,10 +765,12 @@
             pltpu.VMEM(sums, F32),
             pltpu.VMEM((seq - 1,) + sums, F32),
             pltpu.VMEM((count, width), F32),
-            pltpu.VMEM((seqs, seq // 2, length, depth), BF16),
+            pltpu.VMEM((count, width), BF16),
+            pltpu.VMEM((count, width), BF16),
             pltpu.VMEM((seqs, seq // 2, length, depth), BF16),
             pltpu.VMEM((seqs, seq // 2, length, depth), BF16),
             pltpu.VMEM((width, depth), BF16),
+            pltpu.VMEM(w_shape[:4] + (width,), BF16),
             pltpu.VMEM((seqs, STATE, width), F32),
             pltpu.VMEM((seqs, HALO + length, width), F32),
             pltpu.VMEM((seqs, HALO + length, 2 * STATE), F32),
@@ -686,7 +780,7 @@
             pltpu.SemaphoreType.DMA((24,)),
         ],
         compiler_params=pltpu.CompilerParams(
-            dimension_semantics=("arbitrary",), vmem_limit_bytes=60 << 20, collective_id=0,
+            dimension_semantics=("arbitrary",), vmem_limit_bytes=63 << 20, collective_id=0,
             has_side_effects=True,
         ),
         cost_estimate=pl.CostEstimate(
@@ -694,22 +788,27 @@
         ),
         name="mix_forward",
     )(normed, zx, tail, segments, cotangent, out_w, packed)
-    proj, y, states, off_col, rem_col, off_row, h_all, w_mine, grad_yn, stats, mixed, part = outs[:12]
-    shape = (seqs, seq, length)
+    (
+        proj, states, off_col, rem_col, off_row, h_all, w_mine, dz, dy, stats, mixed, got, part,
+        part_z, gain_out, gain_in,
+    ) = outs[:16]
     return (
-        proj, y, states, off_col, rem_col, off_row, h_all, w_mine.reshape(depth, cols),
-        grad_yn.reshape(shape + (width,)), stats, mixed, part.reshape(out_shape), outs[12:],
+        proj, states, off_col, rem_col, off_row, h_all, w_mine.reshape(depth, cols), dz,
+        dy.reshape(seqs, seq, length, width), stats, (mixed, got), part.reshape(out_shape),
+        part_z, (gain_in, gain_out), outs[16:],
     )
 
 
 def backward_mix(
-    proj, off_col, off_row, rem_col, y, grad_yn, stats, states, mixed, part_out, packed, consts, seq, fsdp
+    proj, off_col, off_row, rem_col, dy, dz, w_mine, stats, states, mixed, part_out, part_z, packed, consts, seq, fsdp
 ):
     seqs, steps, length, cols = proj.shape
-    depth = mixed.shape[3]
+    depth = mixed[0].shape[3]
     width = (cols - TAIL) // 2
     block, before = chunk_specs(seqs, steps, length, True)
     tail_at = 2 * width // TAIL
+    x_cols, x_at = (width, 1) if width % LANES == 0 else (2 * width, 0)
+    rows_in = part_z.shape[3]
     half, pairs = seq // 2, fsdp // 2
     rows_out = part_out.shape[2]
     sums = [(8, lane_rows(width) * LANES), (8, 2 * STATE), (8, LANES)]
@@ -718,32 +817,41 @@
         functools.partial(backward_kernel, seq, fsdp),
         grid=(steps,),
         in_specs=[
-            block(2 * width), before(2 * width), block(TAIL, tail_at), before(TAIL, tail_at),
+            block(x_cols, x_at), before(x_cols, x_at),
+            block(TAIL, tail_at), before(TAIL, tail_at),
             block(1), block(length, 0, 1), block(1), block(width), block(width),
-            block(length, 0, 2), block(width, 0, STATE), whole_spec(stats.shape),
+            block(width, 0, STATE),
+            pl.BlockSpec(w_mine.shape, lambda i: (0, 0), pipeline_mode=pl.Buffered(1)),
+            whole_spec(stats.shape), ANYWHERE, ANYWHERE,
             ANYWHERE, ANYWHERE, whole_spec(consts[0].shape),
             pl.BlockSpec((8, 2 * STATE), lambda i: (0, INNER // (2 * STATE))),
             whole_spec(consts[1].shape), whole_spec(consts[2].shape),
         ],
-        out_specs=[block(cols)] + [whole_spec(v) for v in sums] + [ANYWHERE, ANYWHERE],
+        out_specs=[block(width + TAIL)] + [whole_spec(v) for v in sums] + [ANYWHERE] * 4,
         scratch_shapes=[
             pltpu.VMEM((seqs, STATE, width), F32),
             pltpu.VMEM((seqs, HALO + length, width), F32),
             pltpu.VMEM((seqs, HALO + length, 2 * STATE), F32),
             pltpu.VMEM((seqs, length + HALO, width), F32),
             pltpu.VMEM((seqs, length + HALO, 2 * STATE), F32),
-            token_own, pltpu.VMEM((seqs, max(half - 1, 1), length, depth), BF16),
+            token_own, token_own, pltpu.VMEM((seqs, max(half - 1, 1), length, depth), BF16),
             pltpu.VMEM((2, rows_out, depth), BF16),
             pltpu.VMEM((max(pairs - 1, 1), 2, rows_out, depth), BF16),
-            pltpu.SemaphoreType.DMA((64,)),
-            pltpu.SemaphoreType.DMA((64,)),
+            pltpu.VMEM((seq, 2, rows_in, width), BF16),
+            pltpu.VMEM((max(pairs - 1, 1), seq, 2, rows_in, width), BF16),
+            pltpu.VMEM((half, 2, rows_in, width), BF16),
+            token_own, token_own, token_own,
+            pltpu.SemaphoreType.DMA((128,)),
+            pltpu.SemaphoreType.DMA((128,)),
             pltpu.SemaphoreType.DMA((16,)),
         ],
-        out_shape=[jax.ShapeDtypeStruct(proj.shape, BF16)]
+        out_shape=[jax.ShapeDtypeStruct(proj.shape[:3] + (width + TAIL,), BF16)]
         + [jax.ShapeDtypeStruct(v, F32) for v in sums]
         + [
             jax.ShapeDtypeStruct((seqs, length, depth), BF16),
             jax.ShapeDtypeStruct((2, rows_out, depth), BF16),
+            jax.ShapeDtypeStruct((2, half, rows_in, width), BF16),
+            jax.ShapeDtypeStruct((seqs, half, length, depth), BF16),
         ],
         compiler_params=pltpu.CompilerParams(
             dimension_semantics=("arbitrary",), vmem_limit_bytes=56 << 20, collective_id=3,
@@ -754,9 +862,9 @@
         ),
         name="mix_backward",
     )(
-        proj, proj, proj, proj, off_col, off_row, rem_col, y, grad_yn,
-        stats.reshape(seqs, steps, 2, length), states, stats, mixed, part_out, consts[0], packed,
-        consts[1], consts[2],
+        proj, proj, proj, proj, off_col, off_row, rem_col, dy, dz.reshape(dy.shape), states,
+        w_mine, stats, *mixed, part_out,
+        part_z, consts[0], packed, consts[1], consts[2],
     )
 
 
@@ -1143,14 +1251,15 @@
     def __init__(self, place, links, src, out, own, first, later, held):
         self.place = place
         self.out, self.own, self.first, self.later = out, own, first, later
-        self.seqs = src.shape[0]
+        self.seqs = own.shape[0]
         half = place.half
-
-        def give(q):
-            return links.far(lambda: (src.at[q], first.at[q], place.at(core=1)))
-
-        self.cores = [give(q) for q in range(self.seqs)] if held == "give" else []
-        self.loads = [links.local(lambda: (src, own))] if held == "halves" else []
+        self.loads = []
+        if held == "sums":
+            self.loads = [links.local(lambda: (src, own))]
+        if held == "halves":
+            self.loads = [
+                links.local(lambda: (src[0], own)), links.local(lambda: (src[1], first)),
+            ]
         self.stages = [[] for _ in place.low_bits]
         for q in range(self.seqs):
             live, slot = list(range(half)), 0
@@ -1170,14 +1279,13 @@
         )
 
     def begin(self):
-        for copy in self.cores + self.loads:
+        for copy in self.loads:
             copy.start()
 
     def add_cores(self):
         for copy in self.loads:
             copy.wait()
-        for q, copy in enumerate(self.cores):
-            copy.wait_recv()
+        for q in range(self.seqs if self.first is not None else 0):
             for low in range(self.place.half):
                 add_rows(self.own.at[q, low], self.own.at[q, low], self.first.at[q, low])
 
@@ -1196,8 +1304,6 @@
         self.stay.wait()
 
     def finish(self):
-        for copy in self.cores:
-            copy.wait_send()
         for stage in self.stages:
             for copy, _, _, _ in stage:
                 copy.wait_send()
@@ -1263,6 +1369,90 @@
                 copy.wait_send()
 
 
+class PartScatter:
+    def __init__(self, place, links, src, own, first, other, slots, tiles):
+        self.place, self.own, self.first, self.other = place, own, first, other
+        self.high = high = place.half // tiles
+        pairs = range(1, place.pairs)
+
+        def rows(top, k):
+            return pl.ds(place.half * flip(place.top, top) + k * high, high)
+
+        def over(top, k, p):
+            return links.far(
+                lambda: (
+                    src.at[rows(top, k), flip(place.pair, p)], first.at[p - 1, rows(top, k)],
+                    place.at(pair=p),
+                )
+            )
+
+        def cross(i, c):
+            def make():
+                at = place.half * flip(place.top, 1) + i
+                return own(at, c), other.at[i, c], place.at(top=1)
+
+            return links.far(make)
+
+        def spread(l, c):
+            return links.far(
+                lambda: (
+                    self.block(l, c), slots.at[place.core, place.low], place.at(low=l, core=c)
+                )
+            )
+
+        self.over = [[[over(top, k, p) for p in pairs] for k in range(tiles)] for top in (0, 1)]
+        self.cross = [
+            [cross(k * high + i, c) for i in range(high) for c in (0, 1)] for k in range(tiles)
+        ]
+        self.near = [(l, c) for t, l, c in peers_of(place) if t == 0]
+        self.slots = {p: spread(*p) for p in self.near}
+        self.slots[0, 0] = links.local(
+            lambda: (self.block(0, 0), slots.at[place.core, place.low])
+        )
+
+    def block(self, l, c):
+        place = self.place
+        return self.own(place.half * place.top + flip(place.low, l), flip(place.core, c))
+
+    def send_pairs(self, top, k):
+        for copy in self.over[top][k]:
+            copy.start()
+
+    def add_pairs(self, top, k):
+        for i, copy in enumerate(self.over[top][k]):
+            copy.wait_recv()
+            for low in range(self.high):
+                for c in (0, 1):
+                    at = self.place.half * flip(self.place.top, top) + k * self.high + low
+                    ref = self.own(at, c)
+                    add_rows(ref, ref, self.first.at[i, at, c], 16)
+
+    def send_cross(self, k):
+        for copy in self.cross[k]:
+            copy.start()
+
+    def wait_cross(self, k):
+        for copy in self.cross[k]:
+            copy.wait_recv()
+
+    def spread(self, waits=True):
+        if waits:
+            for k in range(len(self.cross)):
+                self.wait_cross(k)
+        place = self.place
+        for l, c in self.near + [(0, 0)]:
+            ref = self.block(l, c)
+            add_rows(ref, ref, self.other.at[flip(place.low, l), flip(place.core, c)], 16)
+            self.slots[l, c].start()
+
+    def finish(self):
+        for copy in self.slots.values():
+            copy.wait()
+        for copies in self.cross + [c for top in self.over for c in top]:
+            for copy in copies:
+                copy.wait_send()
+
+
 class Deliver:
     def __init__(self, place, links, src, out):
         self.place = place
@@ -1288,16 +1478,11 @@
             self.stay.wait()
 
 
-TILE = 384
-ROWS = 256
-
-
 def exit_kernel(
     seq, fsdp,
-    h_ref, grad_ref, w_ref, mixed_ref, gx_ref, gt_ref, gh_ref,
+    h_ref, dh_ref, grad_ref, w_ref, mixed_ref, gain_in_ref, gain_out_ref, gx_ref, gt_ref, gh_ref,
     dh_out, mixed_out, slots_out, vec_out,
-    h_all, grads, weights, part,
-    dh_give, dh_own, dh_first, dh_later, part_first, part_top, vec_val, vec_got,
+    h_all, grads, weights, part, dh_own, dh_later, part_first, part_top, vec_val, vec_got,
     send, recv, near,
 ):
     place = Place(seq, fsdp)
@@ -1306,9 +1491,9 @@
     others = list(range(1, place.pairs))
     seqs, _, length, depth = dh_own.shape
     rows = part.shape[3]
-    width = (weights.shape[1] - TAIL) // 2
+    width = weights.shape[1] - grads.shape[1]
     dh = TokenScatter(
-        place, links, dh_give, dh_out, dh_own, dh_first, dh_later, "give"
+        place, links, dh_ref, dh_out, dh_own, None, dh_later, "sums"
     )
     dh_last = Deliver(place, links, lambda: dh_own.at[:, place.low], dh_out)
     mixed = Deliver(place, links, lambda: mixed_ref, mixed_out)
@@ -1319,76 +1504,35 @@
     ]
 
     tiles = depth // 2 // TILE
-    high = half // tiles
-
-    def rows_of(top, k):
-        return pl.ds(half * flip(place.top, top) + k * high, high)
-
-    def over(top, k, p):
+    rest = PartScatter(
+        place, links, part, lambda s, c: part.at[s, place.pair, c], part_first, part_top, slots_out,
+        tiles,
+    )
+
+    hops = [dict(pair=1 << i) for i in range(place.pairs.bit_length() - 1)] + [dict(top=1)]
+
+    def hop(i):
+        return links.far(lambda: (vec_val.at[i], vec_got.at[i], place.at(**hops[i])))
+
+    def share(l, c):
         return links.far(
             lambda: (
-                part.at[rows_of(top, k), flip(place.pair, p)],
-                part_first.at[p - 1, rows_of(top, k)],
-                place.at(pair=p),
+                vec_val.at[len(hops)], vec_out.at[place.core, place.low],
+                place.at(low=l, core=c),
             )
         )
 
-    def crossing(k):
-        return links.far(
-            lambda: (
-                part.at[rows_of(1, k), place.pair], part_top.at[pl.ds(k * high, high)],
-                place.at(top=1),
-            )
-        )
-
-    over_pairs = [[[over(top, k, p) for p in others] for k in range(tiles)] for top in (0, 1)]
-    cross = [crossing(k) for k in range(tiles)]
-
-    def row_block(l, c):
-        return part.at[
-            half * place.top + flip(place.low, l), place.pair, flip(place.core, c)
-        ]
-
-    def spread(l, c):
-        return links.far(
-            lambda: (
-                row_block(l, c), slots_out.at[place.core, place.low], place.at(low=l, core=c)
-            )
-        )
-
-    near_peers = [(l, c) for t, l, c in peers_of(place) if t == 0]
-    slots = {p: spread(*p) for p in near_peers}
-    slots[0, 0] = links.local(lambda: (row_block(0, 0), slots_out.at[place.core, place.low]))
-
-    hops = [dict(pair=1 << i) for i in range(place.pairs.bit_length() - 1)]
-    hops += [dict(top=1)] + [dict(low=b) for b in place.low_bits] + [dict(core=1)]
-
-    def hop(i):
-        return links.far(lambda: (vec_val.at[i], vec_got.at[i], place.at(**hops[i])))
-
     vec = [hop(i) for i in range(len(hops))]
-    vec_store = links.local(lambda: (vec_val.at[len(hops)], vec_out))
-    state = {"at": 0}
-
-    def vec_next():
-        i = state["at"]
-        state["at"] += 1
-        if i < len(hops):
-            vec[i].wait_recv()
-            vec_val[i + 1] = vec_val[i] + vec_got[i]
-            if i + 1 < len(hops):
-                vec[i + 1].start()
-            else:
-                vec_store.start()
-
-    def add_pairs(top, k):
-        for i, copy in enumerate(over_pairs[top][k]):
-            copy.wait_recv()
-            for low in range(high):
-                for c in (0, 1):
-                    at = half * flip(place.top, top) + k * high + low
-                    ref = part.at[at, place.pair, c]
-                    add_rows(ref, ref, part_first.at[i, at, c], 16)
+    vec_shares = [share(l, c) for t, l, c in peers_of(place) if t == 0]
+    vec_shares.append(
+        links.local(lambda: (vec_val.at[len(hops)], vec_out.at[place.core, place.low]))
+    )
+
+    def vec_next(i):
+        vec[i].wait_recv()
+        vec_val[i + 1] = vec_val[i] + vec_got[i]
+        for copy in vec[i + 1 : i + 2] if i + 1 < len(hops) else vec_shares:
+            copy.start()
 
     blocks = TILE // rows
 
@@ -1399,69 +1543,48 @@
         for b in range(blocks):
             at = t * (blocks // fsdp) + b // fsdp
             part[at, b % fsdp // 2, b % 2] = term[b * rows : (b + 1) * rows].astype(BF16)
-        sums = jnp.sum(term * weights[lanes, :].astype(F32), axis=1, keepdims=True)
+        sums = jnp.sum(term * weights[lanes, width:].astype(F32), axis=1, keepdims=True)
         wide = jnp.broadcast_to(sums, (TILE, LANES))
         for i in range(TILE // LANES):
-            vec_val[0, pl.ds(t * (TILE // LANES) + i, 1), :] = (
-                wide[i * LANES : (i + 1) * LANES].T[0:1, :]
-            )
-        for copy in over_pairs[top][k]:
-            copy.start()
+            row = pl.ds(t * (TILE // LANES) + i, 1)
+            vec_val[0, row, :] = gain_in_ref[row, :] + wide[i * LANES : (i + 1) * LANES].T[0:1, :]
+        rest.send_pairs(top, k)
 
     def place_sums():
-        shared, group, _ = sum_rows(width, seq)
+        at, group, _ = sum_rows(width)
         vec_val[0] = jnp.zeros_like(vec_val[0])
-        at = D // LANES
         for tap in range(KERNEL + 1):
             for j in range(2 * STATE // LANES):
                 vec_val[0, at : at + 1, :] = gt_ref[
                     tap : tap + 1, j * LANES : (j + 1) * LANES
                 ]
                 at += 1
-        at = shared + place.chunk * group
         pieces_of = [
-            gx_ref[line : line + 1, j * LANES : (j + 1) * LANES]
-            for line in range(KERNEL + 3)
+            ref[line : line + 1, j * LANES : (j + 1) * LANES]
+            for ref, line in [(gx_ref, i) for i in range(KERNEL + 2)] + [(gain_out_ref, 0)]
             for j in range(lane_rows(width))
         ] + [gh_ref[0:1, :], gh_ref[1:2, :]]
         for i, piece in enumerate(pieces_of):
-            vec_val[0, pl.ds(at + i, 1), :] = piece
-
-    def token_rows(out, side):
-        per_chunk = ROWS // length
-        count = half // per_chunk
-        for q in range(seqs):
-
-            @pl.loop(0, count)
-            def _(k):
-                at = (q * seq + half * side + k * per_chunk) * length
-                term = mm_tr(grads[pl.ds(pl.multiple_of(at, LANES), ROWS), :], weights[...])
-                out[q, pl.ds(k * per_chunk, per_chunk)] = term.astype(BF16).reshape(
-                    per_chunk, length, depth
-                )
-
+            vec_val[0, group + i : group + i + 1, :] = piece
+
+    dh.begin()
     for copy in loads:
         copy.start()
+    meet_pair(place)
+    dh.add_cores()
+    dh.send_stage(0)
+    mixed.begin()
     place_sums()
-    meet_pair(place)
-    mixed.begin()
     for copy in loads:
         copy.wait()
-    token_rows(dh_give, 1 - place.core)
-    dh.begin()
     for k in range(tiles):
         weight_rows(1, k)
-    token_rows(dh_own, place.core)
-    dh.add_cores()
-    dh.send_stage(0)
-    add_pairs(1, 0)
-    cross[0].start()
     for k in range(tiles):
         weight_rows(0, k)
     vec[0].start()
-    for k in range(1, tiles):
-        add_pairs(1, k)
-        cross[k].start()
+    for k in range(tiles):
+        rest.add_pairs(1, k)
+        rest.send_cross(k)
     stages = len(place.low_bits)
     for i in range(stages):
         dh.add_stage(i)
@@ -1469,59 +1592,56 @@
             dh.send_stage(i + 1)
         else:
             dh_last.begin()
-        vec_next()
+        if i < len(hops):
+            vec_next(i)
+    for i in range(stages, len(hops)):
+        vec_next(i)
     for k in range(tiles):
-        add_pairs(0, k)
-    vec_next()
-    for copy in cross:
-        copy.wait_recv()
-    for l, c in near_peers + [(0, 0)]:
-        ref = row_block(l, c)
-        add_rows(ref, ref, part_top.at[flip(place.low, l), flip(place.core, c)], 16)
-        slots[l, c].start()
-    while state["at"] < len(hops):
-        vec_next()
-    for copy in slots.values():
+        rest.add_pairs(0, k)
+    rest.spread()
+    for copy in vec_shares:
         copy.wait()
-    vec_store.wait()
+    rest.finish()
     mixed.finish()
     dh_last.finish()
     dh.finish()
-    for copy in cross + vec + [c for top in over_pairs for tile in top for c in tile]:
+    for copy in vec:
         copy.wait_send()
 
 
-def exit_scatter(seq, fsdp, h_all, grad_proj, w_mine, mixed, sums):
+def exit_scatter(seq, fsdp, h_all, grad_h, grad_proj, w_mine, mixed, sums):
     seqs, _, length, depth = h_all.shape
     half, pairs = seq // 2, fsdp // 2
     cols = w_mine.shape[1]
+    rest = grad_proj.shape[3]
+    width = cols - rest
     rows = depth // (seq * fsdp)
     count = seqs * seq * length
-    vector = (sum_rows((cols - TAIL) // 2, seq)[2], LANES)
-    bits = (half.bit_length() - 1) + (pairs.bit_length() - 1) + 2
+    vector = (sum_rows(width)[2], LANES)
+    hops = pairs.bit_length()
     token_own = pltpu.VMEM((seqs, half, length, depth), BF16)
     tokens = jax.ShapeDtypeStruct((seqs, length, depth), BF16)
     return pl.pallas_call(
         functools.partial(exit_kernel, seq, fsdp),
-        in_specs=[ANYWHERE] * 4 + [pl.BlockSpec(memory_space=pltpu.VMEM)] * 3,
+        in_specs=[ANYWHERE] * 5 + [pl.BlockSpec(memory_space=pltpu.VMEM)] * 5,
         out_specs=[ANYWHERE] * 4,
         out_shape=[
             tokens,
             tokens,
-            jax.ShapeDtypeStruct((2, half, rows, cols), BF16),
-            jax.ShapeDtypeStruct(vector, F32),
+            jax.ShapeDtypeStruct((2, half, rows, rest), BF16),
+            jax.ShapeDtypeStruct((2, half) + vector, F32),
         ],
         scratch_shapes=[
             pltpu.VMEM((count, depth), BF16),
-            pltpu.VMEM((count, cols), BF16),
+            pltpu.VMEM((count, rest), BF16),
             pltpu.VMEM((depth, cols), BF16),
-            pltpu.VMEM((seq, pairs, 2, rows, cols), BF16),
-            token_own, token_own, token_own,
+            pltpu.VMEM((seq, pairs, 2, rows, rest), BF16),
+            token_own,
             pltpu.VMEM((seqs, max(half - 1, 1), length, depth), BF16),
-            pltpu.VMEM((max(pairs - 1, 1), seq, 2, rows, cols), BF16),
-            pltpu.VMEM((half, 2, rows, cols), BF16),
-            pltpu.VMEM((bits + 1,) + vector, F32),
-            pltpu.VMEM((bits,) + vector, F32),
+            pltpu.VMEM((max(pairs - 1, 1), seq, 2, rows, rest), BF16),
+            pltpu.VMEM((half, 2, rows, rest), BF16),
+            pltpu.VMEM((hops + 1,) + vector, F32),
+            pltpu.VMEM((hops,) + vector, F32),
             pltpu.SemaphoreType.DMA((96,)),
             pltpu.SemaphoreType.DMA((96,)),
             pltpu.SemaphoreType.DMA((16,)),
@@ -1533,12 +1653,14 @@
             flops=0, transcendentals=0, bytes_accessed=200_000_000
         ),
         name="exit_scatter",
-    )(h_all.reshape(count, depth), grad_proj.reshape(count, cols), w_mine, mixed, *sums)
+    )(
+        h_all.reshape(count, depth), grad_h, grad_proj.reshape(count, rest), w_mine, mixed, *sums
+    )
 
 
 def finish_kernel(
     seq,
-    tok_ref, cot_ref, gain_ref, dh_ref, mixed_ref, slots_ref, rows_ref, vec_ref,
+    tok_ref, cot_ref, gain_ref, dh_ref, mixed_ref, slots_z_ref, slots_ref, rows_ref, vec_ref,
     mixed_out, tokens_out, gain_in_out, w_in_out, conv_w_out, conv_b_out, heads_out, gain_out_out,
     w_out_out,
 ):
@@ -1553,39 +1675,39 @@
             scaled - unit * jnp.mean(scaled * unit, axis=-1, keepdims=True)
         )
     groups, _, cols = slots_ref.shape
-    width = (cols - TAIL) // 2
+    width = cols - TAIL
     tail = jnp.zeros((slots_ref.shape[1], TAIL), F32)
     for g in range(groups):
-        w_in_out[:, g * width : (g + 1) * width] = slots_ref[g, :, :width].astype(F32)
+        w_in_out[:, g * width : (g + 1) * width] = slots_z_ref[g].astype(F32)
         w_in_out[:, INNER + g * width : INNER + (g + 1) * width] = (
-            slots_ref[g, :, width : 2 * width].astype(F32)
+            slots_ref[g, :, :width].astype(F32)
         )
-        tail = tail + slots_ref[g, :, 2 * width :].astype(F32)
+        tail = tail + slots_ref[g, :, width:].astype(F32)
     w_in_out[:, 2 * INNER :] = tail[:, : 2 * STATE + HEADS]
     w_out_out[...] = rows_ref[0].astype(F32) + rows_ref[1].astype(F32)
 
-    shared, size, _ = sum_rows(width, seq)
+    row, group, _ = sum_rows(width)
     heads = HEADS // seq
+    common = vec_ref[0, :group]
+    for g in range(1, groups):
+        common = common + vec_ref[g, :group]
     for j in range(D // LANES):
         at = slice(j * LANES, (j + 1) * LANES)
-        gain_in_out[:, at] = vec_ref[j : j + 1, :] / gain_ref[:, at]
-    row = D // LANES
+        gain_in_out[:, at] = common[j : j + 1] / gain_ref[:, at]
     targets = [conv_w_out.at[k : k + 1] for k in range(KERNEL)] + [conv_b_out]
     for out in targets:
         for j in range(2 * STATE // LANES):
-            out[:, INNER + j * LANES : INNER + (j + 1) * LANES] = vec_ref[row : row + 1, :]
+            out[:, INNER + j * LANES : INNER + (j + 1) * LANES] = common[row : row + 1]
             row += 1
     across = lane_rows(width)
     lane = iota((8, LANES), 1)
     per_head = jnp.zeros((8, LANES), F32)
     fold = expander(across * LANES)
     for g in range(groups):
-        row = shared + g * size
-
         def lanes_of(line):
-            first = row + line * across
+            first = group + line * across
             return jnp.concatenate(
-                [vec_ref[first + j : first + j + 1, :] for j in range(across)], axis=1
+                [vec_ref[g, first + j : first + j + 1, :] for j in range(across)], axis=1
             )
 
         at = slice(g * width, (g + 1) * width)
@@ -1593,16 +1715,16 @@
             out[:, at] = lanes_of(line)[:, :width]
         gain_out_out[:, at] = lanes_of(KERNEL + 2)[:, :width]
         skip = mm_ones_tr(jnp.broadcast_to(lanes_of(KERNEL + 1), (8, across * LANES)), fold, 3)
-        last = row + (KERNEL + 3) * across
+        last = group + (KERNEL + 3) * across
         lines = jnp.concatenate(
-            [skip[0:1, :], vec_ref[last : last + 2, :], jnp.zeros((5, LANES), F32)], axis=0
+            [skip[0:1, :], vec_ref[g, last : last + 2, :], jnp.zeros((5, LANES), F32)], axis=0
         )
         lines = jnp.where(lane < heads, lines, 0.0)
         per_head = per_head + (pltpu.roll(lines, g * heads, 1) if g else lines)
     heads_out[...] = per_head
 
 
-def finish(seq, tokens, cotangent, gain_in, grad_h, mixed, slots, rows, vector, shapes):
+def finish(seq, tokens, cotangent, gain_in, grad_h, mixed, slots_z, slots, rows, vector, shapes):
     columns = INNER + 2 * STATE
     kinds = [
         (tokens.shape, BF16), (tokens.shape, F32), ((1, D), F32), (shapes[0], F32),
@@ -1614,7 +1736,7 @@
         out_shape=[jax.ShapeDtypeStruct(*kind) for kind in kinds],
         compiler_params=pltpu.CompilerParams(vmem_limit_bytes=32 << 20),
         name="finish",
-    )(tokens, cotangent, gain_in[None], grad_h, mixed, slots, rows, vector)
+    )(tokens, cotangent, gain_in[None], grad_h, mixed, slots_z, slots, rows, vector)
 
 
 def local(
@@ -1648,23 +1770,23 @@
         ]
     )
     (
-        proj, y, states, off_col, rem_col, off_row, h_all, w_mine, grad_yn, stats, mixed, part_out,
-        consts,
+        proj, states, off_col, rem_col, off_row, h_all, w_mine, dz, dy, stats, mixed, part_out,
+        part_z, gains, consts,
     ) = forward_mix(normed, zx, tail, segments, cotangent, w_out, packed, steps, shards)
-    grad_proj, sums_x, sums_t, sums_h, mixed, rows = backward_mix(
-        proj, off_col, off_row, rem_col, y, grad_yn, stats, states, mixed, part_out,
-        packed, consts, steps, shards,
-    )
-
+    grad_proj, sums_x, sums_t, sums_h, mixed, rows, slots_z, grad_h = backward_mix(
+        proj, off_col, off_row, rem_col, dy, dz, w_mine, stats, states, mixed,
+        part_out, part_z, packed, consts, steps, shards,
+    )
     grad_h, mixed, slots, vector = exit_scatter(
-        steps, shards, h_all, grad_proj, w_mine, mixed, (sums_x, sums_t, sums_h)
+        steps, shards, h_all, grad_h, grad_proj, w_mine, mixed, gains + (sums_x, sums_t, sums_h)
     )
     (
         mixed, tokens_grad, gain_in_grad, w_in_grad, conv_w_grad, conv_b_grad, per_head,
         gain_out_grad, w_out_grad,
     ) = finish(
         steps, tokens, cotangent, gain_in, grad_h, mixed,
-        slots.reshape(steps, rows_in, 2 * width + TAIL), rows, vector, (w_in.shape, w_out.shape),
+        slots_z.reshape(steps, rows_in, width), slots.reshape(steps, rows_in, width + TAIL), rows,
+        vector.reshape((steps,) + vector.shape[2:]), (w_in.shape, w_out.shape),
     )
     return (
         mixed, tokens_grad, gain_in_grad[0], w_in_grad, conv_w_grad, conv_b_grad[0],

time: 323 us -> 315 us (0.975)
  Pallas kernels: 308 us -> 299 us
    pallas_call x1, Pallas kernels: 96.8 us -> 73 us  [exit_scatter(): pl.pallas_call(functools.partial(exit_kernel, seq, fsdp), in_specs=[ANYWH...]
    pallas_call x1, Pallas kernels: 50.8 us -> 62.1 us  [backward_mix(): pl.pallas_call(functools.partial(backward_kernel, seq, fsdp), grid=(steps...]
    pallas_call x1, Pallas kernels: 158 us -> 161 us  [forward_mix(): pl.pallas_call(functools.partial(forward_kernel, seq, fsdp), grid=(seq +...]
where the time goes in v9:
time: 315 us; the launch traced here: 314 us
  Pallas kernels  299 us (95%)
  local copies, waits for them, and re-layouts  10.2 us (3%)
  other arithmetic  3.39 us (1%)
    pallas_call x1, Pallas kernels, forward_mix(): pl.pallas_call(functools.partial(forward_kernel, seq, fsdp), grid=(seq +...  161 us
    pallas_call x1, Pallas kernels, exit_scatter(): pl.pallas_call(functools.partial(exit_kernel, seq, fsdp), in_specs=[ANYWH...  73 us
    pallas_call x1, Pallas kernels, backward_mix(): pl.pallas_call(functools.partial(backward_kernel, seq, fsdp), grid=(steps...  62.1 us

profile of v9, /device:TPU:1, one launch (start us, length us, event | category | flops | bytes accessed | tf_op | source)
XLA Modules:
  0.0 313.7 jit_solution(7133330730266090995)
XLA Ops:
  0.6 0.0 slice-start
  0.7 0.8 select_maximum_fusion
  1.4 0.7 pad.23
  2.2 0.7 stack.9
  2.9 1.5 concatenate.7.pack_ref.ct_ref
  4.5 0.0 slice-done
  4.5 0.0 copy-start
  4.5 0.1 copy.24
  4.5 0.0 copy-start.8
  4.6 0.5 copy.26
  5.0 0.0 slice-start.1
  5.0 1.2 reshape.65.zx_ref
  6.2 0.0 copy-done
  6.2 0.2 fusion
  6.5 0.0 copy-done.8
  6.5 1.1 fusion.2.h_ref
  7.6 0.0 slice-done.1
  7.6 0.6 pad.22.tail_ref
  8.2 161.2 %mix_forward.1 = (bf16[2,8,128,1152]{3,2,1,0:T(8,128)(2,1)}, bf16[2,8,128,384]{3,2,1,0:T(8,128)(2,1)}, f32[2,8,128,1]{3,2,1,0:T(8,128)}, f32[2,8,128,1]{3,2,1,0:...) custom-call(bf16[2,128,1536]{2,1,0:T(8,128)(2,1)} %fusion.2.h_ref, ...), custom_call_target="tpu_custom_call" | custom-call | flops 30000001024 | bytes 60000000 | tf_op jit(solution)/shard_map/mix_forward/pallas_call | solution.py:728
  169.5 62.1 %mix_backward.1 = (bf16[2,8,128,768]{3,2,1,0:T(8,128)(2,1)}, f32[8,384]{1,0:T(8,128)}, f32[8,256]{1,0:T(8,128)}, f32[8,128]{1,0:T(8,128)}, bf16[2,128,1536]{2,1,...) custom-call(bf16[2,8,128,1152]{3,2,1,0:T(8,128)(2,1)} %get-tuple-ele, ...), custom_call_target="tpu_custom_call" | custom-call | flops 32000000000 | bytes 16000000 | tf_op jit(solution)/shard_map/mix_backward/pallas_call | solution.py:816
  231.6 0.0 copy-start.1
  231.6 0.0 copy-start.4
  231.6 0.0 copy-start.6
  231.6 73.0 %exit_scatter.1 = (bf16[2,128,1536]{2,1,0:T(8,128)(2,1)}, bf16[2,128,1536]{2,1,0:T(8,128)(2,1)}, bf16[2,4,48,768]{3,2,1,0:T(8,128)(2,1)}, f32[2,4,48,128]{3,2,1,0:T(8,128)}) custom-call(bf16[2048,1536]{1,0:T(8,128)(2,1)} %bitcast.25, bf16[2,4,128,1536]{3,2,1,0:T(8,128)(2,1)} %get-tuple-element.68.dh_ref, bf16[2048,768]{1,0:T(8,128)(2,1)} %bitcast.28, ...), custom_call_target="tpu_custom_call" | custom-call | bytes 200000000 | tf_op jit(solution)/shard_map/exit_scatter/pallas_call | solution.py:1624
  304.6 0.0 copy-done.1
  304.7 0.0 copy-done.4
  304.7 0.0 copy-done.6
  304.7 0.0 copy-start.2
  304.7 1.1 copy-done.2
  305.8 0.0 copy-start.3
  305.8 1.1 copy-done.3
  306.9 0.0 copy-start.5
  306.9 1.1 copy-done.5
  308.0 0.0 copy-start.7
  308.0 0.9 copy-done.7
  308.9 3.0 finish.1
  311.9 0.6 reduce.1
  312.6 0.6 reduce
  313.2 0.5 slice_bitcast_fusion
  (6 shorter events, 0.1 us)
Async XLA Ops:
  0.6 3.8 %slice-start = ((bf16[48,6448]{1,0:T(8,128)(2,1)}), bf16[48,6144]{1,0:T(8,128)(2,1)S(1)}, s32[]{:S(2)}) async-start(bf16[48,6448]{1,0:T(8,128)(2,1)} %param.15), calls=%async_computation | async-start | bytes 1179648 | tf_op jit(solution)/shard_map/slice | solution.py:1755
  4.5 1.8 copy-start
  4.5 1.9 copy-start.8
  5.0 2.6 slice-start.1
  231.6 73.0 %copy-start.1 = (bf16[2,128,1536]{2,1,0:T(8,128)(2,1)S(1)}, bf16[2,128,1536]{2,1,0:T(8,128)(2,1)}, u32[]{:S(2)}) copy-start(bf16[2,128,1536]{2,1,0:T(8,128)(2,1)} %cot_ref.3) | copy-start | bytes 2359300
  231.6 73.0 %copy-start.4 = (bf16[2,96,1536]{2,1,0:T(8,128)(2,1)S(1)}, bf16[2,96,1536]{2,1,0:T(8,128)(2,1)}, u32[]{:S(2)}) copy-start(bf16[2,96,1536]{2,1,0:T(8,128)(2,1)} %get-tuple-element.80.rows_ref) | copy-start | bytes 1769476
  231.6 73.0 %copy-start.6 = (bf16[2,4,48,384]{3,2,1,0:T(8,128)(2,1)S(1)}, bf16[2,4,48,384]{3,2,1,0:T(8,128)(2,1)}, u32[]{:S(2)}) copy-start(bf16[2,4,48,384]{3,2,1,0:T(8,128)(2,1)} %get-tuple-element.78) | copy-start | bytes 884740
  304.7 1.1 copy-start.2
  305.8 1.1 copy-start.3
  306.9 1.1 copy-start.5
  308.0 0.9 copy-start.7

commit v10 on v9

--- a/solution.py
+++ b/solution.py
@@ -467,6 +467,12 @@
         )
 
     dh_chunks = [give_chunk(low) for low in range(half)]
+
+    def add_chunk(low):
+        dh_chunks[low].wait_recv()
+        for q in range(seqs):
+            add_rows(dh_own.at[q, low], dh_own.at[q, low], dh_first.at[q, low])
+
     dh_store = links.local(lambda: (dh_own, dh_out))
     stages = len(place.low_bits)
 
@@ -476,11 +482,11 @@
         pz_load.start()
         meet_pair(place)
         z_part.send_pairs(1, 0)
+        mixed.add_cores()
+        mixed.send_stage(0)
 
     @pl.when(step_at == 1)
     def _():
-        mixed.add_cores()
-        mixed.send_stage(0)
         z_part.send_pairs(0, 0)
 
     @pl.when(step_at == 2)
@@ -502,7 +508,7 @@
     def _():
         z_part.spread()
 
-    @pl.when(step_at == pl.num_programs(0) - 3)
+    @pl.when(step_at == pl.num_programs(0) - 4)
     def _():
         mixed.add_stage(0)
         if stages > 1:
@@ -639,6 +645,12 @@
         def _():
             dh_own[:, chunk % half] = grad_h
 
+        if i + 1 < seq:
+
+            @pl.when((step_at == i + 1) & (place.core == chunk // half))
+            def _():
+                add_chunk(chunk % half)
+
         @pl.when((step_at == i) & (place.core != chunk // half))
         def _():
             dh_give[:, chunk % half] = grad_h
@@ -657,11 +669,13 @@
             done[...] = (done[...].astype(F32) * column).astype(BF16)
         mixed.store()
         z_part.finish()
+
+        @pl.when(place.core == 0)
+        def _():
+            add_chunk(0)
+
         for copy in dh_chunks:
-            copy.wait()
-        for q in range(seqs):
-            for low in range(half):
-                add_rows(dh_own.at[q, low], dh_own.at[q, low], dh_first.at[q, low])
+            copy.wait_send()
         dh_store.start()
         dh_store.wait()
         w_rows.finish()
@@ -672,6 +686,7 @@
 AXES = ("seq", "fsdp")
 MESH = pl.DeviceIdType.MESH
 ANYWHERE = pl.BlockSpec(memory_space=pl.ANY)
+IN_HBM = pl.BlockSpec(memory_space=pltpu.HBM)
 
 
 def lane_rows(width):
@@ -707,8 +722,8 @@
 def forward_mix(normed, zx, tail, segments, cotangent, out_w, packed, seq, fsdp):
     seqs, length, depth = normed.shape
     rows = tail.shape[0]
-    cols = zx.shape[2] + TAIL
-    width = zx.shape[2] // 2
+    width = INNER // seq
+    cols = 2 * width + TAIL
     pairs = fsdp // 2
     count = seqs * seq * length
 
@@ -917,6 +932,23 @@
         self.make().wait_recv()
 
 
+class Copies:
+    def __init__(self, copies):
+        self.copies = copies
+
+    def start(self):
+        for copy in self.copies:
+            copy.start()
+
+    def wait_recv(self):
+        for copy in self.copies:
+            copy.wait_recv()
+
+    def wait_send(self):
+        for copy in self.copies:
+            copy.wait_send()
+
+
 class Links:
     def __init__(self, send, recv, near):
         self.send, self.recv, self.near = send, recv, near
@@ -1118,7 +1150,7 @@
 class Entry:
     def __init__(self, place, links, h_ref, zx_ref, tail_ref, seg_ref, h_v, w_v, seg_v):
         self.place = place
-        cols = zx_ref.shape[2]
+        cols = zx_ref.shape[-1]
         self.peers = peers = peers_of(place)
         others = range(1, place.pairs)
         self.tokens = TokenGather(place, links, h_ref, h_v)
@@ -1127,20 +1159,38 @@
             s, f = place.at(top=t, low=l, core=c)
             return w_v.at[s, place.pair, lax.rem(f, 2)]
 
-        def columns(ref):
+        direct = len(zx_ref.shape) == 2
+        if direct:
+            cols = w_v.shape[4] - TAIL
+        width = cols // 2
+
+        def source(group, part):
+            if direct:
+                return zx_ref.at[:, pl.ds(pl.multiple_of(part * INNER + group * width, LANES), width)]
+            return zx_ref.at[group]
+
+        def columns(ref, part):
+            if direct:
+                return ref.at[:, pl.ds(part * width, width)]
             return ref.at[:, pl.ds(0, cols)]
 
         def tail_of(ref):
             return ref.at[:, pl.ds(cols, TAIL)]
 
-        def send_zx(t, l, c):
+        def send_zx(part, t, l, c):
             group = flip(place.core, c) * place.half + flip(place.low, l)
-            return zx_ref.at[group], columns(block()), place.at(top=t, low=l, core=c)
-
-        self.zx = {p: links.far(functools.partial(send_zx, *p)) for p in peers}
-        self.own = [
-            links.local(lambda: (zx_ref.at[place.chunk], columns(block()))),
-            links.local(lambda: (tail_ref, tail_of(block()))),
+            return source(group, part), columns(block(), part), place.at(top=t, low=l, core=c)
+
+        def keep_zx(part):
+            return links.local(lambda: (source(place.chunk, part), columns(block(), part)))
+
+        parts = (0, 1) if direct else (0,)
+        self.zx = {
+            p: Copies([links.far(functools.partial(send_zx, part, *p)) for part in parts])
+            for p in peers
+        }
+        self.own = [keep_zx(part) for part in parts] + [
+            links.local(lambda: (tail_ref, tail_of(block())))
         ]
         self.tail_cross = links.far(lambda: (tail_ref, tail_of(block()), place.at(top=1)))
         self.near_peers = [(l, c) for t, l, c in peers if t == 0]
@@ -1238,13 +1288,13 @@
     step = next((size for size in (rows, 16) if total % size == 0), total)
 
     if step == total:
-        out[...] = (left[...].astype(F32) + right[...].astype(F32)).astype(out.dtype)
+        out[...] = left[...] + right[...]
         return
 
     @pl.loop(0, total // step)
     def _(i):
         at = pl.ds(pl.multiple_of(i * step, step), step)
-        out[at] = (left[at].astype(F32) + right[at].astype(F32)).astype(out.dtype)
+        out[at] = left[at] + right[at]
 
 
 class TokenScatter:
@@ -1660,20 +1710,21 @@
 
 def finish_kernel(
     seq,
-    tok_ref, cot_ref, gain_ref, dh_ref, mixed_ref, slots_z_ref, slots_ref, rows_ref, vec_ref,
+    tok_in, cot_in, gain_ref, dh_in, mixed_in, slots_z_in, slots_in, rows_in, vec_in,
     mixed_out, tokens_out, gain_in_out, w_in_out, conv_w_out, conv_b_out, heads_out, gain_out_out,
     w_out_out,
+    tok_ref, cot_ref, dh_ref, mixed_ref, slots_z_ref, slots_ref, rows_ref, vec_ref, near,
 ):
+    pairs = [
+        (slots_z_in, slots_z_ref), (slots_in, slots_ref), (rows_in, rows_ref), (vec_in, vec_ref),
+        (tok_in, tok_ref), (dh_in, dh_ref), (mixed_in, mixed_ref), (cot_in, cot_ref),
+    ]
+    loads = [pltpu.make_async_copy(*pair, near.at[i]) for i, pair in enumerate(pairs)]
+    for copy in loads:
+        copy.start()
     gain = gain_ref[...]
-    for q in range(tok_ref.shape[0]):
-        wide = tok_ref[q].astype(F32)
-        mixed_out[q] = (wide + mixed_ref[q].astype(F32)).astype(BF16)
-        scale = lax.rsqrt(jnp.mean(wide * wide, axis=-1, keepdims=True) + EPSILON)
-        unit = wide * scale
-        scaled = dh_ref[q].astype(F32) * gain
-        tokens_out[q] = cot_ref[q].astype(F32) + scale * (
-            scaled - unit * jnp.mean(scaled * unit, axis=-1, keepdims=True)
-        )
+    for copy in loads[:4]:
+        copy.wait()
     groups, _, cols = slots_ref.shape
     width = cols - TAIL
     tail = jnp.zeros((slots_ref.shape[1], TAIL), F32)
@@ -1722,6 +1773,17 @@
         lines = jnp.where(lane < heads, lines, 0.0)
         per_head = per_head + (pltpu.roll(lines, g * heads, 1) if g else lines)
     heads_out[...] = per_head
+    for copy in loads[4:]:
+        copy.wait()
+    for q in range(tok_ref.shape[0]):
+        wide = tok_ref[q].astype(F32)
+        mixed_out[q] = (wide + mixed_ref[q].astype(F32)).astype(BF16)
+        scale = lax.rsqrt(jnp.mean(wide * wide, axis=-1, keepdims=True) + EPSILON)
+        unit = wide * scale
+        scaled = dh_ref[q].astype(F32) * gain
+        tokens_out[q] = cot_ref[q].astype(F32) + scale * (
+            scaled - unit * jnp.mean(scaled * unit, axis=-1, keepdims=True)
+        )
 
 
 def finish(seq, tokens, cotangent, gain_in, grad_h, mixed, slots_z, slots, rows, vector, shapes):
@@ -1731,10 +1793,14 @@
         ((KERNEL, columns), F32), ((1, columns), F32), ((8, LANES), F32), ((1, INNER), F32),
         (shapes[1], F32),
     ]
+    arrays = (tokens, cotangent, grad_h, mixed, slots_z, slots, rows, vector)
     return pl.pallas_call(
         functools.partial(finish_kernel, seq),
+        in_specs=[IN_HBM] * 2 + [pl.BlockSpec(memory_space=pltpu.VMEM)] + [IN_HBM] * 6,
+        scratch_shapes=[pltpu.VMEM(v.shape, v.dtype) for v in arrays]
+        + [pltpu.SemaphoreType.DMA((len(arrays),))],
         out_shape=[jax.ShapeDtypeStruct(*kind) for kind in kinds],
-        compiler_params=pltpu.CompilerParams(vmem_limit_bytes=32 << 20),
+        compiler_params=pltpu.CompilerParams(vmem_limit_bytes=62 << 20),
         name="finish",
     )(tokens, cotangent, gain_in[None], grad_h, mixed, slots_z, slots, rows, vector)
 
@@ -1752,8 +1818,10 @@
     wide = tokens.astype(F32)
     scale_in = lax.rsqrt(jnp.mean(wide * wide, axis=-1, keepdims=True) + EPSILON)
     normed = (wide * scale_in * gain_in).astype(BF16)
-    zx = w_in[:, : 2 * INNER].reshape(rows_in, 2, steps, width).transpose(2, 0, 1, 3)
-    zx = zx.reshape(steps, rows_in, 2 * width)
+    zx = w_in
+    if width % LANES:
+        zx = w_in[:, : 2 * INNER].reshape(rows_in, 2, steps, width).transpose(2, 0, 1, 3)
+        zx = zx.reshape(steps, rows_in, 2 * width)
     tail = jnp.pad(w_in[:, 2 * INNER :], ((0, 0), (0, LANES - HEADS)))
     columns = INNER + 2 * STATE
 

time: 315 us -> 313 us (level)
  local copies, waits for them, and re-layouts: 10.2 us -> 5.58 us
  other arithmetic: 3.39 us -> 6.63 us
    unnamed x19 -> x4, local copies, waits for them, and re-layouts: 4.35 us -> 0.01 us
where the time goes in v10:
time: 313 us; the launch traced here: 312 us
  Pallas kernels  299 us (96%)
  other arithmetic  6.63 us (2%)
  local copies, waits for them, and re-layouts  5.58 us (2%)
    pallas_call x1, Pallas kernels, forward_mix(): pl.pallas_call(functools.partial(forward_kernel, seq, fsdp), grid=(seq +...  161 us
    pallas_call x1, Pallas kernels, exit_scatter(): pl.pallas_call(functools.partial(exit_kernel, seq, fsdp), in_specs=[ANYWH...  71.8 us
    pallas_call x1, Pallas kernels, backward_mix(): pl.pallas_call(functools.partial(backward_kernel, seq, fsdp), grid=(steps...  61.1 us

profile of v10, /device:TPU:1, one launch (start us, length us, event | category | flops | bytes accessed | tf_op | source)
XLA Modules:
  0.0 312.2 jit_solution(6499063868701301385)
XLA Ops:
  0.6 0.0 copy-start
  0.7 0.0 slice-start
  0.7 0.8 select_maximum_fusion
  1.5 0.7 pad.23
  2.2 0.7 stack.9
  2.9 1.5 concatenate.7.pack_ref.ct_ref
  4.5 1.4 fusion
  5.9 0.0 copy-done
  5.9 1.8 fusion.2.h_ref
  7.7 0.0 slice-done
  7.7 0.6 pad.22.tail_ref
  8.3 161.3 %mix_forward.1 = (bf16[2,8,128,1152]{3,2,1,0:T(8,128)(2,1)}, bf16[2,8,128,384]{3,2,1,0:T(8,128)(2,1)}, f32[2,8,128,1]{3,2,1,0:T(8,128)}, f32[2,8,128,1]{3,2,1,0:...) custom-call(bf16[2,128,1536]{2,1,0:T(8,128)(2,1)} %fusion.2.h_ref, ...), custom_call_target="tpu_custom_call" | custom-call | flops 30000001024 | bytes 60000000 | tf_op jit(solution)/shard_map/mix_forward/pallas_call | solution.py:743
  169.6 61.1 %mix_backward.1 = (bf16[2,8,128,768]{3,2,1,0:T(8,128)(2,1)}, f32[8,384]{1,0:T(8,128)}, f32[8,256]{1,0:T(8,128)}, f32[8,128]{1,0:T(8,128)}, bf16[2,128,1536]{2,1,...) custom-call(bf16[2,8,128,1152]{3,2,1,0:T(8,128)(2,1)} %get-tuple-ele, ...), custom_call_target="tpu_custom_call" | custom-call | flops 32000000000 | bytes 16000000 | tf_op jit(solution)/shard_map/mix_backward/pallas_call | solution.py:831
  230.7 0.0 copy-start.1
  230.7 71.8 %exit_scatter.1 = (bf16[2,128,1536]{2,1,0:T(8,128)(2,1)}, bf16[2,128,1536]{2,1,0:T(8,128)(2,1)}, bf16[2,4,48,768]{3,2,1,0:T(8,128)(2,1)}, f32[2,4,48,128]{3,2,1,0:T(8,128)}) custom-call(bf16[2048,1536]{1,0:T(8,128)(2,1)} %bitcast.16, bf16[2,4,128,1536]{3,2,1,0:T(8,128)(2,1)} %get-tuple-element.68.dh_ref, bf16[2048,768]{1,0:T(8,128)(2,1)} %bitcast.19, ...), custom_call_target="tpu_custom_call" | custom-call | bytes 200000000 | tf_op jit(solution)/shard_map/exit_scatter/pallas_call | solution.py:1674
  302.5 0.0 copy-done.1
  302.5 0.6 broadcast_in_dim.2.gain_ref
  303.1 5.2 %finish.1 = (bf16[2,128,1536]{2,1,0:T(8,128)(2,1)}, f32[2,128,1536]{2,1,0:T(8,128)}, f32[1,1536]{1,0:T(1,128)}, f32[48,6448]{1,0:T(8,128)}, f32[4,3328]{1,0:T(4,...) custom-call(bf16[2,128,1536]{2,1,0:T(8,128)(2,1)} %tok_in.1, ...), custom_call_target="tpu_custom_call" | custom-call | tf_op jit(solution)/shard_map/finish/pallas_call | solution.py:1797
  308.3 1.4 reduce.1
  309.6 1.3 reduce
  310.9 1.3 slice_bitcast_fusion
  (5 shorter events, 0.0 us)
Async XLA Ops:
  0.6 5.2 %copy-start = (bf16[2,128,1536]{2,1,0:T(8,128)(2,1)S(1)}, bf16[2,128,1536]{2,1,0:T(8,128)(2,1)}, u32[]{:S(2)}) copy-start(bf16[2,128,1536]{2,1,0:T(8,128)(2,1)} %tok_in.1) | copy-start | bytes 2359300
  0.7 7.0 %slice-start = ((bf16[48,6448]{1,0:T(8,128)(2,1)}), bf16[48,304]{1,0:T(8,128)(2,1)S(1)}, s32[]{:S(2)}) async-start(bf16[48,6448]{1,0:T(8,128)(2,1)} %zx_ref.1), calls=%async_computation | async-start | bytes 73728 | tf_op jit(solution)/shard_map/slice | solution.py:1825
  230.7 71.8 %copy-start.1 = (f32[1536]{0:T(1024)S(1)}, f32[1536]{0:T(1024)}, u32[]{:S(2)}) copy-start(f32[1536]{0:T(1024)} %param.14) | copy-start | bytes 18436

commit v11 on v10

--- a/solution.py
+++ b/solution.py
@@ -249,7 +249,7 @@
         def _():
             cot.pass_on(i, "away")
 
-    @pl.when(step_at == seq - 2)
+    @pl.when(step_at == seq - 3)
     def _():
         w_rows.forward()
 

time: 313 us -> 306 us (0.978)
  Pallas kernels: 299 us -> 292 us
    pallas_call x1, Pallas kernels: 161 us -> 153 us  [forward_mix(): pl.pallas_call(functools.partial(forward_kernel, seq, fsdp), grid=(seq +...]
where the time goes in v11:
time: 306 us; the launch traced here: 305 us
  Pallas kernels  292 us (95%)
  other arithmetic  6.63 us (2%)
  local copies, waits for them, and re-layouts  5.58 us (2%)
    pallas_call x1, Pallas kernels, forward_mix(): pl.pallas_call(functools.partial(forward_kernel, seq, fsdp), grid=(seq +...  153 us
    pallas_call x1, Pallas kernels, exit_scatter(): pl.pallas_call(functools.partial(exit_kernel, seq, fsdp), in_specs=[ANYWH...  71.7 us
    pallas_call x1, Pallas kernels, backward_mix(): pl.pallas_call(functools.partial(backward_kernel, seq, fsdp), grid=(steps...  61.7 us

profile of v11, /device:TPU:1, one launch (start us, length us, event | category | flops | bytes accessed | tf_op | source)
XLA Modules:
  0.0 304.7 jit_solution(16944509927584967505)
XLA Ops:
  0.6 0.0 copy-start
  0.7 0.0 slice-start
  0.7 0.8 select_maximum_fusion
  1.5 0.7 pad.23
  2.2 0.7 stack.9
  2.9 1.5 concatenate.7.pack_ref.ct_ref
  4.5 1.4 fusion
  5.9 0.0 copy-done
  5.9 1.8 fusion.2.h_ref
  7.7 0.0 slice-done
  7.7 0.6 pad.22.tail_ref
  8.3 153.2 %mix_forward.1 = (bf16[2,8,128,1152]{3,2,1,0:T(8,128)(2,1)}, bf16[2,8,128,384]{3,2,1,0:T(8,128)(2,1)}, f32[2,8,128,1]{3,2,1,0:T(8,128)}, f32[2,8,128,1]{3,2,1,0:...) custom-call(bf16[2,128,1536]{2,1,0:T(8,128)(2,1)} %fusion.2.h_ref, ...), custom_call_target="tpu_custom_call" | custom-call | flops 30000001024 | bytes 60000000 | tf_op jit(solution)/shard_map/mix_forward/pallas_call | solution.py:743
  161.6 61.7 %mix_backward.1 = (bf16[2,8,128,768]{3,2,1,0:T(8,128)(2,1)}, f32[8,384]{1,0:T(8,128)}, f32[8,256]{1,0:T(8,128)}, f32[8,128]{1,0:T(8,128)}, bf16[2,128,1536]{2,1,...) custom-call(bf16[2,8,128,1152]{3,2,1,0:T(8,128)(2,1)} %get-tuple-ele, ...), custom_call_target="tpu_custom_call" | custom-call | flops 32000000000 | bytes 16000000 | tf_op jit(solution)/shard_map/mix_backward/pallas_call | solution.py:831
  223.3 0.0 copy-start.1
  223.3 71.7 %exit_scatter.1 = (bf16[2,128,1536]{2,1,0:T(8,128)(2,1)}, bf16[2,128,1536]{2,1,0:T(8,128)(2,1)}, bf16[2,4,48,768]{3,2,1,0:T(8,128)(2,1)}, f32[2,4,48,128]{3,2,1,0:T(8,128)}) custom-call(bf16[2048,1536]{1,0:T(8,128)(2,1)} %bitcast.16, bf16[2,4,128,1536]{3,2,1,0:T(8,128)(2,1)} %get-tuple-element.68.dh_ref, bf16[2048,768]{1,0:T(8,128)(2,1)} %bitcast.19, ...), custom_call_target="tpu_custom_call" | custom-call | bytes 200000000 | tf_op jit(solution)/shard_map/exit_scatter/pallas_call | solution.py:1674
  295.0 0.0 copy-done.1
  295.0 0.6 broadcast_in_dim.2.gain_ref
  295.6 5.2 %finish.1 = (bf16[2,128,1536]{2,1,0:T(8,128)(2,1)}, f32[2,128,1536]{2,1,0:T(8,128)}, f32[1,1536]{1,0:T(1,128)}, f32[48,6448]{1,0:T(8,128)}, f32[4,3328]{1,0:T(4,...) custom-call(bf16[2,128,1536]{2,1,0:T(8,128)(2,1)} %tok_in.1, ...), custom_call_target="tpu_custom_call" | custom-call | tf_op jit(solution)/shard_map/finish/pallas_call | solution.py:1797
  300.7 1.4 reduce.1
  302.1 1.3 reduce
  303.4 1.3 slice_bitcast_fusion
  (5 shorter events, 0.0 us)
Async XLA Ops:
  0.6 5.2 %copy-start = (bf16[2,128,1536]{2,1,0:T(8,128)(2,1)S(1)}, bf16[2,128,1536]{2,1,0:T(8,128)(2,1)}, u32[]{:S(2)}) copy-start(bf16[2,128,1536]{2,1,0:T(8,128)(2,1)} %tok_in.1) | copy-start | bytes 2359300
  0.7 7.0 %slice-start = ((bf16[48,6448]{1,0:T(8,128)(2,1)}), bf16[48,304]{1,0:T(8,128)(2,1)S(1)}, s32[]{:S(2)}) async-start(bf16[48,6448]{1,0:T(8,128)(2,1)} %zx_ref.1), calls=%async_computation | async-start | bytes 73728 | tf_op jit(solution)/shard_map/slice | solution.py:1825
  223.3 71.7 %copy-start.1 = (f32[1536]{0:T(1024)S(1)}, f32[1536]{0:T(1024)}, u32[]{:S(2)}) copy-start(f32[1536]{0:T(1024)} %param.14) | copy-start | bytes 18436

commit v12 on v11

--- a/solution.py
+++ b/solution.py
@@ -500,7 +500,7 @@
     def _():
         z_part.add_pairs(0, 0)
 
-    @pl.when(step_at == 5)
+    @pl.when(step_at == 4)
     def _():
         w_rows.add_pairs()
 

time: 306 us -> 309 us (level)
  no operation moved by 1% of the time
where the time goes in v12:
time: 309 us; the launch traced here: 308 us
  Pallas kernels  295 us (95%)
  other arithmetic  6.63 us (2%)
  local copies, waits for them, and re-layouts  5.58 us (2%)
    pallas_call x1, Pallas kernels, forward_mix(): pl.pallas_call(functools.partial(forward_kernel, seq, fsdp), grid=(seq +...  153 us
    pallas_call x1, Pallas kernels, exit_scatter(): pl.pallas_call(functools.partial(exit_kernel, seq, fsdp), in_specs=[ANYWH...  73.2 us
    pallas_call x1, Pallas kernels, backward_mix(): pl.pallas_call(functools.partial(backward_kernel, seq, fsdp), grid=(steps...  63.5 us

profile of v12, /device:TPU:1, one launch (start us, length us, event | category | flops | bytes accessed | tf_op | source)
XLA Modules:
  0.0 308.0 jit_solution(4488558658965075999)
XLA Ops:
  0.6 0.0 copy-start
  0.7 0.0 slice-start
  0.7 0.8 select_maximum_fusion
  1.5 0.7 pad.23
  2.2 0.7 stack.9
  2.9 1.5 concatenate.7.pack_ref.ct_ref
  4.5 1.4 fusion
  5.9 0.0 copy-done
  5.9 1.8 fusion.2.h_ref
  7.7 0.0 slice-done
  7.7 0.6 pad.22.tail_ref
  8.3 153.2 %mix_forward.1 = (bf16[2,8,128,1152]{3,2,1,0:T(8,128)(2,1)}, bf16[2,8,128,384]{3,2,1,0:T(8,128)(2,1)}, f32[2,8,128,1]{3,2,1,0:T(8,128)}, f32[2,8,128,1]{3,2,1,0:...) custom-call(bf16[2,128,1536]{2,1,0:T(8,128)(2,1)} %fusion.2.h_ref, ...), custom_call_target="tpu_custom_call" | custom-call | flops 30000001024 | bytes 60000000 | tf_op jit(solution)/shard_map/mix_forward/pallas_call | solution.py:743
  161.6 63.5 %mix_backward.1 = (bf16[2,8,128,768]{3,2,1,0:T(8,128)(2,1)}, f32[8,384]{1,0:T(8,128)}, f32[8,256]{1,0:T(8,128)}, f32[8,128]{1,0:T(8,128)}, bf16[2,128,1536]{2,1,...) custom-call(bf16[2,8,128,1152]{3,2,1,0:T(8,128)(2,1)} %get-tuple-ele, ...), custom_call_target="tpu_custom_call" | custom-call | flops 32000000000 | bytes 16000000 | tf_op jit(solution)/shard_map/mix_backward/pallas_call | solution.py:831
  225.1 0.0 copy-start.1
  225.1 73.2 %exit_scatter.1 = (bf16[2,128,1536]{2,1,0:T(8,128)(2,1)}, bf16[2,128,1536]{2,1,0:T(8,128)(2,1)}, bf16[2,4,48,768]{3,2,1,0:T(8,128)(2,1)}, f32[2,4,48,128]{3,2,1,0:T(8,128)}) custom-call(bf16[2048,1536]{1,0:T(8,128)(2,1)} %bitcast.16, bf16[2,4,128,1536]{3,2,1,0:T(8,128)(2,1)} %get-tuple-element.68.dh_ref, bf16[2048,768]{1,0:T(8,128)(2,1)} %bitcast.19, ...), custom_call_target="tpu_custom_call" | custom-call | bytes 200000000 | tf_op jit(solution)/shard_map/exit_scatter/pallas_call | solution.py:1674
  298.3 0.0 copy-done.1
  298.3 0.6 broadcast_in_dim.2.gain_ref
  298.9 5.2 %finish.1 = (bf16[2,128,1536]{2,1,0:T(8,128)(2,1)}, f32[2,128,1536]{2,1,0:T(8,128)}, f32[1,1536]{1,0:T(1,128)}, f32[48,6448]{1,0:T(8,128)}, f32[4,3328]{1,0:T(4,...) custom-call(bf16[2,128,1536]{2,1,0:T(8,128)(2,1)} %tok_in.1, ...), custom_call_target="tpu_custom_call" | custom-call | tf_op jit(solution)/shard_map/finish/pallas_call | solution.py:1797
  304.1 1.4 reduce.1
  305.4 1.3 reduce
  306.7 1.3 slice_bitcast_fusion
  (5 shorter events, 0.0 us)
Async XLA Ops:
  0.6 5.2 %copy-start = (bf16[2,128,1536]{2,1,0:T(8,128)(2,1)S(1)}, bf16[2,128,1536]{2,1,0:T(8,128)(2,1)}, u32[]{:S(2)}) copy-start(bf16[2,128,1536]{2,1,0:T(8,128)(2,1)} %tok_in.1) | copy-start | bytes 2359300
  0.7 7.0 %slice-start = ((bf16[48,6448]{1,0:T(8,128)(2,1)}), bf16[48,304]{1,0:T(8,128)(2,1)S(1)}, s32[]{:S(2)}) async-start(bf16[48,6448]{1,0:T(8,128)(2,1)} %zx_ref.1), calls=%async_computation | async-start | bytes 73728 | tf_op jit(solution)/shard_map/slice | solution.py:1825
  225.1 73.2 %copy-start.1 = (f32[1536]{0:T(1024)S(1)}, f32[1536]{0:T(1024)}, u32[]{:S(2)}) copy-start(f32[1536]{0:T(1024)} %param.14) | copy-start | bytes 18436
